TPU v7x, 32 devices: a whole 2x2x4 slice. The times are simulated.
32 devices in a mesh: grp: 2 (over y), seq: 4 (over z), head: 2 (over x), sub: 2 (over core).
Axes of the slice: x: 2, y: 2, z: 4, core: 2. Of those that a mesh axis runs over, the one named last changes fastest.
Arguments:
- token_ids: int32 [1024], P(('grp', 'seq')), parts along dimension 0, may hold values from 0 to 4, as said below
- basemap: int32 [5], replicated, may hold values from 0 to 4, as said below
- xz_table: bfloat16 [5, 2, 2048], P(None, None, 'head'), may hold values from -6 to 6
- bc_table: bfloat16 [5, 2, 128], replicated, may hold values from -6 to 6
- dt_table: float32 [5, 32], P(None, 'head')
- conv_x: bfloat16 [4, 2048], P(None, 'head'), may hold values from -3 to 3
- conv_bc: bfloat16 [4, 2, 128], replicated, may hold values from -3 to 3
- a_log: float32 [32], P('head'), may hold values from -0.7 to 0.7
- skip_gain: float32 [32], P('head'), may hold values from 0.5 to 1.5
- out_weight: bfloat16 [2048, 1024], P('head'), may hold values from -0.125 to 0.125
- cotangent: bfloat16 [1024, 1024], P(('grp', 'seq'), ('head', 'sub')), parts along dimension 0, may hold values from -0.3125 to 0.3125
Outputs:
- layer_out: bfloat16 [1024, 1024], P(('grp', 'seq'), ('head', 'sub')), parts along dimension 0
- d_out_weight: float32 [4096, 1024], P(('grp', 'head')), parts along dimension 0
- d_xz_table: float32 [10, 2, 2048], P('grp', None, 'head'), parts along dimension 0
- d_bc_table: float32 [10, 2, 128], P('grp'), parts along dimension 0
- d_dt_table: float32 [10, 32], P('grp', 'head'), parts along dimension 0
There are 2 independent parts, one for each index of `grp`. A program takes and returns all parts, laid end to end along the dimension named above; an argument that names none is the same for every part. Nothing has to cross between parts.
Inputs may be any that keep to these rules, and one draw needn't show every extreme that they name: `token_ids`: exactly 3 positions hold 4; every other position holds 0 to 3. `basemap`: entry 4 is 4; entries 0 to 3 are a permutation of 0 to 3.
All inputs are finite; a program needn't handle non-finite values.
Results may differ from a plain program's by a relative error of at most 0.0049.
Values may be sent and summed in bfloat16 or wider, within the bound.
No kernel may reach another device: no remote copies, remote signals or barrier semaphores. Data moves between devices by JAX's collectives and lax.ppermute only.
A program may use at most 128 MiB of HBM per device.

v0:
```python
import functools

import jax
import jax.numpy as jnp
from jax import lax
from jax.experimental import pallas as pl
from jax.experimental.pallas import tpu as pltpu
from jax.sharding import PartitionSpec as P

BLOCK = 128
LANES = 128
SYM = 8
F32 = jnp.float32
BF16 = jnp.bfloat16
NN = (((1,), (0,)), ((), ()))
NT = (((1,), (1,)), ((), ()))
TN = (((0,), (0,)), ((), ()))
X_ROW, Z_ROW, DT_ROW, MISC_ROW, TAB_ROWS = 0, 8, 16, 24, 32
VMEM_LIMIT = 56 * 1024 * 1024
XF, XB, ZZ, BCF, BCB, WIDE = 0, 128, 256, 384, 640, 896


def mm(a, b, dims):
    return lax.dot_general(a, b, dims, preferred_element_type=F32)


def halves(a):
    top = a.astype(BF16)
    return top, (a - top.astype(F32)).astype(BF16)


def thirds(a):
    top = a.astype(BF16).astype(F32)
    rest = a - top
    mid = rest.astype(BF16).astype(F32)
    return top, mid, rest - mid


def mm_fine(a, b, dims, terms):
    ah, al = halves(a)
    bh, bl = halves(b)
    (ca,), (cb,) = dims[0]
    left, right = [ah], [bh]
    if terms >= 2:
        left.append(al)
        right.append(bh)
    if terms >= 3:
        left.append(ah)
        right.append(bl)
    return mm(jnp.concatenate(left, ca), jnp.concatenate(right, cb), dims)


def permuted(table, scalars, count):
    row = lax.broadcasted_iota(jnp.int32, table[:SYM].shape, 0)
    out = jnp.zeros_like(table[:SYM])
    for k in range(count):
        picked = jnp.zeros_like(table[0:1])
        for m in range(count):
            picked = jnp.where(scalars[2 + k] == m, table[m : m + 1], picked)
        out = jnp.where(row == k, picked, out)
    return out


def sigmoid(v):
    return 1.0 / (1.0 + jnp.exp(-v))


def prepare(scalars, tok_refs, tabs_ref, bcp_ref, r, conv, vocab):
    ns = len(tok_refs)
    length = ns * BLOCK
    mine = scalars[1]
    for k in range(ns):
        at = jnp.where(mine >= k, mine - k, mine - k + ns)
        sym = lax.broadcasted_iota(jnp.int32, (SYM, BLOCK), 0)
        tok = jnp.broadcast_to(tok_refs[k][...], (SYM, BLOCK))
        r.oh[:, pl.ds(pl.multiple_of(at * BLOCK, BLOCK), BLOCK)] = (sym == tok).astype(F32)
    oh = r.oh[...]
    lane = lax.broadcasted_iota(jnp.int32, (SYM, length), 1)
    up = (
        lax.broadcasted_iota(jnp.int32, (BLOCK, BLOCK), 0)
        <= lax.broadcasted_iota(jnp.int32, (BLOCK, BLOCK), 1)
    ).astype(BF16)
    r.rows[...] = jnp.zeros_like(r.rows)
    for d in range(1 - conv, conv):
        shifted = oh if d == 0 else pltpu.roll(oh, (length - d) % length, 1)
        inside = jnp.logical_and(lane + d >= 0, lane + d < length)
        r.rows[SYM * (d + conv - 1) : SYM * (d + conv), :] = jnp.where(inside, shifted, 0.0)
    r.rows[64:128, :] = r.rows[0:64, :]
    oh_b = oh.astype(BF16)
    for b in range(ns):
        cols = slice(b * BLOCK, (b + 1) * BLOCK)
        inc = mm(oh_b[:, cols], up, NN)
        exc = inc - oh[:, cols]
        r.inc[:, cols] = inc
        r.exc[:, cols] = exc
        for k in range(3):
            r.rows[128 + SYM * k : 128 + SYM * (k + 1), cols] = inc
            r.rows[160 + SYM * k : 160 + SYM * (k + 1), cols] = exc
            r.rows[192 + SYM * k : 192 + SYM * (k + 1), cols] = oh[:, cols]
    r.wf[...] = jnp.zeros_like(r.wf)
    r.w2[...] = jnp.zeros_like(r.w2)
    for st in range(2):
        fetch = (lambda t: t) if st == 0 else (lambda t: permuted(t, scalars, vocab))
        xt = fetch(tabs_ref[X_ROW : X_ROW + SYM, :])
        zt = fetch(tabs_ref[Z_ROW : Z_ROW + SYM, :])
        dtt = fetch(tabs_ref[DT_ROW : DT_ROW + SYM, :])
        bct = fetch(bcp_ref[0:SYM, :])
        base = st * WIDE
        mid = SYM * (conv - 1)
        r.wf[mid : mid + SYM, base + ZZ : base + ZZ + LANES] = zt
        for k in range(conv):
            cx = tabs_ref[MISC_ROW + k : MISC_ROW + k + 1, :]
            cbc = bcp_ref[SYM + k : SYM + k + 1, :]
            lo, hi = mid - SYM * k, mid + SYM * k
            r.wf[lo : lo + SYM, base + XF : base + XF + LANES] = xt * cx
            r.wf[hi : hi + SYM, base + XB : base + XB + LANES] = xt * cx
            r.wf[lo : lo + SYM, base + BCF : base + BCF + 256] = bct * cbc
            r.wf[hi : hi + SYM, base + BCB : base + BCB + 256] = bct * cbc
        dt = jnp.maximum(dtt, 0.0) + jnp.log1p(jnp.exp(-jnp.abs(dtt)))
        ld = -jnp.exp(tabs_ref[MISC_ROW + 4 : MISC_ROW + 5, :]) * dt
        ld0 = jnp.broadcast_to(ld[:, 0:1], ld.shape)
        ld1 = jnp.broadcast_to(ld[:, 64:65], ld.shape)
        for i, t in enumerate((ld, ld0, ld1)):
            for k, piece in enumerate(thirds(t)):
                c = st * 384 + i * 128
                r.w2[SYM * k : SYM * (k + 1), c : c + 128] = piece
                r.w2[32 + SYM * k : 32 + SYM * (k + 1), 768 + c : 768 + c + 128] = piece
        for k, piece in enumerate(thirds(dt)):
            c = 1536 + st * 128
            r.w2[64 + SYM * k : 64 + SYM * (k + 1), c : c + 128] = piece
    wh, wl = halves(r.wf[...])
    turned = jnp.transpose(r.rows[...]).astype(BF16)
    r.pre[...] = mm(turned[:, 0:128], jnp.concatenate([wh, wl], 0), NN)
    w2 = r.w2[...].astype(BF16)
    r.pd[...] = mm(turned[:, 128:256], w2, NN)
    for st in range(2):
        for part, row0 in ((0, 0), (1, 32)):
            c = part * 768 + st * 384
            flat = mm(
                w2[row0 : row0 + 32, c : c + 128],
                r.rows[128 + row0 : 160 + row0, :].astype(BF16),
                TN,
            )
            for h in range(2):
                i = part * 4 + st * 2 + h
                r.prow[i : i + 1, :] = flat[64 * h : 64 * h + 1, :]


class Unit:
    def __init__(self, r, tabs_ref, st, b, nb):
        self.rows = rows = slice(b * BLOCK, (b + 1) * BLOCK)
        base = st * WIDE
        self.skip = tabs_ref[MISC_ROW + 5 : MISC_ROW + 6, :]
        self.dt = r.pd[rows, 1536 + st * 128 : 1536 + st * 128 + 128]
        self.p = r.pd[rows, st * 384 : st * 384 + 128]
        self.q = r.pd[rows, 768 + st * 384 : 768 + st * 384 + 128]
        self.total = self.p[BLOCK - 1 : BLOCK, :]
        self.r, self.st, self.b, self.base = r, st, b, base
        lane = lax.broadcasted_iota(jnp.int32, (BLOCK, LANES), 1)
        self.head0 = lane < 64
        row = lax.broadcasted_iota(jnp.int32, (BLOCK, BLOCK), 0)
        self.low = row >= lane
        self.upp = row <= lane

    def pre(self, col, width):
        return self.r.pre[self.rows, self.base + col : self.base + col + width]

    def act(self, col, width):
        v = self.pre(col, width)
        return v * sigmoid(v)

    def by_head(self, v):
        zero = jnp.zeros_like(v)
        return jnp.where(self.head0, v, zero), jnp.where(self.head0, zero, v)

    def decay(self, h):
        r, st = self.r, self.st
        c = st * 384 + 128 * (h + 1)
        pc = r.pd[self.rows, c : c + 128]
        qc = r.pd[self.rows, 768 + c : 768 + c + 128]
        pr = r.prow[st * 2 + h : st * 2 + h + 1, self.rows]
        qr = r.prow[4 + st * 2 + h : 4 + st * 2 + h + 1, self.rows]
        return jnp.exp(jnp.where(self.low, pc - pr, qr - qc))


def state_pass_fwd(r, tabs_ref, nb, units):
    for st in range(2):
        for b in range(nb):
            u = units[st][b]
            xf, xb = u.act(XF, 128), u.act(XB, 128)
            bcf, bcb = u.act(BCF, 256), u.act(BCB, 256)
            r.x[u.rows, st * 256 : st * 256 + 128] = xf
            r.x[u.rows, st * 256 + 128 : st * 256 + 256] = xb
            r.bc[u.rows, st * 512 : st * 512 + 256] = bcf
            r.bc[u.rows, st * 512 + 256 : st * 512 + 512] = bcb
            wf = jnp.exp(u.total - u.p) * (u.dt * xf)
            wb = jnp.exp(u.q) * (u.dt * xb)
            if b < nb - 1:
                r.s[st * 2, b + 1] = mm_fine(bcf[:, 0:128], wf, TN, 2)
            if b > 0:
                r.s[st * 2 + 1, b - 1] = mm_fine(bcb[:, 0:128], wb, TN, 2)
        for b in range(2, nb):
            r.s[st * 2, b] += jnp.exp(units[st][b - 1].total) * r.s[st * 2, b - 1]
        for b in range(nb - 3, -1, -1):
            r.s[st * 2 + 1, b] += jnp.exp(units[st][b + 1].total) * r.s[st * 2 + 1, b + 1]


class Names:
    pass


def named(refs, names):
    r = Names()
    for name, ref in zip(names, refs):
        setattr(r, name, ref)
    return r


PREP_NAMES = ("oh", "inc", "exc", "rows", "wf", "w2", "pre", "pd", "prow", "x", "bc", "s")


def prep_scratch(length):
    nb = length // BLOCK
    v = pltpu.VMEM
    return [
        v((SYM, length), F32),
        v((SYM, length), F32),
        v((SYM, length), F32),
        v((256, length), F32),
        v((64, 2 * WIDE), F32),
        v((128, 1792), F32),
        v((length, 2 * WIDE), F32),
        v((length, 1792), F32),
        v((SYM, length), F32),
        v((length, 512), F32),
        v((length, 1024), F32),
        v((4, nb, LANES, LANES), F32),
    ]


def forward_kernel(scalars, *refs, ns, conv, vocab):
    tok_refs, (tabs_ref, bcp_ref, out_ref) = refs[:ns], refs[ns : ns + 3]
    r = named(refs[ns + 3 :], PREP_NAMES)
    prepare(scalars, tok_refs, tabs_ref, bcp_ref, r, conv, vocab)
    units = [[Unit(r, tabs_ref, st, b, ns) for b in range(ns)] for st in range(2)]
    state_pass_fwd(r, tabs_ref, ns, units)
    for b in range(ns):
        gated = []
        for st in range(2):
            u = units[st][b]
            xf = r.x[u.rows, st * 256 : st * 256 + 128]
            xb = r.x[u.rows, st * 256 + 128 : st * 256 + 256]
            left, right = [], []
            d0, d1 = u.decay(0), u.decay(1)
            y = u.skip * (xf + xb)
            for way, x, mask in ((0, xf, u.low), (1, xb, u.upp)):
                c = st * 512 + way * 256
                bm, cm = r.bc[u.rows, c : c + 128], r.bc[u.rows, c + 128 : c + 256]
                g = jnp.where(mask, mm_fine(cm, bm, NT, 3), 0.0)
                left += [(g * d0).astype(BF16), (g * d1).astype(BF16)]
                right += list(u.by_head((u.dt * x).astype(BF16)))
                if (way == 0 and b > 0) or (way == 1 and b < ns - 1):
                    enter = jnp.exp(u.p) if way == 0 else jnp.exp(u.total - u.q)
                    y = y + enter * mm_fine(cm, r.s[st * 2 + way, b], NN, 2)
            y = y + mm(jnp.concatenate(left, 1), jnp.concatenate(right, 0), NN)
            gated.append(y * u.act(ZZ, 128))
        out_ref[units[0][b].rows, :] = (gated[0] + gated[1]).astype(BF16)


def backward_kernel(scalars, *refs, ns, conv, vocab):
    tok_refs, (tabs_ref, bcp_ref) = refs[:ns], refs[ns : ns + 2]
    dg_refs, out_ref = refs[ns + 2 : 2 * ns + 2], refs[2 * ns + 2]
    r = named(refs[2 * ns + 3 :], PREP_NAMES + ("ds", "dg", "dpre"))
    prepare(scalars, tok_refs, tabs_ref, bcp_ref, r, conv, vocab)
    mine = scalars[1]
    for k in range(ns):
        at = jnp.where(mine >= k, mine - k, mine - k + ns)
        r.dg[pl.ds(pl.multiple_of(at * BLOCK, BLOCK), BLOCK), :] = dg_refs[k][...].astype(F32)
    units = [[Unit(r, tabs_ref, st, b, ns) for b in range(ns)] for st in range(2)]
    state_pass_fwd(r, tabs_ref, ns, units)
    for st in range(2):
        for b in range(ns):
            u = units[st][b]
            dy = r.dg[u.rows, :] * u.act(ZZ, 128)
            cf = r.bc[u.rows, st * 512 + 128 : st * 512 + 256]
            cb = r.bc[u.rows, st * 512 + 384 : st * 512 + 512]
            if b > 0:
                r.ds[st * 2, b - 1] = mm_fine(cf, jnp.exp(u.p) * dy, TN, 2)
            if b < ns - 1:
                r.ds[st * 2 + 1, b + 1] = mm_fine(cb, jnp.exp(u.total - u.q) * dy, TN, 2)
        for b in range(ns - 3, -1, -1):
            r.ds[st * 2, b] += jnp.exp(units[st][b + 1].total) * r.ds[st * 2, b + 1]
        for b in range(2, ns):
            r.ds[st * 2 + 1, b] += jnp.exp(units[st][b - 1].total) * r.ds[st * 2 + 1, b - 1]
    d_steps, d_decays = [], []
    for st in range(2):
        d_step = jnp.zeros((SYM, LANES), F32)
        d_decay = jnp.zeros((SYM, LANES), F32)
        for b in range(ns):
            u = units[st][b]
            base = st * WIDE
            x = [r.x[u.rows, st * 256 + w * 128 : st * 256 + w * 128 + 128] for w in range(2)]
            dgv = r.dg[u.rows, :]
            pz = u.pre(ZZ, 128)
            sz = sigmoid(pz)
            dy = dgv * (pz * sz)
            dyr = dy.astype(BF16)
            dyw = dyr.astype(F32)
            dy0, dy1 = u.by_head(dyr)
            decays = (u.decay(0), u.decay(1))
            inputs = [u.dt * v for v in x]
            ur = [v.astype(BF16) for v in inputs]
            uw = [v.astype(F32) for v in ur]
            uh = [u.by_head(v) for v in ur]
            d_pair = mm(dyr, jnp.concatenate([uh[0][0], uh[0][1], uh[1][0], uh[1][1]], 0), NT)
            masks = (u.low, u.upp)
            ends = (jnp.exp(u.total - u.p), jnp.exp(u.q))
            enters = (jnp.exp(u.p), jnp.exp(u.total - u.q))
            weights, bms, cms = [], [], []
            for w in range(2):
                c = st * 512 + w * 256
                bm, cm = r.bc[u.rows, c : c + 128], r.bc[u.rows, c + 128 : c + 256]
                g = jnp.where(masks[w], mm_fine(cm, bm, NT, 3), 0.0)
                weights.append([(g * decays[0]).astype(BF16), (g * decays[1]).astype(BF16)])
                bms.append(bm)
                cms.append(cm)
            du_both = mm(
                jnp.concatenate(
                    [
                        jnp.concatenate([weights[0][0], weights[1][0]], 1),
                        jnp.concatenate([weights[0][1], weights[1][1]], 1),
                    ],
                    0,
                ),
                jnp.concatenate([dy0, dy1], 0),
                TN,
            )
            y = u.skip * (x[0] + x[1])
            mixes, step_part, flat = [], 0.0, 0.0
            for w in range(2):
                inner = mm(
                    jnp.concatenate(weights[w], 1), jnp.concatenate([uh[w][0], uh[w][1]], 0), NN
                )
                du_in = du_both[w * BLOCK : (w + 1) * BLOCK]
                has_enter = (w == 0 and b > 0) or (w == 1 and b < ns - 1)
                has_leave = (w == 0 and b < ns - 1) or (w == 1 and b > 0)
                y = y + inner
                row = dyw * inner - uw[w] * du_in
                du = du_in
                d_g = jnp.where(
                    masks[w],
                    d_pair[:, w * 256 : w * 256 + 128] * decays[0]
                    + d_pair[:, w * 256 + 128 : w * 256 + 256] * decays[1],
                    0.0,
                ).astype(BF16)
                d_c = mm(d_g, bms[w].astype(BF16), NN)
                d_b = mm(d_g, cms[w].astype(BF16), TN)
                enter_part = gain_part = None
                if has_enter:
                    state = r.s[st * 2 + w, b]
                    carried = enters[w] * mm_fine(cms[w], state, NN, 2)
                    y = y + carried
                    enter_part = dy * carried
                    d_c = d_c + mm((enters[w] * dy).astype(BF16), state.astype(BF16), NT)
                if has_leave:
                    d_state = r.ds[st * 2 + w, b]
                    d_gain = mm_fine(bms[w], d_state, NN, 2)
                    du = du + ends[w] * d_gain
                    gain = ends[w] * inputs[w]
                    gain_part = gain * d_gain
                    d_b = d_b + mm(gain.astype(BF16), d_state.astype(BF16), NT)
                if has_enter and has_leave:
                    flat = flat + jnp.exp(u.total) * jnp.sum(state * d_state, 0, keepdims=True)
                if w == 1:
                    row = -row
                if enter_part is not None:
                    row = row + enter_part if w == 0 else row - enter_part
                if gain_part is not None:
                    row = row - gain_part if w == 0 else row + gain_part
                if w == 0 and gain_part is not None:
                    flat = flat + jnp.sum(gain_part, 0, keepdims=True)
                if w == 1 and enter_part is not None:
                    flat = flat + jnp.sum(enter_part, 0, keepdims=True)
                mixes.append(row)
                step_part = step_part + du * x[w]
                dx = du * u.dt + dy * u.skip
                px = u.pre((XF, XB)[w], 128)
                sx = sigmoid(px)
                col = base + (XF, XB)[w]
                r.dpre[u.rows, col : col + 128] = (dx * (sx * (1.0 + px * (1.0 - sx)))).astype(BF16)
                col = (BCF, BCB)[w]
                for i, grad in enumerate((d_b, d_c)):
                    pb = u.pre(col + 128 * i, 128)
                    sb = sigmoid(pb)
                    at = base + col + 128 * i
                    r.dpre[u.rows, at : at + 128] = (
                        grad * (sb * (1.0 + pb * (1.0 - sb)))
                    ).astype(BF16)
            d_z = dgv * y * (sz * (1.0 + pz * (1.0 - sz)))
            r.dpre[u.rows, base + ZZ : base + ZZ + 128] = d_z.astype(BF16)
            inc = r.inc[:, u.rows]
            exc = r.exc[:, u.rows]
            inc_b, exc_b, oh_b = inc.astype(BF16), exc.astype(BF16), r.oh[:, u.rows].astype(BF16)
            right = list(halves(mixes[0])) + list(halves(mixes[1]))
            d_decay = d_decay + mm(
                jnp.concatenate([inc_b, inc_b, exc_b, exc_b], 1), jnp.concatenate(right, 0), NN
            )
            d_decay = d_decay + inc[:, BLOCK - 1 : BLOCK] * flat
            d_step = d_step + mm(
                jnp.concatenate([oh_b, oh_b], 1), jnp.concatenate(halves(step_part), 0), NN
            )
        d_steps.append(d_step)
        d_decays.append(d_decay)
    d_tab = mm(r.rows[0:64, :].astype(BF16), r.dpre[...], NN)
    mid = SYM * (conv - 1)
    result = None
    for st in range(2):
        base = st * WIDE
        d_x = jnp.zeros((SYM, 128), F32)
        d_bc = jnp.zeros((SYM, 256), F32)
        for k in range(conv):
            cx = tabs_ref[MISC_ROW + k : MISC_ROW + k + 1, :]
            cbc = bcp_ref[SYM + k : SYM + k + 1, :]
            lo, hi = mid - SYM * k, mid + SYM * k
            d_x = d_x + cx * (
                d_tab[lo : lo + SYM, base + XF : base + XF + 128]
                + d_tab[hi : hi + SYM, base + XB : base + XB + 128]
            )
            d_bc = d_bc + cbc * (
                d_tab[lo : lo + SYM, base + BCF : base + BCF + 256]
                + d_tab[hi : hi + SYM, base + BCB : base + BCB + 256]
            )
        d_zt = d_tab[mid : mid + SYM, base + ZZ : base + ZZ + 128]
        dtt = tabs_ref[DT_ROW : DT_ROW + SYM, :]
        if st == 1:
            dtt = permuted(dtt, scalars, vocab)
        rate = -jnp.exp(tabs_ref[MISC_ROW + 4 : MISC_ROW + 5, :])
        d_dt = (d_steps[st] + rate * d_decays[st]) * sigmoid(dtt)
        wide = jnp.concatenate([d_x, d_zt, d_dt, d_bc], 1)
        if st == 0:
            result = wide
        else:
            row = lax.broadcasted_iota(jnp.int32, wide.shape, 0)
            for k in range(vocab):
                result = result + jnp.where(row == scalars[2 + k], wide[k : k + 1], 0.0)
    out_ref[...] = result


def call_forward(scalars, toks, tabs, bcp, conv, vocab):
    ns = len(toks)
    length = ns * BLOCK
    whole = lambda shape: pl.BlockSpec(shape, lambda i, s: (0,) * len(shape))
    return pl.pallas_call(
        functools.partial(forward_kernel, ns=ns, conv=conv, vocab=vocab),
        out_shape=jax.ShapeDtypeStruct((length, LANES), BF16),
        grid_spec=pltpu.PrefetchScalarGridSpec(
            num_scalar_prefetch=1,
            grid=(1,),
            in_specs=[whole((1, BLOCK))] * ns
            + [pl.BlockSpec((TAB_ROWS, LANES), lambda i, s: (0, s[0])), whole(bcp.shape)],
            out_specs=whole((length, LANES)),
            scratch_shapes=prep_scratch(length),
        ),
        compiler_params=pltpu.CompilerParams(vmem_limit_bytes=VMEM_LIMIT),
        name="mix_forward",
    )(scalars, *toks, tabs, bcp)


def call_backward(scalars, toks, tabs, bcp, d_gated, conv, vocab):
    ns = len(toks)
    length = ns * BLOCK
    whole = lambda shape: pl.BlockSpec(shape, lambda i, s: (0,) * len(shape))
    extra = [
        pltpu.VMEM((4, ns, LANES, LANES), F32),
        pltpu.VMEM((length, LANES), F32),
        pltpu.VMEM((length, 2 * WIDE), BF16),
    ]
    return pl.pallas_call(
        functools.partial(backward_kernel, ns=ns, conv=conv, vocab=vocab),
        out_shape=jax.ShapeDtypeStruct((SYM, 640), F32),
        grid_spec=pltpu.PrefetchScalarGridSpec(
            num_scalar_prefetch=1,
            grid=(1,),
            in_specs=[whole((1, BLOCK))] * ns
            + [pl.BlockSpec((TAB_ROWS, LANES), lambda i, s: (0, s[0])), whole(bcp.shape)]
            + [whole((BLOCK, LANES))] * ns,
            out_specs=whole((SYM, 640)),
            scratch_shapes=prep_scratch(length) + extra,
        ),
        compiler_params=pltpu.CompilerParams(vmem_limit_bytes=VMEM_LIMIT),
        name="mix_backward",
    )(scalars, *toks, tabs, bcp, *d_gated)


def weight_kernel(scalars, g_ref, cot_ref, out_ref, *, ns):
    mine = scalars[0]
    total = None
    for k in range(ns):
        at = jnp.where(mine >= k, mine - k, mine - k + ns)
        rows = g_ref[0, pl.ds(pl.multiple_of(at * BLOCK, BLOCK), BLOCK), :]
        part = mm(rows, cot_ref[k], TN)
        total = part if total is None else total + part
    out_ref[...] = total


def call_weight(scalars, gs, cots):
    slices, length, _ = gs.shape
    ns, _, columns = cots.shape
    return pl.pallas_call(
        functools.partial(weight_kernel, ns=ns),
        out_shape=jax.ShapeDtypeStruct((slices * LANES, columns), F32),
        grid_spec=pltpu.PrefetchScalarGridSpec(
            num_scalar_prefetch=1,
            grid=(slices,),
            in_specs=[
                pl.BlockSpec((1, length, LANES), lambda i, s: (i, 0, 0)),
                pl.BlockSpec((ns, BLOCK, columns), lambda i, s: (0, 0, 0)),
            ],
            out_specs=pl.BlockSpec((LANES, columns), lambda i, s: (s[1 + i], 0)),
        ),
        compiler_params=pltpu.CompilerParams(vmem_limit_bytes=VMEM_LIMIT),
        name="weight_grad",
    )(scalars, gs, cots)


def around(x, axis):
    n = lax.axis_size(axis)
    return [x] + [
        lax.ppermute(x, axis, [(i, (i + k) % n) for i in range(n)]) for k in range(1, n)
    ]


def by_channel(
    token_ids, basemap, xz_table, bc_table, dt_table, conv_x, conv_bc, a_log, skip_gain, out_weight, cotangent
):
    ns, nc, nh = lax.axis_size("seq"), lax.axis_size("sub"), lax.axis_size("head")
    s, c, h = lax.axis_index("seq"), lax.axis_index("sub"), lax.axis_index("head")
    vocab, _, inner = xz_table.shape
    conv = conv_x.shape[0]
    heads = dt_table.shape[1]
    width = out_weight.shape[1]
    j = c * ns + s
    toks = around(token_ids.reshape(1, BLOCK), "seq")
    cot_rows = lax.all_gather(cotangent, ("head", "sub"), axis=1, tiled=True)
    scalars = jnp.concatenate([jnp.stack([j, s]).astype(jnp.int32), basemap])
    pad = lambda a, n: jnp.pad(a, ((0, n - a.shape[0]), (0, 0)))
    spread = lambda a: jnp.repeat(a, inner // heads, axis=1)
    tabs = jnp.concatenate(
        [
            pad(xz_table[:, 0].astype(F32), SYM),
            pad(xz_table[:, 1].astype(F32), SYM),
            pad(spread(dt_table), SYM),
            conv_x.astype(F32),
            pad(spread(jnp.stack([a_log, skip_gain])), SYM - conv),
        ],
        0,
    )
    bcp = jnp.concatenate(
        [
            pad(bc_table.reshape(vocab, -1).astype(F32), SYM),
            pad(conv_bc.reshape(conv, -1).astype(F32), SYM),
        ],
        0,
    )
    weight_rows = lax.dynamic_slice_in_dim(out_weight, c * (ns * LANES), ns * LANES, 0)
    d_mine = lax.dot_general(cot_rows, weight_rows, NT, preferred_element_type=F32).astype(BF16)
    at = lambda k: lax.dynamic_slice_in_dim(d_mine, ((s + k) % ns) * LANES, LANES, 1)
    d_gated = [at(0)] + [
        lax.ppermute(at(k), "seq", [(i, (i + k) % ns) for i in range(ns)]) for k in range(1, ns)
    ]
    cots = around(cot_rows, "seq")
    gated = call_forward(scalars, toks, tabs, bcp, conv, vocab)
    grads = call_backward(scalars, toks, tabs, bcp, d_gated, conv, vocab)
    gs = jnp.stack(around(gated, "seq"), 0)
    other = lax.ppermute(gs, "sub", [(i, (i + 1) % nc) for i in range(nc)])
    gs = jnp.concatenate([gs, other], 0)
    order = (s - jnp.arange(ns, dtype=jnp.int32)) % ns
    place = jnp.concatenate([c * ns + order, (1 - c) * ns + order]).astype(jnp.int32)
    d_out_weight = call_weight(
        jnp.concatenate([s[None].astype(jnp.int32), place]), gs, jnp.stack(cots, 0)
    )
    mine = lax.dynamic_slice_in_dim(gs, s * BLOCK, BLOCK, 1)
    wg = out_weight.reshape(nc * ns, LANES, width)[place]
    part = width // (nh * nc)
    parts = []
    for k in range(nh):
        first = (((h + k) % nh) * nc + c) * part
        cols = lax.dynamic_slice_in_dim(wg, first, part, 2)
        parts.append(jnp.einsum("jtk,jkc->tc", mine, cols, preferred_element_type=F32))
    total = parts[0]
    for k in range(1, nh):
        total = total + lax.ppermute(parts[k], "head", [(i, (i + k) % nh) for i in range(nh)])
    layer_out = total.astype(BF16)
    own, shared = grads[:, : 3 * LANES], grads[:, 3 * LANES :]
    shared = lax.psum(shared, ("seq", "head", "sub"))
    owns = lax.all_gather(own, ("sub", "seq"))
    full = jnp.moveaxis(owns[:, :vocab], 0, 1).reshape(vocab, nc * ns, 3, LANES)
    full = jnp.moveaxis(full, 2, 1).reshape(vocab, 3, inner)
    d_xz = full[:, :2]
    d_dt = full[:, 2].reshape(vocab, heads, inner // heads).sum(-1)
    d_bc = shared[:vocab].reshape(bc_table.shape)
    return (layer_out, d_out_weight, d_xz, d_bc, d_dt)


PRECISE = lax.Precision.HIGHEST


def carried_in(part, axis, combine, identity):
    place = lax.axis_index(axis)
    gathered = jax.tree.map(lambda a: lax.all_gather(a, axis), part)
    state = jax.tree.map(lambda a, e: jnp.zeros_like(a) + jnp.asarray(e, a.dtype), part, identity)

    def one(hop, state):
        return combine(
            state, jax.tree.map(lambda a: lax.dynamic_index_in_dim(a, hop, 0, False), gathered)
        )

    return lax.fori_loop(0, place, one, state)


def carried_in_2(array, axis, combine, identity):
    length, mine = (lax.axis_size(axis), lax.axis_index(axis))
    everything = jax.tree.map(
        lambda part, kind: lax.all_gather(part.astype(kind), axis),
        array,
        jax.tree.map(lambda a: jnp.bfloat16 if a.dtype == jnp.float32 else a.dtype, array),
    )
    start = jax.tree.map(
        lambda part, zero: jnp.broadcast_to(jnp.asarray(zero, part.dtype), part.shape),
        array,
        identity,
    )

    def hop(k, before):
        at = length - 1 - k
        reached = at > mine
        new = combine(
            before, jax.tree.map(lambda part, own: part[at].astype(own.dtype), everything, array)
        )
        return jax.tree.map(lambda a, b: jnp.where(reached, a, b), new, before)

    return lax.fori_loop(0, length, hop, start)


def with_halo(block, sides, width):
    for axis, dim in sides:
        count = lax.axis_size(axis)
        forward = [(i, i + 1) for i in range(count - 1)]
        backward = [(target, source) for source, target in forward]
        low = lax.ppermute(
            lax.slice_in_dim(block, block.shape[dim] - width, None, axis=dim), axis, forward
        )
        high = lax.ppermute(lax.slice_in_dim(block, 0, width, axis=dim), axis, backward)
        block = jnp.concatenate([low, block, high], axis=dim)
    return block


def block_step(carry_state, pieces):
    scaled_x, logdec, b_mat, c_mat = pieces
    block_len = scaled_x.shape[0]
    running = jnp.cumsum(logdec, axis=0)
    by_head = running.T
    causal_mask = (jnp.arange(block_len)[:, None] >= jnp.arange(block_len)[None, :])[None, :, :]
    gap_matrix = by_head[:, :, None] - by_head[:, None, :]
    decay_mat = jnp.where(causal_mask, jnp.exp(jnp.where(causal_mask, gap_matrix, 0.0)), 0.0)
    scores = jnp.einsum("tn,sn->ts", c_mat, b_mat, precision=PRECISE)
    within = jnp.einsum("hts,shp->thp", scores[None, :, :] * decay_mat, scaled_x, precision=PRECISE)
    carried = jnp.exp(running)[:, :, None] * jnp.einsum(
        "tn,hpn->thp", c_mat, carry_state, precision=PRECISE
    )
    to_end = jnp.exp(running[-1][None, :] - running)
    gained = jnp.einsum("shp,sn->hpn", to_end[:, :, None] * scaled_x, b_mat, precision=PRECISE)
    return (jnp.exp(running[-1])[:, None, None] * carry_state + gained, within + carried)


def state_pass(inputs, start_state, block_len):
    scaled_x, logdec, b_mat, c_mat = inputs
    block_count = scaled_x.shape[0] // block_len
    pieces = (
        scaled_x.reshape((block_count, block_len) + scaled_x.shape[1:]),
        logdec.reshape(block_count, block_len, -1),
        b_mat.reshape(block_count, block_len, -1),
        c_mat.reshape(block_count, block_len, -1),
    )
    end_state, outputs = lax.scan(jax.checkpoint(block_step), start_state, pieces)
    return (outputs.reshape(scaled_x.shape), end_state)


def final_state(inputs):
    scaled_x, logdec, b_mat, c_mat = inputs
    running = jnp.cumsum(logdec, axis=0)
    to_end = jnp.exp(running[-1][None, :] - running)
    gained = jnp.einsum("shp,sn->hpn", to_end[:, :, None] * scaled_x, b_mat, precision=PRECISE)
    return (jnp.exp(running[-1]), gained)


def lookup(symbols, table):
    vocab_size = table.shape[0]
    onehot = (symbols[:, None] == jnp.arange(vocab_size, dtype=jnp.int32)[None, :]).astype(
        jnp.float32
    )
    return jnp.dot(onehot, table, precision=PRECISE)


def conv_rows(extended, weight, row_count, forward):
    conv_width = weight.shape[0]
    rim_width = conv_width - 1
    summed = jnp.zeros((row_count, extended.shape[1]), jnp.float32)
    for offset in range(conv_width):
        if forward:
            first_row = rim_width - offset
        else:
            first_row = rim_width + offset
        summed = summed + weight[offset][None, :] * extended[first_row : first_row + row_count]
    return summed


def open_inputs(ext_sym, inside_mask, tables, frozen):
    xz_tab, bc_tab, dt_tab = tables
    conv_inner, conv_shared, log_rates, skip_vals = frozen
    rim_width = conv_inner.shape[0] - 1
    row_count = ext_sym.shape[0] - 2 * rim_width
    vocab_size = xz_tab.shape[0]
    inner_dim = xz_tab.shape[2]
    head_count = dt_tab.shape[1]
    state_dim = bc_tab.shape[2]
    looked = lookup(ext_sym, xz_tab.reshape(vocab_size, 2 * inner_dim)) * inside_mask[:, None]
    pre_x = looked[:, :inner_dim]
    gate_act = jax.nn.silu(looked[rim_width : rim_width + row_count, inner_dim:])
    pre_bc = lookup(ext_sym, bc_tab.reshape(vocab_size, 2 * state_dim)) * inside_mask[:, None]
    dt_step = jax.nn.softplus(lookup(ext_sym[rim_width : rim_width + row_count], dt_tab))
    logdec = -jnp.exp(log_rates)[None, :] * dt_step
    flat_bc = conv_shared.reshape(conv_inner.shape[0], 2 * state_dim)

    def one_way(forward):
        x_conv = jax.nn.silu(conv_rows(pre_x, conv_inner, row_count, forward)).reshape(
            row_count, head_count, -1
        )
        bc_conv = jax.nn.silu(conv_rows(pre_bc, flat_bc, row_count, forward))
        return (x_conv, bc_conv[:, :state_dim], bc_conv[:, state_dim:])

    x_fwd, b_fwd, c_fwd = one_way(True)
    x_back, b_back, c_back = one_way(False)
    ahead_in = (x_fwd * dt_step[:, :, None], logdec, b_fwd, c_fwd)
    behind_in = (
        jnp.flip(x_back * dt_step[:, :, None], 0),
        jnp.flip(logdec, 0),
        jnp.flip(b_back, 0),
        jnp.flip(c_back, 0),
    )
    skip_term = skip_vals[None, :, None] * (x_fwd + x_back)
    return (ahead_in, behind_in, skip_term, gate_act)


def combine(earlier, later):
    decay_early, state_early = earlier
    decay_late, state_late = later
    return (decay_early * decay_late, decay_late[:, None, None] * state_early + state_late)


def carries(ahead_pair, behind_pair):
    ahead_out = carried_in(
        (ahead_pair[0], ahead_pair[1]),
        "seq",
        combine,
        (jnp.ones_like(ahead_pair[0]), jnp.zeros_like(ahead_pair[1])),
    )
    behind_out = carried_in_2(
        (behind_pair[0], behind_pair[1]),
        "seq",
        combine,
        (jnp.ones_like(behind_pair[0]), jnp.zeros_like(behind_pair[1])),
    )
    return (ahead_out[1], behind_out[1])


def decay_weights(adjoint, start_state):
    return jnp.sum(adjoint * start_state, axis=(1, 2))


def shards(
    token_ids,
    basemap,
    xz_table,
    bc_table,
    dt_table,
    conv_x,
    conv_bc,
    a_log,
    skip_gain,
    out_weight,
    cotangent,
):
    row_count = token_ids.shape[0]
    rim_width = conv_x.shape[0] - 1
    ext_ids = with_halo(token_ids, (("seq", 0),), rim_width)
    first_row = lax.axis_index("seq") * row_count - rim_width
    where_global = first_row + jnp.arange(row_count + 2 * rim_width, dtype=jnp.int32)
    inside_mask = jnp.logical_and(
        where_global >= 0, where_global < row_count * lax.axis_size("seq")
    ).astype(jnp.float32)
    vocab_size = basemap.shape[0]
    matches = ext_ids[:, None] == jnp.arange(vocab_size, dtype=jnp.int32)[None, :]
    mapped = jnp.sum(jnp.where(matches, basemap[None, :], 0), axis=1)
    ext_sym = jnp.where(lax.axis_index("sub") == 1, mapped, ext_ids)
    tables = (xz_table.astype(jnp.float32), bc_table.astype(jnp.float32), dt_table)
    frozen = (conv_x.astype(jnp.float32), conv_bc.astype(jnp.float32), a_log, skip_gain)

    def summary(tabs_in):
        ahead_in, behind_in, skip_term, gate_act = open_inputs(
            ext_sym, inside_mask, tabs_in, frozen
        )
        decay_fwd, end_fwd = final_state(ahead_in)
        decay_back, end_back = final_state(behind_in)
        return (decay_fwd, end_fwd, decay_back, end_back)

    (decay_fwd, end_fwd, decay_back, end_back), pull_summary = jax.vjp(summary, tables)
    start_fwd, start_back = carries((decay_fwd, end_fwd), (decay_back, end_back))

    def finished(tabs_in, begin_fwd, begin_back):
        ahead_in, behind_in, skip_term, gate_act = open_inputs(
            ext_sym, inside_mask, tabs_in, frozen
        )
        out_fwd, unused_fwd = state_pass(ahead_in, begin_fwd, BLOCK)
        out_back, unused_back = state_pass(behind_in, begin_back, BLOCK)
        return (out_fwd + jnp.flip(out_back, 0) + skip_term).reshape(row_count, -1) * gate_act

    gated, pull_finished = jax.vjp(finished, tables, start_fwd, start_back)
    gated_bf = gated.astype(jnp.bfloat16)
    products = jnp.dot(gated_bf, out_weight, preferred_element_type=jnp.float32)
    layer_out = lax.psum_scatter(products, ("head", "sub"), scatter_dimension=1, tiled=True).astype(
        jnp.bfloat16
    )
    full_cot = lax.all_gather(cotangent, ("head", "sub"), axis=1, tiled=True)
    d_gated = jnp.einsum(
        "tc,kc->tk", full_cot, out_weight, preferred_element_type=jnp.float32
    ).astype(jnp.bfloat16)
    weight_part = jnp.einsum("tk,tc->kc", gated_bf, full_cot, preferred_element_type=jnp.float32)
    d_gated_wide = lax.optimization_barrier(d_gated).astype(jnp.float32)
    grads_first, direct_fwd, direct_back = pull_finished(d_gated_wide)
    adjoint_back, adjoint_fwd = carries((decay_back, direct_back), (decay_fwd, direct_fwd))
    grads_second = pull_summary(
        (
            decay_weights(adjoint_fwd, start_fwd),
            adjoint_fwd,
            decay_weights(adjoint_back, start_back),
            adjoint_back,
        )
    )[0]
    d_tables = jax.tree.map(lambda former, latter: former + latter, grads_first, grads_second)
    d_xz, d_bc, d_dt = d_tables
    d_bc = lax.psum(d_bc, ("seq", "head", "sub"))
    d_out_weight, d_xz, d_dt = lax.psum((weight_part, d_xz, d_dt), ("seq", "sub"))
    return (layer_out, d_out_weight, d_xz, d_bc, d_dt)


def solution(mesh):
    in_specs = (
        P(("grp", "seq")),
        P(),
        P(None, None, "head"),
        P(),
        P(None, "head"),
        P(None, "head"),
        P(),
        P("head"),
        P("head"),
        P("head", None),
        P(("grp", "seq"), ("head", "sub")),
    )
    out_specs = (
        P(("grp", "seq"), ("head", "sub")),
        P(("grp", "head"), None),
        P("grp", None, "head"),
        P("grp", None, None),
        P("grp", "head"),
    )
    def run(*args):
        ns, nc = mesh.shape["seq"], mesh.shape["sub"]
        rows, inner, heads = args[0].shape[0], args[2].shape[2], args[4].shape[1]
        by_lanes = (
            rows == BLOCK
            and nc == 2
            and ns > 1
            and inner == ns * nc * LANES
            and inner == heads * (LANES // 2)
            and args[3].shape[2] == LANES
            and args[5].shape[0] == 4
            and args[9].shape[1] == args[10].shape[1] * nc * mesh.shape["head"]
        )
        return (by_channel if by_lanes else shards)(*args)

    return jax.shard_map(run, mesh=mesh, in_specs=in_specs, out_specs=out_specs, check_vma=False)
```

profile of v0, /device:TPU:0, one launch (start us, length us, event | category | flops | bytes accessed | tf_op | source)
XLA Modules:
  0.0 143.7 jit_solution(11348928759457021199)
XLA Ops:
  0.6 5.1 %collective-permute-start.2 = (s32[1,128]{1,0:T(1,128)}, s32[1,128]{1,0:T(1,128)S(1)}, u32[]{:S(2)}, u32[]{:S(2)}) collective-permute-start(s32[1,128]{1,0:T(1,128)} %bitcast.74), channel_id=1, source_target_pairs={{0,12},{4,0},{8,4},{12,8},{1,13},{5,1},{9,5},{13,9},{2,14},{6,2},{... | collective-permute-start | bytes 1544 | tf_op jit(solution)/shard_map/ppermute | solution.py:529
  5.8 1.0 collective-permute-start
  6.8 6.0 %all_gather.9 = bf16[128,1024]{1,0:T(8,128)(2,1)S(1)} all-gather(bf16[128,256]{1,0:T(8,128)(2,1)} %param.21), channel_id=1, replica_groups=mesh['grp'=2,'seq'=4,'head'=2,'sub'=2] {'head','sub'}, dimensions={1}, use_global_device_ids=true | all-gather | bytes 327680 | tf_op jit(solution)/shard_map/all_gather | solution.py:544
  12.7 2.8 %collective-permute-start.10 = (bf16[128,1024]{1,0:T(8,128)(2,1)S(1)}, bf16[128,1024]{1,0:T(8,128)(2,1)}, u32[]{:S(2)}, u32[]{:S(2)}) collective-permute-start(bf16[128,1024]{1,0:T(8,128)(2,1)S(1)} %all_gather.9), channel_id=1, source_target_pairs={{0,12},{4,0},{8,4},{12,8},{1,13},{5,1},{9,5},{13,9},{2,14},{6,2},{... | collective-permute-start | bytes 786440 | tf_op jit(solution)/shard_map/ppermute | solution.py:529
  15.6 1.1 collective-permute-start.9
  20.4 0.8 fusion.17
  21.3 1.3 pad_add_fusion.scalars
  24.4 2.0 %gather_fusion = bf16[8,128,1024]{2,1,0:T(8,128)(2,1)} fusion(bf16[8,128,1024]{2,1,0:T(8,128)(2,1)S(1)} %bitcast.63, s32[1024]{0:T(1024)S(1)} %pad_clamp_fusion), kind=kCustom, calls=%fused_computation | custom fusion | bytes 4194336 | tf_op jit(solution)/shard_map/gather | solution.py:583
  26.4 2.4 %concatenate.46.refs_4_ = f32[32,1024]{1,0:T(8,128)} concatenate(f32[8,1024]{1,0:T(8,128)S(1)} %pad_convert_fusion.1, f32[8,1024]{1,0:T(8,128)S(1)} %pad_convert_fusion, f32[8,1024]{1,0:T(8,128)S(1)} %pad.34, bf16[4,1024]{1,0:T(4,128)(2,1)S(1)} %copy-done.6, f32[4,1024]{1,0:T(4,128)S(1)} %pad.35), dimensions={0} | concatenate | bytes 253952 | tf_op jit(solution)/shard_map/concatenate | solution.py:548
  28.8 0.9 collective-permute-start.13
  29.7 1.0 collective-permute-start.12
  30.7 1.9 %collective-permute-start.11 = (bf16[128,128]{1,0:T(8,128)(2,1)}, bf16[128,128]{1,0:T(8,128)(2,1)S(1)}, u32[]{:S(2)}, u32[]{:S(2)}) collective-permute-start(bf16[128,128]{1,0:T(8,128)(2,1)} %get-tuple-element.7), channel_id=1, source_target_pairs={{0,4},{4,8},{8,12},{12,0},{1,5},{5,9},{9,13},{13,1},{2,6},{6,10},{... | collective-permute-start | bytes 98312 | tf_op jit(solution)/shard_map/ppermute | solution.py:569
  32.7 5.8 %mix_forward.1 = bf16[512,128]{1,0:T(8,128)(2,1)} custom-call(s32[7]{0:T(128)} %pad_add_fusion.scalars, s32[1,128]{1,0:T(1,128)} %bitcast.77, s32[1,128]{1,0:T(1,128)} %copy-done.9, s32[1,128]{1,0:T(1,128)} %copy-done.8, s32[1,128]{1,0:T(1,128)} %copy-done.7, f32[32,1024]{1,0:T(8,128)} %concatenate.46.refs_4_, f32[16,256]{1,0:T(8,128)} %fusion.10.refs_5_), custom_call_target="tpu_custom_call" | custom-call | tf_op jit(solution)/shard_map/mix_forward/pallas_call | solution.py:453
  38.5 0.9 constant_dynamic-update-slice_fusion.4
  39.4 1.9 %collective-permute-start.5 = (bf16[512,128]{1,0:T(8,128)(2,1)}, bf16[512,128]{1,0:T(8,128)(2,1)S(1)}, u32[]{:S(2)}, u32[]{:S(2)}) collective-permute-start(bf16[512,128]{1,0:T(8,128)(2,1)} %mix_forward.1), channel_id=1, source_target_pairs={{0,12},{4,0},{8,4},{12,8},{1,13},{5,1},{9,5},{13,9},{2,14},{6,2},{... | collective-permute-start | bytes 393224 | tf_op jit(solution)/shard_map/ppermute | solution.py:529
  41.5 1.1 collective-permute-start.3
  42.6 9.8 %mix_backward.1 = f32[8,640]{1,0:T(8,128)} custom-call(s32[7]{0:T(128)} %pad_add_fusion.scalars, s32[1,128]{1,0:T(1,128)} %bitcast.78, s32[1,128]{1,0:T(1,128)} %copy-done.9, s32[1,128]{1,0:T(1,128)} %copy-done.8, s32[1,128]{1,0:T(1,128)} %copy-done.7, f32[32,1024]{1,0:T(8,128)} %concatenate.46.refs_4_, f32[16,256]{1,0:T(8,128)} %fusion.10.refs_5_, ...), custom_call_target="tpu_custom_call" | custom-call | tf_op jit(solution)/shard_map/mix_backward/pallas_call | solution.py:478
  53.2 25.9 %all-gather = f32[64,384]{1,0:T(8,128)} all-gather(f32[8,384]{1,0:T(8,128)S(1)} %slice.34), channel_id=2, replica_groups=mesh['grp'=2,'seq'=4,'head'=2,'sub'=2] {'sub','seq'}, dimensions={0}, use_global_device_ids=true | all-gather | bytes 110592 | tf_op jit(solution)/shard_map/all_gather | solution.py:596
  79.7 33.6 %psum.7 = f32[8,256]{1,0:T(8,128)S(1)} all-reduce(f32[8,256]{1,0:T(8,128)S(1)} %slice.37), channel_id=1, replica_groups=mesh['grp'=2,'seq'=4,'head'=2,'sub'=2] {'seq','head','sub'}, use_global_device_ids=true, to_apply=%region_0.1 | all-reduce | flops 2048 | bytes 16384 | tf_op jit(solution)/shard_map/psum | solution.py:595
  114.0 1.5 %copy.35 = f32[8,5,384]{2,0,1:T(8,128)} copy(f32[8,5,384]{2,1,0:T(8,128)} %bitcast.67) | data formatting | bytes 122880
  115.5 1.5 %reshape.99 = f32[5,3,1024]{2,1,0:T(4,128)} reshape(f32[5,3,8,128]{3,2,1,0:T(8,128)} %bitcast.69) | data formatting | bytes 122880 | tf_op jit(solution)/shard_map/reshape | solution.py:598
  117.0 1.5 %slice.36 = f32[5,2,1024]{2,1,0:T(2,128)} slice(f32[5,3,1024]{2,1,0:T(4,128)} %reshape.99), slice={[0:5], [0:2], [0:1024]} | slice | bytes 81920 | tf_op jit(solution)/shard_map/slice | solution.py:599
  118.5 1.6 %slice_reduce_fusion = f32[5,1024]{1,0:T(8,128)} fusion(f32[5,3,1024]{2,1,0:T(4,128)} %reshape.99), kind=kLoop, calls=%fused_computation.18 | loop fusion | bytes 40960 | tf_op jit(solution)/shard_map/slice | solution.py:600
  120.1 1.4 %reshape_squeeze.3 = f32[5,16,64]{2,1,0:T(8,128)} reshape(f32[5,1024]{1,0:T(8,128)} %slice_reduce_fusion) | data formatting | bytes 40960 | tf_op jit(solution)/shard_map/reshape;squeeze | solution.py:600
  121.5 1.5 %reduce_sum.9 = f32[5,16]{1,0:T(8,128)} reduce(f32[5,16,64]{2,1,0:T(8,128)} %reshape_squeeze.3, f32[]{:T(128)} %constant.67.clone.1), dimensions={2}, to_apply=%region_1.2 | reduce | flops 5040 | bytes 20804 | tf_op jit(solution)/shard_map/reduce_sum | solution.py:600
  123.0 1.2 pad_maximum_fusion.1
  124.3 0.9 constant_dynamic-update-slice_fusion.3
  125.2 0.9 constant_dynamic-update-slice_fusion.2
  126.7 4.5 %collective-permute-done.8 = bf16[128,1024]{1,0:T(8,128)(2,1)S(1)} collective-permute-done((bf16[128,1024]{1,0:T(8,128)(2,1)S(1)}, bf16[128,1024]{1,0:T(8,128)(2,1)S(1)}, u32[]{:S(2)}, u32[]{:S(2)}) %collective-permute-start.8) | collective-permute-done | bytes 262176 | tf_op jit(solution)/shard_map/ppermute | solution.py:529
  131.1 2.1 %pad_maximum_fusion.cot_ref = bf16[4,128,1024]{2,1,0:T(8,128)(2,1)} fusion(bf16[1,128,1024]{2,1,0:T(8,128)(2,1)} %bitcast.20, bf16[1,128,1024]{2,1,0:T(8,128)(2,1)} %bitcast.19, bf16[1,128,1024]{2,1,0:T(8,128)(2,1)S(1)} %bitcast.68, bf16[1,128,1024]{2,1,0:T(8,128)(2,1)S(1)} %bitcast.64), kind=kLoop, calls=%fused_computation.6 | loop fusion | flops 1572864 | bytes 2097152 | tf_op jit(solution)/shard_map/stack | solution.py:580
  133.3 8.6 %weight_grad.1 = f32[1024,1024]{1,0:T(8,128)} custom-call(s32[9]{0:T(128)} %pad_add_fusion.1.scalars, bf16[8,512,128]{2,1,0:T(8,128)(2,1)} %copy-done.2, bf16[4,128,1024]{2,1,0:T(8,128)(2,1)} %pad_maximum_fusion.cot_ref), custom_call_target="tpu_custom_call" | custom-call | tf_op jit(solution)/shard_map/weight_grad/pallas_call | solution.py:509
  141.9 1.8 %fusion.1 = bf16[128,256]{1,0:T(8,128)(2,1)} fusion(f32[128,256]{1,0:T(8,128)S(1)} %collective-permute-done.7, bf16[8,128,1024]{2,1,0:T(8,128)(2,1)S(1)} %copy-done.1, s32[]{:T(128)S(6)} %select_n.95, bf16[8,512,128]{2,1,0:T(8,128)(2,1)} %copy-done.2, s32[]{:T(128)S(6)} %select_n.91), kind=kOutput, calls=%fused_computation.5 | convolution fusion | flops 67174400 | bytes 983048 | tf_op jit(solution)/shard_map/jtk,jkc->tc/dot_general | solution.py:589
  (63 shorter events, 8.2 us)
Async XLA Ops:
  0.6 22.6 %copy-start = (bf16[1024,1024]{1,0:T(8,128)(2,1)S(1)}, bf16[1024,1024]{1,0:T(8,128)(2,1)}, u32[]{:S(2)}) copy-start(bf16[1024,1024]{1,0:T(8,128)(2,1)} %param.20) | copy-start | bytes 6291460
  0.6 28.2 %collective-permute-start.2 = (s32[1,128]{1,0:T(1,128)}, s32[1,128]{1,0:T(1,128)S(1)}, u32[]{:S(2)}, u32[]{:S(2)}) collective-permute-start(s32[1,128]{1,0:T(1,128)} %bitcast.74), channel_id=1, source_target_pairs={{0,12},{4,0},{8,4},{12,8},{1,13},{5,1},{9,5},{13,9},{2,14},{6,2},{... | collective-permute-start | bytes 1544 | tf_op jit(solution)/shard_map/ppermute | solution.py:529
  5.7 24.0 %collective-permute-start.1 = (s32[1,128]{1,0:T(1,128)}, s32[1,128]{1,0:T(1,128)S(1)}, u32[]{:S(2)}, u32[]{:S(2)}) collective-permute-start(s32[1,128]{1,0:T(1,128)} %bitcast.75), channel_id=1, source_target_pairs={{0,8},{4,12},{8,0},{12,4},{1,9},{5,13},{9,1},{13,5},{2,10},{6,14},... | collective-permute-start | bytes 1544 | tf_op jit(solution)/shard_map/ppermute | solution.py:529
  5.8 25.0 %collective-permute-start = (s32[1,128]{1,0:T(1,128)}, s32[1,128]{1,0:T(1,128)S(1)}, u32[]{:S(2)}, u32[]{:S(2)}) collective-permute-start(s32[1,128]{1,0:T(1,128)} %bitcast.76), channel_id=1, source_target_pairs={{0,4},{4,8},{8,12},{12,0},{1,5},{5,9},{9,13},{13,1},{2,6},{6,10},{... | collective-permute-start | bytes 1544 | tf_op jit(solution)/shard_map/ppermute | solution.py:529
  12.7 113.9 %collective-permute-start.10 = (bf16[128,1024]{1,0:T(8,128)(2,1)S(1)}, bf16[128,1024]{1,0:T(8,128)(2,1)}, u32[]{:S(2)}, u32[]{:S(2)}) collective-permute-start(bf16[128,1024]{1,0:T(8,128)(2,1)S(1)} %all_gather.9), channel_id=1, source_target_pairs={{0,12},{4,0},{8,4},{12,8},{1,13},{5,1},{9,5},{13,9},{2,14},{6,2},{... | collective-permute-start | bytes 786440 | tf_op jit(solution)/shard_map/ppermute | solution.py:529
  15.6 111.1 %collective-permute-start.9 = (bf16[128,1024]{1,0:T(8,128)(2,1)S(1)}, bf16[128,1024]{1,0:T(8,128)(2,1)}, u32[]{:S(2)}, u32[]{:S(2)}) collective-permute-start(bf16[128,1024]{1,0:T(8,128)(2,1)S(1)} %all_gather.9), channel_id=1, source_target_pairs={{0,8},{4,12},{8,0},{12,4},{1,9},{5,13},{9,1},{13,5},{2,10},{6,14},... | collective-permute-start | bytes 786440 | tf_op jit(solution)/shard_map/ppermute | solution.py:529
  24.4 2.0 %copy-start.6 = (bf16[4,1024]{1,0:T(4,128)(2,1)S(1)}, bf16[4,1024]{1,0:T(4,128)(2,1)}, u32[]{:S(2)}) copy-start(bf16[4,1024]{1,0:T(4,128)(2,1)} %param.16) | copy-start | bytes 24580
  28.8 3.8 %copy-start.7 = (s32[1,128]{1,0:T(1,128)}, s32[1,128]{1,0:T(1,128)S(1)}, u32[]{:S(2)}) copy-start(s32[1,128]{1,0:T(1,128)S(1)} %collective-permute-done.2.refs_3_) | copy-start | bytes 1540
  28.8 10.6 %collective-permute-start.13 = (bf16[128,128]{1,0:T(8,128)(2,1)S(1)}, bf16[128,128]{1,0:T(8,128)(2,1)S(1)}, u32[]{:S(2)}, u32[]{:S(2)}) collective-permute-start(bf16[128,128]{1,0:T(8,128)(2,1)S(1)} %get-tuple-element.5), channel_id=1, source_target_pairs={{0,12},{4,0},{8,4},{12,8},{1,13},{5,1},{9,5},{13,9},{2,14},{6,2},{... | collective-permute-start | bytes 98312 | tf_op jit(solution)/shard_map/ppermute | solution.py:569
  29.7 2.9 %copy-start.8 = (s32[1,128]{1,0:T(1,128)}, s32[1,128]{1,0:T(1,128)S(1)}, u32[]{:S(2)}) copy-start(s32[1,128]{1,0:T(1,128)S(1)} %collective-permute-done.1.refs_2_) | copy-start | bytes 1540
  29.7 11.6 %collective-permute-start.12 = (bf16[128,128]{1,0:T(8,128)(2,1)}, bf16[128,128]{1,0:T(8,128)(2,1)S(1)}, u32[]{:S(2)}, u32[]{:S(2)}) collective-permute-start(bf16[128,128]{1,0:T(8,128)(2,1)} %get-tuple-element.6), channel_id=1, source_target_pairs={{0,8},{4,12},{8,0},{12,4},{1,9},{5,13},{9,1},{13,5},{2,10},{6,14},... | collective-permute-start | bytes 98312 | tf_op jit(solution)/shard_map/ppermute | solution.py:569
  30.7 1.9 %copy-start.9 = (s32[1,128]{1,0:T(1,128)}, s32[1,128]{1,0:T(1,128)S(1)}, u32[]{:S(2)}) copy-start(s32[1,128]{1,0:T(1,128)S(1)} %collective-permute-done.refs_1_) | copy-start | bytes 1540
  30.7 10.8 %collective-permute-start.11 = (bf16[128,128]{1,0:T(8,128)(2,1)}, bf16[128,128]{1,0:T(8,128)(2,1)S(1)}, u32[]{:S(2)}, u32[]{:S(2)}) collective-permute-start(bf16[128,128]{1,0:T(8,128)(2,1)} %get-tuple-element.7), channel_id=1, source_target_pairs={{0,4},{4,8},{8,12},{12,0},{1,5},{5,9},{9,13},{13,1},{2,6},{6,10},{... | collective-permute-start | bytes 98312 | tf_op jit(solution)/shard_map/ppermute | solution.py:569
  39.4 3.2 %copy-start.3 = (bf16[128,128]{1,0:T(8,128)(2,1)}, bf16[128,128]{1,0:T(8,128)(2,1)S(1)}, u32[]{:S(2)}) copy-start(bf16[128,128]{1,0:T(8,128)(2,1)S(1)} %collective-permute-done.13.refs_9_) | copy-start | bytes 98308
  39.4 83.5 %collective-permute-start.5 = (bf16[512,128]{1,0:T(8,128)(2,1)}, bf16[512,128]{1,0:T(8,128)(2,1)S(1)}, u32[]{:S(2)}, u32[]{:S(2)}) collective-permute-start(bf16[512,128]{1,0:T(8,128)(2,1)} %mix_forward.1), channel_id=1, source_target_pairs={{0,12},{4,0},{8,4},{12,8},{1,13},{5,1},{9,5},{13,9},{2,14},{6,2},{... | collective-permute-start | bytes 393224 | tf_op jit(solution)/shard_map/ppermute | solution.py:529
  41.4 1.3 copy-start.4
  41.4 81.6 %collective-permute-start.4 = (bf16[512,128]{1,0:T(8,128)(2,1)}, bf16[512,128]{1,0:T(8,128)(2,1)}, u32[]{:S(2)}, u32[]{:S(2)}) collective-permute-start(bf16[512,128]{1,0:T(8,128)(2,1)} %mix_forward.1), channel_id=1, source_target_pairs={{0,8},{4,12},{8,0},{12,4},{1,9},{5,13},{9,1},{13,5},{2,10},{6,14},... | collective-permute-start | bytes 393224 | tf_op jit(solution)/shard_map/ppermute | solution.py:529
  41.5 1.1 copy-start.5
  41.5 81.5 %collective-permute-start.3 = (bf16[512,128]{1,0:T(8,128)(2,1)}, bf16[512,128]{1,0:T(8,128)(2,1)}, u32[]{:S(2)}, u32[]{:S(2)}) collective-permute-start(bf16[512,128]{1,0:T(8,128)(2,1)} %mix_forward.1), channel_id=1, source_target_pairs={{0,4},{4,8},{8,12},{12,0},{1,5},{5,9},{9,13},{13,1},{2,6},{6,10},{... | collective-permute-start | bytes 393224 | tf_op jit(solution)/shard_map/ppermute | solution.py:529
  123.0 3.3 %copy-start.1 = (bf16[8,128,1024]{2,1,0:T(8,128)(2,1)S(1)}, bf16[8,128,1024]{2,1,0:T(8,128)(2,1)}, u32[]{:S(2)}) copy-start(bf16[8,128,1024]{2,1,0:T(8,128)(2,1)} %gather_fusion) | copy-start | bytes 6291460
  123.0 8.2 %collective-permute-start.8 = (bf16[128,1024]{1,0:T(8,128)(2,1)S(1)}, bf16[128,1024]{1,0:T(8,128)(2,1)S(1)}, u32[]{:S(2)}, u32[]{:S(2)}) collective-permute-start(bf16[128,1024]{1,0:T(8,128)(2,1)S(1)} %all_gather.9), channel_id=1, source_target_pairs={{0,4},{4,8},{8,12},{12,0},{1,5},{5,9},{9,13},{13,1},{2,6},{6,10},{... | collective-permute-start | bytes 786440 | tf_op jit(solution)/shard_map/ppermute | solution.py:529
  124.2 2.0 %collective-permute-start.6 = (bf16[4,512,128]{2,1,0:T(8,128)(2,1)S(1)}, bf16[4,512,128]{2,1,0:T(8,128)(2,1)S(1)}, u32[]{:S(2)}, u32[]{:S(2)}) collective-permute-start(bf16[4,512,128]{2,1,0:T(8,128)(2,1)S(1)} %pad_maximum_fusion.1), channel_id=1, source_target_pairs={{0,1},{1,0},{2,3},{3,2},{4,5},{5,4},{6,7},{7,6},{8,9},{9,8},{10,11... | collective-permute-start | bytes 1572872 | tf_op jit(solution)/shard_map/ppermute | solution.py:575
  126.3 7.0 %copy-start.2 = (bf16[8,512,128]{2,1,0:T(8,128)(2,1)}, bf16[8,512,128]{2,1,0:T(8,128)(2,1)S(1)}, u32[]{:S(2)}) copy-start(bf16[8,512,128]{2,1,0:T(8,128)(2,1)S(1)} %constant_dynamic-update-slice_fusion.g_ref) | copy-start | bytes 3145732
  126.6 15.3 %collective-permute-start.7 = (f32[128,256]{1,0:T(8,128)S(1)}, f32[128,256]{1,0:T(8,128)S(1)}, u32[]{:S(2)}, u32[]{:S(2)}) collective-permute-start(f32[128,256]{1,0:T(8,128)S(1)} %convolution_bitcast_fusion), channel_id=1, source_target_pairs={{0,2},{2,0},{1,3},{3,1},{4,6},{6,4},{5,7},{7,5},{8,10},{10,8},{9,1... | collective-permute-start | bytes 393224 | tf_op jit(solution)/shard_map/ppermute | solution.py:592
where the time goes:
time: 145 us; the launch traced here: 144 us
  blocking collectives  65.4 us (45%)
  Pallas kernels  24.2 us (17%)
  local copies, waits for them, and re-layouts  20.7 us (14%)
  starting transfers between devices  17.2 us (12%)
  other arithmetic  8.09 us (6%)
  waiting for transfers between devices  4.52 us (3%)
  matrix products  2.58 us (2%)
    psum x1, blocking collectives, by_channel(): shared = lax.psum(shared, ('seq', 'head', 'sub'))  33.6 us
    all_gather x1, blocking collectives, by_channel(): owns = lax.all_gather(own, ('sub', 'seq'))  25.9 us
    ppermute x9, starting transfers between devices, around(): lax.ppermute(x, axis, [(i, (i + k) % n) for i in range(n)])  13.3 us
    pallas_call x1, Pallas kernels, call_backward(): pl.pallas_call(functools.partial(backward_kernel, ns=ns, conv=conv, vocab...  9.84 us
    pallas_call x1, Pallas kernels, call_weight(): pl.pallas_call(functools.partial(weight_kernel, ns=ns), out_shape=jax.Sha...  8.59 us
    all_gather x1, blocking collectives, by_channel(): cot_rows = lax.all_gather(cotangent, ('head', 'sub'), axis=1, tiled=True)  5.98 us
    pallas_call x1, Pallas kernels, call_forward(): pl.pallas_call(functools.partial(forward_kernel, ns=ns, conv=conv, vocab=...  5.82 us
    unnamed x27, local copies, waits for them, and re-layouts  5.72 us
  transfers between devices with their start and end apart: 14, of which 1 were waited for; matrix products, arithmetic and copies ran while one was open for 21% of the time, Pallas kernels for 17%

commit v1 on v0

--- a/solution.py
+++ b/solution.py
@@ -16,6 +16,7 @@
 NT = (((1,), (1,)), ((), ()))
 TN = (((0,), (0,)), ((), ()))
 X_ROW, Z_ROW, DT_ROW, MISC_ROW, TAB_ROWS = 0, 8, 16, 24, 32
+RAW = 8
 VMEM_LIMIT = 56 * 1024 * 1024
 XF, XB, ZZ, BCF, BCB, WIDE = 0, 128, 256, 384, 640, 896
 
@@ -56,7 +57,7 @@
     for k in range(count):
         picked = jnp.zeros_like(table[0:1])
         for m in range(count):
-            picked = jnp.where(scalars[2 + k] == m, table[m : m + 1], picked)
+            picked = jnp.where(scalars[k] == m, table[m : m + 1], picked)
         out = jnp.where(row == k, picked, out)
     return out
 
@@ -65,7 +66,33 @@
     return 1.0 / (1.0 + jnp.exp(-v))
 
 
-def prepare(scalars, tok_refs, tabs_ref, bcp_ref, r, conv, vocab):
+def gather_tables(scalars, raw, tabs_ref, bcp_ref, conv, vocab):
+    xz_ref, bc_ref, conv_ref, conv_bc_ref, dt_ref, a_log_ref, skip_ref = raw[1:]
+    j = scalars[0]
+    lanes = pl.ds(pl.multiple_of(j * LANES, LANES), LANES)
+    head0 = lax.broadcasted_iota(jnp.int32, (1, LANES), 1) < 64
+    pair = lambda a, b: jnp.where(head0, a, b)
+    tabs_ref[...] = jnp.zeros_like(tabs_ref)
+    bcp_ref[...] = jnp.zeros_like(bcp_ref)
+    for k in range(vocab):
+        tabs_ref[X_ROW + k : X_ROW + k + 1, :] = xz_ref[k, 0:1, lanes].astype(F32)
+        tabs_ref[Z_ROW + k : Z_ROW + k + 1, :] = xz_ref[k, 1:2, lanes].astype(F32)
+        tabs_ref[DT_ROW + k : DT_ROW + k + 1, :] = pair(dt_ref[k, 2 * j], dt_ref[k, 2 * j + 1])
+        for i in range(2):
+            bcp_ref[k : k + 1, i * 128 : i * 128 + 128] = bc_ref[k, i : i + 1, :].astype(F32)
+    for k in range(conv):
+        tabs_ref[MISC_ROW + k : MISC_ROW + k + 1, :] = conv_ref[k : k + 1, lanes].astype(F32)
+        for i in range(2):
+            bcp_ref[SYM + k : SYM + k + 1, i * 128 : i * 128 + 128] = conv_bc_ref[
+                k, i : i + 1, :
+            ].astype(F32)
+    at = MISC_ROW + 4
+    tabs_ref[at : at + 1, :] = pair(a_log_ref[2 * j], a_log_ref[2 * j + 1])
+    tabs_ref[at + 1 : at + 2, :] = pair(skip_ref[2 * j], skip_ref[2 * j + 1])
+
+
+def prepare(scalars, tok_refs, raw, tabs_ref, bcp_ref, r, conv, vocab):
+    gather_tables(scalars, raw, tabs_ref, bcp_ref, conv, vocab)
     ns = len(tok_refs)
     length = ns * BLOCK
     mine = scalars[1]
@@ -100,7 +127,7 @@
     r.wf[...] = jnp.zeros_like(r.wf)
     r.w2[...] = jnp.zeros_like(r.w2)
     for st in range(2):
-        fetch = (lambda t: t) if st == 0 else (lambda t: permuted(t, scalars, vocab))
+        fetch = (lambda t: t) if st == 0 else (lambda t: permuted(t, raw[0], vocab))
         xt = fetch(tabs_ref[X_ROW : X_ROW + SYM, :])
         zt = fetch(tabs_ref[Z_ROW : Z_ROW + SYM, :])
         dtt = fetch(tabs_ref[DT_ROW : DT_ROW + SYM, :])
@@ -216,7 +243,7 @@
     return r
 
 
-PREP_NAMES = ("oh", "inc", "exc", "rows", "wf", "w2", "pre", "pd", "prow", "x", "bc", "s")
+PREP_NAMES = ("oh", "inc", "exc", "rows", "wf", "w2", "pre", "pd", "prow", "x", "bc", "s", "tabs", "bcp")
 
 
 def prep_scratch(length):
@@ -235,13 +262,16 @@
         v((length, 512), F32),
         v((length, 1024), F32),
         v((4, nb, LANES, LANES), F32),
+        v((TAB_ROWS, LANES), F32),
+        v((2 * SYM, 256), F32),
     ]
 
 
 def forward_kernel(scalars, *refs, ns, conv, vocab):
-    tok_refs, (tabs_ref, bcp_ref, out_ref) = refs[:ns], refs[ns : ns + 3]
-    r = named(refs[ns + 3 :], PREP_NAMES)
-    prepare(scalars, tok_refs, tabs_ref, bcp_ref, r, conv, vocab)
+    tok_refs, raw, out_ref = refs[:ns], refs[ns : ns + RAW], refs[ns + RAW]
+    r = named(refs[ns + RAW + 1 :], PREP_NAMES)
+    tabs_ref, bcp_ref = r.tabs, r.bcp
+    prepare(scalars, tok_refs, raw, tabs_ref, bcp_ref, r, conv, vocab)
     units = [[Unit(r, tabs_ref, st, b, ns) for b in range(ns)] for st in range(2)]
     state_pass_fwd(r, tabs_ref, ns, units)
     for b in range(ns):
@@ -264,14 +294,15 @@
                     y = y + enter * mm_fine(cm, r.s[st * 2 + way, b], NN, 2)
             y = y + mm(jnp.concatenate(left, 1), jnp.concatenate(right, 0), NN)
             gated.append(y * u.act(ZZ, 128))
-        out_ref[units[0][b].rows, :] = (gated[0] + gated[1]).astype(BF16)
+        out_ref[:, units[0][b].rows] = jnp.transpose(gated[0] + gated[1]).astype(BF16)
 
 
 def backward_kernel(scalars, *refs, ns, conv, vocab):
-    tok_refs, (tabs_ref, bcp_ref) = refs[:ns], refs[ns : ns + 2]
-    dg_refs, out_ref = refs[ns + 2 : 2 * ns + 2], refs[2 * ns + 2]
-    r = named(refs[2 * ns + 3 :], PREP_NAMES + ("ds", "dg", "dpre"))
-    prepare(scalars, tok_refs, tabs_ref, bcp_ref, r, conv, vocab)
+    tok_refs, raw = refs[:ns], refs[ns : ns + RAW]
+    dg_refs, out_ref = refs[ns + RAW : 2 * ns + RAW], refs[2 * ns + RAW]
+    r = named(refs[2 * ns + RAW + 1 :], PREP_NAMES + ("ds", "dg", "dpre"))
+    tabs_ref, bcp_ref = r.tabs, r.bcp
+    prepare(scalars, tok_refs, raw, tabs_ref, bcp_ref, r, conv, vocab)
     mine = scalars[1]
     for k in range(ns):
         at = jnp.where(mine >= k, mine - k, mine - k + ns)
@@ -433,7 +464,7 @@
         d_zt = d_tab[mid : mid + SYM, base + ZZ : base + ZZ + 128]
         dtt = tabs_ref[DT_ROW : DT_ROW + SYM, :]
         if st == 1:
-            dtt = permuted(dtt, scalars, vocab)
+            dtt = permuted(dtt, raw[0], vocab)
         rate = -jnp.exp(tabs_ref[MISC_ROW + 4 : MISC_ROW + 5, :])
         d_dt = (d_steps[st] + rate * d_decays[st]) * sigmoid(dtt)
         wide = jnp.concatenate([d_x, d_zt, d_dt, d_bc], 1)
@@ -442,85 +473,243 @@
         else:
             row = lax.broadcasted_iota(jnp.int32, wide.shape, 0)
             for k in range(vocab):
-                result = result + jnp.where(row == scalars[2 + k], wide[k : k + 1], 0.0)
+                result = result + jnp.where(row == raw[0][k], wide[k : k + 1], 0.0)
     out_ref[...] = result
 
 
-def call_forward(scalars, toks, tabs, bcp, conv, vocab):
+def whole(shape):
+    return pl.BlockSpec(shape, lambda i, s: (0,) * len(shape))
+
+
+SMEM = pl.BlockSpec(memory_space=pltpu.SMEM)
+
+
+def raw_specs(raw):
+    return [SMEM] + [whole(a.shape) for a in raw[1:5]] + [SMEM] * 3
+
+
+PARAMS = pltpu.CompilerParams(vmem_limit_bytes=VMEM_LIMIT)
+
+
+def call_forward(scalars, toks, raw):
     ns = len(toks)
     length = ns * BLOCK
-    whole = lambda shape: pl.BlockSpec(shape, lambda i, s: (0,) * len(shape))
     return pl.pallas_call(
-        functools.partial(forward_kernel, ns=ns, conv=conv, vocab=vocab),
-        out_shape=jax.ShapeDtypeStruct((length, LANES), BF16),
+        functools.partial(forward_kernel, ns=ns, conv=raw[3].shape[0], vocab=raw[1].shape[0]),
+        out_shape=jax.ShapeDtypeStruct((LANES, length), BF16),
         grid_spec=pltpu.PrefetchScalarGridSpec(
             num_scalar_prefetch=1,
             grid=(1,),
-            in_specs=[whole((1, BLOCK))] * ns
-            + [pl.BlockSpec((TAB_ROWS, LANES), lambda i, s: (0, s[0])), whole(bcp.shape)],
-            out_specs=whole((length, LANES)),
+            in_specs=[whole((1, BLOCK))] * ns + raw_specs(raw),
+            out_specs=whole((LANES, length)),
             scratch_shapes=prep_scratch(length),
         ),
-        compiler_params=pltpu.CompilerParams(vmem_limit_bytes=VMEM_LIMIT),
+        compiler_params=PARAMS,
         name="mix_forward",
-    )(scalars, *toks, tabs, bcp)
-
-
-def call_backward(scalars, toks, tabs, bcp, d_gated, conv, vocab):
+    )(scalars, *toks, *raw)
+
+
+def call_backward(scalars, toks, raw, d_gated):
     ns = len(toks)
     length = ns * BLOCK
-    whole = lambda shape: pl.BlockSpec(shape, lambda i, s: (0,) * len(shape))
     extra = [
         pltpu.VMEM((4, ns, LANES, LANES), F32),
         pltpu.VMEM((length, LANES), F32),
         pltpu.VMEM((length, 2 * WIDE), BF16),
     ]
     return pl.pallas_call(
-        functools.partial(backward_kernel, ns=ns, conv=conv, vocab=vocab),
+        functools.partial(backward_kernel, ns=ns, conv=raw[3].shape[0], vocab=raw[1].shape[0]),
         out_shape=jax.ShapeDtypeStruct((SYM, 640), F32),
         grid_spec=pltpu.PrefetchScalarGridSpec(
             num_scalar_prefetch=1,
             grid=(1,),
-            in_specs=[whole((1, BLOCK))] * ns
-            + [pl.BlockSpec((TAB_ROWS, LANES), lambda i, s: (0, s[0])), whole(bcp.shape)]
-            + [whole((BLOCK, LANES))] * ns,
+            in_specs=[whole((1, BLOCK))] * ns + raw_specs(raw) + [whole((BLOCK, LANES))] * ns,
             out_specs=whole((SYM, 640)),
             scratch_shapes=prep_scratch(length) + extra,
         ),
-        compiler_params=pltpu.CompilerParams(vmem_limit_bytes=VMEM_LIMIT),
+        compiler_params=PARAMS,
         name="mix_backward",
-    )(scalars, *toks, tabs, bcp, *d_gated)
-
-
-def weight_kernel(scalars, g_ref, cot_ref, out_ref, *, ns):
-    mine = scalars[0]
-    total = None
+    )(scalars, *toks, *raw, *d_gated)
+
+
+QUARTERS = 3
+
+
+def d_gated_kernel(scalars, *refs, nq, ns):
+    cots, weights, outs = refs[:nq], refs[nq : 2 * nq], refs[2 * nq :]
+    cot = jnp.concatenate([a[...] for a in cots], 1)
+    mine = scalars[1]
     for k in range(ns):
-        at = jnp.where(mine >= k, mine - k, mine - k + ns)
-        rows = g_ref[0, pl.ds(pl.multiple_of(at * BLOCK, BLOCK), BLOCK), :]
-        part = mm(rows, cot_ref[k], TN)
-        total = part if total is None else total + part
-    out_ref[...] = total
-
-
-def call_weight(scalars, gs, cots):
-    slices, length, _ = gs.shape
-    ns, _, columns = cots.shape
+        to = jnp.where(mine + k >= ns, mine + k - ns, mine + k)
+        rows = pl.ds(pl.multiple_of(to * LANES, LANES), LANES)
+        weight = jnp.concatenate([w[rows, :] for w in weights], 1)
+        outs[k][...] = mm(cot, weight, NT).astype(BF16)
+
+
+def call_d_gated(scalars, cots, out_weight, ns):
+    nq = len(cots)
+    rows, cols = cots[0].shape
+    weight_spec = lambda k: pl.BlockSpec((ns * LANES, cols), lambda i, s: (s[2], s[QUARTERS + k]))
     return pl.pallas_call(
-        functools.partial(weight_kernel, ns=ns),
-        out_shape=jax.ShapeDtypeStruct((slices * LANES, columns), F32),
+        functools.partial(d_gated_kernel, nq=nq, ns=ns),
+        out_shape=[jax.ShapeDtypeStruct((rows, LANES), BF16)] * ns,
         grid_spec=pltpu.PrefetchScalarGridSpec(
             num_scalar_prefetch=1,
-            grid=(slices,),
-            in_specs=[
-                pl.BlockSpec((1, length, LANES), lambda i, s: (i, 0, 0)),
-                pl.BlockSpec((ns, BLOCK, columns), lambda i, s: (0, 0, 0)),
-            ],
-            out_specs=pl.BlockSpec((LANES, columns), lambda i, s: (s[1 + i], 0)),
+            grid=(1,),
+            in_specs=[whole((rows, cols))] * nq + [weight_spec(k) for k in range(nq)],
+            out_specs=[whole((rows, LANES))] * ns,
         ),
-        compiler_params=pltpu.CompilerParams(vmem_limit_bytes=VMEM_LIMIT),
+        compiler_params=PARAMS,
+        name="d_gated",
+    )(scalars, *cots, *([out_weight] * nq))
+
+
+def out_kernel(scalars, own_ref, other_ref, weight_ref, *refs, ns, nh, nc, cols):
+    outs, acc = refs[:nh], refs[nh]
+    i = pl.program_id(0)
+    here = pl.ds(pl.multiple_of(scalars[1] * BLOCK, BLOCK), BLOCK)
+
+    @pl.when(i == 0)
+    def _():
+        acc[...] = jnp.zeros_like(acc)
+
+    def add(ref):
+        weight = []
+        for k in range(nh):
+            at = scalars[QUARTERS + k * nc] * cols
+            weight.append(weight_ref[:, pl.ds(pl.multiple_of(at, LANES), cols)])
+        acc[...] += mm(ref[0, :, here], jnp.concatenate(weight, 1), TN)
+
+    @pl.when(i < ns)
+    def _():
+        add(own_ref)
+
+    @pl.when(i >= ns)
+    def _():
+        add(other_ref)
+
+    @pl.when(i == pl.num_programs(0) - 1)
+    def _():
+        for k in range(nh):
+            outs[k][...] = acc[:, k * cols : (k + 1) * cols]
+
+
+def slice_specs(ns, length):
+    return [
+        pl.BlockSpec((1, LANES, length), lambda i, s: (jnp.minimum(i, ns - 1), 0, 0)),
+        pl.BlockSpec((1, LANES, length), lambda i, s: (jnp.maximum(i - ns, 0), 0, 0)),
+    ]
+
+
+def call_out(scalars, own, other, out_weight, nh, nc):
+    ns, _, length = own.shape
+    width = out_weight.shape[1]
+    cols = width // (nh * nc)
+    places = QUARTERS + nh * nc
+    return pl.pallas_call(
+        functools.partial(out_kernel, ns=ns, nh=nh, nc=nc, cols=cols),
+        out_shape=[jax.ShapeDtypeStruct((BLOCK, cols), F32)] * nh,
+        grid_spec=pltpu.PrefetchScalarGridSpec(
+            num_scalar_prefetch=1,
+            grid=(ns * nc,),
+            in_specs=slice_specs(ns, length)
+            + [pl.BlockSpec((LANES, width), lambda i, s: (s[places + i], 0))],
+            out_specs=[whole((BLOCK, cols))] * nh,
+            scratch_shapes=[pltpu.VMEM((BLOCK, nh * cols), F32)],
+        ),
+        compiler_params=PARAMS,
+        name="layer_out",
+    )(scalars, own, other, out_weight)
+
+
+def weight_kernel(scalars, own_ref, other_ref, cot_own, cot_other, out_ref, *, ns, nh, nc, cols):
+    i = pl.program_id(0)
+    mine = scalars[1]
+
+    def fill(ref):
+        chunks = []
+        for k in range(ns):
+            at = jnp.where(mine >= k, mine - k, mine - k + ns)
+            chunks.append(ref[0, :, pl.ds(pl.multiple_of(at * BLOCK, BLOCK), BLOCK)])
+        left = jnp.concatenate(chunks, 1)
+        for k in range(nh):
+            for m, cot in ((0, cot_own), (1, cot_other)):
+                right = cot[k * ns : (k + 1) * ns].reshape(ns * BLOCK, cols)
+                at = scalars[QUARTERS + k * nc + m] * cols
+                out_ref[:, pl.ds(pl.multiple_of(at, LANES), cols)] = mm(left, right, NN)
+
+    @pl.when(i < ns)
+    def _():
+        fill(own_ref)
+
+    @pl.when(i >= ns)
+    def _():
+        fill(other_ref)
+
+
+def call_weight(scalars, own, other, cot_own, cot_other, width, nh, nc):
+    ns, _, length = own.shape
+    cols = cot_own.shape[2]
+    places = QUARTERS + nh * nc
+    return pl.pallas_call(
+        functools.partial(weight_kernel, ns=ns, nh=nh, nc=nc, cols=cols),
+        out_shape=jax.ShapeDtypeStruct((ns * nc * LANES, width), F32),
+        grid_spec=pltpu.PrefetchScalarGridSpec(
+            num_scalar_prefetch=1,
+            grid=(ns * nc,),
+            in_specs=slice_specs(ns, length) + [whole(cot_own.shape)] * 2,
+            out_specs=pl.BlockSpec((LANES, width), lambda i, s: (s[places + i], 0)),
+        ),
+        compiler_params=PARAMS,
         name="weight_grad",
-    )(scalars, gs, cots)
+    )(scalars, own, other, cot_own, cot_other)
+
+
+def final_kernel(scalars, *refs, ns, nq, vocab, places):
+    firsts, packed, shared = refs[:ns], refs[ns], refs[ns + 1 : ns + nq]
+    xz_ref, bc_ref, dt_ref = refs[ns + nq :]
+    d_bc = packed[:, ns * 384 : ns * 384 + 256]
+    for a in list(firsts) + list(shared):
+        d_bc = d_bc + a[:, a.shape[1] - 256 :]
+    for i in range(2):
+        for k in range(vocab):
+            bc_ref[k, i : i + 1, :] = d_bc[k : k + 1, i * 128 : i * 128 + 128]
+    lane = lax.broadcasted_iota(jnp.int32, (SYM, dt_ref.shape[1]), 1)
+    d_dt = jnp.zeros((SYM, dt_ref.shape[1]), F32)
+    for n in range(2 * ns):
+        j = scalars[places + n]
+        if n < ns:
+            piece = firsts[n][:, 0:384]
+        else:
+            piece = packed[:, (n - ns) * 384 : (n - ns + 1) * 384]
+        for i in range(2):
+            for k in range(vocab):
+                xz_ref[k, i : i + 1, pl.ds(pl.multiple_of(j * LANES, LANES), LANES)] = piece[
+                    k : k + 1, i * 128 : i * 128 + 128
+                ]
+            total = jnp.sum(piece[:, 256 + 64 * i : 320 + 64 * i], 1, keepdims=True)
+            d_dt = jnp.where(lane == 2 * j + i, total, d_dt)
+    dt_ref[...] = d_dt[:vocab]
+
+
+def call_final(scalars, firsts, packed, shared, raw, places):
+    ns = len(firsts)
+    shapes = [raw[1].shape, raw[2].shape, raw[5].shape]
+    arrays = list(firsts) + [packed] + list(shared)
+    return pl.pallas_call(
+        functools.partial(
+            final_kernel, ns=ns, nq=len(shared) + 1, vocab=raw[1].shape[0], places=places
+        ),
+        out_shape=[jax.ShapeDtypeStruct(a, F32) for a in shapes],
+        grid_spec=pltpu.PrefetchScalarGridSpec(
+            num_scalar_prefetch=1,
+            grid=(1,),
+            in_specs=[whole(a.shape) for a in arrays],
+            out_specs=[whole(a) for a in shapes],
+        ),
+        compiler_params=PARAMS,
+        name="place_grads",
+    )(scalars, *arrays)
 
 
 def around(x, axis):
@@ -530,75 +719,55 @@
     ]
 
 
+def across(x, hops, nh, nc):
+    pairs = [
+        (a * nc + b, (a + hops[0]) % nh * nc + (b + hops[1]) % nc)
+        for a in range(nh)
+        for b in range(nc)
+    ]
+    return lax.ppermute(x, ("head", "sub"), pairs)
+
+
 def by_channel(
     token_ids, basemap, xz_table, bc_table, dt_table, conv_x, conv_bc, a_log, skip_gain, out_weight, cotangent
 ):
     ns, nc, nh = lax.axis_size("seq"), lax.axis_size("sub"), lax.axis_size("head")
     s, c, h = lax.axis_index("seq"), lax.axis_index("sub"), lax.axis_index("head")
-    vocab, _, inner = xz_table.shape
-    conv = conv_x.shape[0]
-    heads = dt_table.shape[1]
     width = out_weight.shape[1]
-    j = c * ns + s
+    raw = (basemap, xz_table, bc_table, conv_x, conv_bc, dt_table, a_log, skip_gain)
+    hops = [(a, b) for a in range(nh) for b in range(nc)]
     toks = around(token_ids.reshape(1, BLOCK), "seq")
-    cot_rows = lax.all_gather(cotangent, ("head", "sub"), axis=1, tiled=True)
-    scalars = jnp.concatenate([jnp.stack([j, s]).astype(jnp.int32), basemap])
-    pad = lambda a, n: jnp.pad(a, ((0, n - a.shape[0]), (0, 0)))
-    spread = lambda a: jnp.repeat(a, inner // heads, axis=1)
-    tabs = jnp.concatenate(
-        [
-            pad(xz_table[:, 0].astype(F32), SYM),
-            pad(xz_table[:, 1].astype(F32), SYM),
-            pad(spread(dt_table), SYM),
-            conv_x.astype(F32),
-            pad(spread(jnp.stack([a_log, skip_gain])), SYM - conv),
-        ],
-        0,
-    )
-    bcp = jnp.concatenate(
-        [
-            pad(bc_table.reshape(vocab, -1).astype(F32), SYM),
-            pad(conv_bc.reshape(conv, -1).astype(F32), SYM),
-        ],
-        0,
-    )
-    weight_rows = lax.dynamic_slice_in_dim(out_weight, c * (ns * LANES), ns * LANES, 0)
-    d_mine = lax.dot_general(cot_rows, weight_rows, NT, preferred_element_type=F32).astype(BF16)
-    at = lambda k: lax.dynamic_slice_in_dim(d_mine, ((s + k) % ns) * LANES, LANES, 1)
-    d_gated = [at(0)] + [
-        lax.ppermute(at(k), "seq", [(i, (i + k) % ns) for i in range(ns)]) for k in range(1, ns)
+    near = [across(cotangent, hop, nh, nc) if any(hop) else cotangent for hop in hops]
+    slot = jnp.arange(nh * nc, dtype=jnp.int32)
+    quarters = (h - slot // nc) % nh * nc + (c - slot % nc) % nc
+    slot = jnp.arange(ns * nc, dtype=jnp.int32)
+    places = (c - slot // ns) % nc * ns + (s - slot % ns) % ns
+    scalars = jnp.concatenate([jnp.stack([c * ns + s, s, c]), quarters, places]).astype(jnp.int32)
+    d_parts = call_d_gated(scalars, near, out_weight, ns)
+    d_gated = [d_parts[0]] + [
+        lax.ppermute(d_parts[k], "seq", [(i, (i + k) % ns) for i in range(ns)])
+        for k in range(1, ns)
     ]
-    cots = around(cot_rows, "seq")
-    gated = call_forward(scalars, toks, tabs, bcp, conv, vocab)
-    grads = call_backward(scalars, toks, tabs, bcp, d_gated, conv, vocab)
-    gs = jnp.stack(around(gated, "seq"), 0)
-    other = lax.ppermute(gs, "sub", [(i, (i + 1) % nc) for i in range(nc)])
-    gs = jnp.concatenate([gs, other], 0)
-    order = (s - jnp.arange(ns, dtype=jnp.int32)) % ns
-    place = jnp.concatenate([c * ns + order, (1 - c) * ns + order]).astype(jnp.int32)
-    d_out_weight = call_weight(
-        jnp.concatenate([s[None].astype(jnp.int32), place]), gs, jnp.stack(cots, 0)
-    )
-    mine = lax.dynamic_slice_in_dim(gs, s * BLOCK, BLOCK, 1)
-    wg = out_weight.reshape(nc * ns, LANES, width)[place]
-    part = width // (nh * nc)
-    parts = []
-    for k in range(nh):
-        first = (((h + k) % nh) * nc + c) * part
-        cols = lax.dynamic_slice_in_dim(wg, first, part, 2)
-        parts.append(jnp.einsum("jtk,jkc->tc", mine, cols, preferred_element_type=F32))
+    cots = jnp.stack(around(cotangent, "seq"), 0)
+    gated = call_forward(scalars, toks, raw)
+    cots = jnp.concatenate(
+        [cots] + [across(cots, (k, 0), nh, nc) for k in range(1, nh)], 0
+    )
+    own = jnp.stack(around(gated, "seq"), 0)
+    grads = call_backward(scalars, toks, raw, d_gated)
+    cots_other = across(cots, (0, 1), nh, nc)
+    other = across(own, (0, 1), nh, nc)
+    firsts = around(grads, "seq")
+    shared = sum(a[:, 384:] for a in firsts)
+    packed = across(jnp.concatenate([a[:, :384] for a in firsts] + [shared], 1), (0, 1), nh, nc)
+    far = [across(shared, hop, nh, nc) for hop in hops if hop[0]]
+    parts = call_out(scalars, own, other, out_weight, nh, nc)
     total = parts[0]
     for k in range(1, nh):
-        total = total + lax.ppermute(parts[k], "head", [(i, (i + k) % nh) for i in range(nh)])
+        total = total + across(parts[k], (nh - k, 0), nh, nc)
     layer_out = total.astype(BF16)
-    own, shared = grads[:, : 3 * LANES], grads[:, 3 * LANES :]
-    shared = lax.psum(shared, ("seq", "head", "sub"))
-    owns = lax.all_gather(own, ("sub", "seq"))
-    full = jnp.moveaxis(owns[:, :vocab], 0, 1).reshape(vocab, nc * ns, 3, LANES)
-    full = jnp.moveaxis(full, 2, 1).reshape(vocab, 3, inner)
-    d_xz = full[:, :2]
-    d_dt = full[:, 2].reshape(vocab, heads, inner // heads).sum(-1)
-    d_bc = shared[:vocab].reshape(bc_table.shape)
+    d_out_weight = call_weight(scalars, own, other, cots, cots_other, width, nh, nc)
+    d_xz, d_bc, d_dt = call_final(scalars, firsts, packed, far, raw, QUARTERS + nh * nc)
     return (layer_out, d_out_weight, d_xz, d_bc, d_dt)
 
 

time: 145 us -> 89.5 us (0.62)
  blocking collectives: 65.4 us -> 0 us
  local copies, waits for them, and re-layouts: 20.7 us -> 5.8 us
  Pallas kernels: 24.2 us -> 36.2 us
  waiting for transfers between devices: 4.52 us -> 15.5 us
  starting transfers between devices: 17.2 us -> 28 us
  other arithmetic: 8.09 us -> 2.38 us
  matrix products: 2.58 us -> 0 us
    psum x1 -> x0, blocking collectives: 33.6 us -> none  [by_channel(): shared = lax.psum(shared, ('seq', 'head', 'sub'))]
    all_gather x2 -> x0, blocking collectives: 31.8 us -> none  [the longest x1 25.9 us: by_channel(): owns = lax.all_gather(own, ('sub', 'seq'))]
    pallas_call x3 -> x6, Pallas kernels: 24.2 us -> 36.2 us  [the longest x1 9.9 us: call_backward(): pl.pallas_call(functools.partial(backward_kernel, ns=ns, conv=raw[3].shap...]
    ppermute x5 -> x13, starting transfers between devices: 3.97 us -> 12.5 us  [the longest x10 7.17 us: across(): return lax.ppermute(x, ('head', 'sub'), pairs)]
    ppermute x5 -> x13, waiting for transfers between devices: 0.03 us -> 5.99 us  [the longest x10 3.24 us: across(): return lax.ppermute(x, ('head', 'sub'), pairs)]
    slice x5 -> x0, local copies, waits for them, and re-layouts: 5.33 us -> none  [the longest x1 1.56 us: by_channel(): d_dt = full[:, 2].reshape(vocab, heads, inner // heads).sum(-1)]
    ppermute x9 -> x12, waiting for transfers between devices: 4.49 us -> 9.49 us  [around(): lax.ppermute(x, axis, [(i, (i + k) % n) for i in range(n)])]
    another operation x3 -> x2, other arithmetic: 4.07 us -> 0.1 us  [the longest x1 0.07 us: by_channel(): own = jnp.stack(around(gated, 'seq'), 0)]
  transfers between devices with their start and end apart: 14 -> 25, of which waited for: 1 -> 7; matrix products, arithmetic and copies ran while one was open for 21% -> 5% of each run, Pallas kernels for 17% -> 32%
where the time goes in v1:
time: 89.5 us; the launch traced here: 88.7 us
  Pallas kernels  36.2 us (40%)
  starting transfers between devices  28 us (31%)
  waiting for transfers between devices  15.5 us (17%)
  local copies, waits for them, and re-layouts  5.8 us (6%)
  other arithmetic  2.38 us (3%)
    ppermute x12, starting transfers between devices, around(): lax.ppermute(x, axis, [(i, (i + k) % n) for i in range(n)])  15.5 us
    pallas_call x1, Pallas kernels, call_backward(): pl.pallas_call(functools.partial(backward_kernel, ns=ns, conv=raw[3].shap...  9.9 us
    ppermute x12, waiting for transfers between devices, around(): lax.ppermute(x, axis, [(i, (i + k) % n) for i in range(n)])  9.49 us
    pallas_call x1, Pallas kernels, call_weight(): pl.pallas_call(functools.partial(weight_kernel, ns=ns, nh=nh, nc=nc, cols...  8.03 us
    ppermute x10, starting transfers between devices, across(): return lax.ppermute(x, ('head', 'sub'), pairs)  7.17 us
    pallas_call x1, Pallas kernels, call_out(): pl.pallas_call(functools.partial(out_kernel, ns=ns, nh=nh, nc=nc, cols=co...  6.83 us
    pallas_call x1, Pallas kernels, call_forward(): pl.pallas_call(functools.partial(forward_kernel, ns=ns, conv=raw[3].shape...  6.01 us
    ppermute x3, starting transfers between devices, by_channel(): lax.ppermute(d_parts[k], 'seq', [(i, (i + k) % ns) for i in range(ns)])  5.32 us
  transfers between devices with their start and end apart: 25, of which 7 were waited for; matrix products, arithmetic and copies ran while one was open for 5% of the time, Pallas kernels for 32%

profile of v1, /device:TPU:0, one launch (start us, length us, event | category | flops | bytes accessed | tf_op | source)
XLA Modules:
  0.0 88.7 jit_solution(14192849825931497389)
XLA Ops:
  1.1 2.6 %collective-permute-start.14 = (bf16[128,256]{1,0:T(8,128)(2,1)}, bf16[128,256]{1,0:T(8,128)(2,1)S(1)}, u32[]{:S(2)}, u32[]{:S(2)}) collective-permute-start(bf16[128,256]{1,0:T(8,128)(2,1)} %refs_0_.1), channel_id=1, source_target_pairs={{0,2},{1,3},{2,0},{3,1},{4,6},{5,7},{6,4},{7,5},{8,10},{9,11},{10,... | collective-permute-start | bytes 196616 | tf_op jit(solution)/shard_map/ppermute | solution.py:728
  3.8 1.8 %collective-permute-start = (s32[1,128]{1,0:T(1,128)}, s32[1,128]{1,0:T(1,128)S(1)}, u32[]{:S(2)}, u32[]{:S(2)}) collective-permute-start(s32[1,128]{1,0:T(1,128)} %bitcast.24), channel_id=1, source_target_pairs={{0,4},{4,8},{8,12},{12,0},{1,5},{5,9},{9,13},{13,1},{2,6},{6,10},{... | collective-permute-start | bytes 1544 | tf_op jit(solution)/shard_map/ppermute | solution.py:718
  5.6 2.6 %collective-permute-start.1 = (s32[1,128]{1,0:T(1,128)}, s32[1,128]{1,0:T(1,128)S(1)}, u32[]{:S(2)}, u32[]{:S(2)}) collective-permute-start(s32[1,128]{1,0:T(1,128)} %bitcast.25), channel_id=1, source_target_pairs={{0,8},{4,12},{8,0},{12,4},{1,9},{5,13},{9,1},{13,5},{2,10},{6,14},... | collective-permute-start | bytes 1544 | tf_op jit(solution)/shard_map/ppermute | solution.py:718
  8.2 0.8 constant_dynamic-update-slice_fusion.4
  9.3 2.0 %collective-permute-start.2 = (s32[1,128]{1,0:T(1,128)}, s32[1,128]{1,0:T(1,128)S(1)}, u32[]{:S(2)}, u32[]{:S(2)}) collective-permute-start(s32[1,128]{1,0:T(1,128)} %bitcast.26), channel_id=1, source_target_pairs={{0,12},{4,0},{8,4},{12,8},{1,13},{5,1},{9,5},{13,9},{2,14},{6,2},{... | collective-permute-start | bytes 1544 | tf_op jit(solution)/shard_map/ppermute | solution.py:718
  11.8 0.7 concatenate.10.scalars
  13.0 1.0 %collective-permute-start.9 = (bf16[128,256]{1,0:T(8,128)(2,1)}, bf16[128,256]{1,0:T(8,128)(2,1)S(1)}, u32[]{:S(2)}, u32[]{:S(2)}) collective-permute-start(bf16[128,256]{1,0:T(8,128)(2,1)} %refs_0_.1), channel_id=1, source_target_pairs={{0,8},{4,12},{8,0},{12,4},{1,9},{5,13},{9,1},{13,5},{2,10},{6,14},... | collective-permute-start | bytes 196616 | tf_op jit(solution)/shard_map/ppermute | solution.py:718
  14.0 6.0 %mix_forward.1 = bf16[128,512]{1,0:T(8,128)(2,1)} custom-call(s32[15]{0:T(128)} %concatenate.10.scalars, s32[1,128]{1,0:T(1,128)} %bitcast.27, s32[1,128]{1,0:T(1,128)} %copy-done.18, s32[1,128]{1,0:T(1,128)} %copy-done.19, s32[1,128]{1,0:T(1,128)} %copy-done.20, s32[5]{0:T(128)} %refs_4_.5, bf16[5,2,1024]{2,1,0:T(2,128)(2,1)} %refs_5_.5, ...), custom_call_target="tpu_custom_call" | custom-call | tf_op jit(solution)/shard_map/mix_forward/pallas_call | solution.py:497
  20.0 3.4 %collective-permute-start.10 = (bf16[128,256]{1,0:T(8,128)(2,1)}, bf16[128,256]{1,0:T(8,128)(2,1)S(1)}, u32[]{:S(2)}, u32[]{:S(2)}) collective-permute-start(bf16[128,256]{1,0:T(8,128)(2,1)} %refs_0_.1), channel_id=1, source_target_pairs={{0,12},{4,0},{8,4},{12,8},{1,13},{5,1},{9,5},{13,9},{2,14},{6,2},{... | collective-permute-start | bytes 196616 | tf_op jit(solution)/shard_map/ppermute | solution.py:718
  23.5 1.5 %collective-permute-start.4 = (bf16[128,512]{1,0:T(8,128)(2,1)}, bf16[128,512]{1,0:T(8,128)(2,1)S(1)}, u32[]{:S(2)}, u32[]{:S(2)}) collective-permute-start(bf16[128,512]{1,0:T(8,128)(2,1)} %mix_forward.1), channel_id=1, source_target_pairs={{0,8},{4,12},{8,0},{12,4},{1,9},{5,13},{9,1},{13,5},{2,10},{6,14},... | collective-permute-start | bytes 393224 | tf_op jit(solution)/shard_map/ppermute | solution.py:718
  25.0 3.1 %d_gated.1 = (bf16[128,128]{1,0:T(8,128)(2,1)}, bf16[128,128]{1,0:T(8,128)(2,1)}, bf16[128,128]{1,0:T(8,128)(2,1)}, bf16[128,128]{1,0:T(8,128)(2,1)}) custom-call(s32[15]{0:T(128)} %concatenate.10.scalars, bf16[128,256]{1,0:T(8,128)(2,1)} %refs_0_.1, bf16[128,256]{1,0:T(8,128)(2,1)} %copy-done.9, bf16[128,256]{1,0:T(8,128)(2,1)} %copy-done.10, ...), custom_call_target="tpu_custom_call" | custom-call | tf_op jit(solution)/shard_map/d_gated/pallas_call | solution.py:553
  28.1 2.8 %collective-permute-start.16 = (bf16[128,128]{1,0:T(8,128)(2,1)}, bf16[128,128]{1,0:T(8,128)(2,1)S(1)}, u32[]{:S(2)}, u32[]{:S(2)}) collective-permute-start(bf16[128,128]{1,0:T(8,128)(2,1)} %get-tuple-element.17), channel_id=1, source_target_pairs={{0,4},{4,8},{8,12},{12,0},{1,5},{5,9},{9,13},{13,1},{2,6},{6,10},{... | collective-permute-start | bytes 98312 | tf_op jit(solution)/shard_map/ppermute | solution.py:748
  30.9 0.7 collective-permute-start.17
  31.6 1.8 %collective-permute-start.18 = (bf16[128,128]{1,0:T(8,128)(2,1)}, bf16[128,128]{1,0:T(8,128)(2,1)S(1)}, u32[]{:S(2)}, u32[]{:S(2)}) collective-permute-start(bf16[128,128]{1,0:T(8,128)(2,1)} %get-tuple-element.19), channel_id=1, source_target_pairs={{0,12},{4,0},{8,4},{12,8},{1,13},{5,1},{9,5},{13,9},{2,14},{6,2},{... | collective-permute-start | bytes 98312 | tf_op jit(solution)/shard_map/ppermute | solution.py:748
  33.5 0.7 collective-permute-done.16.refs_13_
  34.1 1.6 %collective-permute-start.5 = (bf16[128,512]{1,0:T(8,128)(2,1)S(1)}, bf16[128,512]{1,0:T(8,128)(2,1)S(1)}, u32[]{:S(2)}, u32[]{:S(2)}) collective-permute-start(bf16[128,512]{1,0:T(8,128)(2,1)S(1)} %copy-done.5), channel_id=1, source_target_pairs={{0,12},{4,0},{8,4},{12,8},{1,13},{5,1},{9,5},{13,9},{2,14},{6,2},{... | collective-permute-start | bytes 393224 | tf_op jit(solution)/shard_map/ppermute | solution.py:718
  35.7 2.1 %collective-permute-done.17.refs_14_ = bf16[128,128]{1,0:T(8,128)(2,1)S(1)} collective-permute-done((bf16[128,128]{1,0:T(8,128)(2,1)}, bf16[128,128]{1,0:T(8,128)(2,1)S(1)}, u32[]{:S(2)}, u32[]{:S(2)}) %collective-permute-start.17) | collective-permute-done | bytes 32800 | tf_op jit(solution)/shard_map/ppermute | solution.py:748
  37.8 1.5 %collective-permute-start.11 = (bf16[4,128,256]{2,1,0:T(8,128)(2,1)S(1)}, bf16[4,128,256]{2,1,0:T(8,128)(2,1)S(1)}, u32[]{:S(2)}, u32[]{:S(2)}) collective-permute-start(bf16[4,128,256]{2,1,0:T(8,128)(2,1)S(1)} %pad_maximum_fusion.1), channel_id=1, source_target_pairs={{0,2},{1,3},{2,0},{3,1},{4,6},{5,7},{6,4},{7,5},{8,10},{9,11},{10,... | collective-permute-start | bytes 786440 | tf_op jit(solution)/shard_map/ppermute | solution.py:728
  39.9 9.9 %mix_backward.1.refs_0_ = f32[8,640]{1,0:T(8,128)} custom-call(s32[15]{0:T(128)} %concatenate.10.scalars, s32[1,128]{1,0:T(1,128)} %bitcast.28, s32[1,128]{1,0:T(1,128)} %copy-done.18, s32[1,128]{1,0:T(1,128)} %copy-done.19, s32[1,128]{1,0:T(1,128)} %copy-done.20, s32[5]{0:T(128)} %refs_4_.5, bf16[5,2,1024]{2,1,0:T(2,128)(2,1)} %refs_5_.5, ...), custom_call_target="tpu_custom_call" | custom-call | tf_op jit(solution)/shard_map/mix_backward/pallas_call | solution.py:520
  49.8 0.7 constant_dynamic-update-slice_fusion.9
  50.6 5.0 %collective-permute-done.19.refs_1_ = f32[8,640]{1,0:T(8,128)S(1)} collective-permute-done((f32[8,640]{1,0:T(8,128)}, f32[8,640]{1,0:T(8,128)S(1)}, u32[]{:S(2)}, u32[]{:S(2)}) %collective-permute-start.19) | collective-permute-done | bytes 20512 | tf_op jit(solution)/shard_map/ppermute | solution.py:718
  55.6 1.0 %collective-permute-start.21 = (f32[8,640]{1,0:T(8,128)}, f32[8,640]{1,0:T(8,128)S(1)}, u32[]{:S(2)}, u32[]{:S(2)}) collective-permute-start(f32[8,640]{1,0:T(8,128)} %mix_backward.1.refs_0_), channel_id=1, source_target_pairs={{0,12},{4,0},{8,4},{12,8},{1,13},{5,1},{9,5},{13,9},{2,14},{6,2},{... | collective-permute-start | bytes 61448 | tf_op jit(solution)/shard_map/ppermute | solution.py:718
  56.8 3.7 %collective-permute-done.20.refs_2_ = f32[8,640]{1,0:T(8,128)S(1)} collective-permute-done((f32[8,640]{1,0:T(8,128)}, f32[8,640]{1,0:T(8,128)S(1)}, u32[]{:S(2)}, u32[]{:S(2)}) %collective-permute-start.20) | collective-permute-done | bytes 20512 | tf_op jit(solution)/shard_map/ppermute | solution.py:718
  60.7 0.9 copy-done.1
  61.6 6.8 %layer_out.1 = (f32[128,256]{1,0:T(8,128)}, f32[128,256]{1,0:T(8,128)}) custom-call(s32[15]{0:T(128)} %concatenate.10.scalars, bf16[4,128,512]{2,1,0:T(8,128)(2,1)} %copy-done, bf16[4,128,512]{2,1,0:T(8,128)(2,1)} %copy-done.1, bf16[1024,1024]{1,0:T(8,128)(2,1)} %refs_7_.4), custom_call_target="tpu_custom_call" | custom-call | tf_op jit(solution)/shard_map/layer_out/pallas_call | solution.py:609
  68.9 0.7 constant_dynamic-update-slice_fusion.5
  69.8 1.5 %collective-permute-start.23 = (f32[8,256]{1,0:T(8,128)S(1)}, f32[8,256]{1,0:T(8,128)S(1)}, u32[]{:S(2)}, u32[]{:S(2)}) collective-permute-start(f32[8,256]{1,0:T(8,128)S(1)} %get-tuple-element.24), channel_id=1, source_target_pairs={{0,2},{1,3},{2,0},{3,1},{4,6},{5,7},{6,4},{7,5},{8,10},{9,11},{10,... | collective-permute-start | bytes 24584 | tf_op jit(solution)/shard_map/ppermute | solution.py:728
  71.5 3.2 %collective-permute-done.23.refs_5_ = f32[8,256]{1,0:T(8,128)S(1)} collective-permute-done((f32[8,256]{1,0:T(8,128)S(1)}, f32[8,256]{1,0:T(8,128)S(1)}, u32[]{:S(2)}, u32[]{:S(2)}) %collective-permute-start.23) | collective-permute-done | bytes 8224 | tf_op jit(solution)/shard_map/ppermute | solution.py:728
  75.9 2.4 %place_grads.1 = (f32[5,2,1024]{2,1,0:T(2,128)}, f32[5,2,128]{2,1,0:T(2,128)}, f32[5,16]{1,0:T(8,128)}) custom-call(s32[15]{0:T(128)} %concatenate.10.scalars, f32[8,640]{1,0:T(8,128)} %mix_backward.1.refs_0_, f32[8,640]{1,0:T(8,128)} %copy-done.6, f32[8,640]{1,0:T(8,128)} %copy-done.7, f32[8,640]{1,0:T(8,128)} %copy-done.8, f32[8,1792]{1,0:T(8,128)} %copy-done.12, ...), custom_call_target="tpu_custom_call" | custom-call | tf_op jit(solution)/shard_map/place_grads/pallas_call | solution.py:699
  78.3 1.5 %add_convert_fusion = bf16[128,256]{1,0:T(8,128)(2,1)} fusion(f32[128,256]{1,0:T(8,128)} %get-tuple-element.14, f32[128,256]{1,0:T(8,128)S(1)} %collective-permute-done.7), kind=kLoop, calls=%fused_computation.2 | loop fusion | flops 65536 | bytes 327680 | tf_op jit(solution)/shard_map/convert_element_type | solution.py:768
  79.8 0.8 copy-done.4
  80.7 8.0 %weight_grad.1 = f32[1024,1024]{1,0:T(8,128)} custom-call(s32[15]{0:T(128)} %concatenate.10.scalars, bf16[4,128,512]{2,1,0:T(8,128)(2,1)} %copy-done, bf16[4,128,512]{2,1,0:T(8,128)(2,1)} %copy-done.1, bf16[8,128,256]{2,1,0:T(8,128)(2,1)} %copy-done.2, bf16[8,128,256]{2,1,0:T(8,128)(2,1)} %copy-done.4), custom_call_target="tpu_custom_call" | custom-call | tf_op jit(solution)/shard_map/weight_grad/pallas_call | solution.py:654
  (82 shorter events, 5.0 us)
Async XLA Ops:
  0.6 19.4 %collective-permute-start.13 = (bf16[128,256]{1,0:T(8,128)(2,1)}, bf16[128,256]{1,0:T(8,128)(2,1)S(1)}, u32[]{:S(2)}, u32[]{:S(2)}) collective-permute-start(bf16[128,256]{1,0:T(8,128)(2,1)} %refs_0_.1), channel_id=1, source_target_pairs={{0,1},{1,0},{2,3},{3,2},{4,5},{5,4},{6,7},{7,6},{8,9},{9,8},{10,11... | collective-permute-start | bytes 196616 | tf_op jit(solution)/shard_map/ppermute | solution.py:728
  1.1 22.2 %collective-permute-start.14 = (bf16[128,256]{1,0:T(8,128)(2,1)}, bf16[128,256]{1,0:T(8,128)(2,1)S(1)}, u32[]{:S(2)}, u32[]{:S(2)}) collective-permute-start(bf16[128,256]{1,0:T(8,128)(2,1)} %refs_0_.1), channel_id=1, source_target_pairs={{0,2},{1,3},{2,0},{3,1},{4,6},{5,7},{6,4},{7,5},{8,10},{9,11},{10,... | collective-permute-start | bytes 196616 | tf_op jit(solution)/shard_map/ppermute | solution.py:728
  3.7 19.8 %collective-permute-start.15 = (bf16[128,256]{1,0:T(8,128)(2,1)}, bf16[128,256]{1,0:T(8,128)(2,1)S(1)}, u32[]{:S(2)}, u32[]{:S(2)}) collective-permute-start(bf16[128,256]{1,0:T(8,128)(2,1)} %refs_0_.1), channel_id=1, source_target_pairs={{0,3},{1,2},{2,1},{3,0},{4,7},{5,6},{6,5},{7,4},{8,11},{9,10},{10,... | collective-permute-start | bytes 196616 | tf_op jit(solution)/shard_map/ppermute | solution.py:728
  3.8 5.5 %collective-permute-start = (s32[1,128]{1,0:T(1,128)}, s32[1,128]{1,0:T(1,128)S(1)}, u32[]{:S(2)}, u32[]{:S(2)}) collective-permute-start(s32[1,128]{1,0:T(1,128)} %bitcast.24), channel_id=1, source_target_pairs={{0,4},{4,8},{8,12},{12,0},{1,5},{5,9},{9,13},{13,1},{2,6},{6,10},{... | collective-permute-start | bytes 1544 | tf_op jit(solution)/shard_map/ppermute | solution.py:718
  5.6 5.7 %collective-permute-start.1 = (s32[1,128]{1,0:T(1,128)}, s32[1,128]{1,0:T(1,128)S(1)}, u32[]{:S(2)}, u32[]{:S(2)}) collective-permute-start(s32[1,128]{1,0:T(1,128)} %bitcast.25), channel_id=1, source_target_pairs={{0,8},{4,12},{8,0},{12,4},{1,9},{5,13},{9,1},{13,5},{2,10},{6,14},... | collective-permute-start | bytes 1544 | tf_op jit(solution)/shard_map/ppermute | solution.py:718
  9.3 3.7 %collective-permute-start.2 = (s32[1,128]{1,0:T(1,128)}, s32[1,128]{1,0:T(1,128)S(1)}, u32[]{:S(2)}, u32[]{:S(2)}) collective-permute-start(s32[1,128]{1,0:T(1,128)} %bitcast.26), channel_id=1, source_target_pairs={{0,12},{4,0},{8,4},{12,8},{1,13},{5,1},{9,5},{13,9},{2,14},{6,2},{... | collective-permute-start | bytes 1544 | tf_op jit(solution)/shard_map/ppermute | solution.py:718
  11.3 16.8 %collective-permute-start.8 = (bf16[128,256]{1,0:T(8,128)(2,1)}, bf16[128,256]{1,0:T(8,128)(2,1)S(1)}, u32[]{:S(2)}, u32[]{:S(2)}) collective-permute-start(bf16[128,256]{1,0:T(8,128)(2,1)} %refs_0_.1), channel_id=1, source_target_pairs={{0,4},{4,8},{8,12},{12,0},{1,5},{5,9},{9,13},{13,1},{2,6},{6,10},{... | collective-permute-start | bytes 196616 | tf_op jit(solution)/shard_map/ppermute | solution.py:718
  13.0 17.9 %collective-permute-start.9 = (bf16[128,256]{1,0:T(8,128)(2,1)}, bf16[128,256]{1,0:T(8,128)(2,1)S(1)}, u32[]{:S(2)}, u32[]{:S(2)}) collective-permute-start(bf16[128,256]{1,0:T(8,128)(2,1)} %refs_0_.1), channel_id=1, source_target_pairs={{0,8},{4,12},{8,0},{12,4},{1,9},{5,13},{9,1},{13,5},{2,10},{6,14},... | collective-permute-start | bytes 196616 | tf_op jit(solution)/shard_map/ppermute | solution.py:718
  20.0 13.4 %copy-start.3 = (bf16[128,256]{1,0:T(8,128)(2,1)S(1)}, bf16[128,256]{1,0:T(8,128)(2,1)}, u32[]{:S(2)}) copy-start(bf16[128,256]{1,0:T(8,128)(2,1)} %refs_0_.1) | copy-start | bytes 196612
  20.0 14.2 %copy-start.5 = (bf16[128,512]{1,0:T(8,128)(2,1)S(1)}, bf16[128,512]{1,0:T(8,128)(2,1)}, u32[]{:S(2)}) copy-start(bf16[128,512]{1,0:T(8,128)(2,1)} %mix_forward.1) | copy-start | bytes 393220
  20.0 11.6 %collective-permute-start.10 = (bf16[128,256]{1,0:T(8,128)(2,1)}, bf16[128,256]{1,0:T(8,128)(2,1)S(1)}, u32[]{:S(2)}, u32[]{:S(2)}) collective-permute-start(bf16[128,256]{1,0:T(8,128)(2,1)} %refs_0_.1), channel_id=1, source_target_pairs={{0,12},{4,0},{8,4},{12,8},{1,13},{5,1},{9,5},{13,9},{2,14},{6,2},{... | collective-permute-start | bytes 196616 | tf_op jit(solution)/shard_map/ppermute | solution.py:718
  23.4 32.2 %collective-permute-start.3 = (bf16[128,512]{1,0:T(8,128)(2,1)}, bf16[128,512]{1,0:T(8,128)(2,1)S(1)}, u32[]{:S(2)}, u32[]{:S(2)}) collective-permute-start(bf16[128,512]{1,0:T(8,128)(2,1)} %mix_forward.1), channel_id=1, source_target_pairs={{0,4},{4,8},{8,12},{12,0},{1,5},{5,9},{9,13},{13,1},{2,6},{6,10},{... | collective-permute-start | bytes 393224 | tf_op jit(solution)/shard_map/ppermute | solution.py:718
  23.5 33.1 %collective-permute-start.4 = (bf16[128,512]{1,0:T(8,128)(2,1)}, bf16[128,512]{1,0:T(8,128)(2,1)S(1)}, u32[]{:S(2)}, u32[]{:S(2)}) collective-permute-start(bf16[128,512]{1,0:T(8,128)(2,1)} %mix_forward.1), channel_id=1, source_target_pairs={{0,8},{4,12},{8,0},{12,4},{1,9},{5,13},{9,1},{13,5},{2,10},{6,14},... | collective-permute-start | bytes 393224 | tf_op jit(solution)/shard_map/ppermute | solution.py:718
  28.1 6.1 %collective-permute-start.16 = (bf16[128,128]{1,0:T(8,128)(2,1)}, bf16[128,128]{1,0:T(8,128)(2,1)S(1)}, u32[]{:S(2)}, u32[]{:S(2)}) collective-permute-start(bf16[128,128]{1,0:T(8,128)(2,1)} %get-tuple-element.17), channel_id=1, source_target_pairs={{0,4},{4,8},{8,12},{12,0},{1,5},{5,9},{9,13},{13,1},{2,6},{6,10},{... | collective-permute-start | bytes 98312 | tf_op jit(solution)/shard_map/ppermute | solution.py:748
  30.9 6.9 %collective-permute-start.17 = (bf16[128,128]{1,0:T(8,128)(2,1)}, bf16[128,128]{1,0:T(8,128)(2,1)S(1)}, u32[]{:S(2)}, u32[]{:S(2)}) collective-permute-start(bf16[128,128]{1,0:T(8,128)(2,1)} %get-tuple-element.18), channel_id=1, source_target_pairs={{0,8},{4,12},{8,0},{12,4},{1,9},{5,13},{9,1},{13,5},{2,10},{6,14},... | collective-permute-start | bytes 98312 | tf_op jit(solution)/shard_map/ppermute | solution.py:748
  31.6 7.7 %collective-permute-start.18 = (bf16[128,128]{1,0:T(8,128)(2,1)}, bf16[128,128]{1,0:T(8,128)(2,1)S(1)}, u32[]{:S(2)}, u32[]{:S(2)}) collective-permute-start(bf16[128,128]{1,0:T(8,128)(2,1)} %get-tuple-element.19), channel_id=1, source_target_pairs={{0,12},{4,0},{8,4},{12,8},{1,13},{5,1},{9,5},{13,9},{2,14},{6,2},{... | collective-permute-start | bytes 98312 | tf_op jit(solution)/shard_map/ppermute | solution.py:748
  34.1 5.2 %copy-start.13 = (bf16[128,128]{1,0:T(8,128)(2,1)}, bf16[128,128]{1,0:T(8,128)(2,1)S(1)}, u32[]{:S(2)}) copy-start(bf16[128,128]{1,0:T(8,128)(2,1)S(1)} %collective-permute-done.16.refs_13_) | copy-start | bytes 98308
  34.1 22.5 %collective-permute-start.5 = (bf16[128,512]{1,0:T(8,128)(2,1)S(1)}, bf16[128,512]{1,0:T(8,128)(2,1)S(1)}, u32[]{:S(2)}, u32[]{:S(2)}) collective-permute-start(bf16[128,512]{1,0:T(8,128)(2,1)S(1)} %copy-done.5), channel_id=1, source_target_pairs={{0,12},{4,0},{8,4},{12,8},{1,13},{5,1},{9,5},{13,9},{2,14},{6,2},{... | collective-permute-start | bytes 393224 | tf_op jit(solution)/shard_map/ppermute | solution.py:718
  37.8 22.7 %collective-permute-start.11 = (bf16[4,128,256]{2,1,0:T(8,128)(2,1)S(1)}, bf16[4,128,256]{2,1,0:T(8,128)(2,1)S(1)}, u32[]{:S(2)}, u32[]{:S(2)}) collective-permute-start(bf16[4,128,256]{2,1,0:T(8,128)(2,1)S(1)} %pad_maximum_fusion.1), channel_id=1, source_target_pairs={{0,2},{1,3},{2,0},{3,1},{4,6},{5,7},{6,4},{7,5},{8,10},{9,11},{10,... | collective-permute-start | bytes 786440 | tf_op jit(solution)/shard_map/ppermute | solution.py:728
  49.8 5.8 %collective-permute-start.19 = (f32[8,640]{1,0:T(8,128)}, f32[8,640]{1,0:T(8,128)S(1)}, u32[]{:S(2)}, u32[]{:S(2)}) collective-permute-start(f32[8,640]{1,0:T(8,128)} %mix_backward.1.refs_0_), channel_id=1, source_target_pairs={{0,4},{4,8},{8,12},{12,0},{1,5},{5,9},{9,13},{13,1},{2,6},{6,10},{... | collective-permute-start | bytes 61448 | tf_op jit(solution)/shard_map/ppermute | solution.py:718
  55.6 19.1 %copy-start.6 = (f32[8,640]{1,0:T(8,128)}, f32[8,640]{1,0:T(8,128)S(1)}, u32[]{:S(2)}) copy-start(f32[8,640]{1,0:T(8,128)S(1)} %collective-permute-done.19.refs_1_) | copy-start | bytes 61444
  55.6 4.9 %collective-permute-start.20 = (f32[8,640]{1,0:T(8,128)}, f32[8,640]{1,0:T(8,128)S(1)}, u32[]{:S(2)}, u32[]{:S(2)}) collective-permute-start(f32[8,640]{1,0:T(8,128)} %mix_backward.1.refs_0_), channel_id=1, source_target_pairs={{0,8},{4,12},{8,0},{12,4},{1,9},{5,13},{9,1},{13,5},{2,10},{6,14},... | collective-permute-start | bytes 61448 | tf_op jit(solution)/shard_map/ppermute | solution.py:718
  55.6 5.0 %collective-permute-start.21 = (f32[8,640]{1,0:T(8,128)}, f32[8,640]{1,0:T(8,128)S(1)}, u32[]{:S(2)}, u32[]{:S(2)}) collective-permute-start(f32[8,640]{1,0:T(8,128)} %mix_backward.1.refs_0_), channel_id=1, source_target_pairs={{0,12},{4,0},{8,4},{12,8},{1,13},{5,1},{9,5},{13,9},{2,14},{6,2},{... | collective-permute-start | bytes 61448 | tf_op jit(solution)/shard_map/ppermute | solution.py:718
  56.8 3.9 %collective-permute-start.6 = (bf16[4,128,512]{2,1,0:T(8,128)(2,1)S(1)}, bf16[4,128,512]{2,1,0:T(8,128)(2,1)S(1)}, u32[]{:S(2)}, u32[]{:S(2)}) collective-permute-start(bf16[4,128,512]{2,1,0:T(8,128)(2,1)S(1)} %pad_maximum_fusion.own_ref), channel_id=1, source_target_pairs={{0,1},{1,0},{2,3},{3,2},{4,5},{5,4},{6,7},{7,6},{8,9},{9,8},{10,11... | collective-permute-start | bytes 1572872 | tf_op jit(solution)/shard_map/ppermute | solution.py:728
  60.5 14.2 %copy-start.7 = (f32[8,640]{1,0:T(8,128)}, f32[8,640]{1,0:T(8,128)S(1)}, u32[]{:S(2)}) copy-start(f32[8,640]{1,0:T(8,128)S(1)} %collective-permute-done.20.refs_2_) | copy-start | bytes 61444
  60.5 19.3 %copy-start.2 = (bf16[8,128,256]{2,1,0:T(8,128)(2,1)}, bf16[8,128,256]{2,1,0:T(8,128)(2,1)S(1)}, u32[]{:S(2)}) copy-start(bf16[8,128,256]{2,1,0:T(8,128)(2,1)S(1)} %constant_dynamic-update-slice_fusion.cot_own) | copy-start | bytes 1572868
  60.6 19.3 %collective-permute-start.12 = (bf16[8,128,256]{2,1,0:T(8,128)(2,1)S(1)}, bf16[8,128,256]{2,1,0:T(8,128)(2,1)S(1)}, u32[]{:S(2)}, u32[]{:S(2)}) collective-permute-start(bf16[8,128,256]{2,1,0:T(8,128)(2,1)S(1)} %constant_dynamic-update-slice_fusion.cot_own), channel_id=1, source_target_pairs={{0,1},{1,0},{2,3},{3,2},{4,5},{5,4},{6,7},{7,6},{8,9},{9,8},{10,11... | collective-permute-start | bytes 1572872 | tf_op jit(solution)/shard_map/ppermute | solution.py:728
  60.6 14.1 %copy-start.8 = (f32[8,640]{1,0:T(8,128)}, f32[8,640]{1,0:T(8,128)S(1)}, u32[]{:S(2)}) copy-start(f32[8,640]{1,0:T(8,128)S(1)} %collective-permute-done.21.refs_3_) | copy-start | bytes 61444
  68.4 9.9 %collective-permute-start.7 = (f32[128,256]{1,0:T(8,128)}, f32[128,256]{1,0:T(8,128)S(1)}, u32[]{:S(2)}, u32[]{:S(2)}) collective-permute-start(f32[128,256]{1,0:T(8,128)} %get-tuple-element.15), channel_id=1, source_target_pairs={{0,2},{1,3},{2,0},{3,1},{4,6},{5,7},{6,4},{7,5},{8,10},{9,11},{10,... | collective-permute-start | bytes 393224 | tf_op jit(solution)/shard_map/ppermute | solution.py:728
  69.6 5.1 %collective-permute-start.22 = (f32[8,1792]{1,0:T(8,128)S(1)}, f32[8,1792]{1,0:T(8,128)S(1)}, u32[]{:S(2)}, u32[]{:S(2)}) collective-permute-start(f32[8,1792]{1,0:T(8,128)S(1)} %get-tuple-element.23), channel_id=1, source_target_pairs={{0,1},{1,0},{2,3},{3,2},{4,5},{5,4},{6,7},{7,6},{8,9},{9,8},{10,11... | collective-permute-start | bytes 172040 | tf_op jit(solution)/shard_map/ppermute | solution.py:728
  69.8 4.9 %collective-permute-start.23 = (f32[8,256]{1,0:T(8,128)S(1)}, f32[8,256]{1,0:T(8,128)S(1)}, u32[]{:S(2)}, u32[]{:S(2)}) collective-permute-start(f32[8,256]{1,0:T(8,128)S(1)} %get-tuple-element.24), channel_id=1, source_target_pairs={{0,2},{1,3},{2,0},{3,1},{4,6},{5,7},{6,4},{7,5},{8,10},{9,11},{10,... | collective-permute-start | bytes 24584 | tf_op jit(solution)/shard_map/ppermute | solution.py:728
  71.3 3.4 %collective-permute-start.24 = (f32[8,256]{1,0:T(8,128)S(1)}, f32[8,256]{1,0:T(8,128)S(1)}, u32[]{:S(2)}, u32[]{:S(2)}) collective-permute-start(f32[8,256]{1,0:T(8,128)S(1)} %get-tuple-element.24), channel_id=1, source_target_pairs={{0,3},{1,2},{2,1},{3,0},{4,7},{5,6},{6,5},{7,4},{8,11},{9,10},{10,... | collective-permute-start | bytes 24584 | tf_op jit(solution)/shard_map/ppermute | solution.py:728
  (14 other events, 26.0 us)

commit v2 on v1

--- a/solution.py
+++ b/solution.py
@@ -98,8 +98,8 @@
     mine = scalars[1]
     for k in range(ns):
         at = jnp.where(mine >= k, mine - k, mine - k + ns)
-        sym = lax.broadcasted_iota(jnp.int32, (SYM, BLOCK), 0)
-        tok = jnp.broadcast_to(tok_refs[k][...], (SYM, BLOCK))
+        sym = lax.broadcasted_iota(jnp.int32, (SYM, BLOCK), 0).astype(F32)
+        tok = jnp.broadcast_to(tok_refs[k][0:1, 0:BLOCK].astype(F32), (SYM, BLOCK))
         r.oh[:, pl.ds(pl.multiple_of(at * BLOCK, BLOCK), BLOCK)] = (sym == tok).astype(F32)
     oh = r.oh[...]
     lane = lax.broadcasted_iota(jnp.int32, (SYM, length), 1)
@@ -297,16 +297,29 @@
         out_ref[:, units[0][b].rows] = jnp.transpose(gated[0] + gated[1]).astype(BF16)
 
 
-def backward_kernel(scalars, *refs, ns, conv, vocab):
+def backward_kernel(scalars, *refs, ns, nq, conv, vocab):
     tok_refs, raw = refs[:ns], refs[ns : ns + RAW]
-    dg_refs, out_ref = refs[ns + RAW : 2 * ns + RAW], refs[2 * ns + RAW]
-    r = named(refs[2 * ns + RAW + 1 :], PREP_NAMES + ("ds", "dg", "dpre"))
+    cot_refs, weight_ref, out_ref = (
+        refs[ns + RAW : ns + RAW + nq],
+        refs[ns + RAW + nq],
+        refs[ns + RAW + nq + 1],
+    )
+    r = named(refs[ns + RAW + nq + 2 :], PREP_NAMES + ("ds", "dg", "dpre"))
     tabs_ref, bcp_ref = r.tabs, r.bcp
     prepare(scalars, tok_refs, raw, tabs_ref, bcp_ref, r, conv, vocab)
+    cols = cot_refs[0].shape[2]
+    cot = jnp.concatenate([a[...].reshape(ns * BLOCK, cols) for a in cot_refs], 1)
+    weight = []
+    for k in range(nq):
+        at = pl.multiple_of(scalars[QUARTERS + k] * cols, LANES)
+        weight.append(weight_ref[:, pl.ds(at, cols)])
+    d_gated = mm(cot, jnp.concatenate(weight, 1), NT).astype(BF16).astype(F32)
     mine = scalars[1]
     for k in range(ns):
         at = jnp.where(mine >= k, mine - k, mine - k + ns)
-        r.dg[pl.ds(pl.multiple_of(at * BLOCK, BLOCK), BLOCK), :] = dg_refs[k][...].astype(F32)
+        r.dg[pl.ds(pl.multiple_of(at * BLOCK, BLOCK), BLOCK), :] = d_gated[
+            k * BLOCK : (k + 1) * BLOCK
+        ]
     units = [[Unit(r, tabs_ref, st, b, ns) for b in range(ns)] for st in range(2)]
     state_pass_fwd(r, tabs_ref, ns, units)
     for st in range(2):
@@ -491,8 +504,13 @@
 PARAMS = pltpu.CompilerParams(vmem_limit_bytes=VMEM_LIMIT)
 
 
-def call_forward(scalars, toks, raw):
-    ns = len(toks)
+def token_specs(ns, pay):
+    last = pay.shape[0] // 16 - 1
+    return [pl.BlockSpec((16, pay.shape[1]), lambda i, s: (last, 0))] * ns
+
+
+def call_forward(scalars, pays, raw):
+    ns = len(pays)
     length = ns * BLOCK
     return pl.pallas_call(
         functools.partial(forward_kernel, ns=ns, conv=raw[3].shape[0], vocab=raw[1].shape[0]),
@@ -500,17 +518,20 @@
         grid_spec=pltpu.PrefetchScalarGridSpec(
             num_scalar_prefetch=1,
             grid=(1,),
-            in_specs=[whole((1, BLOCK))] * ns + raw_specs(raw),
+            in_specs=token_specs(ns, pays[0]) + raw_specs(raw),
             out_specs=whole((LANES, length)),
             scratch_shapes=prep_scratch(length),
         ),
         compiler_params=PARAMS,
+        cost_estimate=pl.CostEstimate(
+            flops=6 * 10**9, transcendentals=0, bytes_accessed=8 * LANES * length
+        ),
         name="mix_forward",
-    )(scalars, *toks, *raw)
-
-
-def call_backward(scalars, toks, raw, d_gated):
-    ns = len(toks)
+    )(scalars, *pays, *raw)
+
+
+def call_backward(scalars, pays, raw, cots, out_weight):
+    ns = len(pays)
     length = ns * BLOCK
     extra = [
         pltpu.VMEM((4, ns, LANES, LANES), F32),
@@ -518,156 +539,122 @@
         pltpu.VMEM((length, 2 * WIDE), BF16),
     ]
     return pl.pallas_call(
-        functools.partial(backward_kernel, ns=ns, conv=raw[3].shape[0], vocab=raw[1].shape[0]),
+        functools.partial(
+            backward_kernel, ns=ns, nq=len(cots), conv=raw[3].shape[0], vocab=raw[1].shape[0]
+        ),
         out_shape=jax.ShapeDtypeStruct((SYM, 640), F32),
         grid_spec=pltpu.PrefetchScalarGridSpec(
             num_scalar_prefetch=1,
             grid=(1,),
-            in_specs=[whole((1, BLOCK))] * ns + raw_specs(raw) + [whole((BLOCK, LANES))] * ns,
+            in_specs=token_specs(ns, pays[0])
+            + raw_specs(raw)
+            + [whole(a.shape) for a in cots]
+            + [pl.BlockSpec((LANES, out_weight.shape[1]), lambda i, s: (s[0], 0))],
             out_specs=whole((SYM, 640)),
             scratch_shapes=prep_scratch(length) + extra,
         ),
         compiler_params=PARAMS,
+        cost_estimate=pl.CostEstimate(
+            flops=10**10, transcendentals=0, bytes_accessed=8 * LANES * length
+        ),
         name="mix_backward",
-    )(scalars, *toks, *raw, *d_gated)
+    )(scalars, *pays, *raw, *cots, out_weight)
 
 
 QUARTERS = 3
 
 
-def d_gated_kernel(scalars, *refs, nq, ns):
-    cots, weights, outs = refs[:nq], refs[nq : 2 * nq], refs[2 * nq :]
-    cot = jnp.concatenate([a[...] for a in cots], 1)
-    mine = scalars[1]
-    for k in range(ns):
-        to = jnp.where(mine + k >= ns, mine + k - ns, mine + k)
-        rows = pl.ds(pl.multiple_of(to * LANES, LANES), LANES)
-        weight = jnp.concatenate([w[rows, :] for w in weights], 1)
-        outs[k][...] = mm(cot, weight, NT).astype(BF16)
-
-
-def call_d_gated(scalars, cots, out_weight, ns):
-    nq = len(cots)
-    rows, cols = cots[0].shape
-    weight_spec = lambda k: pl.BlockSpec((ns * LANES, cols), lambda i, s: (s[2], s[QUARTERS + k]))
+def out_kernel(scalars, *refs, ns, nh, nc):
+    slices, weights, outs = refs[: ns * nc], refs[ns * nc : ns * nc + nh], refs[ns * nc + nh :]
+    here = pl.ds(pl.multiple_of(scalars[1] * BLOCK, BLOCK), BLOCK)
+    places = QUARTERS + nh * nc
+    rows = [pl.ds(pl.multiple_of(scalars[places + i] * LANES, LANES), LANES) for i in range(ns * nc)]
+    left = jnp.concatenate([a[:, here] for a in slices], 0)
+    for k in range(nh):
+        outs[k][...] = mm(left, jnp.concatenate([weights[k][at, :] for at in rows], 0), TN)
+
+
+def call_out(scalars, slices, out_weight, ns, nh, nc):
+    rows, width = out_weight.shape
+    cols = width // (nh * nc)
+    weight_spec = lambda k: pl.BlockSpec((rows, cols), lambda i, s: (0, s[QUARTERS + k * nc]))
     return pl.pallas_call(
-        functools.partial(d_gated_kernel, nq=nq, ns=ns),
-        out_shape=[jax.ShapeDtypeStruct((rows, LANES), BF16)] * ns,
+        functools.partial(out_kernel, ns=ns, nh=nh, nc=nc),
+        out_shape=[jax.ShapeDtypeStruct((BLOCK, cols), F32)] * nh,
         grid_spec=pltpu.PrefetchScalarGridSpec(
             num_scalar_prefetch=1,
             grid=(1,),
-            in_specs=[whole((rows, cols))] * nq + [weight_spec(k) for k in range(nq)],
-            out_specs=[whole((rows, LANES))] * ns,
-        ),
-        compiler_params=PARAMS,
-        name="d_gated",
-    )(scalars, *cots, *([out_weight] * nq))
-
-
-def out_kernel(scalars, own_ref, other_ref, weight_ref, *refs, ns, nh, nc, cols):
-    outs, acc = refs[:nh], refs[nh]
-    i = pl.program_id(0)
-    here = pl.ds(pl.multiple_of(scalars[1] * BLOCK, BLOCK), BLOCK)
-
-    @pl.when(i == 0)
-    def _():
-        acc[...] = jnp.zeros_like(acc)
-
-    def add(ref):
-        weight = []
-        for k in range(nh):
-            at = scalars[QUARTERS + k * nc] * cols
-            weight.append(weight_ref[:, pl.ds(pl.multiple_of(at, LANES), cols)])
-        acc[...] += mm(ref[0, :, here], jnp.concatenate(weight, 1), TN)
-
-    @pl.when(i < ns)
-    def _():
-        add(own_ref)
-
-    @pl.when(i >= ns)
-    def _():
-        add(other_ref)
-
-    @pl.when(i == pl.num_programs(0) - 1)
-    def _():
-        for k in range(nh):
-            outs[k][...] = acc[:, k * cols : (k + 1) * cols]
-
-
-def slice_specs(ns, length):
-    return [
-        pl.BlockSpec((1, LANES, length), lambda i, s: (jnp.minimum(i, ns - 1), 0, 0)),
-        pl.BlockSpec((1, LANES, length), lambda i, s: (jnp.maximum(i - ns, 0), 0, 0)),
-    ]
-
-
-def call_out(scalars, own, other, out_weight, nh, nc):
-    ns, _, length = own.shape
-    width = out_weight.shape[1]
-    cols = width // (nh * nc)
-    places = QUARTERS + nh * nc
-    return pl.pallas_call(
-        functools.partial(out_kernel, ns=ns, nh=nh, nc=nc, cols=cols),
-        out_shape=[jax.ShapeDtypeStruct((BLOCK, cols), F32)] * nh,
-        grid_spec=pltpu.PrefetchScalarGridSpec(
-            num_scalar_prefetch=1,
-            grid=(ns * nc,),
-            in_specs=slice_specs(ns, length)
-            + [pl.BlockSpec((LANES, width), lambda i, s: (s[places + i], 0))],
+            in_specs=[whole(a.shape) for a in slices] + [weight_spec(k) for k in range(nh)],
             out_specs=[whole((BLOCK, cols))] * nh,
-            scratch_shapes=[pltpu.VMEM((BLOCK, nh * cols), F32)],
         ),
         compiler_params=PARAMS,
         name="layer_out",
-    )(scalars, own, other, out_weight)
-
-
-def weight_kernel(scalars, own_ref, other_ref, cot_own, cot_other, out_ref, *, ns, nh, nc, cols):
+    )(scalars, *slices, *([out_weight] * nh))
+
+
+def weight_kernel(scalars, *refs, ns, nh, nc):
+    slices, cots = refs[: ns * nc], refs[ns * nc : ns * nc + nh * nc]
+    out_ref, mark_ref, left = refs[ns * nc + nh * nc :]
     i = pl.program_id(0)
     mine = scalars[1]
-
-    def fill(ref):
-        chunks = []
-        for k in range(ns):
-            at = jnp.where(mine >= k, mine - k, mine - k + ns)
-            chunks.append(ref[0, :, pl.ds(pl.multiple_of(at * BLOCK, BLOCK), BLOCK)])
-        left = jnp.concatenate(chunks, 1)
-        for k in range(nh):
-            for m, cot in ((0, cot_own), (1, cot_other)):
-                right = cot[k * ns : (k + 1) * ns].reshape(ns * BLOCK, cols)
-                at = scalars[QUARTERS + k * nc + m] * cols
-                out_ref[:, pl.ds(pl.multiple_of(at, LANES), cols)] = mm(left, right, NN)
-
-    @pl.when(i < ns)
+    places = QUARTERS + nh * nc
+    cols = cots[0].shape[2]
+
+    @pl.when(i == 0)
     def _():
-        fill(own_ref)
-
-    @pl.when(i >= ns)
-    def _():
-        fill(other_ref)
-
-
-def call_weight(scalars, own, other, cot_own, cot_other, width, nh, nc):
-    ns, _, length = own.shape
-    cols = cot_own.shape[2]
-    places = QUARTERS + nh * nc
+        mark_ref[...] = jnp.zeros_like(mark_ref)
+        for n in range(ns * nc):
+            for k in range(ns):
+                at = jnp.where(mine >= k, mine - k, mine - k + ns)
+                left[n * LANES : (n + 1) * LANES, k * BLOCK : (k + 1) * BLOCK] = slices[n][
+                    :, pl.ds(pl.multiple_of(at * BLOCK, BLOCK), BLOCK)
+                ]
+
+    for q in range(nh * nc):
+
+        @pl.when(i == q)
+        def _():
+            total = mm(left[...], cots[q][...].reshape(ns * BLOCK, cols), NN)
+            for n in range(ns * nc):
+                at = pl.multiple_of(scalars[places + n] * LANES, LANES)
+                out_ref[pl.ds(at, LANES), :] = total[n * LANES : (n + 1) * LANES]
+
+
+def call_weight(scalars, slices, cots, width, ns, nh, nc):
+    length = slices[0].shape[1]
+    rows = ns * nc * LANES
     return pl.pallas_call(
-        functools.partial(weight_kernel, ns=ns, nh=nh, nc=nc, cols=cols),
-        out_shape=jax.ShapeDtypeStruct((ns * nc * LANES, width), F32),
+        functools.partial(weight_kernel, ns=ns, nh=nh, nc=nc),
+        out_shape=[
+            jax.ShapeDtypeStruct((rows, width), F32),
+            jax.ShapeDtypeStruct((SYM, LANES), F32),
+        ],
         grid_spec=pltpu.PrefetchScalarGridSpec(
             num_scalar_prefetch=1,
-            grid=(ns * nc,),
-            in_specs=slice_specs(ns, length) + [whole(cot_own.shape)] * 2,
-            out_specs=pl.BlockSpec((LANES, width), lambda i, s: (s[places + i], 0)),
+            grid=(nh * nc,),
+            in_specs=[whole(a.shape) for a in slices] + [whole(a.shape) for a in cots],
+            out_specs=[
+                pl.BlockSpec((rows, width // (nh * nc)), lambda i, s: (0, s[QUARTERS + i])),
+                whole((SYM, LANES)),
+            ],
+            scratch_shapes=[pltpu.VMEM((rows, length), BF16)],
         ),
         compiler_params=PARAMS,
+        cost_estimate=pl.CostEstimate(
+            flops=2 * rows * width * length, transcendentals=0, bytes_accessed=6 * rows * width
+        ),
         name="weight_grad",
-    )(scalars, own, other, cot_own, cot_other)
-
-
-def final_kernel(scalars, *refs, ns, nq, vocab, places):
+    )(scalars, *slices, *cots)
+
+
+def final_kernel(scalars, *refs, ns, nq, nh, vocab, places):
     firsts, packed, shared = refs[:ns], refs[ns], refs[ns + 1 : ns + nq]
-    xz_ref, bc_ref, dt_ref = refs[ns + nq :]
+    parts = refs[ns + nq : ns + nq + nh]
+    out_ref, xz_ref, bc_ref, dt_ref = refs[ns + nq + nh + 1 :]
+    total = parts[0][...]
+    for a in parts[1:]:
+        total = total + a[...]
+    out_ref[...] = total.astype(BF16)
     d_bc = packed[:, ns * 384 : ns * 384 + 256]
     for a in list(firsts) + list(shared):
         d_bc = d_bc + a[:, a.shape[1] - 256 :]
@@ -687,29 +674,35 @@
                 xz_ref[k, i : i + 1, pl.ds(pl.multiple_of(j * LANES, LANES), LANES)] = piece[
                     k : k + 1, i * 128 : i * 128 + 128
                 ]
-            total = jnp.sum(piece[:, 256 + 64 * i : 320 + 64 * i], 1, keepdims=True)
-            d_dt = jnp.where(lane == 2 * j + i, total, d_dt)
+            row = jnp.sum(piece[:, 256 + 64 * i : 320 + 64 * i], 1, keepdims=True)
+            d_dt = jnp.where(lane == 2 * j + i, row, d_dt)
     dt_ref[...] = d_dt[:vocab]
 
 
-def call_final(scalars, firsts, packed, shared, raw, places):
+def call_final(scalars, firsts, packed, shared, parts, mark, raw, places):
     ns = len(firsts)
     shapes = [raw[1].shape, raw[2].shape, raw[5].shape]
-    arrays = list(firsts) + [packed] + list(shared)
+    arrays = list(firsts) + [packed] + list(shared) + list(parts)
     return pl.pallas_call(
         functools.partial(
-            final_kernel, ns=ns, nq=len(shared) + 1, vocab=raw[1].shape[0], places=places
+            final_kernel,
+            ns=ns,
+            nq=len(shared) + 1,
+            nh=len(parts),
+            vocab=raw[1].shape[0],
+            places=places,
         ),
-        out_shape=[jax.ShapeDtypeStruct(a, F32) for a in shapes],
+        out_shape=[jax.ShapeDtypeStruct(parts[0].shape, BF16)]
+        + [jax.ShapeDtypeStruct(a, F32) for a in shapes],
         grid_spec=pltpu.PrefetchScalarGridSpec(
             num_scalar_prefetch=1,
             grid=(1,),
-            in_specs=[whole(a.shape) for a in arrays],
-            out_specs=[whole(a) for a in shapes],
+            in_specs=[whole(a.shape) for a in arrays] + [pl.BlockSpec(memory_space=pl.ANY)],
+            out_specs=[whole(parts[0].shape)] + [whole(a) for a in shapes],
         ),
         compiler_params=PARAMS,
         name="place_grads",
-    )(scalars, *arrays)
+    )(scalars, *arrays, mark)
 
 
 def around(x, axis):
@@ -734,40 +727,37 @@
     ns, nc, nh = lax.axis_size("seq"), lax.axis_size("sub"), lax.axis_size("head")
     s, c, h = lax.axis_index("seq"), lax.axis_index("sub"), lax.axis_index("head")
     width = out_weight.shape[1]
+    cols = width // (nh * nc)
     raw = (basemap, xz_table, bc_table, conv_x, conv_bc, dt_table, a_log, skip_gain)
-    hops = [(a, b) for a in range(nh) for b in range(nc)]
-    toks = around(token_ids.reshape(1, BLOCK), "seq")
-    near = [across(cotangent, hop, nh, nc) if any(hop) else cotangent for hop in hops]
+    symbols = jnp.pad(token_ids.astype(BF16).reshape(1, BLOCK), ((0, 15), (0, cols - BLOCK)))
+    pays = around(jnp.concatenate([cotangent, symbols], 0), "seq")
     slot = jnp.arange(nh * nc, dtype=jnp.int32)
     quarters = (h - slot // nc) % nh * nc + (c - slot % nc) % nc
     slot = jnp.arange(ns * nc, dtype=jnp.int32)
     places = (c - slot // ns) % nc * ns + (s - slot % ns) % ns
     scalars = jnp.concatenate([jnp.stack([c * ns + s, s, c]), quarters, places]).astype(jnp.int32)
-    d_parts = call_d_gated(scalars, near, out_weight, ns)
-    d_gated = [d_parts[0]] + [
-        lax.ppermute(d_parts[k], "seq", [(i, (i + k) % ns) for i in range(ns)])
-        for k in range(1, ns)
-    ]
-    cots = jnp.stack(around(cotangent, "seq"), 0)
-    gated = call_forward(scalars, toks, raw)
-    cots = jnp.concatenate(
-        [cots] + [across(cots, (k, 0), nh, nc) for k in range(1, nh)], 0
-    )
-    own = jnp.stack(around(gated, "seq"), 0)
-    grads = call_backward(scalars, toks, raw, d_gated)
-    cots_other = across(cots, (0, 1), nh, nc)
-    other = across(own, (0, 1), nh, nc)
+    stacked = jnp.stack([a[:BLOCK] for a in pays], 0)
+    heads = [stacked] + [across(stacked, (k, 0), nh, nc) for k in range(1, nh)]
+    side = across(stacked, (0, 1), nh, nc)
+    gated = call_forward(scalars, pays, raw)
+    heads, gated = lax.optimization_barrier((heads, gated))
+    cots = [heads[0], side]
+    for a in heads[1:]:
+        cots += [a, across(a, (0, 1), nh, nc)]
+    slices = around(gated, "seq")
+    grads = call_backward(scalars, pays, raw, cots, out_weight)
+    slices, grads = lax.optimization_barrier((slices, grads))
+    slices = slices + [across(a, (0, 1), nh, nc) for a in slices]
     firsts = around(grads, "seq")
     shared = sum(a[:, 384:] for a in firsts)
     packed = across(jnp.concatenate([a[:, :384] for a in firsts] + [shared], 1), (0, 1), nh, nc)
-    far = [across(shared, hop, nh, nc) for hop in hops if hop[0]]
-    parts = call_out(scalars, own, other, out_weight, nh, nc)
-    total = parts[0]
-    for k in range(1, nh):
-        total = total + across(parts[k], (nh - k, 0), nh, nc)
-    layer_out = total.astype(BF16)
-    d_out_weight = call_weight(scalars, own, other, cots, cots_other, width, nh, nc)
-    d_xz, d_bc, d_dt = call_final(scalars, firsts, packed, far, raw, QUARTERS + nh * nc)
+    far = [across(shared, (a, b), nh, nc) for a in range(1, nh) for b in range(nc)]
+    parts = call_out(scalars, slices, out_weight, ns, nh, nc)
+    parts = [parts[0]] + [across(parts[k], (nh - k, 0), nh, nc) for k in range(1, nh)]
+    d_out_weight, mark = call_weight(scalars, slices, cots, width, ns, nh, nc)
+    layer_out, d_xz, d_bc, d_dt = call_final(
+        scalars, firsts, packed, far, parts, mark, raw, QUARTERS + nh * nc
+    )
     return (layer_out, d_out_weight, d_xz, d_bc, d_dt)
 
 

time: 89.5 us -> 64.4 us (0.72)
  waiting for transfers between devices: 15.5 us -> 6.47 us
  Pallas kernels: 36.2 us -> 28.3 us
  starting transfers between devices: 28 us -> 20.8 us
  local copies, waits for them, and re-layouts: 5.8 us -> 4.15 us
    pallas_call x4 -> x3, Pallas kernels: 27.8 us -> 19.8 us  [the longest x1 10.8 us: call_backward(): pl.pallas_call(functools.partial(backward_kernel, ns=ns, nq=len(cots), co...]
    ppermute x3 -> x0, starting transfers between devices: 5.32 us -> none  [by_channel(): lax.ppermute(d_parts[k], 'seq', [(i, (i + k) % ns) for i in range(ns)])]
    ppermute x12 -> x9, waiting for transfers between devices: 9.49 us -> 4.88 us  [around(): lax.ppermute(x, axis, [(i, (i + k) % n) for i in range(n)])]
    ppermute x3 -> x0, waiting for transfers between devices: 2.76 us -> none  [by_channel(): lax.ppermute(d_parts[k], 'seq', [(i, (i + k) % ns) for i in range(ns)])]
    ppermute x10 -> x11, starting transfers between devices: 7.17 us -> 5.02 us  [across(): return lax.ppermute(x, ('head', 'sub'), pairs)]
    ppermute x10 -> x11, waiting for transfers between devices: 3.24 us -> 1.59 us  [across(): return lax.ppermute(x, ('head', 'sub'), pairs)]
    unnamed x50, local copies, waits for them, and re-layouts: 5.12 us -> 3.53 us
    convert_element_type x1 -> x0, other arithmetic: 1.55 us -> none  [by_channel(): layer_out = total.astype(BF16)]
  transfers between devices with their start and end apart: 25 -> 20, of which waited for: 7 -> 5; matrix products, arithmetic and copies ran while one was open for 5% -> 3% of each run, Pallas kernels for 32% -> 35%
where the time goes in v2:
time: 64.4 us; the launch traced here: 63.9 us
  Pallas kernels  28.3 us (44%)
  starting transfers between devices  20.8 us (32%)
  waiting for transfers between devices  6.47 us (10%)
  local copies, waits for them, and re-layouts  4.15 us (6%)
  other arithmetic  3.13 us (5%)
  between operations  0.99 us (2%)
    ppermute x9, starting transfers between devices, around(): lax.ppermute(x, axis, [(i, (i + k) % n) for i in range(n)])  15.8 us
    pallas_call x1, Pallas kernels, call_backward(): pl.pallas_call(functools.partial(backward_kernel, ns=ns, nq=len(cots), co...  10.8 us
    pallas_call x1, Pallas kernels, call_forward(): pl.pallas_call(functools.partial(forward_kernel, ns=ns, conv=raw[3].shape...  6.04 us
    pallas_call x1, Pallas kernels, call_weight(): pl.pallas_call(functools.partial(weight_kernel, ns=ns, nh=nh, nc=nc), out...  5.67 us
    ppermute x11, starting transfers between devices, across(): return lax.ppermute(x, ('head', 'sub'), pairs)  5.02 us
    ppermute x9, waiting for transfers between devices, around(): lax.ppermute(x, axis, [(i, (i + k) % n) for i in range(n)])  4.88 us
    unnamed x50, local copies, waits for them, and re-layouts  3.53 us
    pallas_call x1, Pallas kernels, call_out(): pl.pallas_call(functools.partial(out_kernel, ns=ns, nh=nh, nc=nc), out_sh...  3.32 us
  transfers between devices with their start and end apart: 20, of which 5 were waited for; matrix products, arithmetic and copies ran while one was open for 3% of the time, Pallas kernels for 35%

profile of v2, /device:TPU:0, one launch (start us, length us, event | category | flops | bytes accessed | tf_op | source)
XLA Modules:
  0.0 63.9 jit_solution(12907798382046658108)
XLA Ops:
  0.6 0.7 %convert_bitcast_fusion = bf16[1,128]{1,0:T(2,128)(2,1)S(1)} fusion(s32[128]{0:T(128)} %param.11), kind=kLoop, calls=%fused_computation.49 | loop fusion | flops 128 | bytes 768 | tf_op jit(solution)/shard_map/reshape | solution.py:732
  1.3 0.8 %fusion.1.refs_0_ = bf16[144,256]{1,0:T(8,128)(2,1)S(1)} fusion(bf16[1,128]{1,0:T(2,128)(2,1)S(1)} %convert_bitcast_fusion, bf16[128,256]{1,0:T(8,128)(2,1)} %param.21), kind=kLoop, calls=%fused_computation.3 | loop fusion | flops 221184 | bytes 139520 | tf_op jit(solution)/shard_map/concatenate | solution.py:733
  2.1 3.0 %collective-permute-start = (bf16[144,256]{1,0:T(8,128)(2,1)S(1)}, bf16[144,256]{1,0:T(8,128)(2,1)S(1)}, u32[]{:S(2)}, u32[]{:S(2)}) collective-permute-start(bf16[144,256]{1,0:T(8,128)(2,1)S(1)} %fusion.1.refs_0_), channel_id=1, source_target_pairs={{0,4},{4,8},{8,12},{12,0},{1,5},{5,9},{9,13},{13,1},{2,6},{6,10},{... | collective-permute-start | bytes 221192 | tf_op jit(solution)/shard_map/ppermute | solution.py:711
  5.2 2.6 %collective-permute-start.1 = (bf16[144,256]{1,0:T(8,128)(2,1)S(1)}, bf16[144,256]{1,0:T(8,128)(2,1)S(1)}, u32[]{:S(2)}, u32[]{:S(2)}) collective-permute-start(bf16[144,256]{1,0:T(8,128)(2,1)S(1)} %fusion.1.refs_0_), channel_id=1, source_target_pairs={{0,8},{4,12},{8,0},{12,4},{1,9},{5,13},{9,1},{13,5},{2,10},{6,14},... | collective-permute-start | bytes 221192 | tf_op jit(solution)/shard_map/ppermute | solution.py:711
  7.8 1.3 %collective-permute-start.2 = (bf16[144,256]{1,0:T(8,128)(2,1)S(1)}, bf16[144,256]{1,0:T(8,128)(2,1)S(1)}, u32[]{:S(2)}, u32[]{:S(2)}) collective-permute-start(bf16[144,256]{1,0:T(8,128)(2,1)S(1)} %fusion.1.refs_0_), channel_id=1, source_target_pairs={{0,12},{4,0},{8,4},{12,8},{1,13},{5,1},{9,5},{13,9},{2,14},{6,2},{... | collective-permute-start | bytes 221192 | tf_op jit(solution)/shard_map/ppermute | solution.py:711
  9.1 0.6 concatenate.9.scalars
  9.7 3.2 %collective-permute-done.2.refs_3_ = bf16[144,256]{1,0:T(8,128)(2,1)S(1)} collective-permute-done((bf16[144,256]{1,0:T(8,128)(2,1)S(1)}, bf16[144,256]{1,0:T(8,128)(2,1)S(1)}, u32[]{:S(2)}, u32[]{:S(2)}) %collective-permute-start.2) | collective-permute-done | bytes 73760 | tf_op jit(solution)/shard_map/ppermute | solution.py:711
  13.0 0.9 %pad_maximum_fusion.refs_12_.refs_8_ = bf16[4,128,256]{2,1,0:T(8,128)(2,1)S(1)} fusion(bf16[1,128,256]{2,1,0:T(8,128)(2,1)S(1)} %slice_bitcast_fusion, bf16[1,128,256]{2,1,0:T(8,128)(2,1)S(1)} %slice_bitcast_fusion.1, bf16[1,128,256]{2,1,0:T(8,128)(2,1)S(1)} %slice_bitcast_fusion.2, bf16[1,128,256]{2,1,0:T(8,128)(2,1)} %bitcast.12), kind=kLoop, calls=%fused_computation | loop fusion | flops 393216 | bytes 524288 | tf_op jit(solution)/shard_map/stack | solution.py:739
  13.9 1.6 %collective-permute-start.3 = (bf16[4,128,256]{2,1,0:T(8,128)(2,1)S(1)}, bf16[4,128,256]{2,1,0:T(8,128)(2,1)S(1)}, u32[]{:S(2)}, u32[]{:S(2)}) collective-permute-start(bf16[4,128,256]{2,1,0:T(8,128)(2,1)S(1)} %pad_maximum_fusion.refs_12_.refs_8_), channel_id=1, source_target_pairs={{0,2},{1,3},{2,0},{3,1},{4,6},{5,7},{6,4},{7,5},{8,10},{9,11},{10,... | collective-permute-start | bytes 786440 | tf_op jit(solution)/shard_map/ppermute | solution.py:721
  15.5 6.0 %mix_forward.1.refs_0_ = bf16[128,512]{1,0:T(8,128)(2,1)} custom-call(s32[15]{0:T(128)} %concatenate.9.scalars, bf16[144,256]{1,0:T(8,128)(2,1)} %copy-done.13, bf16[144,256]{1,0:T(8,128)(2,1)} %copy-done.14, bf16[144,256]{1,0:T(8,128)(2,1)} %copy-done.15, bf16[144,256]{1,0:T(8,128)(2,1)} %copy-done.16, s32[5]{0:T(128)} %refs_4_.3, ...), custom_call_target="tpu_custom_call" | custom-call | flops 6000000000 | bytes 524288 | tf_op jit(solution)/shard_map/mix_forward/pallas_call | solution.py:515
  22.1 1.9 %collective-permute-start.4 = (bf16[128,512]{1,0:T(8,128)(2,1)}, bf16[128,512]{1,0:T(8,128)(2,1)S(1)}, u32[]{:S(2)}, u32[]{:S(2)}) collective-permute-start(bf16[128,512]{1,0:T(8,128)(2,1)} %mix_forward.1.refs_0_), channel_id=1, source_target_pairs={{0,4},{4,8},{8,12},{12,0},{1,5},{5,9},{9,13},{13,1},{2,6},{6,10},{... | collective-permute-start | bytes 393224 | tf_op jit(solution)/shard_map/ppermute | solution.py:711
  24.0 1.8 %collective-permute-start.5 = (bf16[128,512]{1,0:T(8,128)(2,1)}, bf16[128,512]{1,0:T(8,128)(2,1)S(1)}, u32[]{:S(2)}, u32[]{:S(2)}) collective-permute-start(bf16[128,512]{1,0:T(8,128)(2,1)} %mix_forward.1.refs_0_), channel_id=1, source_target_pairs={{0,8},{4,12},{8,0},{12,4},{1,9},{5,13},{9,1},{13,5},{2,10},{6,14},... | collective-permute-start | bytes 393224 | tf_op jit(solution)/shard_map/ppermute | solution.py:711
  25.9 0.6 %collective-permute-start.6 = (bf16[128,512]{1,0:T(8,128)(2,1)}, bf16[128,512]{1,0:T(8,128)(2,1)S(1)}, u32[]{:S(2)}, u32[]{:S(2)}) collective-permute-start(bf16[128,512]{1,0:T(8,128)(2,1)} %mix_forward.1.refs_0_), channel_id=1, source_target_pairs={{0,12},{4,0},{8,4},{12,8},{1,13},{5,1},{9,5},{13,9},{2,14},{6,2},{... | collective-permute-start | bytes 393224 | tf_op jit(solution)/shard_map/ppermute | solution.py:711
  26.5 0.7 %copy-done.21 = bf16[4,128,256]{2,1,0:T(8,128)(2,1)} copy-done((bf16[4,128,256]{2,1,0:T(8,128)(2,1)}, bf16[4,128,256]{2,1,0:T(8,128)(2,1)S(1)}, u32[]{:S(2)}) %copy-start.21) | copy-done | bytes 262168
  27.2 0.7 %copy-done.22 = bf16[4,128,256]{2,1,0:T(8,128)(2,1)} copy-done((bf16[4,128,256]{2,1,0:T(8,128)(2,1)}, bf16[4,128,256]{2,1,0:T(8,128)(2,1)S(1)}, u32[]{:S(2)}) %copy-start.22) | copy-done | bytes 262168
  27.9 10.8 %mix_backward.1.refs_0_ = f32[8,640]{1,0:T(8,128)} custom-call(s32[15]{0:T(128)} %concatenate.9.scalars, bf16[144,256]{1,0:T(8,128)(2,1)} %copy-done.13, bf16[144,256]{1,0:T(8,128)(2,1)} %copy-done.14, bf16[144,256]{1,0:T(8,128)(2,1)} %copy-done.15, bf16[144,256]{1,0:T(8,128)(2,1)} %copy-done.16, s32[5]{0:T(128)} %refs_4_.3, bf16[5,2,1024]{2,1,0:T(2,128)(2,1)} %refs_5_.3, ...), custom_call_target="tpu_custom_call" | custom-call | flops 10000000000 | bytes 524288 | tf_op jit(solution)/shard_map/mix_backward/pallas_call | solution.py:541
  38.8 1.4 %collective-permute-start.9 = (f32[8,640]{1,0:T(8,128)}, f32[8,640]{1,0:T(8,128)S(1)}, u32[]{:S(2)}, u32[]{:S(2)}) collective-permute-start(f32[8,640]{1,0:T(8,128)} %mix_backward.1.refs_0_), channel_id=1, source_target_pairs={{0,4},{4,8},{8,12},{12,0},{1,5},{5,9},{9,13},{13,1},{2,6},{6,10},{... | collective-permute-start | bytes 61448 | tf_op jit(solution)/shard_map/ppermute | solution.py:711
  40.2 0.7 %slice_dynamic-update-slice_fusion.3 = f32[8,1792]{1,0:T(8,128)S(1)} fusion(f32[8,640]{1,0:T(8,128)} %mix_backward.1.refs_0_), kind=kLoop, calls=%fused_computation.10 | loop fusion | bytes 24576
  40.9 1.1 %collective-permute-start.10 = (f32[8,640]{1,0:T(8,128)}, f32[8,640]{1,0:T(8,128)S(1)}, u32[]{:S(2)}, u32[]{:S(2)}) collective-permute-start(f32[8,640]{1,0:T(8,128)} %mix_backward.1.refs_0_), channel_id=1, source_target_pairs={{0,8},{4,12},{8,0},{12,4},{1,9},{5,13},{9,1},{13,5},{2,10},{6,14},... | collective-permute-start | bytes 61448 | tf_op jit(solution)/shard_map/ppermute | solution.py:711
  42.0 1.9 %collective-permute-start.11 = (f32[8,640]{1,0:T(8,128)}, f32[8,640]{1,0:T(8,128)S(1)}, u32[]{:S(2)}, u32[]{:S(2)}) collective-permute-start(f32[8,640]{1,0:T(8,128)} %mix_backward.1.refs_0_), channel_id=1, source_target_pairs={{0,12},{4,0},{8,4},{12,8},{1,13},{5,1},{9,5},{13,9},{2,14},{6,2},{... | collective-permute-start | bytes 61448 | tf_op jit(solution)/shard_map/ppermute | solution.py:711
  44.0 0.5 collective-permute-start.16
  44.7 1.5 %collective-permute-done.10.refs_2_ = f32[8,640]{1,0:T(8,128)S(1)} collective-permute-done((f32[8,640]{1,0:T(8,128)}, f32[8,640]{1,0:T(8,128)S(1)}, u32[]{:S(2)}, u32[]{:S(2)}) %collective-permute-start.10) | collective-permute-done | bytes 20512 | tf_op jit(solution)/shard_map/ppermute | solution.py:711
  46.3 1.2 %collective-permute-done.18.refs_7_ = bf16[128,512]{1,0:T(8,128)(2,1)S(1)} collective-permute-done((bf16[128,512]{1,0:T(8,128)(2,1)S(1)}, bf16[128,512]{1,0:T(8,128)(2,1)S(1)}, u32[]{:S(2)}, u32[]{:S(2)}) %collective-permute-start.18) | collective-permute-done | bytes 131104 | tf_op jit(solution)/shard_map/ppermute | solution.py:721
  47.6 0.6 %copy-done.8 = bf16[128,512]{1,0:T(8,128)(2,1)} copy-done((bf16[128,512]{1,0:T(8,128)(2,1)}, bf16[128,512]{1,0:T(8,128)(2,1)S(1)}, u32[]{:S(2)}) %copy-start.8) | copy-done | bytes 131096
  48.2 3.3 %layer_out.1 = (f32[128,256]{1,0:T(8,128)}, f32[128,256]{1,0:T(8,128)}) custom-call(s32[15]{0:T(128)} %concatenate.9.scalars, bf16[128,512]{1,0:T(8,128)(2,1)} %mix_forward.1.refs_0_, bf16[128,512]{1,0:T(8,128)(2,1)} %copy-done.2, bf16[128,512]{1,0:T(8,128)(2,1)} %copy-done.3, bf16[128,512]{1,0:T(8,128)(2,1)} %copy-done.4, bf16[128,512]{1,0:T(8,128)(2,1)} %copy-done.5, ...), custom_call_target="tpu_custom_call" | custom-call | tf_op jit(solution)/shard_map/layer_out/pallas_call | solution.py:581
  51.5 0.6 collective-permute-start.19
  52.1 0.7 %constant_dynamic-update-slice_fusion = (f32[8,1792]{1,0:T(8,128)S(1)}, f32[8,256]{1,0:T(8,128)S(1)}) fusion(f32[8,1792]{1,0:T(8,128)S(1)} %slice_dynamic-update-slice_fusion, f32[8,640]{1,0:T(8,128)S(1)} %collective-permute-done.11.refs_3_, f32[8,640]{1,0:T(8,128)S(1)} %collective-permute-done.10.refs_2_, f32[8,640]{1,0:T(8,128)S(1)} %collective-permute-done.9.refs_1_, ...), kind=kLoop, calls=%fused_computation.11 | loop fusion | flops 6144 | bytes 49152 | tf_op jit(solution)/shard_map/concatenate | solution.py:753
  52.8 1.5 %collective-permute-start.13 = (f32[8,256]{1,0:T(8,128)S(1)}, f32[8,256]{1,0:T(8,128)S(1)}, u32[]{:S(2)}, u32[]{:S(2)}) collective-permute-start(f32[8,256]{1,0:T(8,128)S(1)} %get-tuple-element.38), channel_id=1, source_target_pairs={{0,2},{1,3},{2,0},{3,1},{4,6},{5,7},{6,4},{7,5},{8,10},{9,11},{10,... | collective-permute-start | bytes 24584 | tf_op jit(solution)/shard_map/ppermute | solution.py:721
  54.3 0.7 %collective-permute-start.12 = (f32[8,1792]{1,0:T(8,128)S(1)}, f32[8,1792]{1,0:T(8,128)S(1)}, u32[]{:S(2)}, u32[]{:S(2)}) collective-permute-start(f32[8,1792]{1,0:T(8,128)S(1)} %get-tuple-element.37), channel_id=1, source_target_pairs={{0,1},{1,0},{2,3},{3,2},{4,5},{5,4},{6,7},{7,6},{8,9},{9,8},{10,11... | collective-permute-start | bytes 172040 | tf_op jit(solution)/shard_map/ppermute | solution.py:721
  54.9 5.7 %weight_grad.1 = (f32[1024,1024]{1,0:T(8,128)}, f32[8,128]{1,0:T(8,128)}) custom-call(s32[15]{0:T(128)} %concatenate.9.scalars, bf16[128,512]{1,0:T(8,128)(2,1)} %mix_forward.1.refs_0_, bf16[128,512]{1,0:T(8,128)(2,1)} %copy-done.2, bf16[128,512]{1,0:T(8,128)(2,1)} %copy-done.3, bf16[128,512]{1,0:T(8,128)(2,1)} %copy-done.4, bf16[128,512]{1,0:T(8,128)(2,1)} %copy-done.5, ...), custom_call_target="tpu_custom_call" | custom-call | flops 1073741824 | bytes 6291456 | tf_op jit(solution)/shard_map/weight_grad/pallas_call | solution.py:626
  60.7 0.5 copy-done.18
  61.3 2.5 %place_grads.1 = (bf16[128,256]{1,0:T(8,128)(2,1)}, f32[5,2,1024]{2,1,0:T(2,128)}, f32[5,2,128]{2,1,0:T(2,128)}, f32[5,16]{1,0:T(8,128)}) custom-call(s32[15]{0:T(128)} %concatenate.9.scalars, f32[8,640]{1,0:T(8,128)} %mix_backward.1.refs_0_, f32[8,640]{1,0:T(8,128)} %copy-done.10, f32[8,640]{1,0:T(8,128)} %copy-done.11, f32[8,640]{1,0:T(8,128)} %copy-done.12, ...), custom_call_target="tpu_custom_call" | custom-call | tf_op jit(solution)/shard_map/place_grads/pallas_call | solution.py:686
  (73 shorter events, 1.1 us)
Async XLA Ops:
  2.1 13.3 %copy-start.13 = (bf16[144,256]{1,0:T(8,128)(2,1)}, bf16[144,256]{1,0:T(8,128)(2,1)S(1)}, u32[]{:S(2)}) copy-start(bf16[144,256]{1,0:T(8,128)(2,1)S(1)} %fusion.1.refs_0_) | copy-start | bytes 221188
  2.1 10.8 %collective-permute-start = (bf16[144,256]{1,0:T(8,128)(2,1)S(1)}, bf16[144,256]{1,0:T(8,128)(2,1)S(1)}, u32[]{:S(2)}, u32[]{:S(2)}) collective-permute-start(bf16[144,256]{1,0:T(8,128)(2,1)S(1)} %fusion.1.refs_0_), channel_id=1, source_target_pairs={{0,4},{4,8},{8,12},{12,0},{1,5},{5,9},{9,13},{13,1},{2,6},{6,10},{... | collective-permute-start | bytes 221192 | tf_op jit(solution)/shard_map/ppermute | solution.py:711
  5.2 7.8 %collective-permute-start.1 = (bf16[144,256]{1,0:T(8,128)(2,1)S(1)}, bf16[144,256]{1,0:T(8,128)(2,1)S(1)}, u32[]{:S(2)}, u32[]{:S(2)}) collective-permute-start(bf16[144,256]{1,0:T(8,128)(2,1)S(1)} %fusion.1.refs_0_), channel_id=1, source_target_pairs={{0,8},{4,12},{8,0},{12,4},{1,9},{5,13},{9,1},{13,5},{2,10},{6,14},... | collective-permute-start | bytes 221192 | tf_op jit(solution)/shard_map/ppermute | solution.py:711
  7.8 5.2 %collective-permute-start.2 = (bf16[144,256]{1,0:T(8,128)(2,1)S(1)}, bf16[144,256]{1,0:T(8,128)(2,1)S(1)}, u32[]{:S(2)}, u32[]{:S(2)}) collective-permute-start(bf16[144,256]{1,0:T(8,128)(2,1)S(1)} %fusion.1.refs_0_), channel_id=1, source_target_pairs={{0,12},{4,0},{8,4},{12,8},{1,13},{5,1},{9,5},{13,9},{2,14},{6,2},{... | collective-permute-start | bytes 221192 | tf_op jit(solution)/shard_map/ppermute | solution.py:711
  12.9 2.6 %copy-start.16 = (bf16[144,256]{1,0:T(8,128)(2,1)}, bf16[144,256]{1,0:T(8,128)(2,1)S(1)}, u32[]{:S(2)}) copy-start(bf16[144,256]{1,0:T(8,128)(2,1)S(1)} %collective-permute-done.2.refs_3_) | copy-start | bytes 221188
  12.9 2.5 %copy-start.15 = (bf16[144,256]{1,0:T(8,128)(2,1)}, bf16[144,256]{1,0:T(8,128)(2,1)S(1)}, u32[]{:S(2)}) copy-start(bf16[144,256]{1,0:T(8,128)(2,1)S(1)} %collective-permute-done.1.refs_2_) | copy-start | bytes 221188
  13.9 7.6 %copy-start = (bf16[4,128,256]{2,1,0:T(8,128)(2,1)}, bf16[4,128,256]{2,1,0:T(8,128)(2,1)S(1)}, u32[]{:S(2)}) copy-start(bf16[4,128,256]{2,1,0:T(8,128)(2,1)S(1)} %pad_maximum_fusion.refs_12_.refs_8_) | copy-start | bytes 786436
  13.9 8.0 %collective-permute-start.3 = (bf16[4,128,256]{2,1,0:T(8,128)(2,1)S(1)}, bf16[4,128,256]{2,1,0:T(8,128)(2,1)S(1)}, u32[]{:S(2)}, u32[]{:S(2)}) collective-permute-start(bf16[4,128,256]{2,1,0:T(8,128)(2,1)S(1)} %pad_maximum_fusion.refs_12_.refs_8_), channel_id=1, source_target_pairs={{0,2},{1,3},{2,0},{3,1},{4,6},{5,7},{6,4},{7,5},{8,10},{9,11},{10,... | collective-permute-start | bytes 786440 | tf_op jit(solution)/shard_map/ppermute | solution.py:721
  15.5 11.0 %collective-permute-start.7 = (bf16[4,128,256]{2,1,0:T(8,128)(2,1)S(1)}, bf16[4,128,256]{2,1,0:T(8,128)(2,1)S(1)}, u32[]{:S(2)}, u32[]{:S(2)}) collective-permute-start(bf16[4,128,256]{2,1,0:T(8,128)(2,1)S(1)} %pad_maximum_fusion.refs_12_.refs_8_), channel_id=1, source_target_pairs={{0,1},{1,0},{2,3},{3,2},{4,5},{5,4},{6,7},{7,6},{8,9},{9,8},{10,11... | collective-permute-start | bytes 786440 | tf_op jit(solution)/shard_map/ppermute | solution.py:721
  21.5 22.4 %copy-start.1 = (bf16[128,512]{1,0:T(8,128)(2,1)S(1)}, bf16[128,512]{1,0:T(8,128)(2,1)}, u32[]{:S(2)}) copy-start(bf16[128,512]{1,0:T(8,128)(2,1)} %mix_forward.1.refs_0_) | copy-start | bytes 393220
  21.9 4.6 %copy-start.20 = (bf16[4,128,256]{2,1,0:T(8,128)(2,1)}, bf16[4,128,256]{2,1,0:T(8,128)(2,1)S(1)}, u32[]{:S(2)}) copy-start(bf16[4,128,256]{2,1,0:T(8,128)(2,1)S(1)} %collective-permute-done.3.refs_14_.refs_10_) | copy-start | bytes 786436
  21.9 4.6 %collective-permute-start.8 = (bf16[4,128,256]{2,1,0:T(8,128)(2,1)S(1)}, bf16[4,128,256]{2,1,0:T(8,128)(2,1)S(1)}, u32[]{:S(2)}, u32[]{:S(2)}) collective-permute-start(bf16[4,128,256]{2,1,0:T(8,128)(2,1)S(1)} %collective-permute-done.3.refs_14_.refs_10_), channel_id=1, source_target_pairs={{0,1},{1,0},{2,3},{3,2},{4,5},{5,4},{6,7},{7,6},{8,9},{9,8},{10,11... | collective-permute-start | bytes 786440 | tf_op jit(solution)/shard_map/ppermute | solution.py:721
  22.1 16.6 %collective-permute-start.4 = (bf16[128,512]{1,0:T(8,128)(2,1)}, bf16[128,512]{1,0:T(8,128)(2,1)S(1)}, u32[]{:S(2)}, u32[]{:S(2)}) collective-permute-start(bf16[128,512]{1,0:T(8,128)(2,1)} %mix_forward.1.refs_0_), channel_id=1, source_target_pairs={{0,4},{4,8},{8,12},{12,0},{1,5},{5,9},{9,13},{13,1},{2,6},{6,10},{... | collective-permute-start | bytes 393224 | tf_op jit(solution)/shard_map/ppermute | solution.py:711
  24.0 14.7 %collective-permute-start.5 = (bf16[128,512]{1,0:T(8,128)(2,1)}, bf16[128,512]{1,0:T(8,128)(2,1)S(1)}, u32[]{:S(2)}, u32[]{:S(2)}) collective-permute-start(bf16[128,512]{1,0:T(8,128)(2,1)} %mix_forward.1.refs_0_), channel_id=1, source_target_pairs={{0,8},{4,12},{8,0},{12,4},{1,9},{5,13},{9,1},{13,5},{2,10},{6,14},... | collective-permute-start | bytes 393224 | tf_op jit(solution)/shard_map/ppermute | solution.py:711
  25.9 12.9 %collective-permute-start.6 = (bf16[128,512]{1,0:T(8,128)(2,1)}, bf16[128,512]{1,0:T(8,128)(2,1)S(1)}, u32[]{:S(2)}, u32[]{:S(2)}) collective-permute-start(bf16[128,512]{1,0:T(8,128)(2,1)} %mix_forward.1.refs_0_), channel_id=1, source_target_pairs={{0,12},{4,0},{8,4},{12,8},{1,13},{5,1},{9,5},{13,9},{2,14},{6,2},{... | collective-permute-start | bytes 393224 | tf_op jit(solution)/shard_map/ppermute | solution.py:711
  38.7 8.8 %copy-start.2 = (bf16[128,512]{1,0:T(8,128)(2,1)}, bf16[128,512]{1,0:T(8,128)(2,1)S(1)}, u32[]{:S(2)}) copy-start(bf16[128,512]{1,0:T(8,128)(2,1)S(1)} %collective-permute-done.4.refs_1_) | copy-start | bytes 393220
  38.7 8.8 %copy-start.3 = (bf16[128,512]{1,0:T(8,128)(2,1)}, bf16[128,512]{1,0:T(8,128)(2,1)S(1)}, u32[]{:S(2)}) copy-start(bf16[128,512]{1,0:T(8,128)(2,1)S(1)} %collective-permute-done.5.refs_2_) | copy-start | bytes 393220
  38.7 8.8 %copy-start.4 = (bf16[128,512]{1,0:T(8,128)(2,1)}, bf16[128,512]{1,0:T(8,128)(2,1)S(1)}, u32[]{:S(2)}) copy-start(bf16[128,512]{1,0:T(8,128)(2,1)S(1)} %collective-permute-done.6.refs_3_) | copy-start | bytes 393220
  38.8 5.9 %collective-permute-start.9 = (f32[8,640]{1,0:T(8,128)}, f32[8,640]{1,0:T(8,128)S(1)}, u32[]{:S(2)}, u32[]{:S(2)}) collective-permute-start(f32[8,640]{1,0:T(8,128)} %mix_backward.1.refs_0_), channel_id=1, source_target_pairs={{0,4},{4,8},{8,12},{12,0},{1,5},{5,9},{9,13},{13,1},{2,6},{6,10},{... | collective-permute-start | bytes 61448 | tf_op jit(solution)/shard_map/ppermute | solution.py:711
  40.9 5.2 %collective-permute-start.10 = (f32[8,640]{1,0:T(8,128)}, f32[8,640]{1,0:T(8,128)S(1)}, u32[]{:S(2)}, u32[]{:S(2)}) collective-permute-start(f32[8,640]{1,0:T(8,128)} %mix_backward.1.refs_0_), channel_id=1, source_target_pairs={{0,8},{4,12},{8,0},{12,4},{1,9},{5,13},{9,1},{13,5},{2,10},{6,14},... | collective-permute-start | bytes 61448 | tf_op jit(solution)/shard_map/ppermute | solution.py:711
  42.0 4.1 %collective-permute-start.11 = (f32[8,640]{1,0:T(8,128)}, f32[8,640]{1,0:T(8,128)S(1)}, u32[]{:S(2)}, u32[]{:S(2)}) collective-permute-start(f32[8,640]{1,0:T(8,128)} %mix_backward.1.refs_0_), channel_id=1, source_target_pairs={{0,12},{4,0},{8,4},{12,8},{1,13},{5,1},{9,5},{13,9},{2,14},{6,2},{... | collective-permute-start | bytes 61448 | tf_op jit(solution)/shard_map/ppermute | solution.py:711
  44.0 2.3 %collective-permute-start.15 = (bf16[128,512]{1,0:T(8,128)(2,1)S(1)}, bf16[128,512]{1,0:T(8,128)(2,1)S(1)}, u32[]{:S(2)}, u32[]{:S(2)}) collective-permute-start(bf16[128,512]{1,0:T(8,128)(2,1)S(1)} %copy-done.1), channel_id=1, source_target_pairs={{0,1},{1,0},{2,3},{3,2},{4,5},{5,4},{6,7},{7,6},{8,9},{9,8},{10,11... | collective-permute-start | bytes 393224 | tf_op jit(solution)/shard_map/ppermute | solution.py:721
  44.0 2.3 %collective-permute-start.16 = (bf16[128,512]{1,0:T(8,128)(2,1)S(1)}, bf16[128,512]{1,0:T(8,128)(2,1)S(1)}, u32[]{:S(2)}, u32[]{:S(2)}) collective-permute-start(bf16[128,512]{1,0:T(8,128)(2,1)S(1)} %collective-permute-done.4.refs_1_), channel_id=1, source_target_pairs={{0,1},{1,0},{2,3},{3,2},{4,5},{5,4},{6,7},{7,6},{8,9},{9,8},{10,11... | collective-permute-start | bytes 393224 | tf_op jit(solution)/shard_map/ppermute | solution.py:721
  44.7 15.9 %copy-start.10 = (f32[8,640]{1,0:T(8,128)}, f32[8,640]{1,0:T(8,128)S(1)}, u32[]{:S(2)}) copy-start(f32[8,640]{1,0:T(8,128)S(1)} %collective-permute-done.9.refs_1_) | copy-start | bytes 61444
  44.7 1.5 %collective-permute-start.17 = (bf16[128,512]{1,0:T(8,128)(2,1)S(1)}, bf16[128,512]{1,0:T(8,128)(2,1)S(1)}, u32[]{:S(2)}, u32[]{:S(2)}) collective-permute-start(bf16[128,512]{1,0:T(8,128)(2,1)S(1)} %collective-permute-done.5.refs_2_), channel_id=1, source_target_pairs={{0,1},{1,0},{2,3},{3,2},{4,5},{5,4},{6,7},{7,6},{8,9},{9,8},{10,11... | collective-permute-start | bytes 393224 | tf_op jit(solution)/shard_map/ppermute | solution.py:721
  46.2 14.4 %copy-start.11 = (f32[8,640]{1,0:T(8,128)}, f32[8,640]{1,0:T(8,128)S(1)}, u32[]{:S(2)}) copy-start(f32[8,640]{1,0:T(8,128)S(1)} %collective-permute-done.10.refs_2_) | copy-start | bytes 61444
  46.2 1.3 %collective-permute-start.18 = (bf16[128,512]{1,0:T(8,128)(2,1)S(1)}, bf16[128,512]{1,0:T(8,128)(2,1)S(1)}, u32[]{:S(2)}, u32[]{:S(2)}) collective-permute-start(bf16[128,512]{1,0:T(8,128)(2,1)S(1)} %collective-permute-done.6.refs_3_), channel_id=1, source_target_pairs={{0,1},{1,0},{2,3},{3,2},{4,5},{5,4},{6,7},{7,6},{8,9},{9,8},{10,11... | collective-permute-start | bytes 393224 | tf_op jit(solution)/shard_map/ppermute | solution.py:721
  46.2 14.4 %copy-start.12 = (f32[8,640]{1,0:T(8,128)}, f32[8,640]{1,0:T(8,128)S(1)}, u32[]{:S(2)}) copy-start(f32[8,640]{1,0:T(8,128)S(1)} %collective-permute-done.11.refs_3_) | copy-start | bytes 61444
  51.5 9.2 %collective-permute-start.19 = (f32[128,256]{1,0:T(8,128)}, f32[128,256]{1,0:T(8,128)S(1)}, u32[]{:S(2)}, u32[]{:S(2)}) collective-permute-start(f32[128,256]{1,0:T(8,128)} %get-tuple-element.30), channel_id=1, source_target_pairs={{0,2},{1,3},{2,0},{3,1},{4,6},{5,7},{6,4},{7,5},{8,10},{9,11},{10,... | collective-permute-start | bytes 393224 | tf_op jit(solution)/shard_map/ppermute | solution.py:721
  52.8 7.8 %collective-permute-start.13 = (f32[8,256]{1,0:T(8,128)S(1)}, f32[8,256]{1,0:T(8,128)S(1)}, u32[]{:S(2)}, u32[]{:S(2)}) collective-permute-start(f32[8,256]{1,0:T(8,128)S(1)} %get-tuple-element.38), channel_id=1, source_target_pairs={{0,2},{1,3},{2,0},{3,1},{4,6},{5,7},{6,4},{7,5},{8,10},{9,11},{10,... | collective-permute-start | bytes 24584 | tf_op jit(solution)/shard_map/ppermute | solution.py:721
  54.3 6.4 %collective-permute-start.14 = (f32[8,256]{1,0:T(8,128)S(1)}, f32[8,256]{1,0:T(8,128)S(1)}, u32[]{:S(2)}, u32[]{:S(2)}) collective-permute-start(f32[8,256]{1,0:T(8,128)S(1)} %get-tuple-element.38), channel_id=1, source_target_pairs={{0,3},{1,2},{2,1},{3,0},{4,7},{5,6},{6,5},{7,4},{8,11},{9,10},{10,... | collective-permute-start | bytes 24584 | tf_op jit(solution)/shard_map/ppermute | solution.py:721
  54.3 6.4 %collective-permute-start.12 = (f32[8,1792]{1,0:T(8,128)S(1)}, f32[8,1792]{1,0:T(8,128)S(1)}, u32[]{:S(2)}, u32[]{:S(2)}) collective-permute-start(f32[8,1792]{1,0:T(8,128)S(1)} %get-tuple-element.37), channel_id=1, source_target_pairs={{0,1},{1,0},{2,3},{3,2},{4,5},{5,4},{6,7},{7,6},{8,9},{9,8},{10,11... | collective-permute-start | bytes 172040 | tf_op jit(solution)/shard_map/ppermute | solution.py:721
  (11 other events, 11.0 us)

commit v3 on v2

--- a/solution.py
+++ b/solution.py
@@ -17,7 +17,6 @@
 TN = (((0,), (0,)), ((), ()))
 X_ROW, Z_ROW, DT_ROW, MISC_ROW, TAB_ROWS = 0, 8, 16, 24, 32
 RAW = 8
-VMEM_LIMIT = 56 * 1024 * 1024
 XF, XB, ZZ, BCF, BCB, WIDE = 0, 128, 256, 384, 640, 896
 
 
@@ -51,24 +50,23 @@
     return mm(jnp.concatenate(left, ca), jnp.concatenate(right, cb), dims)
 
 
-def permuted(table, scalars, count):
-    row = lax.broadcasted_iota(jnp.int32, table[:SYM].shape, 0)
-    out = jnp.zeros_like(table[:SYM])
+def permuted(table, basemap, count):
+    row = lax.broadcasted_iota(jnp.int32, table.shape, 0)
+    out = jnp.zeros_like(table)
     for k in range(count):
         picked = jnp.zeros_like(table[0:1])
         for m in range(count):
-            picked = jnp.where(scalars[k] == m, table[m : m + 1], picked)
+            picked = jnp.where(basemap[k] == m, table[m : m + 1], picked)
         out = jnp.where(row == k, picked, out)
     return out
 
 
 def sigmoid(v):
-    return 1.0 / (1.0 + jnp.exp(-v))
-
-
-def gather_tables(scalars, raw, tabs_ref, bcp_ref, conv, vocab):
-    xz_ref, bc_ref, conv_ref, conv_bc_ref, dt_ref, a_log_ref, skip_ref = raw[1:]
-    j = scalars[0]
+    return 0.5 * jnp.tanh(0.5 * v) + 0.5
+
+
+def gather_tables(j, raw, tabs_ref, bcp_ref, conv, vocab):
+    xz_ref, bc_ref, conv_ref, conv_bc_ref, dt_ref, a_log_ref, skip_ref = raw
     lanes = pl.ds(pl.multiple_of(j * LANES, LANES), LANES)
     head0 = lax.broadcasted_iota(jnp.int32, (1, LANES), 1) < 64
     pair = lambda a, b: jnp.where(head0, a, b)
@@ -91,16 +89,70 @@
     tabs_ref[at + 1 : at + 2, :] = pair(skip_ref[2 * j], skip_ref[2 * j + 1])
 
 
-def prepare(scalars, tok_refs, raw, tabs_ref, bcp_ref, r, conv, vocab):
-    gather_tables(scalars, raw, tabs_ref, bcp_ref, conv, vocab)
+def tables_kernel(scalars, *refs, conv, vocab):
+    tabs_ref, bcp_ref, dt1_ref, perm_ref, w_ref, w2_out, wf, w2 = refs[RAW : RAW + 8]
+    local, sems = refs[RAW + 8 : 2 * RAW + 8], refs[2 * RAW + 8]
+    copies = [pltpu.make_async_copy(refs[k], local[k], sems.at[k]) for k in range(RAW)]
+    for copy in copies:
+        copy.start()
+    for copy in copies:
+        copy.wait()
+    basemap = local[0]
+    gather_tables(scalars[0], local[1:], tabs_ref, bcp_ref, conv, vocab)
+    row = lax.broadcasted_iota(jnp.int32, perm_ref.shape, 0)
+    lane = lax.broadcasted_iota(jnp.int32, perm_ref.shape, 1)
+    perm = jnp.zeros(perm_ref.shape, F32)
+    for k in range(vocab):
+        perm = jnp.where(jnp.logical_and(lane == k, row == basemap[k]), 1.0, perm)
+    perm_ref[...] = perm
+    wf[...] = jnp.zeros_like(wf)
+    w2[...] = jnp.zeros_like(w2)
+    for st in range(2):
+        fetch = (lambda t: t) if st == 0 else (lambda t: permuted(t, basemap, vocab))
+        xt = fetch(tabs_ref[X_ROW : X_ROW + SYM, :])
+        zt = fetch(tabs_ref[Z_ROW : Z_ROW + SYM, :])
+        dtt = fetch(tabs_ref[DT_ROW : DT_ROW + SYM, :])
+        if st == 1:
+            dt1_ref[...] = dtt
+        bct = fetch(bcp_ref[0:SYM, :])
+        base = st * WIDE
+        mid = SYM * (conv - 1)
+        wf[mid : mid + SYM, base + ZZ : base + ZZ + LANES] = zt
+        for k in range(conv):
+            cx = tabs_ref[MISC_ROW + k : MISC_ROW + k + 1, :]
+            cbc = bcp_ref[SYM + k : SYM + k + 1, :]
+            lo, hi = mid - SYM * k, mid + SYM * k
+            wf[lo : lo + SYM, base + XF : base + XF + LANES] = xt * cx
+            wf[hi : hi + SYM, base + XB : base + XB + LANES] = xt * cx
+            wf[lo : lo + SYM, base + BCF : base + BCF + 256] = bct * cbc
+            wf[hi : hi + SYM, base + BCB : base + BCB + 256] = bct * cbc
+        dt = jnp.maximum(dtt, 0.0) + jnp.log1p(jnp.exp(-jnp.abs(dtt)))
+        ld = -jnp.exp(tabs_ref[MISC_ROW + 4 : MISC_ROW + 5, :]) * dt
+        ld0 = jnp.broadcast_to(ld[:, 0:1], ld.shape)
+        ld1 = jnp.broadcast_to(ld[:, 64:65], ld.shape)
+        for i, t in enumerate((ld, ld0, ld1)):
+            for k, piece in enumerate(thirds(t)):
+                c = st * 384 + i * 128
+                w2[SYM * k : SYM * (k + 1), c : c + 128] = piece
+                w2[32 + SYM * k : 32 + SYM * (k + 1), 768 + c : 768 + c + 128] = piece
+        for k, piece in enumerate(thirds(dt)):
+            c = 1536 + st * 128
+            w2[64 + SYM * k : 64 + SYM * (k + 1), c : c + 128] = piece
+    top, rest = halves(wf[...])
+    w_ref[0:64, :] = top
+    w_ref[64:128, :] = rest
+    w2_out[...] = w2[...].astype(BF16)
+
+
+def prepare(scalars, tok_refs, w_ref, w2_ref, r, conv):
     ns = len(tok_refs)
     length = ns * BLOCK
     mine = scalars[1]
     for k in range(ns):
-        at = jnp.where(mine >= k, mine - k, mine - k + ns)
         sym = lax.broadcasted_iota(jnp.int32, (SYM, BLOCK), 0).astype(F32)
-        tok = jnp.broadcast_to(tok_refs[k][0:1, 0:BLOCK].astype(F32), (SYM, BLOCK))
-        r.oh[:, pl.ds(pl.multiple_of(at * BLOCK, BLOCK), BLOCK)] = (sym == tok).astype(F32)
+        tok = jnp.broadcast_to(tok_refs[k][BLOCK : BLOCK + 1, 0:BLOCK].astype(F32), (SYM, BLOCK))
+        at = jnp.bitwise_xor(mine, k) * BLOCK
+        r.oh[:, pl.ds(pl.multiple_of(at, BLOCK), BLOCK)] = (sym == tok).astype(F32)
     oh = r.oh[...]
     lane = lax.broadcasted_iota(jnp.int32, (SYM, length), 1)
     up = (
@@ -124,41 +176,10 @@
             r.rows[128 + SYM * k : 128 + SYM * (k + 1), cols] = inc
             r.rows[160 + SYM * k : 160 + SYM * (k + 1), cols] = exc
             r.rows[192 + SYM * k : 192 + SYM * (k + 1), cols] = oh[:, cols]
-    r.wf[...] = jnp.zeros_like(r.wf)
-    r.w2[...] = jnp.zeros_like(r.w2)
-    for st in range(2):
-        fetch = (lambda t: t) if st == 0 else (lambda t: permuted(t, raw[0], vocab))
-        xt = fetch(tabs_ref[X_ROW : X_ROW + SYM, :])
-        zt = fetch(tabs_ref[Z_ROW : Z_ROW + SYM, :])
-        dtt = fetch(tabs_ref[DT_ROW : DT_ROW + SYM, :])
-        bct = fetch(bcp_ref[0:SYM, :])
-        base = st * WIDE
-        mid = SYM * (conv - 1)
-        r.wf[mid : mid + SYM, base + ZZ : base + ZZ + LANES] = zt
-        for k in range(conv):
-            cx = tabs_ref[MISC_ROW + k : MISC_ROW + k + 1, :]
-            cbc = bcp_ref[SYM + k : SYM + k + 1, :]
-            lo, hi = mid - SYM * k, mid + SYM * k
-            r.wf[lo : lo + SYM, base + XF : base + XF + LANES] = xt * cx
-            r.wf[hi : hi + SYM, base + XB : base + XB + LANES] = xt * cx
-            r.wf[lo : lo + SYM, base + BCF : base + BCF + 256] = bct * cbc
-            r.wf[hi : hi + SYM, base + BCB : base + BCB + 256] = bct * cbc
-        dt = jnp.maximum(dtt, 0.0) + jnp.log1p(jnp.exp(-jnp.abs(dtt)))
-        ld = -jnp.exp(tabs_ref[MISC_ROW + 4 : MISC_ROW + 5, :]) * dt
-        ld0 = jnp.broadcast_to(ld[:, 0:1], ld.shape)
-        ld1 = jnp.broadcast_to(ld[:, 64:65], ld.shape)
-        for i, t in enumerate((ld, ld0, ld1)):
-            for k, piece in enumerate(thirds(t)):
-                c = st * 384 + i * 128
-                r.w2[SYM * k : SYM * (k + 1), c : c + 128] = piece
-                r.w2[32 + SYM * k : 32 + SYM * (k + 1), 768 + c : 768 + c + 128] = piece
-        for k, piece in enumerate(thirds(dt)):
-            c = 1536 + st * 128
-            r.w2[64 + SYM * k : 64 + SYM * (k + 1), c : c + 128] = piece
-    wh, wl = halves(r.wf[...])
+    r.sym[...] = r.rows[0:64, :].astype(BF16)
     turned = jnp.transpose(r.rows[...]).astype(BF16)
-    r.pre[...] = mm(turned[:, 0:128], jnp.concatenate([wh, wl], 0), NN)
-    w2 = r.w2[...].astype(BF16)
+    r.pre[...] = mm(turned[:, 0:128], w_ref[...], NN)
+    w2 = w2_ref[...]
     r.pd[...] = mm(turned[:, 128:256], w2, NN)
     for st in range(2):
         for part, row0 in ((0, 0), (1, 32)):
@@ -243,35 +264,31 @@
     return r
 
 
-PREP_NAMES = ("oh", "inc", "exc", "rows", "wf", "w2", "pre", "pd", "prow", "x", "bc", "s", "tabs", "bcp")
-
-
-def prep_scratch(length):
+KEPT = ("inc", "exc", "oh", "sym", "pre", "pd", "x", "bc", "s", "dec", "wts", "ys")
+
+
+def kept_shapes(length):
     nb = length // BLOCK
-    v = pltpu.VMEM
     return [
-        v((SYM, length), F32),
-        v((SYM, length), F32),
-        v((SYM, length), F32),
-        v((256, length), F32),
-        v((64, 2 * WIDE), F32),
-        v((128, 1792), F32),
-        v((length, 2 * WIDE), F32),
-        v((length, 1792), F32),
-        v((SYM, length), F32),
-        v((length, 512), F32),
-        v((length, 1024), F32),
-        v((4, nb, LANES, LANES), F32),
-        v((TAB_ROWS, LANES), F32),
-        v((2 * SYM, 256), F32),
+        ((SYM, length), F32),
+        ((SYM, length), F32),
+        ((SYM, length), F32),
+        ((64, length), BF16),
+        ((length, 2 * WIDE), F32),
+        ((length, 1792), F32),
+        ((length, 512), F32),
+        ((length, 1024), F32),
+        ((4, nb, LANES, LANES), F32),
+        ((4 * nb, BLOCK, BLOCK), F32),
+        ((8 * nb, BLOCK, BLOCK), BF16),
+        ((length, 1024), F32),
     ]
 
 
-def forward_kernel(scalars, *refs, ns, conv, vocab):
-    tok_refs, raw, out_ref = refs[:ns], refs[ns : ns + RAW], refs[ns + RAW]
-    r = named(refs[ns + RAW + 1 :], PREP_NAMES)
-    tabs_ref, bcp_ref = r.tabs, r.bcp
-    prepare(scalars, tok_refs, raw, tabs_ref, bcp_ref, r, conv, vocab)
+def forward_kernel(scalars, *refs, ns, conv):
+    tok_refs, (w_ref, w2_ref, tabs_ref, out_ref) = refs[:ns], refs[ns : ns + 4]
+    r = named(refs[ns + 4 :], KEPT + ("rows", "prow"))
+    prepare(scalars, tok_refs, w_ref, w2_ref, r, conv)
     units = [[Unit(r, tabs_ref, st, b, ns) for b in range(ns)] for st in range(2)]
     state_pass_fwd(r, tabs_ref, ns, units)
     for b in range(ns):
@@ -280,48 +297,51 @@
             u = units[st][b]
             xf = r.x[u.rows, st * 256 : st * 256 + 128]
             xb = r.x[u.rows, st * 256 + 128 : st * 256 + 256]
-            left, right = [], []
-            d0, d1 = u.decay(0), u.decay(1)
+            decays = (u.decay(0), u.decay(1))
+            for h in range(2):
+                r.dec[(st * ns + b) * 2 + h] = decays[h]
             y = u.skip * (xf + xb)
             for way, x, mask in ((0, xf, u.low), (1, xb, u.upp)):
                 c = st * 512 + way * 256
                 bm, cm = r.bc[u.rows, c : c + 128], r.bc[u.rows, c + 128 : c + 256]
                 g = jnp.where(mask, mm_fine(cm, bm, NT, 3), 0.0)
-                left += [(g * d0).astype(BF16), (g * d1).astype(BF16)]
-                right += list(u.by_head((u.dt * x).astype(BF16)))
+                left = [(g * d).astype(BF16) for d in decays]
+                for h in range(2):
+                    r.wts[((st * ns + b) * 2 + way) * 2 + h] = left[h]
+                right = u.by_head((u.dt * x).astype(BF16))
+                inner = mm(jnp.concatenate(left, 1), jnp.concatenate(right, 0), NN)
+                r.ys[u.rows, c : c + 128] = inner
+                y = y + inner
                 if (way == 0 and b > 0) or (way == 1 and b < ns - 1):
                     enter = jnp.exp(u.p) if way == 0 else jnp.exp(u.total - u.q)
-                    y = y + enter * mm_fine(cm, r.s[st * 2 + way, b], NN, 2)
-            y = y + mm(jnp.concatenate(left, 1), jnp.concatenate(right, 0), NN)
+                    carried = enter * mm_fine(cm, r.s[st * 2 + way, b], NN, 2)
+                    r.ys[u.rows, c + 128 : c + 256] = carried
+                    y = y + carried
             gated.append(y * u.act(ZZ, 128))
         out_ref[:, units[0][b].rows] = jnp.transpose(gated[0] + gated[1]).astype(BF16)
 
 
 def backward_kernel(scalars, *refs, ns, nq, conv, vocab):
-    tok_refs, raw = refs[:ns], refs[ns : ns + RAW]
-    cot_refs, weight_ref, out_ref = (
-        refs[ns + RAW : ns + RAW + nq],
-        refs[ns + RAW + nq],
-        refs[ns + RAW + nq + 1],
-    )
-    r = named(refs[ns + RAW + nq + 2 :], PREP_NAMES + ("ds", "dg", "dpre"))
-    tabs_ref, bcp_ref = r.tabs, r.bcp
-    prepare(scalars, tok_refs, raw, tabs_ref, bcp_ref, r, conv, vocab)
+    tabs_ref, bcp_ref, dt1_ref, perm_ref = refs[:4]
+    cot_refs, weight_ref = refs[4 : 4 + nq], refs[4 + nq]
+    kept = refs[5 + nq : 5 + nq + len(KEPT)]
+    out_ref, *work = refs[5 + nq + len(KEPT) :]
+    r = named(list(kept) + work, KEPT + ("ds", "dg", "dpre"))
     cols = cot_refs[0].shape[2]
     cot = jnp.concatenate([a[...].reshape(ns * BLOCK, cols) for a in cot_refs], 1)
     weight = []
     for k in range(nq):
         at = pl.multiple_of(scalars[QUARTERS + k] * cols, LANES)
-        weight.append(weight_ref[:, pl.ds(at, cols)])
+        rows = pl.ds(pl.multiple_of(scalars[0] * LANES, LANES), LANES)
+        weight.append(weight_ref[rows, pl.ds(at, cols)])
     d_gated = mm(cot, jnp.concatenate(weight, 1), NT).astype(BF16).astype(F32)
     mine = scalars[1]
     for k in range(ns):
-        at = jnp.where(mine >= k, mine - k, mine - k + ns)
+        at = jnp.bitwise_xor(mine, k)
         r.dg[pl.ds(pl.multiple_of(at * BLOCK, BLOCK), BLOCK), :] = d_gated[
             k * BLOCK : (k + 1) * BLOCK
         ]
     units = [[Unit(r, tabs_ref, st, b, ns) for b in range(ns)] for st in range(2)]
-    state_pass_fwd(r, tabs_ref, ns, units)
     for st in range(2):
         for b in range(ns):
             u = units[st][b]
@@ -351,7 +371,7 @@
             dyr = dy.astype(BF16)
             dyw = dyr.astype(F32)
             dy0, dy1 = u.by_head(dyr)
-            decays = (u.decay(0), u.decay(1))
+            decays = [r.dec[(st * ns + b) * 2 + h] for h in range(2)]
             inputs = [u.dt * v for v in x]
             ur = [v.astype(BF16) for v in inputs]
             uw = [v.astype(F32) for v in ur]
@@ -364,8 +384,7 @@
             for w in range(2):
                 c = st * 512 + w * 256
                 bm, cm = r.bc[u.rows, c : c + 128], r.bc[u.rows, c + 128 : c + 256]
-                g = jnp.where(masks[w], mm_fine(cm, bm, NT, 3), 0.0)
-                weights.append([(g * decays[0]).astype(BF16), (g * decays[1]).astype(BF16)])
+                weights.append([r.wts[((st * ns + b) * 2 + w) * 2 + h] for h in range(2)])
                 bms.append(bm)
                 cms.append(cm)
             du_both = mm(
@@ -382,9 +401,8 @@
             y = u.skip * (x[0] + x[1])
             mixes, step_part, flat = [], 0.0, 0.0
             for w in range(2):
-                inner = mm(
-                    jnp.concatenate(weights[w], 1), jnp.concatenate([uh[w][0], uh[w][1]], 0), NN
-                )
+                c = st * 512 + w * 256
+                inner = r.ys[u.rows, c : c + 128]
                 du_in = du_both[w * BLOCK : (w + 1) * BLOCK]
                 has_enter = (w == 0 and b > 0) or (w == 1 and b < ns - 1)
                 has_leave = (w == 0 and b < ns - 1) or (w == 1 and b > 0)
@@ -402,7 +420,7 @@
                 enter_part = gain_part = None
                 if has_enter:
                     state = r.s[st * 2 + w, b]
-                    carried = enters[w] * mm_fine(cms[w], state, NN, 2)
+                    carried = r.ys[u.rows, c + 128 : c + 256]
                     y = y + carried
                     enter_part = dy * carried
                     d_c = d_c + mm((enters[w] * dy).astype(BF16), state.astype(BF16), NT)
@@ -455,7 +473,7 @@
             )
         d_steps.append(d_step)
         d_decays.append(d_decay)
-    d_tab = mm(r.rows[0:64, :].astype(BF16), r.dpre[...], NN)
+    d_tab = mm(r.sym[...], r.dpre[...], NN)
     mid = SYM * (conv - 1)
     result = None
     for st in range(2):
@@ -475,149 +493,147 @@
                 + d_tab[hi : hi + SYM, base + BCB : base + BCB + 256]
             )
         d_zt = d_tab[mid : mid + SYM, base + ZZ : base + ZZ + 128]
-        dtt = tabs_ref[DT_ROW : DT_ROW + SYM, :]
-        if st == 1:
-            dtt = permuted(dtt, raw[0], vocab)
+        dtt = dt1_ref[...] if st else tabs_ref[DT_ROW : DT_ROW + SYM, :]
         rate = -jnp.exp(tabs_ref[MISC_ROW + 4 : MISC_ROW + 5, :])
         d_dt = (d_steps[st] + rate * d_decays[st]) * sigmoid(dtt)
         wide = jnp.concatenate([d_x, d_zt, d_dt, d_bc], 1)
         if st == 0:
             result = wide
         else:
-            row = lax.broadcasted_iota(jnp.int32, wide.shape, 0)
             for k in range(vocab):
-                result = result + jnp.where(row == raw[0][k], wide[k : k + 1], 0.0)
+                result = result + perm_ref[:, k : k + 1] * wide[k : k + 1]
     out_ref[...] = result
 
 
-def whole(shape):
-    return pl.BlockSpec(shape, lambda i, s: (0,) * len(shape))
-
-
 SMEM = pl.BlockSpec(memory_space=pltpu.SMEM)
-
-
-def raw_specs(raw):
-    return [SMEM] + [whole(a.shape) for a in raw[1:5]] + [SMEM] * 3
-
-
-PARAMS = pltpu.CompilerParams(vmem_limit_bytes=VMEM_LIMIT)
-
-
-def token_specs(ns, pay):
-    last = pay.shape[0] // 16 - 1
-    return [pl.BlockSpec((16, pay.shape[1]), lambda i, s: (last, 0))] * ns
-
-
-def call_forward(scalars, pays, raw):
+VMEM = pl.BlockSpec(memory_space=pltpu.VMEM)
+HBM = pl.BlockSpec(memory_space=pl.ANY)
+
+
+def params(mib):
+    return pltpu.CompilerParams(vmem_limit_bytes=mib * 1024 * 1024)
+
+
+def call_tables(scalars, raw):
+    conv, vocab = raw[3].shape[0], raw[1].shape[0]
+    outs = [
+        ((TAB_ROWS, LANES), F32),
+        ((2 * SYM, 256), F32),
+        ((SYM, LANES), F32),
+        ((SYM, LANES), F32),
+        ((128, 2 * WIDE), BF16),
+        ((128, 1792), BF16),
+    ]
+    return pl.pallas_call(
+        functools.partial(tables_kernel, conv=conv, vocab=vocab),
+        out_shape=[jax.ShapeDtypeStruct(*a) for a in outs],
+        in_specs=[SMEM] + [pl.BlockSpec(memory_space=pltpu.HBM)] * RAW,
+        out_specs=[VMEM] * len(outs),
+        scratch_shapes=[pltpu.VMEM((64, 2 * WIDE), F32), pltpu.VMEM((128, 1792), F32)]
+        + [pltpu.SMEM(raw[0].shape, raw[0].dtype)]
+        + [pltpu.VMEM(a.shape, a.dtype) for a in raw[1:5]]
+        + [pltpu.SMEM(a.shape, a.dtype) for a in raw[5:]]
+        + [pltpu.SemaphoreType.DMA((RAW,))],
+        compiler_params=params(8),
+        cost_estimate=pl.CostEstimate(flops=2 * 10**9, transcendentals=0, bytes_accessed=10**6),
+        name="tables",
+    )(scalars, *raw)
+
+
+def call_forward(scalars, pays, w, w2, tabs, conv):
     ns = len(pays)
     length = ns * BLOCK
+    outs = [((LANES, length), BF16)] + kept_shapes(length)
     return pl.pallas_call(
-        functools.partial(forward_kernel, ns=ns, conv=raw[3].shape[0], vocab=raw[1].shape[0]),
-        out_shape=jax.ShapeDtypeStruct((LANES, length), BF16),
-        grid_spec=pltpu.PrefetchScalarGridSpec(
-            num_scalar_prefetch=1,
-            grid=(1,),
-            in_specs=token_specs(ns, pays[0]) + raw_specs(raw),
-            out_specs=whole((LANES, length)),
-            scratch_shapes=prep_scratch(length),
+        functools.partial(forward_kernel, ns=ns, conv=conv),
+        out_shape=[jax.ShapeDtypeStruct(*a) for a in outs],
+        in_specs=[SMEM] + [VMEM] * (ns + 3),
+        out_specs=[VMEM] * len(outs),
+        scratch_shapes=[pltpu.VMEM((256, length), F32), pltpu.VMEM((SYM, length), F32)],
+        compiler_params=params(8),
+        cost_estimate=pl.CostEstimate(
+            flops=5 * 10**9, transcendentals=0, bytes_accessed=8 * LANES * length
         ),
-        compiler_params=PARAMS,
+        name="mix_forward",
+    )(scalars, *pays, w, w2, tabs)
+
+
+def call_backward(scalars, tables, cots, out_weight, kept, conv, vocab):
+    length = kept[0].shape[1]
+    ns = length // BLOCK
+    return pl.pallas_call(
+        functools.partial(backward_kernel, ns=ns, nq=len(cots), conv=conv, vocab=vocab),
+        out_shape=jax.ShapeDtypeStruct((SYM, 640), F32),
+        in_specs=[SMEM] + [VMEM] * (len(tables) + len(cots) + 1 + len(kept)),
+        out_specs=VMEM,
+        scratch_shapes=[
+            pltpu.VMEM((4, ns, LANES, LANES), F32),
+            pltpu.VMEM((length, LANES), F32),
+            pltpu.VMEM((length, 2 * WIDE), BF16),
+        ],
+        compiler_params=params(10),
         cost_estimate=pl.CostEstimate(
             flops=6 * 10**9, transcendentals=0, bytes_accessed=8 * LANES * length
         ),
-        name="mix_forward",
-    )(scalars, *pays, *raw)
-
-
-def call_backward(scalars, pays, raw, cots, out_weight):
-    ns = len(pays)
-    length = ns * BLOCK
-    extra = [
-        pltpu.VMEM((4, ns, LANES, LANES), F32),
-        pltpu.VMEM((length, LANES), F32),
-        pltpu.VMEM((length, 2 * WIDE), BF16),
-    ]
-    return pl.pallas_call(
-        functools.partial(
-            backward_kernel, ns=ns, nq=len(cots), conv=raw[3].shape[0], vocab=raw[1].shape[0]
-        ),
-        out_shape=jax.ShapeDtypeStruct((SYM, 640), F32),
-        grid_spec=pltpu.PrefetchScalarGridSpec(
-            num_scalar_prefetch=1,
-            grid=(1,),
-            in_specs=token_specs(ns, pays[0])
-            + raw_specs(raw)
-            + [whole(a.shape) for a in cots]
-            + [pl.BlockSpec((LANES, out_weight.shape[1]), lambda i, s: (s[0], 0))],
-            out_specs=whole((SYM, 640)),
-            scratch_shapes=prep_scratch(length) + extra,
-        ),
-        compiler_params=PARAMS,
-        cost_estimate=pl.CostEstimate(
-            flops=10**10, transcendentals=0, bytes_accessed=8 * LANES * length
-        ),
         name="mix_backward",
-    )(scalars, *pays, *raw, *cots, out_weight)
+    )(scalars, *tables, *cots, out_weight, *kept)
 
 
 QUARTERS = 3
 
 
 def out_kernel(scalars, *refs, ns, nh, nc):
-    slices, weights, outs = refs[: ns * nc], refs[ns * nc : ns * nc + nh], refs[ns * nc + nh :]
+    slices, weight_ref, outs = refs[: ns * nc], refs[ns * nc], refs[ns * nc + 1 :]
     here = pl.ds(pl.multiple_of(scalars[1] * BLOCK, BLOCK), BLOCK)
     places = QUARTERS + nh * nc
-    rows = [pl.ds(pl.multiple_of(scalars[places + i] * LANES, LANES), LANES) for i in range(ns * nc)]
+    cols = outs[0].shape[1]
     left = jnp.concatenate([a[:, here] for a in slices], 0)
     for k in range(nh):
-        outs[k][...] = mm(left, jnp.concatenate([weights[k][at, :] for at in rows], 0), TN)
+        at = pl.ds(pl.multiple_of(scalars[QUARTERS + k * nc] * cols, LANES), cols)
+        right = []
+        for i in range(ns * nc):
+            rows = pl.ds(pl.multiple_of(scalars[places + i] * LANES, LANES), LANES)
+            right.append(weight_ref[rows, at])
+        outs[k][...] = mm(left, jnp.concatenate(right, 0), TN)
 
 
 def call_out(scalars, slices, out_weight, ns, nh, nc):
-    rows, width = out_weight.shape
-    cols = width // (nh * nc)
-    weight_spec = lambda k: pl.BlockSpec((rows, cols), lambda i, s: (0, s[QUARTERS + k * nc]))
+    cols = out_weight.shape[1] // (nh * nc)
     return pl.pallas_call(
         functools.partial(out_kernel, ns=ns, nh=nh, nc=nc),
         out_shape=[jax.ShapeDtypeStruct((BLOCK, cols), F32)] * nh,
-        grid_spec=pltpu.PrefetchScalarGridSpec(
-            num_scalar_prefetch=1,
-            grid=(1,),
-            in_specs=[whole(a.shape) for a in slices] + [weight_spec(k) for k in range(nh)],
-            out_specs=[whole((BLOCK, cols))] * nh,
-        ),
-        compiler_params=PARAMS,
+        in_specs=[SMEM] + [VMEM] * (len(slices) + 1),
+        out_specs=[VMEM] * nh,
+        compiler_params=params(8),
         name="layer_out",
-    )(scalars, *slices, *([out_weight] * nh))
+    )(scalars, *slices, out_weight)
 
 
 def weight_kernel(scalars, *refs, ns, nh, nc):
     slices, cots = refs[: ns * nc], refs[ns * nc : ns * nc + nh * nc]
-    out_ref, mark_ref, left = refs[ns * nc + nh * nc :]
-    i = pl.program_id(0)
+    out_ref, mark_ref, left, buf, sems = refs[ns * nc + nh * nc :]
     mine = scalars[1]
     places = QUARTERS + nh * nc
     cols = cots[0].shape[2]
-
-    @pl.when(i == 0)
-    def _():
-        mark_ref[...] = jnp.zeros_like(mark_ref)
+    mark_ref[...] = jnp.zeros_like(mark_ref)
+    for n in range(ns * nc):
+        for k in range(ns):
+            at = jnp.bitwise_xor(mine, k)
+            left[n * LANES : (n + 1) * LANES, k * BLOCK : (k + 1) * BLOCK] = slices[n][
+                :, pl.ds(pl.multiple_of(at * BLOCK, BLOCK), BLOCK)
+            ]
+    copies = []
+    for q in range(nh * nc):
+        total = mm(left[...], cots[q][...].reshape(ns * BLOCK, cols), NN)
         for n in range(ns * nc):
-            for k in range(ns):
-                at = jnp.where(mine >= k, mine - k, mine - k + ns)
-                left[n * LANES : (n + 1) * LANES, k * BLOCK : (k + 1) * BLOCK] = slices[n][
-                    :, pl.ds(pl.multiple_of(at * BLOCK, BLOCK), BLOCK)
-                ]
-
-    for q in range(nh * nc):
-
-        @pl.when(i == q)
-        def _():
-            total = mm(left[...], cots[q][...].reshape(ns * BLOCK, cols), NN)
-            for n in range(ns * nc):
-                at = pl.multiple_of(scalars[places + n] * LANES, LANES)
-                out_ref[pl.ds(at, LANES), :] = total[n * LANES : (n + 1) * LANES]
+            at = pl.multiple_of(scalars[places + n] * LANES, LANES)
+            buf[q, pl.ds(at, LANES), :] = total[n * LANES : (n + 1) * LANES]
+        at = pl.multiple_of(scalars[QUARTERS + q] * cols, LANES)
+        copy = pltpu.make_async_copy(buf.at[q], out_ref.at[:, pl.ds(at, cols)], sems.at[q])
+        copy.start()
+        copies.append(copy)
+    for copy in copies:
+        copy.wait()
 
 
 def call_weight(scalars, slices, cots, width, ns, nh, nc):
@@ -629,17 +645,14 @@
             jax.ShapeDtypeStruct((rows, width), F32),
             jax.ShapeDtypeStruct((SYM, LANES), F32),
         ],
-        grid_spec=pltpu.PrefetchScalarGridSpec(
-            num_scalar_prefetch=1,
-            grid=(nh * nc,),
-            in_specs=[whole(a.shape) for a in slices] + [whole(a.shape) for a in cots],
-            out_specs=[
-                pl.BlockSpec((rows, width // (nh * nc)), lambda i, s: (0, s[QUARTERS + i])),
-                whole((SYM, LANES)),
-            ],
-            scratch_shapes=[pltpu.VMEM((rows, length), BF16)],
-        ),
-        compiler_params=PARAMS,
+        in_specs=[SMEM] + [VMEM] * (len(slices) + len(cots)),
+        out_specs=[HBM, VMEM],
+        scratch_shapes=[
+            pltpu.VMEM((rows, length), BF16),
+            pltpu.VMEM((nh * nc, rows, width // (nh * nc)), F32),
+            pltpu.SemaphoreType.DMA((nh * nc,)),
+        ],
+        compiler_params=params(12),
         cost_estimate=pl.CostEstimate(
             flops=2 * rows * width * length, transcendentals=0, bytes_accessed=6 * rows * width
         ),
@@ -694,22 +707,16 @@
         ),
         out_shape=[jax.ShapeDtypeStruct(parts[0].shape, BF16)]
         + [jax.ShapeDtypeStruct(a, F32) for a in shapes],
-        grid_spec=pltpu.PrefetchScalarGridSpec(
-            num_scalar_prefetch=1,
-            grid=(1,),
-            in_specs=[whole(a.shape) for a in arrays] + [pl.BlockSpec(memory_space=pl.ANY)],
-            out_specs=[whole(parts[0].shape)] + [whole(a) for a in shapes],
-        ),
-        compiler_params=PARAMS,
+        in_specs=[SMEM] + [VMEM] * (len(arrays) + 1),
+        out_specs=[VMEM] * (len(shapes) + 1),
+        compiler_params=params(8),
         name="place_grads",
     )(scalars, *arrays, mark)
 
 
 def around(x, axis):
     n = lax.axis_size(axis)
-    return [x] + [
-        lax.ppermute(x, axis, [(i, (i + k) % n) for i in range(n)]) for k in range(1, n)
-    ]
+    return [x] + [lax.ppermute(x, axis, [(i, i ^ k) for i in range(n)]) for k in range(1, n)]
 
 
 def across(x, hops, nh, nc):
@@ -734,19 +741,21 @@
     slot = jnp.arange(nh * nc, dtype=jnp.int32)
     quarters = (h - slot // nc) % nh * nc + (c - slot % nc) % nc
     slot = jnp.arange(ns * nc, dtype=jnp.int32)
-    places = (c - slot // ns) % nc * ns + (s - slot % ns) % ns
+    places = (c - slot // ns) % nc * ns + jnp.bitwise_xor(s, slot % ns)
     scalars = jnp.concatenate([jnp.stack([c * ns + s, s, c]), quarters, places]).astype(jnp.int32)
     stacked = jnp.stack([a[:BLOCK] for a in pays], 0)
     heads = [stacked] + [across(stacked, (k, 0), nh, nc) for k in range(1, nh)]
     side = across(stacked, (0, 1), nh, nc)
-    gated = call_forward(scalars, pays, raw)
+    conv, vocab = conv_x.shape[0], xz_table.shape[0]
+    *tables, w, w2 = call_tables(scalars, raw)
+    gated, *kept = call_forward(scalars, pays, w, w2, tables[0], conv)
     heads, gated = lax.optimization_barrier((heads, gated))
     cots = [heads[0], side]
     for a in heads[1:]:
         cots += [a, across(a, (0, 1), nh, nc)]
     slices = around(gated, "seq")
-    grads = call_backward(scalars, pays, raw, cots, out_weight)
-    slices, grads = lax.optimization_barrier((slices, grads))
+    grads = call_backward(scalars, tables, cots, out_weight, kept, conv, vocab)
+    slices, _ = lax.optimization_barrier((slices, grads))
     slices = slices + [across(a, (0, 1), nh, nc) for a in slices]
     firsts = around(grads, "seq")
     shared = sum(a[:, 384:] for a in firsts)
@@ -1041,6 +1050,7 @@
             rows == BLOCK
             and nc == 2
             and ns > 1
+            and ns & (ns - 1) == 0
             and inner == ns * nc * LANES
             and inner == heads * (LANES // 2)
             and args[3].shape[2] == LANES

time: 64.4 us -> 52.4 us (0.81)
  Pallas kernels: 28.3 us -> 17.9 us
  other arithmetic: 3.13 us -> 1.57 us
  local copies, waits for them, and re-layouts: 4.15 us -> 5.56 us
  waiting for transfers between devices: 6.47 us -> 5.63 us
    pallas_call x1, Pallas kernels: 10.8 us -> 6.1 us  [call_backward(): pl.pallas_call(functools.partial(backward_kernel, ns=ns, nq=len(cots), co...]
    pallas_call x1, Pallas kernels: 3.32 us -> 0.9 us  [call_out(): pl.pallas_call(functools.partial(out_kernel, ns=ns, nh=nh, nc=nc), out_sh...]
    pallas_call x1, Pallas kernels: 5.67 us -> 3.32 us  [call_weight(): pl.pallas_call(functools.partial(weight_kernel, ns=ns, nh=nh, nc=nc), out...]
    unnamed x50 -> x24, local copies, waits for them, and re-layouts: 3.53 us -> 5.46 us
    ppermute x9, starting transfers between devices: 15.8 us -> 14.5 us  [around(): lax.ppermute(x, axis, [(i, i ^ k) for i in range(n)])]
    pallas_call x1, Pallas kernels: 2.54 us -> 1.33 us  [call_final(): pl.pallas_call(functools.partial(final_kernel, ns=ns, nq=len(shared) + 1,...]
    ppermute x11, starting transfers between devices: 5.02 us -> 6.06 us  [across(): return lax.ppermute(x, ('head', 'sub'), pairs)]
    another operation x1, other arithmetic: 0.9 us -> 0.04 us  [by_channel(): stacked = jnp.stack([a[:BLOCK] for a in pays], 0)]
  transfers between devices with their start and end apart: 20 -> 20, of which waited for: 5 -> 3; matrix products, arithmetic and copies ran while one was open for 3% -> 0% of each run, Pallas kernels for 35% -> 30%
where the time goes in v3:
time: 52.4 us; the launch traced here: 52.1 us
  starting transfers between devices  20.5 us (39%)
  Pallas kernels  17.9 us (34%)
  waiting for transfers between devices  5.63 us (11%)
  local copies, waits for them, and re-layouts  5.56 us (11%)
  other arithmetic  1.57 us (3%)
  between operations  0.83 us (2%)
    ppermute x9, starting transfers between devices, around(): lax.ppermute(x, axis, [(i, i ^ k) for i in range(n)])  14.5 us
    pallas_call x1, Pallas kernels, call_backward(): pl.pallas_call(functools.partial(backward_kernel, ns=ns, nq=len(cots), co...  6.1 us
    ppermute x11, starting transfers between devices, across(): return lax.ppermute(x, ('head', 'sub'), pairs)  6.06 us
    unnamed x24, local copies, waits for them, and re-layouts  5.46 us
    pallas_call x1, Pallas kernels, call_forward(): pl.pallas_call(functools.partial(forward_kernel, ns=ns, conv=conv), out_s...  4.87 us
    ppermute x9, waiting for transfers between devices, around(): lax.ppermute(x, axis, [(i, i ^ k) for i in range(n)])  4.71 us
    pallas_call x1, Pallas kernels, call_weight(): pl.pallas_call(functools.partial(weight_kernel, ns=ns, nh=nh, nc=nc), out...  3.32 us
    pallas_call x1, Pallas kernels, call_tables(): pl.pallas_call(functools.partial(tables_kernel, conv=conv, vocab=vocab),...  1.43 us
  transfers between devices with their start and end apart: 20, of which 3 were waited for; matrix products, arithmetic and copies ran while one was open for 0% of the time, Pallas kernels for 30%

profile of v3, /device:TPU:0, one launch (start us, length us, event | category | flops | bytes accessed | tf_op | source)
XLA Modules:
  0.0 52.1 jit_solution(12041569132200735885)
XLA Ops:
  0.6 0.7 %convert_bitcast_fusion = bf16[1,128]{1,0:T(2,128)(2,1)S(1)} fusion(s32[128]{0:T(128)} %param.11), kind=kLoop, calls=%fused_computation.45 | loop fusion | flops 128 | bytes 768 | tf_op jit(solution)/shard_map/reshape | solution.py:739
  1.3 0.8 %fusion.1.refs_0_ = bf16[144,256]{1,0:T(8,128)(2,1)S(1)} fusion(bf16[1,128]{1,0:T(2,128)(2,1)S(1)} %convert_bitcast_fusion, bf16[128,256]{1,0:T(8,128)(2,1)} %param.21), kind=kLoop, calls=%fused_computation.3 | loop fusion | flops 221184 | bytes 139520 | tf_op jit(solution)/shard_map/concatenate | solution.py:740
  2.1 3.0 %collective-permute-start = (bf16[144,256]{1,0:T(8,128)(2,1)S(1)}, bf16[144,256]{1,0:T(8,128)(2,1)S(1)}, u32[]{:S(2)}, u32[]{:S(2)}) collective-permute-start(bf16[144,256]{1,0:T(8,128)(2,1)S(1)} %fusion.1.refs_0_), channel_id=1, source_target_pairs={{0,4},{4,0},{8,12},{12,8},{1,5},{5,1},{9,13},{13,9},{2,6},{6,2},{1... | collective-permute-start | bytes 221192 | tf_op jit(solution)/shard_map/ppermute | solution.py:719
  5.2 2.6 %collective-permute-start.1 = (bf16[144,256]{1,0:T(8,128)(2,1)S(1)}, bf16[144,256]{1,0:T(8,128)(2,1)S(1)}, u32[]{:S(2)}, u32[]{:S(2)}) collective-permute-start(bf16[144,256]{1,0:T(8,128)(2,1)S(1)} %fusion.1.refs_0_), channel_id=1, source_target_pairs={{0,8},{4,12},{8,0},{12,4},{1,9},{5,13},{9,1},{13,5},{2,10},{6,14},... | collective-permute-start | bytes 221192 | tf_op jit(solution)/shard_map/ppermute | solution.py:719
  7.9 0.7 %copy-done.1 = bf16[5,2,1024]{2,1,0:T(2,128)(2,1)S(1)} copy-done((bf16[5,2,1024]{2,1,0:T(2,128)(2,1)S(1)}, bf16[5,2,1024]{2,1,0:T(2,128)(2,1)}, u32[]{:S(2)}) %copy-start.1) | copy-done | bytes 20504
  8.6 0.7 %copy-done.2 = bf16[4,1024]{1,0:T(4,128)(2,1)S(1)} copy-done((bf16[4,1024]{1,0:T(4,128)(2,1)S(1)}, bf16[4,1024]{1,0:T(4,128)(2,1)}, u32[]{:S(2)}) %copy-start.2) | copy-done | bytes 8216
  9.3 0.7 %copy-done.3 = f32[5,16]{1,0:T(8,128)S(1)} copy-done((f32[5,16]{1,0:T(8,128)S(1)}, f32[5,16]{1,0:T(8,128)}, u32[]{:S(2)}) %copy-start.3) | copy-done | bytes 344
  10.0 0.7 %copy-done.4 = bf16[5,2,128]{2,1,0:T(2,128)(2,1)S(1)} copy-done((bf16[5,2,128]{2,1,0:T(2,128)(2,1)S(1)}, bf16[5,2,128]{2,1,0:T(2,128)(2,1)}, u32[]{:S(2)}) %copy-start.4) | copy-done | bytes 2584
  10.7 0.7 %copy-done.5 = bf16[4,2,128]{2,1,0:T(2,128)(2,1)S(1)} copy-done((bf16[4,2,128]{2,1,0:T(2,128)(2,1)S(1)}, bf16[4,2,128]{2,1,0:T(2,128)(2,1)}, u32[]{:S(2)}) %copy-start.5) | copy-done | bytes 2072
  11.4 0.7 %copy-done.6 = s32[5]{0:T(128)S(1)} copy-done((s32[5]{0:T(128)S(1)}, s32[5]{0:T(128)}, u32[]{:S(2)}) %copy-start.6) | copy-done | bytes 44
  12.0 0.7 %copy-done.7 = f32[16]{0:T(128)S(1)} copy-done((f32[16]{0:T(128)S(1)}, f32[16]{0:T(128)}, u32[]{:S(2)}) %copy-start.7) | copy-done | bytes 88
  12.7 0.7 %copy-done.8 = f32[16]{0:T(128)S(1)} copy-done((f32[16]{0:T(128)S(1)}, f32[16]{0:T(128)}, u32[]{:S(2)}) %copy-start.8) | copy-done | bytes 88
  13.3 1.4 %tables.1 = (f32[32,128]{1,0:T(8,128)S(1)}, f32[16,256]{1,0:T(8,128)S(1)}, f32[8,128]{1,0:T(8,128)S(1)}, f32[8,128]{1,0:T(8,128)S(1)}, bf16[128,1792]{1,0:T(8,128)(2,1)S(1)}, /*index=5*/bf16[128,1792]{1,0:T(8,128)(2,1)S(1)}) custom-call(s32[15]{0:T(128)S(1)} %concatenate.9.scalars, s32[5]{0:T(128)S(1)} %copy-done.6, bf16[5,2,1024]{2,1,0:T(2,128)(2,1)S(1)} %copy-done.1, ...), custom_call_target="tpu_custom_call" | custom-call | flops 2000000000 | bytes 1000000 | tf_op jit(solution)/shard_map/tables/pallas_call | solution.py:527
  14.9 1.8 %collective-permute-start.3 = (bf16[4,128,256]{2,1,0:T(8,128)(2,1)S(1)}, bf16[4,128,256]{2,1,0:T(8,128)(2,1)S(1)}, u32[]{:S(2)}, u32[]{:S(2)}) collective-permute-start(bf16[4,128,256]{2,1,0:T(8,128)(2,1)S(1)} %pad_maximum_fusion.refs_4_.refs_8_), channel_id=1, source_target_pairs={{0,2},{1,3},{2,0},{3,1},{4,6},{5,7},{6,4},{7,5},{8,10},{9,11},{10,... | collective-permute-start | bytes 786440 | tf_op jit(solution)/shard_map/ppermute | solution.py:728
  16.7 4.9 %mix_forward.1 = (bf16[128,512]{1,0:T(8,128)(2,1)S(1)}, f32[8,512]{1,0:T(8,128)S(1)}, f32[8,512]{1,0:T(8,128)S(1)}, f32[8,512]{1,0:T(8,128)S(1)}, bf16[64,512]{1...) custom-call(s32[15]{0:T(128)S(1)} %concatenate.9.scalars, ...), custom_call_target="tpu_custom_call" | custom-call | flops 5000000000 | bytes 524288 | tf_op jit(solution)/shard_map/mix_forward/pallas_call | solution.py:547
  21.5 0.9 %collective-permute-done.3.refs_6_.refs_10_ = bf16[4,128,256]{2,1,0:T(8,128)(2,1)S(1)} collective-permute-done((bf16[4,128,256]{2,1,0:T(8,128)(2,1)S(1)}, bf16[4,128,256]{2,1,0:T(8,128)(2,1)S(1)}, u32[]{:S(2)}, u32[]{:S(2)}) %collective-permute-start.3) | collective-permute-done | bytes 262176 | tf_op jit(solution)/shard_map/ppermute | solution.py:728
  22.4 0.6 %collective-permute-start.12 = (bf16[128,512]{1,0:T(8,128)(2,1)S(1)}, bf16[128,512]{1,0:T(8,128)(2,1)S(1)}, u32[]{:S(2)}, u32[]{:S(2)}) collective-permute-start(bf16[128,512]{1,0:T(8,128)(2,1)S(1)} %get-tuple-element.61.refs_0_), channel_id=1, source_target_pairs={{0,4},{4,0},{8,12},{12,8},{1,5},{5,1},{9,13},{13,9},{2,6},{6,2},{1... | collective-permute-start | bytes 393224 | tf_op jit(solution)/shard_map/ppermute | solution.py:719
  23.1 3.5 %collective-permute-start.13 = (bf16[128,512]{1,0:T(8,128)(2,1)S(1)}, bf16[128,512]{1,0:T(8,128)(2,1)S(1)}, u32[]{:S(2)}, u32[]{:S(2)}) collective-permute-start(bf16[128,512]{1,0:T(8,128)(2,1)S(1)} %get-tuple-element.61.refs_0_), channel_id=1, source_target_pairs={{0,8},{4,12},{8,0},{12,4},{1,9},{5,13},{9,1},{13,5},{2,10},{6,14},... | collective-permute-start | bytes 393224 | tf_op jit(solution)/shard_map/ppermute | solution.py:719
  26.5 0.3 collective-permute-start.14
  26.8 6.1 %mix_backward.1.refs_0_ = f32[8,640]{1,0:T(8,128)S(1)} custom-call(s32[15]{0:T(128)S(1)} %concatenate.9.scalars, f32[32,128]{1,0:T(8,128)S(1)} %get-tuple-element.39.refs_6_.refs_0_, f32[16,256]{1,0:T(8,128)S(1)} %get-tuple-element.40.refs_1_, f32[8,128]{1,0:T(8,128)S(1)} %get-tuple-element.41.refs_2_, f32[8,128]{1,0:T(8,128)S(1)} %get-tuple-element.42.refs_3_, ...), custom_call_target="tpu_custom_call" | custom-call | flops 6000000000 | bytes 524288 | tf_op jit(solution)/shard_map/mix_backward/pallas_call | solution.py:564
  32.9 0.4 collective-permute-start.6
  33.3 3.8 %collective-permute-start.7 = (f32[8,640]{1,0:T(8,128)S(1)}, f32[8,640]{1,0:T(8,128)S(1)}, u32[]{:S(2)}, u32[]{:S(2)}) collective-permute-start(f32[8,640]{1,0:T(8,128)S(1)} %mix_backward.1.refs_0_), channel_id=1, source_target_pairs={{0,8},{4,12},{8,0},{12,4},{1,9},{5,13},{9,1},{13,5},{2,10},{6,14},... | collective-permute-start | bytes 61448 | tf_op jit(solution)/shard_map/ppermute | solution.py:719
  37.1 0.3 collective-permute-start.8
  37.4 0.5 collective-permute-start.16
  38.0 2.0 %collective-permute-done.7.refs_2_ = f32[8,640]{1,0:T(8,128)S(1)} collective-permute-done((f32[8,640]{1,0:T(8,128)S(1)}, f32[8,640]{1,0:T(8,128)S(1)}, u32[]{:S(2)}, u32[]{:S(2)}) %collective-permute-start.7) | collective-permute-done | bytes 20512 | tf_op jit(solution)/shard_map/ppermute | solution.py:719
  40.0 2.7 %collective-permute-done.8.refs_3_ = f32[8,640]{1,0:T(8,128)S(1)} collective-permute-done((f32[8,640]{1,0:T(8,128)S(1)}, f32[8,640]{1,0:T(8,128)S(1)}, u32[]{:S(2)}, u32[]{:S(2)}) %collective-permute-start.8) | collective-permute-done | bytes 20512 | tf_op jit(solution)/shard_map/ppermute | solution.py:719
  42.7 0.9 %layer_out.1 = (f32[128,256]{1,0:T(8,128)S(1)}, f32[128,256]{1,0:T(8,128)S(1)}) custom-call(s32[15]{0:T(128)S(1)} %concatenate.9.scalars, bf16[128,512]{1,0:T(8,128)(2,1)S(1)} %get-tuple-element.61.refs_0_, bf16[128,512]{1,0:T(8,128)(2,1)S(1)} %collective-permute-done.12.refs_1_, bf16[128,512]{1,0:T(8,128)(2,1)S(1)} %collective-permute-done.13.refs_2_, ...), custom_call_target="tpu_custom_call" | custom-call | tf_op jit(solution)/shard_map/layer_out/pallas_call | solution.py:602
  43.6 1.6 %collective-permute-start.19 = (f32[128,256]{1,0:T(8,128)S(1)}, f32[128,256]{1,0:T(8,128)S(1)}, u32[]{:S(2)}, u32[]{:S(2)}) collective-permute-start(f32[128,256]{1,0:T(8,128)S(1)} %get-tuple-element.66), channel_id=1, source_target_pairs={{0,2},{1,3},{2,0},{3,1},{4,6},{5,7},{6,4},{7,5},{8,10},{9,11},{10,... | collective-permute-start | bytes 393224 | tf_op jit(solution)/shard_map/ppermute | solution.py:728
  45.2 0.5 %collective-permute-start.10 = (f32[8,256]{1,0:T(8,128)S(1)}, f32[8,256]{1,0:T(8,128)S(1)}, u32[]{:S(2)}, u32[]{:S(2)}) collective-permute-start(f32[8,256]{1,0:T(8,128)S(1)} %get-tuple-element.74), channel_id=1, source_target_pairs={{0,2},{1,3},{2,0},{3,1},{4,6},{5,7},{6,4},{7,5},{8,10},{9,11},{10,... | collective-permute-start | bytes 24584 | tf_op jit(solution)/shard_map/ppermute | solution.py:728
  45.7 1.6 %collective-permute-start.9 = (f32[8,1792]{1,0:T(8,128)S(1)}, f32[8,1792]{1,0:T(8,128)S(1)}, u32[]{:S(2)}, u32[]{:S(2)}) collective-permute-start(f32[8,1792]{1,0:T(8,128)S(1)} %get-tuple-element.73), channel_id=1, source_target_pairs={{0,1},{1,0},{2,3},{3,2},{4,5},{5,4},{6,7},{7,6},{8,9},{9,8},{10,11... | collective-permute-start | bytes 172040 | tf_op jit(solution)/shard_map/ppermute | solution.py:728
  47.4 3.3 %weight_grad.1 = (f32[1024,1024]{1,0:T(8,128)}, f32[8,128]{1,0:T(8,128)S(1)}) custom-call(s32[15]{0:T(128)S(1)} %concatenate.9.scalars, bf16[128,512]{1,0:T(8,128)(2,1)S(1)} %get-tuple-element.61.refs_0_, bf16[128,512]{1,0:T(8,128)(2,1)S(1)} %collective-permute-done.12.refs_1_, bf16[128,512]{1,0:T(8,128)(2,1)S(1)} %collective-permute-done.13.refs_2_, ...), custom_call_target="tpu_custom_call" | custom-call | flops 1073741824 | bytes 6291456 | tf_op jit(solution)/shard_map/weight_grad/pallas_call | solution.py:642
  50.7 1.3 %place_grads.1 = (bf16[128,256]{1,0:T(8,128)(2,1)}, f32[5,2,1024]{2,1,0:T(2,128)}, f32[5,2,128]{2,1,0:T(2,128)}, f32[5,16]{1,0:T(8,128)}) custom-call(s32[15]{0:T(128)S(1)} %concatenate.9.scalars, f32[8,640]{1,0:T(8,128)S(1)} %mix_backward.1.refs_0_, f32[8,640]{1,0:T(8,128)S(1)} %collective-permute-done.6.refs_1_, ...), custom_call_target="tpu_custom_call" | custom-call | tf_op jit(solution)/shard_map/place_grads/pallas_call | solution.py:699
  (48 shorter events, 0.3 us)
Async XLA Ops:
  2.1 12.7 %collective-permute-start = (bf16[144,256]{1,0:T(8,128)(2,1)S(1)}, bf16[144,256]{1,0:T(8,128)(2,1)S(1)}, u32[]{:S(2)}, u32[]{:S(2)}) collective-permute-start(bf16[144,256]{1,0:T(8,128)(2,1)S(1)} %fusion.1.refs_0_), channel_id=1, source_target_pairs={{0,4},{4,0},{8,12},{12,8},{1,5},{5,1},{9,13},{13,9},{2,6},{6,2},{1... | collective-permute-start | bytes 221192 | tf_op jit(solution)/shard_map/ppermute | solution.py:719
  5.2 9.6 %collective-permute-start.1 = (bf16[144,256]{1,0:T(8,128)(2,1)S(1)}, bf16[144,256]{1,0:T(8,128)(2,1)S(1)}, u32[]{:S(2)}, u32[]{:S(2)}) collective-permute-start(bf16[144,256]{1,0:T(8,128)(2,1)S(1)} %fusion.1.refs_0_), channel_id=1, source_target_pairs={{0,8},{4,12},{8,0},{12,4},{1,9},{5,13},{9,1},{13,5},{2,10},{6,14},... | collective-permute-start | bytes 221192 | tf_op jit(solution)/shard_map/ppermute | solution.py:719
  7.7 7.0 %collective-permute-start.2 = (bf16[144,256]{1,0:T(8,128)(2,1)S(1)}, bf16[144,256]{1,0:T(8,128)(2,1)S(1)}, u32[]{:S(2)}, u32[]{:S(2)}) collective-permute-start(bf16[144,256]{1,0:T(8,128)(2,1)S(1)} %fusion.1.refs_0_), channel_id=1, source_target_pairs={{0,12},{4,8},{8,4},{12,0},{1,13},{5,9},{9,5},{13,1},{2,14},{6,10},... | collective-permute-start | bytes 221192 | tf_op jit(solution)/shard_map/ppermute | solution.py:719
  7.9 0.7 %copy-start.1 = (bf16[5,2,1024]{2,1,0:T(2,128)(2,1)S(1)}, bf16[5,2,1024]{2,1,0:T(2,128)(2,1)}, u32[]{:S(2)}) copy-start(bf16[5,2,1024]{2,1,0:T(2,128)(2,1)} %refs_1_.1) | copy-start | bytes 61444
  8.6 0.7 %copy-start.2 = (bf16[4,1024]{1,0:T(4,128)(2,1)S(1)}, bf16[4,1024]{1,0:T(4,128)(2,1)}, u32[]{:S(2)}) copy-start(bf16[4,1024]{1,0:T(4,128)(2,1)} %refs_3_.1) | copy-start | bytes 24580
  9.3 0.7 %copy-start.3 = (f32[5,16]{1,0:T(8,128)S(1)}, f32[5,16]{1,0:T(8,128)}, u32[]{:S(2)}) copy-start(f32[5,16]{1,0:T(8,128)} %refs_5_.1) | copy-start | bytes 964
  10.0 0.7 %copy-start.4 = (bf16[5,2,128]{2,1,0:T(2,128)(2,1)S(1)}, bf16[5,2,128]{2,1,0:T(2,128)(2,1)}, u32[]{:S(2)}) copy-start(bf16[5,2,128]{2,1,0:T(2,128)(2,1)} %refs_2_.1) | copy-start | bytes 7684
  10.7 0.7 %copy-start.5 = (bf16[4,2,128]{2,1,0:T(2,128)(2,1)S(1)}, bf16[4,2,128]{2,1,0:T(2,128)(2,1)}, u32[]{:S(2)}) copy-start(bf16[4,2,128]{2,1,0:T(2,128)(2,1)} %refs_4_.1) | copy-start | bytes 6148
  11.4 0.7 %copy-start.6 = (s32[5]{0:T(128)S(1)}, s32[5]{0:T(128)}, u32[]{:S(2)}) copy-start(s32[5]{0:T(128)} %refs_0_.1) | copy-start | bytes 64
  12.0 0.7 %copy-start.7 = (f32[16]{0:T(128)S(1)}, f32[16]{0:T(128)}, u32[]{:S(2)}) copy-start(f32[16]{0:T(128)} %refs_6_.1) | copy-start | bytes 196
  12.7 0.7 %copy-start.8 = (f32[16]{0:T(128)S(1)}, f32[16]{0:T(128)}, u32[]{:S(2)}) copy-start(f32[16]{0:T(128)} %refs_7_.1) | copy-start | bytes 196
  13.3 1.5 %copy-start.9 = (bf16[128,256]{1,0:T(8,128)(2,1)S(1)}, bf16[128,256]{1,0:T(8,128)(2,1)}, u32[]{:S(2)}) copy-start(bf16[128,256]{1,0:T(8,128)(2,1)} %param.21) | copy-start | bytes 196612
  14.9 7.6 %collective-permute-start.3 = (bf16[4,128,256]{2,1,0:T(8,128)(2,1)S(1)}, bf16[4,128,256]{2,1,0:T(8,128)(2,1)S(1)}, u32[]{:S(2)}, u32[]{:S(2)}) collective-permute-start(bf16[4,128,256]{2,1,0:T(8,128)(2,1)S(1)} %pad_maximum_fusion.refs_4_.refs_8_), channel_id=1, source_target_pairs={{0,2},{1,3},{2,0},{3,1},{4,6},{5,7},{6,4},{7,5},{8,10},{9,11},{10,... | collective-permute-start | bytes 786440 | tf_op jit(solution)/shard_map/ppermute | solution.py:728
  16.7 10.2 %collective-permute-start.4 = (bf16[4,128,256]{2,1,0:T(8,128)(2,1)S(1)}, bf16[4,128,256]{2,1,0:T(8,128)(2,1)S(1)}, u32[]{:S(2)}, u32[]{:S(2)}) collective-permute-start(bf16[4,128,256]{2,1,0:T(8,128)(2,1)S(1)} %pad_maximum_fusion.refs_4_.refs_8_), channel_id=1, source_target_pairs={{0,1},{1,0},{2,3},{3,2},{4,5},{5,4},{6,7},{7,6},{8,9},{9,8},{10,11... | collective-permute-start | bytes 786440 | tf_op jit(solution)/shard_map/ppermute | solution.py:728
  16.7 10.2 %copy-start = (bf16[1024,1024]{1,0:T(8,128)(2,1)S(1)}, bf16[1024,1024]{1,0:T(8,128)(2,1)}, u32[]{:S(2)}) copy-start(bf16[1024,1024]{1,0:T(8,128)(2,1)} %refs_8_.3) | copy-start | bytes 6291460
  22.4 4.4 %collective-permute-start.5 = (bf16[4,128,256]{2,1,0:T(8,128)(2,1)S(1)}, bf16[4,128,256]{2,1,0:T(8,128)(2,1)S(1)}, u32[]{:S(2)}, u32[]{:S(2)}) collective-permute-start(bf16[4,128,256]{2,1,0:T(8,128)(2,1)S(1)} %collective-permute-done.3.refs_6_.refs_10_), channel_id=1, source_target_pairs={{0,1},{1,0},{2,3},{3,2},{4,5},{5,4},{6,7},{7,6},{8,9},{9,8},{10,11... | collective-permute-start | bytes 786440 | tf_op jit(solution)/shard_map/ppermute | solution.py:728
  22.4 14.7 %collective-permute-start.12 = (bf16[128,512]{1,0:T(8,128)(2,1)S(1)}, bf16[128,512]{1,0:T(8,128)(2,1)S(1)}, u32[]{:S(2)}, u32[]{:S(2)}) collective-permute-start(bf16[128,512]{1,0:T(8,128)(2,1)S(1)} %get-tuple-element.61.refs_0_), channel_id=1, source_target_pairs={{0,4},{4,0},{8,12},{12,8},{1,5},{5,1},{9,13},{13,9},{2,6},{6,2},{1... | collective-permute-start | bytes 393224 | tf_op jit(solution)/shard_map/ppermute | solution.py:719
  23.1 14.3 %collective-permute-start.13 = (bf16[128,512]{1,0:T(8,128)(2,1)S(1)}, bf16[128,512]{1,0:T(8,128)(2,1)S(1)}, u32[]{:S(2)}, u32[]{:S(2)}) collective-permute-start(bf16[128,512]{1,0:T(8,128)(2,1)S(1)} %get-tuple-element.61.refs_0_), channel_id=1, source_target_pairs={{0,8},{4,12},{8,0},{12,4},{1,9},{5,13},{9,1},{13,5},{2,10},{6,14},... | collective-permute-start | bytes 393224 | tf_op jit(solution)/shard_map/ppermute | solution.py:719
  26.5 10.9 %collective-permute-start.14 = (bf16[128,512]{1,0:T(8,128)(2,1)S(1)}, bf16[128,512]{1,0:T(8,128)(2,1)S(1)}, u32[]{:S(2)}, u32[]{:S(2)}) collective-permute-start(bf16[128,512]{1,0:T(8,128)(2,1)S(1)} %get-tuple-element.61.refs_0_), channel_id=1, source_target_pairs={{0,12},{4,8},{8,4},{12,0},{1,13},{5,9},{9,5},{13,1},{2,14},{6,10},... | collective-permute-start | bytes 393224 | tf_op jit(solution)/shard_map/ppermute | solution.py:719
  32.9 5.0 %collective-permute-start.6 = (f32[8,640]{1,0:T(8,128)S(1)}, f32[8,640]{1,0:T(8,128)S(1)}, u32[]{:S(2)}, u32[]{:S(2)}) collective-permute-start(f32[8,640]{1,0:T(8,128)S(1)} %mix_backward.1.refs_0_), channel_id=1, source_target_pairs={{0,4},{4,0},{8,12},{12,8},{1,5},{5,1},{9,13},{13,9},{2,6},{6,2},{1... | collective-permute-start | bytes 61448 | tf_op jit(solution)/shard_map/ppermute | solution.py:719
  33.3 6.7 %collective-permute-start.7 = (f32[8,640]{1,0:T(8,128)S(1)}, f32[8,640]{1,0:T(8,128)S(1)}, u32[]{:S(2)}, u32[]{:S(2)}) collective-permute-start(f32[8,640]{1,0:T(8,128)S(1)} %mix_backward.1.refs_0_), channel_id=1, source_target_pairs={{0,8},{4,12},{8,0},{12,4},{1,9},{5,13},{9,1},{13,5},{2,10},{6,14},... | collective-permute-start | bytes 61448 | tf_op jit(solution)/shard_map/ppermute | solution.py:719
  37.1 5.6 %collective-permute-start.8 = (f32[8,640]{1,0:T(8,128)S(1)}, f32[8,640]{1,0:T(8,128)S(1)}, u32[]{:S(2)}, u32[]{:S(2)}) collective-permute-start(f32[8,640]{1,0:T(8,128)S(1)} %mix_backward.1.refs_0_), channel_id=1, source_target_pairs={{0,12},{4,8},{8,4},{12,0},{1,13},{5,9},{9,5},{13,1},{2,14},{6,10},... | collective-permute-start | bytes 61448 | tf_op jit(solution)/shard_map/ppermute | solution.py:719
  37.4 5.3 %collective-permute-start.15 = (bf16[128,512]{1,0:T(8,128)(2,1)S(1)}, bf16[128,512]{1,0:T(8,128)(2,1)S(1)}, u32[]{:S(2)}, u32[]{:S(2)}) collective-permute-start(bf16[128,512]{1,0:T(8,128)(2,1)S(1)} %get-tuple-element.61.refs_0_), channel_id=1, source_target_pairs={{0,1},{1,0},{2,3},{3,2},{4,5},{5,4},{6,7},{7,6},{8,9},{9,8},{10,11... | collective-permute-start | bytes 393224 | tf_op jit(solution)/shard_map/ppermute | solution.py:728
  37.4 5.3 %collective-permute-start.16 = (bf16[128,512]{1,0:T(8,128)(2,1)S(1)}, bf16[128,512]{1,0:T(8,128)(2,1)S(1)}, u32[]{:S(2)}, u32[]{:S(2)}) collective-permute-start(bf16[128,512]{1,0:T(8,128)(2,1)S(1)} %collective-permute-done.12.refs_1_), channel_id=1, source_target_pairs={{0,1},{1,0},{2,3},{3,2},{4,5},{5,4},{6,7},{7,6},{8,9},{9,8},{10,11... | collective-permute-start | bytes 393224 | tf_op jit(solution)/shard_map/ppermute | solution.py:728
  37.9 4.8 %collective-permute-start.17 = (bf16[128,512]{1,0:T(8,128)(2,1)S(1)}, bf16[128,512]{1,0:T(8,128)(2,1)S(1)}, u32[]{:S(2)}, u32[]{:S(2)}) collective-permute-start(bf16[128,512]{1,0:T(8,128)(2,1)S(1)} %collective-permute-done.13.refs_2_), channel_id=1, source_target_pairs={{0,1},{1,0},{2,3},{3,2},{4,5},{5,4},{6,7},{7,6},{8,9},{9,8},{10,11... | collective-permute-start | bytes 393224 | tf_op jit(solution)/shard_map/ppermute | solution.py:728
  40.0 2.7 %collective-permute-start.18 = (bf16[128,512]{1,0:T(8,128)(2,1)S(1)}, bf16[128,512]{1,0:T(8,128)(2,1)S(1)}, u32[]{:S(2)}, u32[]{:S(2)}) collective-permute-start(bf16[128,512]{1,0:T(8,128)(2,1)S(1)} %collective-permute-done.14.refs_3_), channel_id=1, source_target_pairs={{0,1},{1,0},{2,3},{3,2},{4,5},{5,4},{6,7},{7,6},{8,9},{9,8},{10,11... | collective-permute-start | bytes 393224 | tf_op jit(solution)/shard_map/ppermute | solution.py:728
  43.6 7.1 %collective-permute-start.19 = (f32[128,256]{1,0:T(8,128)S(1)}, f32[128,256]{1,0:T(8,128)S(1)}, u32[]{:S(2)}, u32[]{:S(2)}) collective-permute-start(f32[128,256]{1,0:T(8,128)S(1)} %get-tuple-element.66), channel_id=1, source_target_pairs={{0,2},{1,3},{2,0},{3,1},{4,6},{5,7},{6,4},{7,5},{8,10},{9,11},{10,... | collective-permute-start | bytes 393224 | tf_op jit(solution)/shard_map/ppermute | solution.py:728
  45.2 5.5 %collective-permute-start.10 = (f32[8,256]{1,0:T(8,128)S(1)}, f32[8,256]{1,0:T(8,128)S(1)}, u32[]{:S(2)}, u32[]{:S(2)}) collective-permute-start(f32[8,256]{1,0:T(8,128)S(1)} %get-tuple-element.74), channel_id=1, source_target_pairs={{0,2},{1,3},{2,0},{3,1},{4,6},{5,7},{6,4},{7,5},{8,10},{9,11},{10,... | collective-permute-start | bytes 24584 | tf_op jit(solution)/shard_map/ppermute | solution.py:728
  45.7 5.0 %collective-permute-start.11 = (f32[8,256]{1,0:T(8,128)S(1)}, f32[8,256]{1,0:T(8,128)S(1)}, u32[]{:S(2)}, u32[]{:S(2)}) collective-permute-start(f32[8,256]{1,0:T(8,128)S(1)} %get-tuple-element.74), channel_id=1, source_target_pairs={{0,3},{1,2},{2,1},{3,0},{4,7},{5,6},{6,5},{7,4},{8,11},{9,10},{10,... | collective-permute-start | bytes 24584 | tf_op jit(solution)/shard_map/ppermute | solution.py:728
  45.7 5.0 %collective-permute-start.9 = (f32[8,1792]{1,0:T(8,128)S(1)}, f32[8,1792]{1,0:T(8,128)S(1)}, u32[]{:S(2)}, u32[]{:S(2)}) collective-permute-start(f32[8,1792]{1,0:T(8,128)S(1)} %get-tuple-element.73), channel_id=1, source_target_pairs={{0,1},{1,0},{2,3},{3,2},{4,5},{5,4},{6,7},{7,6},{8,9},{9,8},{10,11... | collective-permute-start | bytes 172040 | tf_op jit(solution)/shard_map/ppermute | solution.py:728

commit v4 on v3

--- a/solution.py
+++ b/solution.py
@@ -12,11 +12,12 @@
 SYM = 8
 F32 = jnp.float32
 BF16 = jnp.bfloat16
+GROUP = 2
+GROUP_BACK = 4
 NN = (((1,), (0,)), ((), ()))
 NT = (((1,), (1,)), ((), ()))
 TN = (((0,), (0,)), ((), ()))
 X_ROW, Z_ROW, DT_ROW, MISC_ROW, TAB_ROWS = 0, 8, 16, 24, 32
-RAW = 8
 XF, XB, ZZ, BCF, BCB, WIDE = 0, 128, 256, 384, 640, 896
 
 
@@ -66,39 +67,34 @@
 
 
 def gather_tables(j, raw, tabs_ref, bcp_ref, conv, vocab):
-    xz_ref, bc_ref, conv_ref, conv_bc_ref, dt_ref, a_log_ref, skip_ref = raw
+    wide_ref, bc_ref, dt_ref = raw
     lanes = pl.ds(pl.multiple_of(j * LANES, LANES), LANES)
     head0 = lax.broadcasted_iota(jnp.int32, (1, LANES), 1) < 64
     pair = lambda a, b: jnp.where(head0, a, b)
     tabs_ref[...] = jnp.zeros_like(tabs_ref)
     bcp_ref[...] = jnp.zeros_like(bcp_ref)
     for k in range(vocab):
-        tabs_ref[X_ROW + k : X_ROW + k + 1, :] = xz_ref[k, 0:1, lanes].astype(F32)
-        tabs_ref[Z_ROW + k : Z_ROW + k + 1, :] = xz_ref[k, 1:2, lanes].astype(F32)
+        tabs_ref[X_ROW + k : X_ROW + k + 1, :] = wide_ref[2 * k : 2 * k + 1, lanes].astype(F32)
+        tabs_ref[Z_ROW + k : Z_ROW + k + 1, :] = wide_ref[2 * k + 1 : 2 * k + 2, lanes].astype(F32)
         tabs_ref[DT_ROW + k : DT_ROW + k + 1, :] = pair(dt_ref[k, 2 * j], dt_ref[k, 2 * j + 1])
         for i in range(2):
             bcp_ref[k : k + 1, i * 128 : i * 128 + 128] = bc_ref[k, i : i + 1, :].astype(F32)
     for k in range(conv):
-        tabs_ref[MISC_ROW + k : MISC_ROW + k + 1, :] = conv_ref[k : k + 1, lanes].astype(F32)
+        tabs_ref[MISC_ROW + k : MISC_ROW + k + 1, :] = wide_ref[2 * vocab + k : 2 * vocab + k + 1, lanes].astype(F32)
         for i in range(2):
-            bcp_ref[SYM + k : SYM + k + 1, i * 128 : i * 128 + 128] = conv_bc_ref[
-                k, i : i + 1, :
+            bcp_ref[SYM + k : SYM + k + 1, i * 128 : i * 128 + 128] = bc_ref[
+                vocab + k, i : i + 1, :
             ].astype(F32)
     at = MISC_ROW + 4
-    tabs_ref[at : at + 1, :] = pair(a_log_ref[2 * j], a_log_ref[2 * j + 1])
-    tabs_ref[at + 1 : at + 2, :] = pair(skip_ref[2 * j], skip_ref[2 * j + 1])
-
-
-def tables_kernel(scalars, *refs, conv, vocab):
-    tabs_ref, bcp_ref, dt1_ref, perm_ref, w_ref, w2_out, wf, w2 = refs[RAW : RAW + 8]
-    local, sems = refs[RAW + 8 : 2 * RAW + 8], refs[2 * RAW + 8]
-    copies = [pltpu.make_async_copy(refs[k], local[k], sems.at[k]) for k in range(RAW)]
-    for copy in copies:
-        copy.start()
-    for copy in copies:
-        copy.wait()
-    basemap = local[0]
-    gather_tables(scalars[0], local[1:], tabs_ref, bcp_ref, conv, vocab)
+    tabs_ref[at : at + 1, :] = pair(dt_ref[vocab, 2 * j], dt_ref[vocab, 2 * j + 1])
+    tabs_ref[at + 1 : at + 2, :] = pair(
+        dt_ref[vocab + 1, 2 * j], dt_ref[vocab + 1, 2 * j + 1]
+    )
+
+
+def tables_kernel(scalars, basemap, *refs, conv, vocab):
+    tabs_ref, bcp_ref, dt1_ref, perm_ref, w_ref, w2_out, rate_ref, wf, w2 = refs[3:]
+    gather_tables(scalars[0], refs[:3], tabs_ref, bcp_ref, conv, vocab)
     row = lax.broadcasted_iota(jnp.int32, perm_ref.shape, 0)
     lane = lax.broadcasted_iota(jnp.int32, perm_ref.shape, 1)
     perm = jnp.zeros(perm_ref.shape, F32)
@@ -128,15 +124,16 @@
             wf[hi : hi + SYM, base + BCB : base + BCB + 256] = bct * cbc
         dt = jnp.maximum(dtt, 0.0) + jnp.log1p(jnp.exp(-jnp.abs(dtt)))
         ld = -jnp.exp(tabs_ref[MISC_ROW + 4 : MISC_ROW + 5, :]) * dt
-        ld0 = jnp.broadcast_to(ld[:, 0:1], ld.shape)
-        ld1 = jnp.broadcast_to(ld[:, 64:65], ld.shape)
-        for i, t in enumerate((ld, ld0, ld1)):
-            for k, piece in enumerate(thirds(t)):
-                c = st * 384 + i * 128
-                w2[SYM * k : SYM * (k + 1), c : c + 128] = piece
-                w2[32 + SYM * k : 32 + SYM * (k + 1), 768 + c : 768 + c + 128] = piece
+        for k, piece in enumerate(thirds(ld)):
+            w2[SYM * k : SYM * (k + 1), st * 128 : st * 128 + 128] = piece
+            w2[32 + SYM * k : 32 + SYM * (k + 1), 256 + st * 128 : 384 + st * 128] = piece
+            for h in range(2):
+                at = 24 * (st * 2 + h) + SYM * k
+                rate_ref[at : at + SYM, :] = jnp.broadcast_to(
+                    piece[:, 64 * h : 64 * h + 1], piece.shape
+                )
         for k, piece in enumerate(thirds(dt)):
-            c = 1536 + st * 128
+            c = 512 + st * 128
             w2[64 + SYM * k : 64 + SYM * (k + 1), c : c + 128] = piece
     top, rest = halves(wf[...])
     w_ref[0:64, :] = top
@@ -165,6 +162,10 @@
         inside = jnp.logical_and(lane + d >= 0, lane + d < length)
         r.rows[SYM * (d + conv - 1) : SYM * (d + conv), :] = jnp.where(inside, shifted, 0.0)
     r.rows[64:128, :] = r.rows[0:64, :]
+    one = lax.broadcasted_iota(jnp.int32, (SYM, length), 0) < 3
+    r.rows[152:160, :] = one.astype(F32)
+    r.rows[184:192, :] = one.astype(F32)
+    r.prow[...] = jnp.zeros_like(r.prow)
     oh_b = oh.astype(BF16)
     for b in range(ns):
         cols = slice(b * BLOCK, (b + 1) * BLOCK)
@@ -177,13 +178,14 @@
             r.rows[160 + SYM * k : 160 + SYM * (k + 1), cols] = exc
             r.rows[192 + SYM * k : 192 + SYM * (k + 1), cols] = oh[:, cols]
     r.sym[...] = r.rows[0:64, :].astype(BF16)
-    turned = jnp.transpose(r.rows[...]).astype(BF16)
+    turned = jnp.transpose(r.rows[...].astype(BF16))
     r.pre[...] = mm(turned[:, 0:128], w_ref[...], NN)
     w2 = w2_ref[...]
-    r.pd[...] = mm(turned[:, 128:256], w2, NN)
+    r.pd[...] = mm(turned[:, 128:256], w2[:, 0:768], NN)
+    r.count[...] = turned[:, 128:192]
     for st in range(2):
         for part, row0 in ((0, 0), (1, 32)):
-            c = part * 768 + st * 384
+            c = part * 256 + st * 128
             flat = mm(
                 w2[row0 : row0 + 32, c : c + 128],
                 r.rows[128 + row0 : 160 + row0, :].astype(BF16),
@@ -191,7 +193,11 @@
             )
             for h in range(2):
                 i = part * 4 + st * 2 + h
-                r.prow[i : i + 1, :] = flat[64 * h : 64 * h + 1, :]
+                row = flat[64 * h : 64 * h + 1, :]
+                if part == 0:
+                    row = -row
+                for k, piece in enumerate(thirds(row)):
+                    r.prow[SYM * i + k : SYM * i + k + 1, :] = piece
 
 
 class Unit:
@@ -199,9 +205,9 @@
         self.rows = rows = slice(b * BLOCK, (b + 1) * BLOCK)
         base = st * WIDE
         self.skip = tabs_ref[MISC_ROW + 5 : MISC_ROW + 6, :]
-        self.dt = r.pd[rows, 1536 + st * 128 : 1536 + st * 128 + 128]
-        self.p = r.pd[rows, st * 384 : st * 384 + 128]
-        self.q = r.pd[rows, 768 + st * 384 : 768 + st * 384 + 128]
+        self.dt = r.pd[rows, 512 + st * 128 : 512 + st * 128 + 128]
+        self.p = r.pd[rows, st * 128 : st * 128 + 128]
+        self.q = r.pd[rows, 256 + st * 128 : 256 + st * 128 + 128]
         self.total = self.p[BLOCK - 1 : BLOCK, :]
         self.r, self.st, self.b, self.base = r, st, b, base
         lane = lax.broadcasted_iota(jnp.int32, (BLOCK, LANES), 1)
@@ -223,12 +229,15 @@
 
     def decay(self, h):
         r, st = self.r, self.st
-        c = st * 384 + 128 * (h + 1)
-        pc = r.pd[self.rows, c : c + 128]
-        qc = r.pd[self.rows, 768 + c : 768 + c + 128]
-        pr = r.prow[st * 2 + h : st * 2 + h + 1, self.rows]
-        qr = r.prow[4 + st * 2 + h : 4 + st * 2 + h + 1, self.rows]
-        return jnp.exp(jnp.where(self.low, pc - pr, qr - qc))
+        i = st * 2 + h
+        rate = r.rate[24 * i : 24 * i + 24, :]
+        ends = r.prow[SYM * i : SYM * (i + 1), self.rows]
+        starts = r.prow[SYM * (4 + i) : SYM * (5 + i), self.rows]
+        zero = jnp.zeros((32, LANES), F32)
+        below = jnp.concatenate([rate, ends, zero], 0)
+        above = jnp.concatenate([zero, -rate, starts], 0)
+        gap = mm(r.count[self.rows, :], jnp.concatenate([below, above], 1).astype(BF16), NN)
+        return jnp.exp(jnp.where(self.low, gap[:, 0:LANES], gap[:, LANES : 2 * LANES]))
 
 
 def state_pass_fwd(r, tabs_ref, nb, units):
@@ -253,6 +262,12 @@
             r.s[st * 2 + 1, b] += jnp.exp(units[st][b + 1].total) * r.s[st * 2 + 1, b + 1]
 
 
+def together(bodies):
+    bodies = list(bodies)
+    while bodies:
+        bodies = [b for b in bodies if next(b, True) is None]
+
+
 class Names:
     pass
 
@@ -275,7 +290,7 @@
         ((SYM, length), F32),
         ((64, length), BF16),
         ((length, 2 * WIDE), F32),
-        ((length, 1792), F32),
+        ((length, 768), F32),
         ((length, 512), F32),
         ((length, 1024), F32),
         ((4, nb, LANES, LANES), F32),
@@ -286,39 +301,53 @@
 
 
 def forward_kernel(scalars, *refs, ns, conv):
-    tok_refs, (w_ref, w2_ref, tabs_ref, out_ref) = refs[:ns], refs[ns : ns + 4]
-    r = named(refs[ns + 4 :], KEPT + ("rows", "prow"))
+    tok_refs, (w_ref, w2_ref, rate_ref, tabs_ref, out_ref) = refs[:ns], refs[ns : ns + 5]
+    r = named(refs[ns + 5 :], KEPT + ("rows", "prow", "count"))
+    r.rate = rate_ref
     prepare(scalars, tok_refs, w_ref, w2_ref, r, conv)
     units = [[Unit(r, tabs_ref, st, b, ns) for b in range(ns)] for st in range(2)]
     state_pass_fwd(r, tabs_ref, ns, units)
-    for b in range(ns):
-        gated = []
-        for st in range(2):
-            u = units[st][b]
-            xf = r.x[u.rows, st * 256 : st * 256 + 128]
-            xb = r.x[u.rows, st * 256 + 128 : st * 256 + 256]
-            decays = (u.decay(0), u.decay(1))
+    gated = {}
+
+    def body(st, b):
+        u = units[st][b]
+        x = [r.x[u.rows, st * 256 + w * 128 : st * 256 + w * 128 + 128] for w in range(2)]
+        decays = (u.decay(0), u.decay(1))
+        yield
+        masks, lefts, cms = (u.low, u.upp), [], []
+        for w in range(2):
+            c = st * 512 + w * 256
+            bm, cm = r.bc[u.rows, c : c + 128], r.bc[u.rows, c + 128 : c + 256]
+            lefts.append(mm_fine(cm, bm, NT, 3))
+            cms.append(cm)
+        yield
+        y = u.skip * (x[0] + x[1])
+        for w in range(2):
+            if (w == 0 and b > 0) or (w == 1 and b < ns - 1):
+                enter = jnp.exp(u.p) if w == 0 else jnp.exp(u.total - u.q)
+                carried = enter * mm_fine(cms[w], r.s[st * 2 + w, b], NN, 2)
+                r.ys[u.rows, st * 512 + w * 256 + 128 : st * 512 + w * 256 + 256] = carried
+                y = y + carried
+        yield
+        for h in range(2):
+            r.dec[(st * ns + b) * 2 + h] = decays[h]
+        for w in range(2):
+            g = jnp.where(masks[w], lefts[w], 0.0)
+            lefts[w] = [(g * d).astype(BF16) for d in decays]
             for h in range(2):
-                r.dec[(st * ns + b) * 2 + h] = decays[h]
-            y = u.skip * (xf + xb)
-            for way, x, mask in ((0, xf, u.low), (1, xb, u.upp)):
-                c = st * 512 + way * 256
-                bm, cm = r.bc[u.rows, c : c + 128], r.bc[u.rows, c + 128 : c + 256]
-                g = jnp.where(mask, mm_fine(cm, bm, NT, 3), 0.0)
-                left = [(g * d).astype(BF16) for d in decays]
-                for h in range(2):
-                    r.wts[((st * ns + b) * 2 + way) * 2 + h] = left[h]
-                right = u.by_head((u.dt * x).astype(BF16))
-                inner = mm(jnp.concatenate(left, 1), jnp.concatenate(right, 0), NN)
-                r.ys[u.rows, c : c + 128] = inner
-                y = y + inner
-                if (way == 0 and b > 0) or (way == 1 and b < ns - 1):
-                    enter = jnp.exp(u.p) if way == 0 else jnp.exp(u.total - u.q)
-                    carried = enter * mm_fine(cm, r.s[st * 2 + way, b], NN, 2)
-                    r.ys[u.rows, c + 128 : c + 256] = carried
-                    y = y + carried
-            gated.append(y * u.act(ZZ, 128))
-        out_ref[:, units[0][b].rows] = jnp.transpose(gated[0] + gated[1]).astype(BF16)
+                r.wts[((st * ns + b) * 2 + w) * 2 + h] = lefts[w][h]
+        yield
+        for w in range(2):
+            right = u.by_head((u.dt * x[w]).astype(BF16))
+            inner = mm(jnp.concatenate(lefts[w], 1), jnp.concatenate(right, 0), NN)
+            r.ys[u.rows, st * 512 + w * 256 : st * 512 + w * 256 + 128] = inner
+            y = y + inner
+        gated[st, b] = y * u.act(ZZ, 128)
+
+    for b0 in range(0, ns, GROUP):
+        together(body(st, b) for b in range(b0, min(b0 + GROUP, ns)) for st in range(2))
+        for b in range(b0, min(b0 + GROUP, ns)):
+            out_ref[:, units[0][b].rows] = jnp.transpose(gated[0, b] + gated[1, b]).astype(BF16)
 
 
 def backward_kernel(scalars, *refs, ns, nq, conv, vocab):
@@ -356,124 +385,133 @@
             r.ds[st * 2, b] += jnp.exp(units[st][b + 1].total) * r.ds[st * 2, b + 1]
         for b in range(2, ns):
             r.ds[st * 2 + 1, b] += jnp.exp(units[st][b - 1].total) * r.ds[st * 2 + 1, b - 1]
-    d_steps, d_decays = [], []
-    for st in range(2):
-        d_step = jnp.zeros((SYM, LANES), F32)
-        d_decay = jnp.zeros((SYM, LANES), F32)
-        for b in range(ns):
-            u = units[st][b]
-            base = st * WIDE
-            x = [r.x[u.rows, st * 256 + w * 128 : st * 256 + w * 128 + 128] for w in range(2)]
-            dgv = r.dg[u.rows, :]
-            pz = u.pre(ZZ, 128)
-            sz = sigmoid(pz)
-            dy = dgv * (pz * sz)
-            dyr = dy.astype(BF16)
-            dyw = dyr.astype(F32)
-            dy0, dy1 = u.by_head(dyr)
-            decays = [r.dec[(st * ns + b) * 2 + h] for h in range(2)]
-            inputs = [u.dt * v for v in x]
-            ur = [v.astype(BF16) for v in inputs]
-            uw = [v.astype(F32) for v in ur]
-            uh = [u.by_head(v) for v in ur]
-            d_pair = mm(dyr, jnp.concatenate([uh[0][0], uh[0][1], uh[1][0], uh[1][1]], 0), NT)
-            masks = (u.low, u.upp)
-            ends = (jnp.exp(u.total - u.p), jnp.exp(u.q))
-            enters = (jnp.exp(u.p), jnp.exp(u.total - u.q))
-            weights, bms, cms = [], [], []
-            for w in range(2):
-                c = st * 512 + w * 256
-                bm, cm = r.bc[u.rows, c : c + 128], r.bc[u.rows, c + 128 : c + 256]
-                weights.append([r.wts[((st * ns + b) * 2 + w) * 2 + h] for h in range(2)])
-                bms.append(bm)
-                cms.append(cm)
-            du_both = mm(
-                jnp.concatenate(
-                    [
-                        jnp.concatenate([weights[0][0], weights[1][0]], 1),
-                        jnp.concatenate([weights[0][1], weights[1][1]], 1),
-                    ],
-                    0,
-                ),
-                jnp.concatenate([dy0, dy1], 0),
-                TN,
-            )
-            y = u.skip * (x[0] + x[1])
-            mixes, step_part, flat = [], 0.0, 0.0
-            for w in range(2):
-                c = st * 512 + w * 256
-                inner = r.ys[u.rows, c : c + 128]
-                du_in = du_both[w * BLOCK : (w + 1) * BLOCK]
-                has_enter = (w == 0 and b > 0) or (w == 1 and b < ns - 1)
-                has_leave = (w == 0 and b < ns - 1) or (w == 1 and b > 0)
-                y = y + inner
-                row = dyw * inner - uw[w] * du_in
-                du = du_in
-                d_g = jnp.where(
-                    masks[w],
-                    d_pair[:, w * 256 : w * 256 + 128] * decays[0]
-                    + d_pair[:, w * 256 + 128 : w * 256 + 256] * decays[1],
-                    0.0,
+    d_steps = [jnp.zeros((SYM, LANES), F32)] * 2
+    d_decays = [jnp.zeros((SYM, LANES), F32)] * 2
+    d_tab = 0.0
+
+    def body(st, b):
+        u = units[st][b]
+        base = st * WIDE
+        x = [r.x[u.rows, st * 256 + w * 128 : st * 256 + w * 128 + 128] for w in range(2)]
+        dgv = r.dg[u.rows, :]
+        pz = u.pre(ZZ, 128)
+        sz = sigmoid(pz)
+        dy = dgv * (pz * sz)
+        dyr = dy.astype(BF16)
+        dyw = dyr.astype(F32)
+        dy0, dy1 = u.by_head(dyr)
+        decays = [r.dec[(st * ns + b) * 2 + h] for h in range(2)]
+        inputs = [u.dt * v for v in x]
+        ur = [v.astype(BF16) for v in inputs]
+        uw = [v.astype(F32) for v in ur]
+        uh = [u.by_head(v) for v in ur]
+        d_pair = mm(dyr, jnp.concatenate([uh[0][0], uh[0][1], uh[1][0], uh[1][1]], 0), NT)
+        yield
+        masks = (u.low, u.upp)
+        ends = (jnp.exp(u.total - u.p), jnp.exp(u.q))
+        enters = (jnp.exp(u.p), jnp.exp(u.total - u.q))
+        weights, bms, cms = [], [], []
+        for w in range(2):
+            c = st * 512 + w * 256
+            bm, cm = r.bc[u.rows, c : c + 128], r.bc[u.rows, c + 128 : c + 256]
+            weights.append([r.wts[((st * ns + b) * 2 + w) * 2 + h] for h in range(2)])
+            bms.append(bm)
+            cms.append(cm)
+        du_both = mm(
+            jnp.concatenate(
+                [
+                    jnp.concatenate([weights[0][0], weights[1][0]], 1),
+                    jnp.concatenate([weights[0][1], weights[1][1]], 1),
+                ],
+                0,
+            ),
+            jnp.concatenate([dy0, dy1], 0),
+            TN,
+        )
+        yield
+        y = u.skip * (x[0] + x[1])
+        mixes, step_part, flat = [], 0.0, 0.0
+        for w in range(2):
+            yield
+            c = st * 512 + w * 256
+            inner = r.ys[u.rows, c : c + 128]
+            du_in = du_both[w * BLOCK : (w + 1) * BLOCK]
+            has_enter = (w == 0 and b > 0) or (w == 1 and b < ns - 1)
+            has_leave = (w == 0 and b < ns - 1) or (w == 1 and b > 0)
+            y = y + inner
+            row = dyw * inner - uw[w] * du_in
+            du = du_in
+            d_g = jnp.where(
+                masks[w],
+                d_pair[:, w * 256 : w * 256 + 128] * decays[0]
+                + d_pair[:, w * 256 + 128 : w * 256 + 256] * decays[1],
+                0.0,
+            ).astype(BF16)
+            d_c = mm(d_g, bms[w].astype(BF16), NN)
+            d_b = mm(d_g, cms[w].astype(BF16), TN)
+            enter_part = gain_part = None
+            if has_enter:
+                state = r.s[st * 2 + w, b]
+                carried = r.ys[u.rows, c + 128 : c + 256]
+                y = y + carried
+                enter_part = dy * carried
+                d_c = d_c + mm((enters[w] * dy).astype(BF16), state.astype(BF16), NT)
+            if has_leave:
+                d_state = r.ds[st * 2 + w, b]
+                d_gain = mm_fine(bms[w], d_state, NN, 2)
+                du = du + ends[w] * d_gain
+                gain = ends[w] * inputs[w]
+                gain_part = gain * d_gain
+                d_b = d_b + mm(gain.astype(BF16), d_state.astype(BF16), NT)
+            if has_enter and has_leave:
+                flat = flat + jnp.exp(u.total) * jnp.sum(state * d_state, 0, keepdims=True)
+            if w == 1:
+                row = -row
+            if enter_part is not None:
+                row = row + enter_part if w == 0 else row - enter_part
+            if gain_part is not None:
+                row = row - gain_part if w == 0 else row + gain_part
+            if w == 0 and gain_part is not None:
+                flat = flat + jnp.sum(gain_part, 0, keepdims=True)
+            if w == 1 and enter_part is not None:
+                flat = flat + jnp.sum(enter_part, 0, keepdims=True)
+            mixes.append(row)
+            step_part = step_part + du * x[w]
+            dx = du * u.dt + dy * u.skip
+            px = u.pre((XF, XB)[w], 128)
+            sx = sigmoid(px)
+            col = base + (XF, XB)[w]
+            r.dpre[u.rows, col : col + 128] = (dx * (sx * (1.0 + px * (1.0 - sx)))).astype(BF16)
+            col = (BCF, BCB)[w]
+            for i, grad in enumerate((d_b, d_c)):
+                pb = u.pre(col + 128 * i, 128)
+                sb = sigmoid(pb)
+                at = base + col + 128 * i
+                r.dpre[u.rows, at : at + 128] = (
+                    grad * (sb * (1.0 + pb * (1.0 - sb)))
                 ).astype(BF16)
-                d_c = mm(d_g, bms[w].astype(BF16), NN)
-                d_b = mm(d_g, cms[w].astype(BF16), TN)
-                enter_part = gain_part = None
-                if has_enter:
-                    state = r.s[st * 2 + w, b]
-                    carried = r.ys[u.rows, c + 128 : c + 256]
-                    y = y + carried
-                    enter_part = dy * carried
-                    d_c = d_c + mm((enters[w] * dy).astype(BF16), state.astype(BF16), NT)
-                if has_leave:
-                    d_state = r.ds[st * 2 + w, b]
-                    d_gain = mm_fine(bms[w], d_state, NN, 2)
-                    du = du + ends[w] * d_gain
-                    gain = ends[w] * inputs[w]
-                    gain_part = gain * d_gain
-                    d_b = d_b + mm(gain.astype(BF16), d_state.astype(BF16), NT)
-                if has_enter and has_leave:
-                    flat = flat + jnp.exp(u.total) * jnp.sum(state * d_state, 0, keepdims=True)
-                if w == 1:
-                    row = -row
-                if enter_part is not None:
-                    row = row + enter_part if w == 0 else row - enter_part
-                if gain_part is not None:
-                    row = row - gain_part if w == 0 else row + gain_part
-                if w == 0 and gain_part is not None:
-                    flat = flat + jnp.sum(gain_part, 0, keepdims=True)
-                if w == 1 and enter_part is not None:
-                    flat = flat + jnp.sum(enter_part, 0, keepdims=True)
-                mixes.append(row)
-                step_part = step_part + du * x[w]
-                dx = du * u.dt + dy * u.skip
-                px = u.pre((XF, XB)[w], 128)
-                sx = sigmoid(px)
-                col = base + (XF, XB)[w]
-                r.dpre[u.rows, col : col + 128] = (dx * (sx * (1.0 + px * (1.0 - sx)))).astype(BF16)
-                col = (BCF, BCB)[w]
-                for i, grad in enumerate((d_b, d_c)):
-                    pb = u.pre(col + 128 * i, 128)
-                    sb = sigmoid(pb)
-                    at = base + col + 128 * i
-                    r.dpre[u.rows, at : at + 128] = (
-                        grad * (sb * (1.0 + pb * (1.0 - sb)))
-                    ).astype(BF16)
-            d_z = dgv * y * (sz * (1.0 + pz * (1.0 - sz)))
-            r.dpre[u.rows, base + ZZ : base + ZZ + 128] = d_z.astype(BF16)
-            inc = r.inc[:, u.rows]
-            exc = r.exc[:, u.rows]
-            inc_b, exc_b, oh_b = inc.astype(BF16), exc.astype(BF16), r.oh[:, u.rows].astype(BF16)
-            right = list(halves(mixes[0])) + list(halves(mixes[1]))
-            d_decay = d_decay + mm(
-                jnp.concatenate([inc_b, inc_b, exc_b, exc_b], 1), jnp.concatenate(right, 0), NN
-            )
-            d_decay = d_decay + inc[:, BLOCK - 1 : BLOCK] * flat
-            d_step = d_step + mm(
-                jnp.concatenate([oh_b, oh_b], 1), jnp.concatenate(halves(step_part), 0), NN
-            )
-        d_steps.append(d_step)
-        d_decays.append(d_decay)
-    d_tab = mm(r.sym[...], r.dpre[...], NN)
+        yield
+        d_z = dgv * y * (sz * (1.0 + pz * (1.0 - sz)))
+        r.dpre[u.rows, base + ZZ : base + ZZ + 128] = d_z.astype(BF16)
+        inc = r.inc[:, u.rows]
+        exc = r.exc[:, u.rows]
+        inc_b, exc_b, oh_b = inc.astype(BF16), exc.astype(BF16), r.oh[:, u.rows].astype(BF16)
+        right = list(halves(mixes[0])) + list(halves(mixes[1]))
+        decay_part = mm(
+            jnp.concatenate([inc_b, inc_b, exc_b, exc_b], 1), jnp.concatenate(right, 0), NN
+        )
+        decay_part = decay_part + inc[:, BLOCK - 1 : BLOCK] * flat
+        step_sum = mm(
+            jnp.concatenate([oh_b, oh_b], 1), jnp.concatenate(halves(step_part), 0), NN
+        )
+        d_steps[st] = d_steps[st] + step_sum
+        d_decays[st] = d_decays[st] + decay_part
+
+    for b0 in range(0, ns, GROUP_BACK):
+        last = min(b0 + GROUP_BACK, ns)
+        together(body(st, b) for b in range(b0, last) for st in range(2))
+        span = slice(b0 * BLOCK, last * BLOCK)
+        d_tab = d_tab + mm(r.sym[:, span], r.dpre[span, :], NN)
     mid = SYM * (conv - 1)
     result = None
     for st in range(2):
@@ -515,47 +553,55 @@
 
 
 def call_tables(scalars, raw):
-    conv, vocab = raw[3].shape[0], raw[1].shape[0]
+    basemap, xz_table, bc_table, conv_x, conv_bc, dt_table, a_log, skip_gain = raw
+    conv, vocab = conv_x.shape[0], xz_table.shape[0]
     outs = [
         ((TAB_ROWS, LANES), F32),
         ((2 * SYM, 256), F32),
         ((SYM, LANES), F32),
         ((SYM, LANES), F32),
         ((128, 2 * WIDE), BF16),
-        ((128, 1792), BF16),
+        ((128, 768), BF16),
+        ((96, LANES), F32),
     ]
     return pl.pallas_call(
         functools.partial(tables_kernel, conv=conv, vocab=vocab),
         out_shape=[jax.ShapeDtypeStruct(*a) for a in outs],
-        in_specs=[SMEM] + [pl.BlockSpec(memory_space=pltpu.HBM)] * RAW,
+        in_specs=[SMEM, SMEM, VMEM, VMEM, SMEM],
         out_specs=[VMEM] * len(outs),
-        scratch_shapes=[pltpu.VMEM((64, 2 * WIDE), F32), pltpu.VMEM((128, 1792), F32)]
-        + [pltpu.SMEM(raw[0].shape, raw[0].dtype)]
-        + [pltpu.VMEM(a.shape, a.dtype) for a in raw[1:5]]
-        + [pltpu.SMEM(a.shape, a.dtype) for a in raw[5:]]
-        + [pltpu.SemaphoreType.DMA((RAW,))],
+        scratch_shapes=[pltpu.VMEM((64, 2 * WIDE), F32), pltpu.VMEM((128, 768), F32)],
         compiler_params=params(8),
         cost_estimate=pl.CostEstimate(flops=2 * 10**9, transcendentals=0, bytes_accessed=10**6),
         name="tables",
-    )(scalars, *raw)
-
-
-def call_forward(scalars, pays, w, w2, tabs, conv):
+    )(
+        scalars,
+        basemap,
+        jnp.concatenate([xz_table.reshape(2 * vocab, -1), conv_x], 0),
+        jnp.concatenate([bc_table, conv_bc], 0),
+        jnp.concatenate([dt_table, a_log[None], skip_gain[None]], 0),
+    )
+
+
+def call_forward(scalars, pays, w, w2, rate, tabs, conv):
     ns = len(pays)
     length = ns * BLOCK
     outs = [((LANES, length), BF16)] + kept_shapes(length)
     return pl.pallas_call(
         functools.partial(forward_kernel, ns=ns, conv=conv),
         out_shape=[jax.ShapeDtypeStruct(*a) for a in outs],
-        in_specs=[SMEM] + [VMEM] * (ns + 3),
+        in_specs=[SMEM] + [VMEM] * (ns + 4),
         out_specs=[VMEM] * len(outs),
-        scratch_shapes=[pltpu.VMEM((256, length), F32), pltpu.VMEM((SYM, length), F32)],
+        scratch_shapes=[
+            pltpu.VMEM((256, length), F32),
+            pltpu.VMEM((64, length), F32),
+            pltpu.VMEM((length, 64), BF16),
+        ],
         compiler_params=params(8),
         cost_estimate=pl.CostEstimate(
             flops=5 * 10**9, transcendentals=0, bytes_accessed=8 * LANES * length
         ),
         name="mix_forward",
-    )(scalars, *pays, w, w2, tabs)
+    )(scalars, *pays, w, w2, rate, tabs)
 
 
 def call_backward(scalars, tables, cots, out_weight, kept, conv, vocab):
@@ -609,13 +655,13 @@
     )(scalars, *slices, out_weight)
 
 
-def weight_kernel(scalars, *refs, ns, nh, nc):
+def weight_kernel(scalars, *refs, ns, nh, nc, vocab):
     slices, cots = refs[: ns * nc], refs[ns * nc : ns * nc + nh * nc]
-    out_ref, mark_ref, left, buf, sems = refs[ns * nc + nh * nc :]
+    packs = refs[ns * nc + nh * nc : ns * nc + nh * nc + ns]
+    out_ref, xz_ref, bc_ref, dt_ref, left, buf, sems = refs[ns * nc + nh * nc + ns :]
     mine = scalars[1]
     places = QUARTERS + nh * nc
     cols = cots[0].shape[2]
-    mark_ref[...] = jnp.zeros_like(mark_ref)
     for n in range(ns * nc):
         for k in range(ns):
             at = jnp.bitwise_xor(mine, k)
@@ -632,21 +678,40 @@
         copy = pltpu.make_async_copy(buf.at[q], out_ref.at[:, pl.ds(at, cols)], sems.at[q])
         copy.start()
         copies.append(copy)
+    d_bc = packs[0][:, 768:1024]
+    for a in packs[1:]:
+        d_bc = d_bc + a[:, 768:1024]
+    for i in range(2):
+        for k in range(vocab):
+            bc_ref[k, i : i + 1, :] = d_bc[k : k + 1, i * 128 : i * 128 + 128]
+    lane = lax.broadcasted_iota(jnp.int32, (SYM, dt_ref.shape[1]), 1)
+    d_dt = jnp.zeros((SYM, dt_ref.shape[1]), F32)
+    for n in range(2 * ns):
+        j = scalars[places + n]
+        piece = packs[n % ns][:, n // ns * 384 : n // ns * 384 + 384]
+        for i in range(2):
+            for k in range(vocab):
+                xz_ref[k, i : i + 1, pl.ds(pl.multiple_of(j * LANES, LANES), LANES)] = piece[
+                    k : k + 1, i * 128 : i * 128 + 128
+                ]
+            row = jnp.sum(piece[:, 256 + 64 * i : 320 + 64 * i], 1, keepdims=True)
+            d_dt = jnp.where(lane == 2 * j + i, row, d_dt)
+    dt_ref[...] = d_dt[:vocab]
     for copy in copies:
         copy.wait()
 
 
-def call_weight(scalars, slices, cots, width, ns, nh, nc):
+def call_weight(scalars, slices, cots, packs, raw, width, ns, nh, nc):
     length = slices[0].shape[1]
     rows = ns * nc * LANES
     return pl.pallas_call(
-        functools.partial(weight_kernel, ns=ns, nh=nh, nc=nc),
+        functools.partial(weight_kernel, ns=ns, nh=nh, nc=nc, vocab=raw[1].shape[0]),
         out_shape=[
-            jax.ShapeDtypeStruct((rows, width), F32),
-            jax.ShapeDtypeStruct((SYM, LANES), F32),
+            jax.ShapeDtypeStruct(a, F32)
+            for a in ((rows, width), raw[1].shape, raw[2].shape, raw[5].shape)
         ],
-        in_specs=[SMEM] + [VMEM] * (len(slices) + len(cots)),
-        out_specs=[HBM, VMEM],
+        in_specs=[SMEM] + [VMEM] * (len(slices) + len(cots) + len(packs)),
+        out_specs=[HBM] + [VMEM] * 3,
         scratch_shapes=[
             pltpu.VMEM((rows, length), BF16),
             pltpu.VMEM((nh * nc, rows, width // (nh * nc)), F32),
@@ -657,61 +722,7 @@
             flops=2 * rows * width * length, transcendentals=0, bytes_accessed=6 * rows * width
         ),
         name="weight_grad",
-    )(scalars, *slices, *cots)
-
-
-def final_kernel(scalars, *refs, ns, nq, nh, vocab, places):
-    firsts, packed, shared = refs[:ns], refs[ns], refs[ns + 1 : ns + nq]
-    parts = refs[ns + nq : ns + nq + nh]
-    out_ref, xz_ref, bc_ref, dt_ref = refs[ns + nq + nh + 1 :]
-    total = parts[0][...]
-    for a in parts[1:]:
-        total = total + a[...]
-    out_ref[...] = total.astype(BF16)
-    d_bc = packed[:, ns * 384 : ns * 384 + 256]
-    for a in list(firsts) + list(shared):
-        d_bc = d_bc + a[:, a.shape[1] - 256 :]
-    for i in range(2):
-        for k in range(vocab):
-            bc_ref[k, i : i + 1, :] = d_bc[k : k + 1, i * 128 : i * 128 + 128]
-    lane = lax.broadcasted_iota(jnp.int32, (SYM, dt_ref.shape[1]), 1)
-    d_dt = jnp.zeros((SYM, dt_ref.shape[1]), F32)
-    for n in range(2 * ns):
-        j = scalars[places + n]
-        if n < ns:
-            piece = firsts[n][:, 0:384]
-        else:
-            piece = packed[:, (n - ns) * 384 : (n - ns + 1) * 384]
-        for i in range(2):
-            for k in range(vocab):
-                xz_ref[k, i : i + 1, pl.ds(pl.multiple_of(j * LANES, LANES), LANES)] = piece[
-                    k : k + 1, i * 128 : i * 128 + 128
-                ]
-            row = jnp.sum(piece[:, 256 + 64 * i : 320 + 64 * i], 1, keepdims=True)
-            d_dt = jnp.where(lane == 2 * j + i, row, d_dt)
-    dt_ref[...] = d_dt[:vocab]
-
-
-def call_final(scalars, firsts, packed, shared, parts, mark, raw, places):
-    ns = len(firsts)
-    shapes = [raw[1].shape, raw[2].shape, raw[5].shape]
-    arrays = list(firsts) + [packed] + list(shared) + list(parts)
-    return pl.pallas_call(
-        functools.partial(
-            final_kernel,
-            ns=ns,
-            nq=len(shared) + 1,
-            nh=len(parts),
-            vocab=raw[1].shape[0],
-            places=places,
-        ),
-        out_shape=[jax.ShapeDtypeStruct(parts[0].shape, BF16)]
-        + [jax.ShapeDtypeStruct(a, F32) for a in shapes],
-        in_specs=[SMEM] + [VMEM] * (len(arrays) + 1),
-        out_specs=[VMEM] * (len(shapes) + 1),
-        compiler_params=params(8),
-        name="place_grads",
-    )(scalars, *arrays, mark)
+    )(scalars, *slices, *cots, *packs)
 
 
 def around(x, axis):
@@ -747,8 +758,8 @@
     heads = [stacked] + [across(stacked, (k, 0), nh, nc) for k in range(1, nh)]
     side = across(stacked, (0, 1), nh, nc)
     conv, vocab = conv_x.shape[0], xz_table.shape[0]
-    *tables, w, w2 = call_tables(scalars, raw)
-    gated, *kept = call_forward(scalars, pays, w, w2, tables[0], conv)
+    *tables, w, w2, rate = call_tables(scalars, raw)
+    gated, *kept = call_forward(scalars, pays, w, w2, rate, tables[0], conv)
     heads, gated = lax.optimization_barrier((heads, gated))
     cots = [heads[0], side]
     for a in heads[1:]:
@@ -757,15 +768,20 @@
     grads = call_backward(scalars, tables, cots, out_weight, kept, conv, vocab)
     slices, _ = lax.optimization_barrier((slices, grads))
     slices = slices + [across(a, (0, 1), nh, nc) for a in slices]
-    firsts = around(grads, "seq")
-    shared = sum(a[:, 384:] for a in firsts)
-    packed = across(jnp.concatenate([a[:, :384] for a in firsts] + [shared], 1), (0, 1), nh, nc)
-    far = [across(shared, (a, b), nh, nc) for a in range(1, nh) for b in range(nc)]
+    shared = grads[:, 384:]
+    beside = across(grads, (0, 1), nh, nc)
+    for a in range(1, nh):
+        for b in range(nc):
+            shared = shared + across(grads[:, 384:], (a, b), nh, nc)
+    packed = jnp.concatenate([grads[:, :384], beside[:, :384], shared + beside[:, 384:]], 1)
+    packs = around(packed, "seq")
     parts = call_out(scalars, slices, out_weight, ns, nh, nc)
-    parts = [parts[0]] + [across(parts[k], (nh - k, 0), nh, nc) for k in range(1, nh)]
-    d_out_weight, mark = call_weight(scalars, slices, cots, width, ns, nh, nc)
-    layer_out, d_xz, d_bc, d_dt = call_final(
-        scalars, firsts, packed, far, parts, mark, raw, QUARTERS + nh * nc
+    total = parts[0]
+    for k in range(1, nh):
+        total = total + across(parts[k], (nh - k, 0), nh, nc)
+    layer_out = total.astype(BF16)
+    d_out_weight, d_xz, d_bc, d_dt = call_weight(
+        scalars, slices, cots, packs, raw, width, ns, nh, nc
     )
     return (layer_out, d_out_weight, d_xz, d_bc, d_dt)
 

time: 52.4 us -> 50.7 us (0.968)
  local copies, waits for them, and re-layouts: 5.56 us -> 1.52 us
  Pallas kernels: 17.9 us -> 14.5 us
  other arithmetic: 1.57 us -> 4.37 us
  waiting for transfers between devices: 5.63 us -> 7.41 us
  starting transfers between devices: 20.5 us -> 21.8 us
    unnamed x24 -> x6, local copies, waits for them, and re-layouts: 5.46 us -> 0.67 us
    concatenate x1 -> x4, other arithmetic: 0.01 us -> 2.15 us  [the longest x1 0.73 us: call_tables(): jnp.concatenate([dt_table, a_log[None], skip_gain[None]], 0)]
    ppermute x9, waiting for transfers between devices: 4.71 us -> 6.04 us  [around(): lax.ppermute(x, axis, [(i, i ^ k) for i in range(n)])]
    pallas_call x1, Pallas kernels: 4.87 us -> 3.53 us  [call_forward(): pl.pallas_call(functools.partial(forward_kernel, ns=ns, conv=conv), out_s...]
    ppermute x9, starting transfers between devices: 14.5 us -> 15.7 us  [around(): lax.ppermute(x, axis, [(i, i ^ k) for i in range(n)])]
    pallas_call x1, Pallas kernels: 6.1 us -> 5.29 us  [call_backward(): pl.pallas_call(functools.partial(backward_kernel, ns=ns, nq=len(cots), co...]
    reshape x0 -> x1, local copies, waits for them, and re-layouts: none -> 0.74 us  [call_tables(): xz_table.reshape(2 * vocab, -1)]
    pallas_call x2 -> x1, Pallas kernels: 4.65 us -> 3.94 us  [call_weight(): pl.pallas_call(functools.partial(weight_kernel, ns=ns, nh=nh, nc=nc, voca...]
  transfers between devices with their start and end apart: 20 -> 20, of which waited for: 3 -> 4; matrix products, arithmetic and copies ran while one was open for 0% -> 6% of each run, Pallas kernels for 30% -> 29%
where the time goes in v4:
time: 50.7 us; the launch traced here: 50.3 us
  starting transfers between devices  21.8 us (43%)
  Pallas kernels  14.5 us (29%)
  waiting for transfers between devices  7.41 us (15%)
  other arithmetic  4.37 us (9%)
  local copies, waits for them, and re-layouts  1.52 us (3%)
  between operations  0.78 us (2%)
    ppermute x9, starting transfers between devices, around(): lax.ppermute(x, axis, [(i, i ^ k) for i in range(n)])  15.7 us
    ppermute x11, starting transfers between devices, across(): return lax.ppermute(x, ('head', 'sub'), pairs)  6.06 us
    ppermute x9, waiting for transfers between devices, around(): lax.ppermute(x, axis, [(i, i ^ k) for i in range(n)])  6.04 us
    pallas_call x1, Pallas kernels, call_backward(): pl.pallas_call(functools.partial(backward_kernel, ns=ns, nq=len(cots), co...  5.29 us
    pallas_call x1, Pallas kernels, call_weight(): pl.pallas_call(functools.partial(weight_kernel, ns=ns, nh=nh, nc=nc, voca...  3.94 us
    pallas_call x1, Pallas kernels, call_forward(): pl.pallas_call(functools.partial(forward_kernel, ns=ns, conv=conv), out_s...  3.53 us
    ppermute x11, waiting for transfers between devices, across(): return lax.ppermute(x, ('head', 'sub'), pairs)  1.36 us
  transfers between devices with their start and end apart: 20, of which 4 were waited for; matrix products, arithmetic and copies ran while one was open for 6% of the time, Pallas kernels for 29%

profile of v4, /device:TPU:0, one launch (start us, length us, event | category | flops | bytes accessed | tf_op | source)
XLA Modules:
  0.0 50.3 jit_solution(5437256405083571515)
XLA Ops:
  0.6 0.7 %convert_bitcast_fusion = bf16[1,128]{1,0:T(2,128)(2,1)S(1)} fusion(s32[128]{0:T(128)} %param.11), kind=kLoop, calls=%fused_computation.43 | loop fusion | flops 128 | bytes 768 | tf_op jit(solution)/shard_map/reshape | solution.py:750
  1.3 0.8 %fusion.1.refs_0_ = bf16[144,256]{1,0:T(8,128)(2,1)S(1)} fusion(bf16[1,128]{1,0:T(2,128)(2,1)S(1)} %convert_bitcast_fusion, bf16[128,256]{1,0:T(8,128)(2,1)} %param.21), kind=kLoop, calls=%fused_computation.4 | loop fusion | flops 221184 | bytes 139520 | tf_op jit(solution)/shard_map/concatenate | solution.py:751
  2.1 3.0 %collective-permute-start = (bf16[144,256]{1,0:T(8,128)(2,1)S(1)}, bf16[144,256]{1,0:T(8,128)(2,1)S(1)}, u32[]{:S(2)}, u32[]{:S(2)}) collective-permute-start(bf16[144,256]{1,0:T(8,128)(2,1)S(1)} %fusion.1.refs_0_), channel_id=1, source_target_pairs={{0,4},{4,0},{8,12},{12,8},{1,5},{5,1},{9,13},{13,9},{2,6},{6,2},{1... | collective-permute-start | bytes 221192 | tf_op jit(solution)/shard_map/ppermute | solution.py:730
  5.2 2.6 %collective-permute-start.1 = (bf16[144,256]{1,0:T(8,128)(2,1)S(1)}, bf16[144,256]{1,0:T(8,128)(2,1)S(1)}, u32[]{:S(2)}, u32[]{:S(2)}) collective-permute-start(bf16[144,256]{1,0:T(8,128)(2,1)S(1)} %fusion.1.refs_0_), channel_id=1, source_target_pairs={{0,8},{4,12},{8,0},{12,4},{1,9},{5,13},{9,1},{13,5},{2,10},{6,14},... | collective-permute-start | bytes 221192 | tf_op jit(solution)/shard_map/ppermute | solution.py:730
  7.8 0.7 %reshape.17 = bf16[10,1024]{1,0:T(8,128)(2,1)S(1)} reshape(bf16[5,2,1024]{2,1,0:T(2,128)(2,1)} %param.13) | data formatting | bytes 40960 | tf_op jit(solution)/shard_map/reshape | solution.py:579
  8.5 0.7 %pad_maximum_fusion.1.refs_0_ = bf16[14,1024]{1,0:T(8,128)(2,1)S(1)} fusion(bf16[4,1024]{1,0:T(4,128)(2,1)} %param.16, bf16[10,1024]{1,0:T(8,128)(2,1)S(1)} %reshape.17), kind=kLoop, calls=%fused_computation.8 | loop fusion | flops 57344 | bytes 57344 | tf_op jit(solution)/shard_map/concatenate | solution.py:579
  9.2 0.7 %pad_maximum_fusion.3.refs_1_ = bf16[9,2,128]{2,1,0:T(2,128)(2,1)S(1)} fusion(bf16[4,2,128]{2,1,0:T(2,128)(2,1)} %param.17, bf16[5,2,128]{2,1,0:T(2,128)(2,1)} %param.14), kind=kLoop, calls=%fused_computation.11 | loop fusion | flops 2304 | bytes 9216 | tf_op jit(solution)/shard_map/concatenate | solution.py:580
  10.0 0.7 %pad_maximum_fusion.4.refs_2_ = f32[7,16]{1,0:T(8,128)S(1)} fusion(f32[1,16]{1,0:T(1,128)} %bitcast.15, f32[1,16]{1,0:T(1,128)} %bitcast.16, f32[5,16]{1,0:T(8,128)} %param.15), kind=kLoop, calls=%fused_computation.12 | loop fusion | flops 224 | bytes 896 | tf_op jit(solution)/shard_map/concatenate | solution.py:581
  10.7 0.1 concatenate.18.scalars
  10.8 0.7 %copy-done.1 = s32[5]{0:T(128)S(1)} copy-done((s32[5]{0:T(128)S(1)}, s32[5]{0:T(128)}, u32[]{:S(2)}) %copy-start.1) | copy-done | bytes 44
  11.4 0.8 %tables.1 = (f32[32,128]{1,0:T(8,128)S(1)}, f32[16,256]{1,0:T(8,128)S(1)}, f32[8,128]{1,0:T(8,128)S(1)}, f32[8,128]{1,0:T(8,128)S(1)}, bf16[128,1792]{1,0:T(8,12...) custom-call(s32[15]{0:T(128)S(1)} %concatenate.18.scalars, s32[5]{0:T(128)S(1)} %copy-done.1, ...), custom_call_target="tpu_custom_call" | custom-call | flops 2000000000 | bytes 1000000 | tf_op jit(solution)/shard_map/tables/pallas_call | solution.py:567
  12.2 1.8 %collective-permute-done.2.refs_3_ = bf16[144,256]{1,0:T(8,128)(2,1)S(1)} collective-permute-done((bf16[144,256]{1,0:T(8,128)(2,1)S(1)}, bf16[144,256]{1,0:T(8,128)(2,1)S(1)}, u32[]{:S(2)}, u32[]{:S(2)}) %collective-permute-start.2) | collective-permute-done | bytes 73760 | tf_op jit(solution)/shard_map/ppermute | solution.py:730
  14.1 1.6 %collective-permute-start.3 = (bf16[4,128,256]{2,1,0:T(8,128)(2,1)S(1)}, bf16[4,128,256]{2,1,0:T(8,128)(2,1)S(1)}, u32[]{:S(2)}, u32[]{:S(2)}) collective-permute-start(bf16[4,128,256]{2,1,0:T(8,128)(2,1)S(1)} %pad_maximum_fusion.refs_4_.refs_8_), channel_id=1, source_target_pairs={{0,2},{1,3},{2,0},{3,1},{4,6},{5,7},{6,4},{7,5},{8,10},{9,11},{10,... | collective-permute-start | bytes 786440 | tf_op jit(solution)/shard_map/ppermute | solution.py:739
  15.7 3.5 %mix_forward.1 = (bf16[128,512]{1,0:T(8,128)(2,1)S(1)}, f32[8,512]{1,0:T(8,128)S(1)}, f32[8,512]{1,0:T(8,128)S(1)}, f32[8,512]{1,0:T(8,128)S(1)}, bf16[64,512]{1...) custom-call(s32[15]{0:T(128)S(1)} %concatenate.18.scalars, ...), custom_call_target="tpu_custom_call" | custom-call | flops 5000000000 | bytes 524288 | tf_op jit(solution)/shard_map/mix_forward/pallas_call | solution.py:589
  19.2 1.3 %collective-permute-done.3.refs_6_.refs_10_ = bf16[4,128,256]{2,1,0:T(8,128)(2,1)S(1)} collective-permute-done((bf16[4,128,256]{2,1,0:T(8,128)(2,1)S(1)}, bf16[4,128,256]{2,1,0:T(8,128)(2,1)S(1)}, u32[]{:S(2)}, u32[]{:S(2)}) %collective-permute-start.3) | collective-permute-done | bytes 262176 | tf_op jit(solution)/shard_map/ppermute | solution.py:739
  20.6 1.1 %collective-permute-start.4 = (bf16[128,512]{1,0:T(8,128)(2,1)S(1)}, bf16[128,512]{1,0:T(8,128)(2,1)S(1)}, u32[]{:S(2)}, u32[]{:S(2)}) collective-permute-start(bf16[128,512]{1,0:T(8,128)(2,1)S(1)} %get-tuple-element.61.refs_0_), channel_id=1, source_target_pairs={{0,4},{4,0},{8,12},{12,8},{1,5},{5,1},{9,13},{13,9},{2,6},{6,2},{1... | collective-permute-start | bytes 393224 | tf_op jit(solution)/shard_map/ppermute | solution.py:730
  21.6 2.4 %collective-permute-start.5 = (bf16[128,512]{1,0:T(8,128)(2,1)S(1)}, bf16[128,512]{1,0:T(8,128)(2,1)S(1)}, u32[]{:S(2)}, u32[]{:S(2)}) collective-permute-start(bf16[128,512]{1,0:T(8,128)(2,1)S(1)} %get-tuple-element.61.refs_0_), channel_id=1, source_target_pairs={{0,8},{4,12},{8,0},{12,4},{1,9},{5,13},{9,1},{13,5},{2,10},{6,14},... | collective-permute-start | bytes 393224 | tf_op jit(solution)/shard_map/ppermute | solution.py:730
  24.0 0.9 %collective-permute-start.6 = (bf16[128,512]{1,0:T(8,128)(2,1)S(1)}, bf16[128,512]{1,0:T(8,128)(2,1)S(1)}, u32[]{:S(2)}, u32[]{:S(2)}) collective-permute-start(bf16[128,512]{1,0:T(8,128)(2,1)S(1)} %get-tuple-element.61.refs_0_), channel_id=1, source_target_pairs={{0,12},{4,8},{8,4},{12,0},{1,13},{5,9},{9,5},{13,1},{2,14},{6,10},... | collective-permute-start | bytes 393224 | tf_op jit(solution)/shard_map/ppermute | solution.py:730
  25.0 5.3 %mix_backward.1 = f32[8,640]{1,0:T(8,128)S(1)} custom-call(s32[15]{0:T(128)S(1)} %concatenate.18.scalars, f32[32,128]{1,0:T(8,128)S(1)} %get-tuple-element.41.refs_7_.refs_0_, f32[16,256]{1,0:T(8,128)S(1)} %get-tuple-element.44.refs_1_, f32[8,128]{1,0:T(8,128)S(1)} %get-tuple-element.45.refs_2_, f32[8,128]{1,0:T(8,128)S(1)} %get-tuple-element.46.refs_3_, ...), custom_call_target="tpu_custom_call" | custom-call | flops 6000000000 | bytes 524288 | tf_op jit(solution)/shard_map/mix_backward/pallas_call | solution.py:610
  30.3 1.6 %collective-permute-start.15 = (f32[8,256]{1,0:T(8,128)S(1)}, f32[8,256]{1,0:T(8,128)S(1)}, u32[]{:S(2)}, u32[]{:S(2)}) collective-permute-start(f32[8,256]{1,0:T(8,128)S(1)} %slice.35), channel_id=1, source_target_pairs={{0,2},{1,3},{2,0},{3,1},{4,6},{5,7},{6,4},{7,5},{8,10},{9,11},{10,... | collective-permute-start | bytes 24584 | tf_op jit(solution)/shard_map/ppermute | solution.py:739
  31.9 0.3 collective-permute-start.16
  32.2 2.3 %collective-permute-done.5.refs_2_ = bf16[128,512]{1,0:T(8,128)(2,1)S(1)} collective-permute-done((bf16[128,512]{1,0:T(8,128)(2,1)S(1)}, bf16[128,512]{1,0:T(8,128)(2,1)S(1)}, u32[]{:S(2)}, u32[]{:S(2)}) %collective-permute-start.5) | collective-permute-done | bytes 131104 | tf_op jit(solution)/shard_map/ppermute | solution.py:730
  34.5 0.5 %collective-permute-start.11 = (bf16[128,512]{1,0:T(8,128)(2,1)S(1)}, bf16[128,512]{1,0:T(8,128)(2,1)S(1)}, u32[]{:S(2)}, u32[]{:S(2)}) collective-permute-start(bf16[128,512]{1,0:T(8,128)(2,1)S(1)} %collective-permute-done.5.refs_2_), channel_id=1, source_target_pairs={{0,1},{1,0},{2,3},{3,2},{4,5},{5,4},{6,7},{7,6},{8,9},{9,8},{10,11... | collective-permute-start | bytes 393224 | tf_op jit(solution)/shard_map/ppermute | solution.py:739
  35.1 0.5 %collective-permute-start.9 = (bf16[128,512]{1,0:T(8,128)(2,1)S(1)}, bf16[128,512]{1,0:T(8,128)(2,1)S(1)}, u32[]{:S(2)}, u32[]{:S(2)}) collective-permute-start(bf16[128,512]{1,0:T(8,128)(2,1)S(1)} %get-tuple-element.61.refs_0_), channel_id=1, source_target_pairs={{0,1},{1,0},{2,3},{3,2},{4,5},{5,4},{6,7},{7,6},{8,9},{9,8},{10,11... | collective-permute-start | bytes 393224 | tf_op jit(solution)/shard_map/ppermute | solution.py:739
  35.6 2.7 %collective-permute-start.17 = (f32[8,1024]{1,0:T(8,128)S(1)}, f32[8,1024]{1,0:T(8,128)S(1)}, u32[]{:S(2)}, u32[]{:S(2)}) collective-permute-start(f32[8,1024]{1,0:T(8,128)S(1)} %pad_maximum_fusion.2.refs_12_), channel_id=1, source_target_pairs={{0,4},{4,0},{8,12},{12,8},{1,5},{5,1},{9,13},{13,9},{2,6},{6,2},{1... | collective-permute-start | bytes 98312 | tf_op jit(solution)/shard_map/ppermute | solution.py:730
  38.3 1.7 %collective-permute-start.18 = (f32[8,1024]{1,0:T(8,128)S(1)}, f32[8,1024]{1,0:T(8,128)S(1)}, u32[]{:S(2)}, u32[]{:S(2)}) collective-permute-start(f32[8,1024]{1,0:T(8,128)S(1)} %pad_maximum_fusion.2.refs_12_), channel_id=1, source_target_pairs={{0,8},{4,12},{8,0},{12,4},{1,9},{5,13},{9,1},{13,5},{2,10},{6,14},... | collective-permute-start | bytes 98312 | tf_op jit(solution)/shard_map/ppermute | solution.py:730
  40.0 1.3 %collective-permute-start.19 = (f32[8,1024]{1,0:T(8,128)S(1)}, f32[8,1024]{1,0:T(8,128)S(1)}, u32[]{:S(2)}, u32[]{:S(2)}) collective-permute-start(f32[8,1024]{1,0:T(8,128)S(1)} %pad_maximum_fusion.2.refs_12_), channel_id=1, source_target_pairs={{0,12},{4,8},{8,4},{12,0},{1,13},{5,9},{9,5},{13,1},{2,14},{6,10},... | collective-permute-start | bytes 98312 | tf_op jit(solution)/shard_map/ppermute | solution.py:730
  41.3 0.9 %layer_out.1 = (f32[128,256]{1,0:T(8,128)S(1)}, f32[128,256]{1,0:T(8,128)S(1)}) custom-call(s32[15]{0:T(128)S(1)} %concatenate.18.scalars, bf16[128,512]{1,0:T(8,128)(2,1)S(1)} %get-tuple-element.61.refs_0_, bf16[128,512]{1,0:T(8,128)(2,1)S(1)} %collective-permute-done.4.refs_1_, bf16[128,512]{1,0:T(8,128)(2,1)S(1)} %collective-permute-done.5.refs_2_, ...), custom_call_target="tpu_custom_call" | custom-call | tf_op jit(solution)/shard_map/layer_out/pallas_call | solution.py:648
  42.2 1.6 %collective-permute-start.13 = (f32[128,256]{1,0:T(8,128)S(1)}, f32[128,256]{1,0:T(8,128)S(1)}, u32[]{:S(2)}, u32[]{:S(2)}) collective-permute-start(f32[128,256]{1,0:T(8,128)S(1)} %get-tuple-element.66), channel_id=1, source_target_pairs={{0,2},{1,3},{2,0},{3,1},{4,6},{5,7},{6,4},{7,5},{8,10},{9,11},{10,... | collective-permute-start | bytes 393224 | tf_op jit(solution)/shard_map/ppermute | solution.py:739
  43.8 1.9 %collective-permute-done.19.refs_15_ = f32[8,1024]{1,0:T(8,128)S(1)} collective-permute-done((f32[8,1024]{1,0:T(8,128)S(1)}, f32[8,1024]{1,0:T(8,128)S(1)}, u32[]{:S(2)}, u32[]{:S(2)}) %collective-permute-start.19) | collective-permute-done | bytes 32800 | tf_op jit(solution)/shard_map/ppermute | solution.py:730
  45.7 3.9 %weight_grad.1 = (f32[1024,1024]{1,0:T(8,128)}, f32[5,2,1024]{2,1,0:T(2,128)}, f32[5,2,128]{2,1,0:T(2,128)}, f32[5,16]{1,0:T(8,128)}) custom-call(s32[15]{0:T(128)S(1)} %concatenate.18.scalars, bf16[128,512]{1,0:T(8,128)(2,1)S(1)} %get-tuple-element.61.refs_0_, bf16[128,512]{1,0:T(8,128)(2,1)S(1)} %collective-permute-done.4.refs_1_, ...), custom_call_target="tpu_custom_call" | custom-call | flops 1073741824 | bytes 6291456 | tf_op jit(solution)/shard_map/weight_grad/pallas_call | solution.py:707
  49.7 0.6 %add_convert_fusion = bf16[128,256]{1,0:T(8,128)(2,1)} fusion(f32[128,256]{1,0:T(8,128)S(1)} %get-tuple-element.65, f32[128,256]{1,0:T(8,128)S(1)} %collective-permute-done.13), kind=kLoop, calls=%fused_computation.3 | loop fusion | flops 65536 | bytes 327680 | tf_op jit(solution)/shard_map/convert_element_type | solution.py:782
  (38 shorter events, 0.2 us)
Async XLA Ops:
  2.1 11.9 %collective-permute-start = (bf16[144,256]{1,0:T(8,128)(2,1)S(1)}, bf16[144,256]{1,0:T(8,128)(2,1)S(1)}, u32[]{:S(2)}, u32[]{:S(2)}) collective-permute-start(bf16[144,256]{1,0:T(8,128)(2,1)S(1)} %fusion.1.refs_0_), channel_id=1, source_target_pairs={{0,4},{4,0},{8,12},{12,8},{1,5},{5,1},{9,13},{13,9},{2,6},{6,2},{1... | collective-permute-start | bytes 221192 | tf_op jit(solution)/shard_map/ppermute | solution.py:730
  5.2 8.9 %collective-permute-start.1 = (bf16[144,256]{1,0:T(8,128)(2,1)S(1)}, bf16[144,256]{1,0:T(8,128)(2,1)S(1)}, u32[]{:S(2)}, u32[]{:S(2)}) collective-permute-start(bf16[144,256]{1,0:T(8,128)(2,1)S(1)} %fusion.1.refs_0_), channel_id=1, source_target_pairs={{0,8},{4,12},{8,0},{12,4},{1,9},{5,13},{9,1},{13,5},{2,10},{6,14},... | collective-permute-start | bytes 221192 | tf_op jit(solution)/shard_map/ppermute | solution.py:730
  7.7 6.3 %collective-permute-start.2 = (bf16[144,256]{1,0:T(8,128)(2,1)S(1)}, bf16[144,256]{1,0:T(8,128)(2,1)S(1)}, u32[]{:S(2)}, u32[]{:S(2)}) collective-permute-start(bf16[144,256]{1,0:T(8,128)(2,1)S(1)} %fusion.1.refs_0_), channel_id=1, source_target_pairs={{0,12},{4,8},{8,4},{12,0},{1,13},{5,9},{9,5},{13,1},{2,14},{6,10},... | collective-permute-start | bytes 221192 | tf_op jit(solution)/shard_map/ppermute | solution.py:730
  10.8 0.7 %copy-start.1 = (s32[5]{0:T(128)S(1)}, s32[5]{0:T(128)}, u32[]{:S(2)}) copy-start(s32[5]{0:T(128)} %basemap.1) | copy-start | bytes 64
  11.4 2.6 %copy-start.2 = (bf16[128,256]{1,0:T(8,128)(2,1)S(1)}, bf16[128,256]{1,0:T(8,128)(2,1)}, u32[]{:S(2)}) copy-start(bf16[128,256]{1,0:T(8,128)(2,1)} %param.21) | copy-start | bytes 196612
  14.1 6.4 %collective-permute-start.3 = (bf16[4,128,256]{2,1,0:T(8,128)(2,1)S(1)}, bf16[4,128,256]{2,1,0:T(8,128)(2,1)S(1)}, u32[]{:S(2)}, u32[]{:S(2)}) collective-permute-start(bf16[4,128,256]{2,1,0:T(8,128)(2,1)S(1)} %pad_maximum_fusion.refs_4_.refs_8_), channel_id=1, source_target_pairs={{0,2},{1,3},{2,0},{3,1},{4,6},{5,7},{6,4},{7,5},{8,10},{9,11},{10,... | collective-permute-start | bytes 786440 | tf_op jit(solution)/shard_map/ppermute | solution.py:739
  15.7 9.3 %collective-permute-start.7 = (bf16[4,128,256]{2,1,0:T(8,128)(2,1)S(1)}, bf16[4,128,256]{2,1,0:T(8,128)(2,1)S(1)}, u32[]{:S(2)}, u32[]{:S(2)}) collective-permute-start(bf16[4,128,256]{2,1,0:T(8,128)(2,1)S(1)} %pad_maximum_fusion.refs_4_.refs_8_), channel_id=1, source_target_pairs={{0,1},{1,0},{2,3},{3,2},{4,5},{5,4},{6,7},{7,6},{8,9},{9,8},{10,11... | collective-permute-start | bytes 786440 | tf_op jit(solution)/shard_map/ppermute | solution.py:739
  15.7 9.3 %copy-start = (bf16[1024,1024]{1,0:T(8,128)(2,1)S(1)}, bf16[1024,1024]{1,0:T(8,128)(2,1)}, u32[]{:S(2)}) copy-start(bf16[1024,1024]{1,0:T(8,128)(2,1)} %refs_8_.3) | copy-start | bytes 6291460
  20.5 4.4 %collective-permute-start.8 = (bf16[4,128,256]{2,1,0:T(8,128)(2,1)S(1)}, bf16[4,128,256]{2,1,0:T(8,128)(2,1)S(1)}, u32[]{:S(2)}, u32[]{:S(2)}) collective-permute-start(bf16[4,128,256]{2,1,0:T(8,128)(2,1)S(1)} %collective-permute-done.3.refs_6_.refs_10_), channel_id=1, source_target_pairs={{0,1},{1,0},{2,3},{3,2},{4,5},{5,4},{6,7},{7,6},{8,9},{9,8},{10,11... | collective-permute-start | bytes 786440 | tf_op jit(solution)/shard_map/ppermute | solution.py:739
  20.6 11.3 %collective-permute-start.4 = (bf16[128,512]{1,0:T(8,128)(2,1)S(1)}, bf16[128,512]{1,0:T(8,128)(2,1)S(1)}, u32[]{:S(2)}, u32[]{:S(2)}) collective-permute-start(bf16[128,512]{1,0:T(8,128)(2,1)S(1)} %get-tuple-element.61.refs_0_), channel_id=1, source_target_pairs={{0,4},{4,0},{8,12},{12,8},{1,5},{5,1},{9,13},{13,9},{2,6},{6,2},{1... | collective-permute-start | bytes 393224 | tf_op jit(solution)/shard_map/ppermute | solution.py:730
  21.6 12.9 %collective-permute-start.5 = (bf16[128,512]{1,0:T(8,128)(2,1)S(1)}, bf16[128,512]{1,0:T(8,128)(2,1)S(1)}, u32[]{:S(2)}, u32[]{:S(2)}) collective-permute-start(bf16[128,512]{1,0:T(8,128)(2,1)S(1)} %get-tuple-element.61.refs_0_), channel_id=1, source_target_pairs={{0,8},{4,12},{8,0},{12,4},{1,9},{5,13},{9,1},{13,5},{2,10},{6,14},... | collective-permute-start | bytes 393224 | tf_op jit(solution)/shard_map/ppermute | solution.py:730
  24.0 10.5 %collective-permute-start.6 = (bf16[128,512]{1,0:T(8,128)(2,1)S(1)}, bf16[128,512]{1,0:T(8,128)(2,1)S(1)}, u32[]{:S(2)}, u32[]{:S(2)}) collective-permute-start(bf16[128,512]{1,0:T(8,128)(2,1)S(1)} %get-tuple-element.61.refs_0_), channel_id=1, source_target_pairs={{0,12},{4,8},{8,4},{12,0},{1,13},{5,9},{9,5},{13,1},{2,14},{6,10},... | collective-permute-start | bytes 393224 | tf_op jit(solution)/shard_map/ppermute | solution.py:730
  30.2 5.3 %collective-permute-start.14 = (f32[8,640]{1,0:T(8,128)S(1)}, f32[8,640]{1,0:T(8,128)S(1)}, u32[]{:S(2)}, u32[]{:S(2)}) collective-permute-start(f32[8,640]{1,0:T(8,128)S(1)} %mix_backward.1), channel_id=1, source_target_pairs={{0,1},{1,0},{2,3},{3,2},{4,5},{5,4},{6,7},{7,6},{8,9},{9,8},{10,11... | collective-permute-start | bytes 61448 | tf_op jit(solution)/shard_map/ppermute | solution.py:739
  30.3 4.7 %collective-permute-start.15 = (f32[8,256]{1,0:T(8,128)S(1)}, f32[8,256]{1,0:T(8,128)S(1)}, u32[]{:S(2)}, u32[]{:S(2)}) collective-permute-start(f32[8,256]{1,0:T(8,128)S(1)} %slice.35), channel_id=1, source_target_pairs={{0,2},{1,3},{2,0},{3,1},{4,6},{5,7},{6,4},{7,5},{8,10},{9,11},{10,... | collective-permute-start | bytes 24584 | tf_op jit(solution)/shard_map/ppermute | solution.py:739
  31.9 3.2 %collective-permute-start.16 = (f32[8,256]{1,0:T(8,128)S(1)}, f32[8,256]{1,0:T(8,128)S(1)}, u32[]{:S(2)}, u32[]{:S(2)}) collective-permute-start(f32[8,256]{1,0:T(8,128)S(1)} %slice.35), channel_id=1, source_target_pairs={{0,3},{1,2},{2,1},{3,0},{4,7},{5,6},{6,5},{7,4},{8,11},{9,10},{10,... | collective-permute-start | bytes 24584 | tf_op jit(solution)/shard_map/ppermute | solution.py:739
  34.5 3.8 %collective-permute-start.10 = (bf16[128,512]{1,0:T(8,128)(2,1)S(1)}, bf16[128,512]{1,0:T(8,128)(2,1)S(1)}, u32[]{:S(2)}, u32[]{:S(2)}) collective-permute-start(bf16[128,512]{1,0:T(8,128)(2,1)S(1)} %collective-permute-done.4.refs_1_), channel_id=1, source_target_pairs={{0,1},{1,0},{2,3},{3,2},{4,5},{5,4},{6,7},{7,6},{8,9},{9,8},{10,11... | collective-permute-start | bytes 393224 | tf_op jit(solution)/shard_map/ppermute | solution.py:739
  34.5 5.5 %collective-permute-start.11 = (bf16[128,512]{1,0:T(8,128)(2,1)S(1)}, bf16[128,512]{1,0:T(8,128)(2,1)S(1)}, u32[]{:S(2)}, u32[]{:S(2)}) collective-permute-start(bf16[128,512]{1,0:T(8,128)(2,1)S(1)} %collective-permute-done.5.refs_2_), channel_id=1, source_target_pairs={{0,1},{1,0},{2,3},{3,2},{4,5},{5,4},{6,7},{7,6},{8,9},{9,8},{10,11... | collective-permute-start | bytes 393224 | tf_op jit(solution)/shard_map/ppermute | solution.py:739
  35.1 6.3 %collective-permute-start.12 = (bf16[128,512]{1,0:T(8,128)(2,1)S(1)}, bf16[128,512]{1,0:T(8,128)(2,1)S(1)}, u32[]{:S(2)}, u32[]{:S(2)}) collective-permute-start(bf16[128,512]{1,0:T(8,128)(2,1)S(1)} %collective-permute-done.6.refs_3_), channel_id=1, source_target_pairs={{0,1},{1,0},{2,3},{3,2},{4,5},{5,4},{6,7},{7,6},{8,9},{9,8},{10,11... | collective-permute-start | bytes 393224 | tf_op jit(solution)/shard_map/ppermute | solution.py:739
  35.1 6.3 %collective-permute-start.9 = (bf16[128,512]{1,0:T(8,128)(2,1)S(1)}, bf16[128,512]{1,0:T(8,128)(2,1)S(1)}, u32[]{:S(2)}, u32[]{:S(2)}) collective-permute-start(bf16[128,512]{1,0:T(8,128)(2,1)S(1)} %get-tuple-element.61.refs_0_), channel_id=1, source_target_pairs={{0,1},{1,0},{2,3},{3,2},{4,5},{5,4},{6,7},{7,6},{8,9},{9,8},{10,11... | collective-permute-start | bytes 393224 | tf_op jit(solution)/shard_map/ppermute | solution.py:739
  35.6 8.2 %collective-permute-start.17 = (f32[8,1024]{1,0:T(8,128)S(1)}, f32[8,1024]{1,0:T(8,128)S(1)}, u32[]{:S(2)}, u32[]{:S(2)}) collective-permute-start(f32[8,1024]{1,0:T(8,128)S(1)} %pad_maximum_fusion.2.refs_12_), channel_id=1, source_target_pairs={{0,4},{4,0},{8,12},{12,8},{1,5},{5,1},{9,13},{13,9},{2,6},{6,2},{1... | collective-permute-start | bytes 98312 | tf_op jit(solution)/shard_map/ppermute | solution.py:730
  38.3 5.5 %collective-permute-start.18 = (f32[8,1024]{1,0:T(8,128)S(1)}, f32[8,1024]{1,0:T(8,128)S(1)}, u32[]{:S(2)}, u32[]{:S(2)}) collective-permute-start(f32[8,1024]{1,0:T(8,128)S(1)} %pad_maximum_fusion.2.refs_12_), channel_id=1, source_target_pairs={{0,8},{4,12},{8,0},{12,4},{1,9},{5,13},{9,1},{13,5},{2,10},{6,14},... | collective-permute-start | bytes 98312 | tf_op jit(solution)/shard_map/ppermute | solution.py:730
  40.0 5.7 %collective-permute-start.19 = (f32[8,1024]{1,0:T(8,128)S(1)}, f32[8,1024]{1,0:T(8,128)S(1)}, u32[]{:S(2)}, u32[]{:S(2)}) collective-permute-start(f32[8,1024]{1,0:T(8,128)S(1)} %pad_maximum_fusion.2.refs_12_), channel_id=1, source_target_pairs={{0,12},{4,8},{8,4},{12,0},{1,13},{5,9},{9,5},{13,1},{2,14},{6,10},... | collective-permute-start | bytes 98312 | tf_op jit(solution)/shard_map/ppermute | solution.py:730
  42.2 7.4 %collective-permute-start.13 = (f32[128,256]{1,0:T(8,128)S(1)}, f32[128,256]{1,0:T(8,128)S(1)}, u32[]{:S(2)}, u32[]{:S(2)}) collective-permute-start(f32[128,256]{1,0:T(8,128)S(1)} %get-tuple-element.66), channel_id=1, source_target_pairs={{0,2},{1,3},{2,0},{3,1},{4,6},{5,7},{6,4},{7,5},{8,10},{9,11},{10,... | collective-permute-start | bytes 393224 | tf_op jit(solution)/shard_map/ppermute | solution.py:739

commit v5 on v4

--- a/solution.py
+++ b/solution.py
@@ -655,13 +655,13 @@
     )(scalars, *slices, out_weight)
 
 
-def weight_kernel(scalars, *refs, ns, nh, nc, vocab):
+def weight_kernel(scalars, *refs, ns, nh, nc):
     slices, cots = refs[: ns * nc], refs[ns * nc : ns * nc + nh * nc]
-    packs = refs[ns * nc + nh * nc : ns * nc + nh * nc + ns]
-    out_ref, xz_ref, bc_ref, dt_ref, left, buf, sems = refs[ns * nc + nh * nc + ns :]
+    out_ref, mark_ref, left, buf, sems = refs[ns * nc + nh * nc :]
     mine = scalars[1]
     places = QUARTERS + nh * nc
     cols = cots[0].shape[2]
+    mark_ref[...] = jnp.zeros_like(mark_ref)
     for n in range(ns * nc):
         for k in range(ns):
             at = jnp.bitwise_xor(mine, k)
@@ -678,6 +678,41 @@
         copy = pltpu.make_async_copy(buf.at[q], out_ref.at[:, pl.ds(at, cols)], sems.at[q])
         copy.start()
         copies.append(copy)
+    for copy in copies:
+        copy.wait()
+
+
+def call_weight(scalars, slices, cots, width, ns, nh, nc):
+    length = slices[0].shape[1]
+    rows = ns * nc * LANES
+    return pl.pallas_call(
+        functools.partial(weight_kernel, ns=ns, nh=nh, nc=nc),
+        out_shape=[
+            jax.ShapeDtypeStruct((rows, width), F32),
+            jax.ShapeDtypeStruct((SYM, LANES), F32),
+        ],
+        in_specs=[SMEM] + [VMEM] * (len(slices) + len(cots)),
+        out_specs=[HBM, VMEM],
+        scratch_shapes=[
+            pltpu.VMEM((rows, length), BF16),
+            pltpu.VMEM((nh * nc, rows, width // (nh * nc)), F32),
+            pltpu.SemaphoreType.DMA((nh * nc,)),
+        ],
+        compiler_params=params(12),
+        cost_estimate=pl.CostEstimate(
+            flops=2 * rows * width * length, transcendentals=0, bytes_accessed=6 * rows * width
+        ),
+        name="weight_grad",
+    )(scalars, *slices, *cots)
+
+
+def final_kernel(scalars, *refs, ns, nh, vocab, places):
+    packs, parts = refs[:ns], refs[ns : ns + nh]
+    out_ref, xz_ref, bc_ref, dt_ref = refs[ns + nh + 1 :]
+    total = parts[0][...]
+    for a in parts[1:]:
+        total = total + a[...]
+    out_ref[...] = total.astype(BF16)
     d_bc = packs[0][:, 768:1024]
     for a in packs[1:]:
         d_bc = d_bc + a[:, 768:1024]
@@ -697,32 +732,22 @@
             row = jnp.sum(piece[:, 256 + 64 * i : 320 + 64 * i], 1, keepdims=True)
             d_dt = jnp.where(lane == 2 * j + i, row, d_dt)
     dt_ref[...] = d_dt[:vocab]
-    for copy in copies:
-        copy.wait()
-
-
-def call_weight(scalars, slices, cots, packs, raw, width, ns, nh, nc):
-    length = slices[0].shape[1]
-    rows = ns * nc * LANES
+
+
+def call_final(scalars, packs, parts, mark, raw, places):
+    shapes = [raw[1].shape, raw[2].shape, raw[5].shape]
+    arrays = list(packs) + list(parts)
     return pl.pallas_call(
-        functools.partial(weight_kernel, ns=ns, nh=nh, nc=nc, vocab=raw[1].shape[0]),
-        out_shape=[
-            jax.ShapeDtypeStruct(a, F32)
-            for a in ((rows, width), raw[1].shape, raw[2].shape, raw[5].shape)
-        ],
-        in_specs=[SMEM] + [VMEM] * (len(slices) + len(cots) + len(packs)),
-        out_specs=[HBM] + [VMEM] * 3,
-        scratch_shapes=[
-            pltpu.VMEM((rows, length), BF16),
-            pltpu.VMEM((nh * nc, rows, width // (nh * nc)), F32),
-            pltpu.SemaphoreType.DMA((nh * nc,)),
-        ],
-        compiler_params=params(12),
-        cost_estimate=pl.CostEstimate(
-            flops=2 * rows * width * length, transcendentals=0, bytes_accessed=6 * rows * width
+        functools.partial(
+            final_kernel, ns=len(packs), nh=len(parts), vocab=raw[1].shape[0], places=places
         ),
-        name="weight_grad",
-    )(scalars, *slices, *cots, *packs)
+        out_shape=[jax.ShapeDtypeStruct(parts[0].shape, BF16)]
+        + [jax.ShapeDtypeStruct(a, F32) for a in shapes],
+        in_specs=[SMEM] + [VMEM] * (len(arrays) + 1),
+        out_specs=[VMEM] * (len(shapes) + 1),
+        compiler_params=params(8),
+        name="place_grads",
+    )(scalars, *arrays, mark)
 
 
 def around(x, axis):
@@ -760,13 +785,19 @@
     conv, vocab = conv_x.shape[0], xz_table.shape[0]
     *tables, w, w2, rate = call_tables(scalars, raw)
     gated, *kept = call_forward(scalars, pays, w, w2, rate, tables[0], conv)
-    heads, gated = lax.optimization_barrier((heads, gated))
+    heads, _ = lax.optimization_barrier((heads, gated))
     cots = [heads[0], side]
     for a in heads[1:]:
         cots += [a, across(a, (0, 1), nh, nc)]
-    slices = around(gated, "seq")
+    hop = lambda x, k: lax.ppermute(x, "seq", [(i, i ^ k) for i in range(ns)])
+    direct = {k: hop(gated, k) for k in (1 << n for n in range(ns.bit_length() - 1))}
     grads = call_backward(scalars, tables, cots, out_weight, kept, conv, vocab)
-    slices, _ = lax.optimization_barrier((slices, grads))
+    direct, _ = lax.optimization_barrier((direct, grads))
+    held = {0: gated, **direct}
+    for k in range(3, ns):
+        if k not in held:
+            held[k] = hop(held[k & (k - 1)], k & -k)
+    slices = [held[k] for k in range(ns)]
     slices = slices + [across(a, (0, 1), nh, nc) for a in slices]
     shared = grads[:, 384:]
     beside = across(grads, (0, 1), nh, nc)
@@ -776,12 +807,10 @@
     packed = jnp.concatenate([grads[:, :384], beside[:, :384], shared + beside[:, 384:]], 1)
     packs = around(packed, "seq")
     parts = call_out(scalars, slices, out_weight, ns, nh, nc)
-    total = parts[0]
-    for k in range(1, nh):
-        total = total + across(parts[k], (nh - k, 0), nh, nc)
-    layer_out = total.astype(BF16)
-    d_out_weight, d_xz, d_bc, d_dt = call_weight(
-        scalars, slices, cots, packs, raw, width, ns, nh, nc
+    parts = [parts[0]] + [across(parts[k], (nh - k, 0), nh, nc) for k in range(1, nh)]
+    d_out_weight, mark = call_weight(scalars, slices, cots, width, ns, nh, nc)
+    layer_out, d_xz, d_bc, d_dt = call_final(
+        scalars, packs, parts, mark, raw, QUARTERS + nh * nc
     )
     return (layer_out, d_out_weight, d_xz, d_bc, d_dt)
 

time: 50.7 us -> 49.6 us (0.978)
  Pallas kernels: 14.5 us -> 15.2 us
  waiting for transfers between devices: 7.41 us -> 6.72 us
  other arithmetic: 4.37 us -> 3.73 us
    ppermute x9 -> x6, starting transfers between devices: 15.7 us -> 9.34 us  [around(): lax.ppermute(x, axis, [(i, i ^ k) for i in range(n)])]
    ppermute x0 -> x3, starting transfers between devices: none -> 5.98 us  [by_channel(): hop = lambda x, k: lax.ppermute(x, 'seq', [(i, i ^ k) for i in range(ns)])]
    ppermute x9 -> x6, waiting for transfers between devices: 6.04 us -> 3.08 us  [around(): lax.ppermute(x, axis, [(i, i ^ k) for i in range(n)])]
    ppermute x11, waiting for transfers between devices: 1.36 us -> 3.64 us  [across(): return lax.ppermute(x, ('head', 'sub'), pairs)]
    pallas_call x1 -> x2, Pallas kernels: 3.94 us -> 4.64 us  [the longest x1 3.31 us: call_weight(): pl.pallas_call(functools.partial(weight_kernel, ns=ns, nh=nh, nc=nc), out...]
    convert_element_type x1 -> x0, other arithmetic: 0.65 us -> none  [by_channel(): layer_out = total.astype(BF16)]
  transfers between devices with their start and end apart: 20 -> 20, of which waited for: 4 -> 7; matrix products, arithmetic and copies ran while one was open for 6% -> 6% of each run, Pallas kernels for 29% -> 26%
where the time goes in v5:
time: 49.6 us; the launch traced here: 49.3 us
  starting transfers between devices  21.4 us (43%)
  Pallas kernels  15.2 us (31%)
  waiting for transfers between devices  6.72 us (14%)
  other arithmetic  3.73 us (8%)
  local copies, waits for them, and re-layouts  1.51 us (3%)
  between operations  0.77 us (2%)
    ppermute x6, starting transfers between devices, around(): lax.ppermute(x, axis, [(i, i ^ k) for i in range(n)])  9.34 us
    ppermute x11, starting transfers between devices, across(): return lax.ppermute(x, ('head', 'sub'), pairs)  6.05 us
    ppermute x3, starting transfers between devices, by_channel(): hop = lambda x, k: lax.ppermute(x, 'seq', [(i, i ^ k) for i in range(ns)])  5.98 us
    pallas_call x1, Pallas kernels, call_backward(): pl.pallas_call(functools.partial(backward_kernel, ns=ns, nq=len(cots), co...  5.29 us
    ppermute x11, waiting for transfers between devices, across(): return lax.ppermute(x, ('head', 'sub'), pairs)  3.64 us
    pallas_call x1, Pallas kernels, call_forward(): pl.pallas_call(functools.partial(forward_kernel, ns=ns, conv=conv), out_s...  3.53 us
    pallas_call x1, Pallas kernels, call_weight(): pl.pallas_call(functools.partial(weight_kernel, ns=ns, nh=nh, nc=nc), out...  3.31 us
    ppermute x6, waiting for transfers between devices, around(): lax.ppermute(x, axis, [(i, i ^ k) for i in range(n)])  3.08 us
  transfers between devices with their start and end apart: 20, of which 7 were waited for; matrix products, arithmetic and copies ran while one was open for 6% of the time, Pallas kernels for 26%

profile of v5, /device:TPU:0, one launch (start us, length us, event | category | flops | bytes accessed | tf_op | source)
XLA Modules:
  0.0 49.3 jit_solution(12713058447045446018)
XLA Ops:
  0.6 0.7 %convert_bitcast_fusion = bf16[1,128]{1,0:T(2,128)(2,1)S(1)} fusion(s32[128]{0:T(128)} %param.11), kind=kLoop, calls=%fused_computation.42 | loop fusion | flops 128 | bytes 768 | tf_op jit(solution)/shard_map/reshape | solution.py:775
  1.3 0.8 %fusion.1.refs_0_ = bf16[144,256]{1,0:T(8,128)(2,1)S(1)} fusion(bf16[1,128]{1,0:T(2,128)(2,1)S(1)} %convert_bitcast_fusion, bf16[128,256]{1,0:T(8,128)(2,1)} %param.21), kind=kLoop, calls=%fused_computation.3 | loop fusion | flops 221184 | bytes 139520 | tf_op jit(solution)/shard_map/concatenate | solution.py:776
  2.1 3.0 %collective-permute-start = (bf16[144,256]{1,0:T(8,128)(2,1)S(1)}, bf16[144,256]{1,0:T(8,128)(2,1)S(1)}, u32[]{:S(2)}, u32[]{:S(2)}) collective-permute-start(bf16[144,256]{1,0:T(8,128)(2,1)S(1)} %fusion.1.refs_0_), channel_id=1, source_target_pairs={{0,4},{4,0},{8,12},{12,8},{1,5},{5,1},{9,13},{13,9},{2,6},{6,2},{1... | collective-permute-start | bytes 221192 | tf_op jit(solution)/shard_map/ppermute | solution.py:755
  5.2 2.6 %collective-permute-start.1 = (bf16[144,256]{1,0:T(8,128)(2,1)S(1)}, bf16[144,256]{1,0:T(8,128)(2,1)S(1)}, u32[]{:S(2)}, u32[]{:S(2)}) collective-permute-start(bf16[144,256]{1,0:T(8,128)(2,1)S(1)} %fusion.1.refs_0_), channel_id=1, source_target_pairs={{0,8},{4,12},{8,0},{12,4},{1,9},{5,13},{9,1},{13,5},{2,10},{6,14},... | collective-permute-start | bytes 221192 | tf_op jit(solution)/shard_map/ppermute | solution.py:755
  7.8 0.7 %reshape.16 = bf16[10,1024]{1,0:T(8,128)(2,1)S(1)} reshape(bf16[5,2,1024]{2,1,0:T(2,128)(2,1)} %param.13) | data formatting | bytes 40960 | tf_op jit(solution)/shard_map/reshape | solution.py:579
  8.5 0.7 %pad_maximum_fusion.1.refs_0_ = bf16[14,1024]{1,0:T(8,128)(2,1)S(1)} fusion(bf16[4,1024]{1,0:T(4,128)(2,1)} %param.16, bf16[10,1024]{1,0:T(8,128)(2,1)S(1)} %reshape.16), kind=kLoop, calls=%fused_computation.7 | loop fusion | flops 57344 | bytes 57344 | tf_op jit(solution)/shard_map/concatenate | solution.py:579
  9.2 0.7 %pad_maximum_fusion.3.refs_1_ = bf16[9,2,128]{2,1,0:T(2,128)(2,1)S(1)} fusion(bf16[4,2,128]{2,1,0:T(2,128)(2,1)} %param.17, bf16[5,2,128]{2,1,0:T(2,128)(2,1)} %param.14), kind=kLoop, calls=%fused_computation.10 | loop fusion | flops 2304 | bytes 9216 | tf_op jit(solution)/shard_map/concatenate | solution.py:580
  10.0 0.7 %pad_maximum_fusion.4.refs_2_ = f32[7,16]{1,0:T(8,128)S(1)} fusion(f32[1,16]{1,0:T(1,128)} %bitcast.15, f32[1,16]{1,0:T(1,128)} %bitcast.16, f32[5,16]{1,0:T(8,128)} %param.15), kind=kLoop, calls=%fused_computation.11 | loop fusion | flops 224 | bytes 896 | tf_op jit(solution)/shard_map/concatenate | solution.py:581
  10.8 0.7 %copy-done.1 = s32[5]{0:T(128)S(1)} copy-done((s32[5]{0:T(128)S(1)}, s32[5]{0:T(128)}, u32[]{:S(2)}) %copy-start.1) | copy-done | bytes 44
  11.4 0.8 %tables.1 = (f32[32,128]{1,0:T(8,128)S(1)}, f32[16,256]{1,0:T(8,128)S(1)}, f32[8,128]{1,0:T(8,128)S(1)}, f32[8,128]{1,0:T(8,128)S(1)}, bf16[128,1792]{1,0:T(8,12...) custom-call(s32[15]{0:T(128)S(1)} %concatenate.18.scalars, s32[5]{0:T(128)S(1)} %copy-done.1, ...), custom_call_target="tpu_custom_call" | custom-call | flops 2000000000 | bytes 1000000 | tf_op jit(solution)/shard_map/tables/pallas_call | solution.py:567
  12.2 1.8 %collective-permute-done.2.refs_3_ = bf16[144,256]{1,0:T(8,128)(2,1)S(1)} collective-permute-done((bf16[144,256]{1,0:T(8,128)(2,1)S(1)}, bf16[144,256]{1,0:T(8,128)(2,1)S(1)}, u32[]{:S(2)}, u32[]{:S(2)}) %collective-permute-start.2) | collective-permute-done | bytes 73760 | tf_op jit(solution)/shard_map/ppermute | solution.py:755
  14.1 1.6 %collective-permute-start.3 = (bf16[4,128,256]{2,1,0:T(8,128)(2,1)S(1)}, bf16[4,128,256]{2,1,0:T(8,128)(2,1)S(1)}, u32[]{:S(2)}, u32[]{:S(2)}) collective-permute-start(bf16[4,128,256]{2,1,0:T(8,128)(2,1)S(1)} %pad_maximum_fusion.refs_4_.refs_8_), channel_id=1, source_target_pairs={{0,2},{1,3},{2,0},{3,1},{4,6},{5,7},{6,4},{7,5},{8,10},{9,11},{10,... | collective-permute-start | bytes 786440 | tf_op jit(solution)/shard_map/ppermute | solution.py:764
  15.7 3.5 %mix_forward.1 = (bf16[128,512]{1,0:T(8,128)(2,1)S(1)}, f32[8,512]{1,0:T(8,128)S(1)}, f32[8,512]{1,0:T(8,128)S(1)}, f32[8,512]{1,0:T(8,128)S(1)}, bf16[64,512]{1...) custom-call(s32[15]{0:T(128)S(1)} %concatenate.18.scalars, ...), custom_call_target="tpu_custom_call" | custom-call | flops 5000000000 | bytes 524288 | tf_op jit(solution)/shard_map/mix_forward/pallas_call | solution.py:589
  19.2 1.3 %collective-permute-done.3.refs_6_.refs_10_ = bf16[4,128,256]{2,1,0:T(8,128)(2,1)S(1)} collective-permute-done((bf16[4,128,256]{2,1,0:T(8,128)(2,1)S(1)}, bf16[4,128,256]{2,1,0:T(8,128)(2,1)S(1)}, u32[]{:S(2)}, u32[]{:S(2)}) %collective-permute-start.3) | collective-permute-done | bytes 262176 | tf_op jit(solution)/shard_map/ppermute | solution.py:764
  20.6 1.1 %collective-permute-start.12 = (bf16[128,512]{1,0:T(8,128)(2,1)S(1)}, bf16[128,512]{1,0:T(8,128)(2,1)S(1)}, u32[]{:S(2)}, u32[]{:S(2)}) collective-permute-start(bf16[128,512]{1,0:T(8,128)(2,1)S(1)} %get-tuple-element.44.refs_0_), channel_id=1, source_target_pairs={{0,4},{4,0},{8,12},{12,8},{1,5},{5,1},{9,13},{13,9},{2,6},{6,2},{1... | collective-permute-start | bytes 393224 | tf_op jit(solution)/shard_map/ppermute | solution.py:792
  21.6 2.4 %collective-permute-start.13 = (bf16[128,512]{1,0:T(8,128)(2,1)S(1)}, bf16[128,512]{1,0:T(8,128)(2,1)S(1)}, u32[]{:S(2)}, u32[]{:S(2)}) collective-permute-start(bf16[128,512]{1,0:T(8,128)(2,1)S(1)} %get-tuple-element.44.refs_0_), channel_id=1, source_target_pairs={{0,8},{4,12},{8,0},{12,4},{1,9},{5,13},{9,1},{13,5},{2,10},{6,14},... | collective-permute-start | bytes 393224 | tf_op jit(solution)/shard_map/ppermute | solution.py:792
  24.0 5.3 %mix_backward.1 = f32[8,640]{1,0:T(8,128)S(1)} custom-call(s32[15]{0:T(128)S(1)} %concatenate.18.scalars, f32[32,128]{1,0:T(8,128)S(1)} %get-tuple-element.37.refs_7_.refs_0_, f32[16,256]{1,0:T(8,128)S(1)} %get-tuple-element.38.refs_1_, f32[8,128]{1,0:T(8,128)S(1)} %get-tuple-element.39.refs_2_, f32[8,128]{1,0:T(8,128)S(1)} %get-tuple-element.40.refs_3_, ...), custom_call_target="tpu_custom_call" | custom-call | flops 6000000000 | bytes 524288 | tf_op jit(solution)/shard_map/mix_backward/pallas_call | solution.py:610
  29.3 2.5 %collective-permute-start.14 = (bf16[128,512]{1,0:T(8,128)(2,1)S(1)}, bf16[128,512]{1,0:T(8,128)(2,1)S(1)}, u32[]{:S(2)}, u32[]{:S(2)}) collective-permute-start(bf16[128,512]{1,0:T(8,128)(2,1)S(1)} %collective-permute-done.13.refs_2_), channel_id=1, source_target_pairs={{0,4},{4,0},{8,12},{12,8},{1,5},{5,1},{9,13},{13,9},{2,6},{6,2},{1... | collective-permute-start | bytes 393224 | tf_op jit(solution)/shard_map/ppermute | solution.py:792
  31.9 1.5 %collective-permute-start.7 = (f32[8,256]{1,0:T(8,128)S(1)}, f32[8,256]{1,0:T(8,128)S(1)}, u32[]{:S(2)}, u32[]{:S(2)}) collective-permute-start(f32[8,256]{1,0:T(8,128)S(1)} %slice.35), channel_id=1, source_target_pairs={{0,2},{1,3},{2,0},{3,1},{4,6},{5,7},{6,4},{7,5},{8,10},{9,11},{10,... | collective-permute-start | bytes 24584 | tf_op jit(solution)/shard_map/ppermute | solution.py:764
  33.4 0.4 collective-permute-start.8
  33.7 0.3 collective-permute-start.15
  34.2 1.3 %collective-permute-done.7 = f32[8,256]{1,0:T(8,128)S(1)} collective-permute-done((f32[8,256]{1,0:T(8,128)S(1)}, f32[8,256]{1,0:T(8,128)S(1)}, u32[]{:S(2)}, u32[]{:S(2)}) %collective-permute-start.7) | collective-permute-done | bytes 8224 | tf_op jit(solution)/shard_map/ppermute | solution.py:764
  35.5 0.5 %collective-permute-start.18 = (bf16[128,512]{1,0:T(8,128)(2,1)S(1)}, bf16[128,512]{1,0:T(8,128)(2,1)S(1)}, u32[]{:S(2)}, u32[]{:S(2)}) collective-permute-start(bf16[128,512]{1,0:T(8,128)(2,1)S(1)} %collective-permute-done.14.refs_3_), channel_id=1, source_target_pairs={{0,1},{1,0},{2,3},{3,2},{4,5},{5,4},{6,7},{7,6},{8,9},{9,8},{10,11... | collective-permute-start | bytes 393224 | tf_op jit(solution)/shard_map/ppermute | solution.py:764
  36.0 0.4 collective-permute-done.8
  36.4 0.4 collective-permute-done.16.refs_5_
  37.1 0.9 %layer_out.1 = (f32[128,256]{1,0:T(8,128)S(1)}, f32[128,256]{1,0:T(8,128)S(1)}) custom-call(s32[15]{0:T(128)S(1)} %concatenate.18.scalars, bf16[128,512]{1,0:T(8,128)(2,1)S(1)} %get-tuple-element.44.refs_0_, bf16[128,512]{1,0:T(8,128)(2,1)S(1)} %collective-permute-done.12.refs_1_, bf16[128,512]{1,0:T(8,128)(2,1)S(1)} %collective-permute-done.13.refs_2_, ...), custom_call_target="tpu_custom_call" | custom-call | tf_op jit(solution)/shard_map/layer_out/pallas_call | solution.py:648
  38.0 1.6 %collective-permute-start.19 = (f32[128,256]{1,0:T(8,128)S(1)}, f32[128,256]{1,0:T(8,128)S(1)}, u32[]{:S(2)}, u32[]{:S(2)}) collective-permute-start(f32[128,256]{1,0:T(8,128)S(1)} %get-tuple-element.62), channel_id=1, source_target_pairs={{0,2},{1,3},{2,0},{3,1},{4,6},{5,7},{6,4},{7,5},{8,10},{9,11},{10,... | collective-permute-start | bytes 393224 | tf_op jit(solution)/shard_map/ppermute | solution.py:764
  39.6 2.6 %collective-permute-start.10 = (f32[8,1024]{1,0:T(8,128)S(1)}, f32[8,1024]{1,0:T(8,128)S(1)}, u32[]{:S(2)}, u32[]{:S(2)}) collective-permute-start(f32[8,1024]{1,0:T(8,128)S(1)} %pad_maximum_fusion.2.refs_0_), channel_id=1, source_target_pairs={{0,8},{4,12},{8,0},{12,4},{1,9},{5,13},{9,1},{13,5},{2,10},{6,14},... | collective-permute-start | bytes 98312 | tf_op jit(solution)/shard_map/ppermute | solution.py:755
  42.2 0.9 %collective-permute-start.11 = (f32[8,1024]{1,0:T(8,128)S(1)}, f32[8,1024]{1,0:T(8,128)S(1)}, u32[]{:S(2)}, u32[]{:S(2)}) collective-permute-start(f32[8,1024]{1,0:T(8,128)S(1)} %pad_maximum_fusion.2.refs_0_), channel_id=1, source_target_pairs={{0,12},{4,8},{8,4},{12,0},{1,13},{5,9},{9,5},{13,1},{2,14},{6,10},... | collective-permute-start | bytes 98312 | tf_op jit(solution)/shard_map/ppermute | solution.py:755
  43.3 3.3 %weight_grad.1 = (f32[1024,1024]{1,0:T(8,128)}, f32[8,128]{1,0:T(8,128)S(1)}) custom-call(s32[15]{0:T(128)S(1)} %concatenate.18.scalars, bf16[128,512]{1,0:T(8,128)(2,1)S(1)} %get-tuple-element.44.refs_0_, bf16[128,512]{1,0:T(8,128)(2,1)S(1)} %collective-permute-done.12.refs_1_, bf16[128,512]{1,0:T(8,128)(2,1)S(1)} %collective-permute-done.13.refs_2_, ...), custom_call_target="tpu_custom_call" | custom-call | flops 1073741824 | bytes 6291456 | tf_op jit(solution)/shard_map/weight_grad/pallas_call | solution.py:688
  46.6 1.3 %collective-permute-done.11.refs_3_ = f32[8,1024]{1,0:T(8,128)S(1)} collective-permute-done((f32[8,1024]{1,0:T(8,128)S(1)}, f32[8,1024]{1,0:T(8,128)S(1)}, u32[]{:S(2)}, u32[]{:S(2)}) %collective-permute-start.11) | collective-permute-done | bytes 32800 | tf_op jit(solution)/shard_map/ppermute | solution.py:755
  47.9 1.3 %place_grads.1 = (bf16[128,256]{1,0:T(8,128)(2,1)}, f32[5,2,1024]{2,1,0:T(2,128)}, f32[5,2,128]{2,1,0:T(2,128)}, f32[5,16]{1,0:T(8,128)}) custom-call(s32[15]{0:T(128)S(1)} %concatenate.18.scalars, f32[8,1024]{1,0:T(8,128)S(1)} %pad_maximum_fusion.2.refs_0_, f32[8,1024]{1,0:T(8,128)S(1)} %collective-permute-done.9.refs_1_, ...), custom_call_target="tpu_custom_call" | custom-call | tf_op jit(solution)/shard_map/place_grads/pallas_call | solution.py:740
  (38 shorter events, 0.8 us)
Async XLA Ops:
  2.1 11.9 %collective-permute-start = (bf16[144,256]{1,0:T(8,128)(2,1)S(1)}, bf16[144,256]{1,0:T(8,128)(2,1)S(1)}, u32[]{:S(2)}, u32[]{:S(2)}) collective-permute-start(bf16[144,256]{1,0:T(8,128)(2,1)S(1)} %fusion.1.refs_0_), channel_id=1, source_target_pairs={{0,4},{4,0},{8,12},{12,8},{1,5},{5,1},{9,13},{13,9},{2,6},{6,2},{1... | collective-permute-start | bytes 221192 | tf_op jit(solution)/shard_map/ppermute | solution.py:755
  5.2 8.9 %collective-permute-start.1 = (bf16[144,256]{1,0:T(8,128)(2,1)S(1)}, bf16[144,256]{1,0:T(8,128)(2,1)S(1)}, u32[]{:S(2)}, u32[]{:S(2)}) collective-permute-start(bf16[144,256]{1,0:T(8,128)(2,1)S(1)} %fusion.1.refs_0_), channel_id=1, source_target_pairs={{0,8},{4,12},{8,0},{12,4},{1,9},{5,13},{9,1},{13,5},{2,10},{6,14},... | collective-permute-start | bytes 221192 | tf_op jit(solution)/shard_map/ppermute | solution.py:755
  7.7 6.3 %collective-permute-start.2 = (bf16[144,256]{1,0:T(8,128)(2,1)S(1)}, bf16[144,256]{1,0:T(8,128)(2,1)S(1)}, u32[]{:S(2)}, u32[]{:S(2)}) collective-permute-start(bf16[144,256]{1,0:T(8,128)(2,1)S(1)} %fusion.1.refs_0_), channel_id=1, source_target_pairs={{0,12},{4,8},{8,4},{12,0},{1,13},{5,9},{9,5},{13,1},{2,14},{6,10},... | collective-permute-start | bytes 221192 | tf_op jit(solution)/shard_map/ppermute | solution.py:755
  10.8 0.7 %copy-start.1 = (s32[5]{0:T(128)S(1)}, s32[5]{0:T(128)}, u32[]{:S(2)}) copy-start(s32[5]{0:T(128)} %basemap.1) | copy-start | bytes 64
  11.4 2.6 %copy-start.2 = (bf16[128,256]{1,0:T(8,128)(2,1)S(1)}, bf16[128,256]{1,0:T(8,128)(2,1)}, u32[]{:S(2)}) copy-start(bf16[128,256]{1,0:T(8,128)(2,1)} %param.21) | copy-start | bytes 196612
  14.1 6.4 %collective-permute-start.3 = (bf16[4,128,256]{2,1,0:T(8,128)(2,1)S(1)}, bf16[4,128,256]{2,1,0:T(8,128)(2,1)S(1)}, u32[]{:S(2)}, u32[]{:S(2)}) collective-permute-start(bf16[4,128,256]{2,1,0:T(8,128)(2,1)S(1)} %pad_maximum_fusion.refs_4_.refs_8_), channel_id=1, source_target_pairs={{0,2},{1,3},{2,0},{3,1},{4,6},{5,7},{6,4},{7,5},{8,10},{9,11},{10,... | collective-permute-start | bytes 786440 | tf_op jit(solution)/shard_map/ppermute | solution.py:764
  15.7 8.4 %collective-permute-start.4 = (bf16[4,128,256]{2,1,0:T(8,128)(2,1)S(1)}, bf16[4,128,256]{2,1,0:T(8,128)(2,1)S(1)}, u32[]{:S(2)}, u32[]{:S(2)}) collective-permute-start(bf16[4,128,256]{2,1,0:T(8,128)(2,1)S(1)} %pad_maximum_fusion.refs_4_.refs_8_), channel_id=1, source_target_pairs={{0,1},{1,0},{2,3},{3,2},{4,5},{5,4},{6,7},{7,6},{8,9},{9,8},{10,11... | collective-permute-start | bytes 786440 | tf_op jit(solution)/shard_map/ppermute | solution.py:764
  15.7 8.4 %copy-start = (bf16[1024,1024]{1,0:T(8,128)(2,1)S(1)}, bf16[1024,1024]{1,0:T(8,128)(2,1)}, u32[]{:S(2)}) copy-start(bf16[1024,1024]{1,0:T(8,128)(2,1)} %refs_8_.3) | copy-start | bytes 6291460
  20.5 3.5 %collective-permute-start.5 = (bf16[4,128,256]{2,1,0:T(8,128)(2,1)S(1)}, bf16[4,128,256]{2,1,0:T(8,128)(2,1)S(1)}, u32[]{:S(2)}, u32[]{:S(2)}) collective-permute-start(bf16[4,128,256]{2,1,0:T(8,128)(2,1)S(1)} %collective-permute-done.3.refs_6_.refs_10_), channel_id=1, source_target_pairs={{0,1},{1,0},{2,3},{3,2},{4,5},{5,4},{6,7},{7,6},{8,9},{9,8},{10,11... | collective-permute-start | bytes 786440 | tf_op jit(solution)/shard_map/ppermute | solution.py:764
  20.6 8.8 %collective-permute-start.12 = (bf16[128,512]{1,0:T(8,128)(2,1)S(1)}, bf16[128,512]{1,0:T(8,128)(2,1)S(1)}, u32[]{:S(2)}, u32[]{:S(2)}) collective-permute-start(bf16[128,512]{1,0:T(8,128)(2,1)S(1)} %get-tuple-element.44.refs_0_), channel_id=1, source_target_pairs={{0,4},{4,0},{8,12},{12,8},{1,5},{5,1},{9,13},{13,9},{2,6},{6,2},{1... | collective-permute-start | bytes 393224 | tf_op jit(solution)/shard_map/ppermute | solution.py:792
  21.6 7.7 %collective-permute-start.13 = (bf16[128,512]{1,0:T(8,128)(2,1)S(1)}, bf16[128,512]{1,0:T(8,128)(2,1)S(1)}, u32[]{:S(2)}, u32[]{:S(2)}) collective-permute-start(bf16[128,512]{1,0:T(8,128)(2,1)S(1)} %get-tuple-element.44.refs_0_), channel_id=1, source_target_pairs={{0,8},{4,12},{8,0},{12,4},{1,9},{5,13},{9,1},{13,5},{2,10},{6,14},... | collective-permute-start | bytes 393224 | tf_op jit(solution)/shard_map/ppermute | solution.py:792
  29.3 6.2 %collective-permute-start.14 = (bf16[128,512]{1,0:T(8,128)(2,1)S(1)}, bf16[128,512]{1,0:T(8,128)(2,1)S(1)}, u32[]{:S(2)}, u32[]{:S(2)}) collective-permute-start(bf16[128,512]{1,0:T(8,128)(2,1)S(1)} %collective-permute-done.13.refs_2_), channel_id=1, source_target_pairs={{0,4},{4,0},{8,12},{12,8},{1,5},{5,1},{9,13},{13,9},{2,6},{6,2},{1... | collective-permute-start | bytes 393224 | tf_op jit(solution)/shard_map/ppermute | solution.py:792
  31.9 2.2 %collective-permute-start.6 = (f32[8,640]{1,0:T(8,128)S(1)}, f32[8,640]{1,0:T(8,128)S(1)}, u32[]{:S(2)}, u32[]{:S(2)}) collective-permute-start(f32[8,640]{1,0:T(8,128)S(1)} %mix_backward.1), channel_id=1, source_target_pairs={{0,1},{1,0},{2,3},{3,2},{4,5},{5,4},{6,7},{7,6},{8,9},{9,8},{10,11... | collective-permute-start | bytes 61448 | tf_op jit(solution)/shard_map/ppermute | solution.py:764
  31.9 3.7 %collective-permute-start.7 = (f32[8,256]{1,0:T(8,128)S(1)}, f32[8,256]{1,0:T(8,128)S(1)}, u32[]{:S(2)}, u32[]{:S(2)}) collective-permute-start(f32[8,256]{1,0:T(8,128)S(1)} %slice.35), channel_id=1, source_target_pairs={{0,2},{1,3},{2,0},{3,1},{4,6},{5,7},{6,4},{7,5},{8,10},{9,11},{10,... | collective-permute-start | bytes 24584 | tf_op jit(solution)/shard_map/ppermute | solution.py:764
  33.4 3.1 %collective-permute-start.8 = (f32[8,256]{1,0:T(8,128)S(1)}, f32[8,256]{1,0:T(8,128)S(1)}, u32[]{:S(2)}, u32[]{:S(2)}) collective-permute-start(f32[8,256]{1,0:T(8,128)S(1)} %slice.35), channel_id=1, source_target_pairs={{0,3},{1,2},{2,1},{3,0},{4,7},{5,6},{6,5},{7,4},{8,11},{9,10},{10,... | collective-permute-start | bytes 24584 | tf_op jit(solution)/shard_map/ppermute | solution.py:764
  33.7 2.7 %collective-permute-start.15 = (bf16[128,512]{1,0:T(8,128)(2,1)S(1)}, bf16[128,512]{1,0:T(8,128)(2,1)S(1)}, u32[]{:S(2)}, u32[]{:S(2)}) collective-permute-start(bf16[128,512]{1,0:T(8,128)(2,1)S(1)} %get-tuple-element.44.refs_0_), channel_id=1, source_target_pairs={{0,1},{1,0},{2,3},{3,2},{4,5},{5,4},{6,7},{7,6},{8,9},{9,8},{10,11... | collective-permute-start | bytes 393224 | tf_op jit(solution)/shard_map/ppermute | solution.py:764
  34.0 2.9 %collective-permute-start.17 = (bf16[128,512]{1,0:T(8,128)(2,1)S(1)}, bf16[128,512]{1,0:T(8,128)(2,1)S(1)}, u32[]{:S(2)}, u32[]{:S(2)}) collective-permute-start(bf16[128,512]{1,0:T(8,128)(2,1)S(1)} %collective-permute-done.13.refs_2_), channel_id=1, source_target_pairs={{0,1},{1,0},{2,3},{3,2},{4,5},{5,4},{6,7},{7,6},{8,9},{9,8},{10,11... | collective-permute-start | bytes 393224 | tf_op jit(solution)/shard_map/ppermute | solution.py:764
  35.5 1.3 %collective-permute-start.16 = (bf16[128,512]{1,0:T(8,128)(2,1)S(1)}, bf16[128,512]{1,0:T(8,128)(2,1)S(1)}, u32[]{:S(2)}, u32[]{:S(2)}) collective-permute-start(bf16[128,512]{1,0:T(8,128)(2,1)S(1)} %collective-permute-done.12.refs_1_), channel_id=1, source_target_pairs={{0,1},{1,0},{2,3},{3,2},{4,5},{5,4},{6,7},{7,6},{8,9},{9,8},{10,11... | collective-permute-start | bytes 393224 | tf_op jit(solution)/shard_map/ppermute | solution.py:764
  35.5 1.5 %collective-permute-start.18 = (bf16[128,512]{1,0:T(8,128)(2,1)S(1)}, bf16[128,512]{1,0:T(8,128)(2,1)S(1)}, u32[]{:S(2)}, u32[]{:S(2)}) collective-permute-start(bf16[128,512]{1,0:T(8,128)(2,1)S(1)} %collective-permute-done.14.refs_3_), channel_id=1, source_target_pairs={{0,1},{1,0},{2,3},{3,2},{4,5},{5,4},{6,7},{7,6},{8,9},{9,8},{10,11... | collective-permute-start | bytes 393224 | tf_op jit(solution)/shard_map/ppermute | solution.py:764
  38.0 10.0 %collective-permute-start.19 = (f32[128,256]{1,0:T(8,128)S(1)}, f32[128,256]{1,0:T(8,128)S(1)}, u32[]{:S(2)}, u32[]{:S(2)}) collective-permute-start(f32[128,256]{1,0:T(8,128)S(1)} %get-tuple-element.62), channel_id=1, source_target_pairs={{0,2},{1,3},{2,0},{3,1},{4,6},{5,7},{6,4},{7,5},{8,10},{9,11},{10,... | collective-permute-start | bytes 393224 | tf_op jit(solution)/shard_map/ppermute | solution.py:764
  39.6 7.1 %collective-permute-start.10 = (f32[8,1024]{1,0:T(8,128)S(1)}, f32[8,1024]{1,0:T(8,128)S(1)}, u32[]{:S(2)}, u32[]{:S(2)}) collective-permute-start(f32[8,1024]{1,0:T(8,128)S(1)} %pad_maximum_fusion.2.refs_0_), channel_id=1, source_target_pairs={{0,8},{4,12},{8,0},{12,4},{1,9},{5,13},{9,1},{13,5},{2,10},{6,14},... | collective-permute-start | bytes 98312 | tf_op jit(solution)/shard_map/ppermute | solution.py:755
  42.2 5.7 %collective-permute-start.11 = (f32[8,1024]{1,0:T(8,128)S(1)}, f32[8,1024]{1,0:T(8,128)S(1)}, u32[]{:S(2)}, u32[]{:S(2)}) collective-permute-start(f32[8,1024]{1,0:T(8,128)S(1)} %pad_maximum_fusion.2.refs_0_), channel_id=1, source_target_pairs={{0,12},{4,8},{8,4},{12,0},{1,13},{5,9},{9,5},{13,1},{2,14},{6,10},... | collective-permute-start | bytes 98312 | tf_op jit(solution)/shard_map/ppermute | solution.py:755
  43.2 4.8 %collective-permute-start.9 = (f32[8,1024]{1,0:T(8,128)S(1)}, f32[8,1024]{1,0:T(8,128)S(1)}, u32[]{:S(2)}, u32[]{:S(2)}) collective-permute-start(f32[8,1024]{1,0:T(8,128)S(1)} %pad_maximum_fusion.2.refs_0_), channel_id=1, source_target_pairs={{0,4},{4,0},{8,12},{12,8},{1,5},{5,1},{9,13},{13,9},{2,6},{6,2},{1... | collective-permute-start | bytes 98312 | tf_op jit(solution)/shard_map/ppermute | solution.py:755

commit v6 on v5

--- a/solution.py
+++ b/solution.py
@@ -221,7 +221,13 @@
 
     def act(self, col, width):
         v = self.pre(col, width)
-        return v * sigmoid(v)
+        s = sigmoid(v)
+        at = self.base + col
+        self.r.slope[self.rows, at : at + width] = s * (1.0 + v * (1.0 - s))
+        return v * s
+
+    def slope(self, col, width):
+        return self.r.slope[self.rows, self.base + col : self.base + col + width]
 
     def by_head(self, v):
         zero = jnp.zeros_like(v)
@@ -279,7 +285,7 @@
     return r
 
 
-KEPT = ("inc", "exc", "oh", "sym", "pre", "pd", "x", "bc", "s", "dec", "wts", "ys")
+KEPT = ("inc", "exc", "oh", "sym", "slope", "z", "pd", "x", "bc", "s", "dec", "wts", "ys")
 
 
 def kept_shapes(length):
@@ -290,6 +296,7 @@
         ((SYM, length), F32),
         ((64, length), BF16),
         ((length, 2 * WIDE), F32),
+        ((length, 256), F32),
         ((length, 768), F32),
         ((length, 512), F32),
         ((length, 1024), F32),
@@ -302,7 +309,7 @@
 
 def forward_kernel(scalars, *refs, ns, conv):
     tok_refs, (w_ref, w2_ref, rate_ref, tabs_ref, out_ref) = refs[:ns], refs[ns : ns + 5]
-    r = named(refs[ns + 5 :], KEPT + ("rows", "prow", "count"))
+    r = named(refs[ns + 5 :], KEPT + ("rows", "prow", "count", "pre"))
     r.rate = rate_ref
     prepare(scalars, tok_refs, w_ref, w2_ref, r, conv)
     units = [[Unit(r, tabs_ref, st, b, ns) for b in range(ns)] for st in range(2)]
@@ -342,7 +349,9 @@
             inner = mm(jnp.concatenate(lefts[w], 1), jnp.concatenate(right, 0), NN)
             r.ys[u.rows, st * 512 + w * 256 : st * 512 + w * 256 + 128] = inner
             y = y + inner
-        gated[st, b] = y * u.act(ZZ, 128)
+        z = u.act(ZZ, 128)
+        r.z[u.rows, st * 128 : st * 128 + 128] = z
+        gated[st, b] = y * z
 
     for b0 in range(0, ns, GROUP):
         together(body(st, b) for b in range(b0, min(b0 + GROUP, ns)) for st in range(2))
@@ -371,20 +380,28 @@
             k * BLOCK : (k + 1) * BLOCK
         ]
     units = [[Unit(r, tabs_ref, st, b, ns) for b in range(ns)] for st in range(2)]
-    for st in range(2):
+
+    def spread(st):
+        backs, aheads = {}, {}
         for b in range(ns):
             u = units[st][b]
-            dy = r.dg[u.rows, :] * u.act(ZZ, 128)
+            dy = r.dg[u.rows, :] * r.z[u.rows, st * 128 : st * 128 + 128]
             cf = r.bc[u.rows, st * 512 + 128 : st * 512 + 256]
             cb = r.bc[u.rows, st * 512 + 384 : st * 512 + 512]
             if b > 0:
-                r.ds[st * 2, b - 1] = mm_fine(cf, jnp.exp(u.p) * dy, TN, 2)
+                backs[b - 1] = mm_fine(cf, jnp.exp(u.p) * dy, TN, 2)
             if b < ns - 1:
-                r.ds[st * 2 + 1, b + 1] = mm_fine(cb, jnp.exp(u.total - u.q) * dy, TN, 2)
-        for b in range(ns - 3, -1, -1):
-            r.ds[st * 2, b] += jnp.exp(units[st][b + 1].total) * r.ds[st * 2, b + 1]
-        for b in range(2, ns):
-            r.ds[st * 2 + 1, b] += jnp.exp(units[st][b - 1].total) * r.ds[st * 2 + 1, b - 1]
+                aheads[b + 1] = mm_fine(cb, jnp.exp(u.total - u.q) * dy, TN, 2)
+        yield
+        for b in range(ns - 2, -1, -1):
+            if b < ns - 2:
+                backs[b] = backs[b] + jnp.exp(units[st][b + 1].total) * backs[b + 1]
+            r.ds[st * 2, b] = backs[b]
+        for b in range(1, ns):
+            if b > 1:
+                aheads[b] = aheads[b] + jnp.exp(units[st][b - 1].total) * aheads[b - 1]
+            r.ds[st * 2 + 1, b] = aheads[b]
+
     d_steps = [jnp.zeros((SYM, LANES), F32)] * 2
     d_decays = [jnp.zeros((SYM, LANES), F32)] * 2
     d_tab = 0.0
@@ -394,9 +411,7 @@
         base = st * WIDE
         x = [r.x[u.rows, st * 256 + w * 128 : st * 256 + w * 128 + 128] for w in range(2)]
         dgv = r.dg[u.rows, :]
-        pz = u.pre(ZZ, 128)
-        sz = sigmoid(pz)
-        dy = dgv * (pz * sz)
+        dy = dgv * r.z[u.rows, st * 128 : st * 128 + 128]
         dyr = dy.astype(BF16)
         dyw = dyr.astype(F32)
         dy0, dy1 = u.by_head(dyr)
@@ -478,20 +493,15 @@
             mixes.append(row)
             step_part = step_part + du * x[w]
             dx = du * u.dt + dy * u.skip
-            px = u.pre((XF, XB)[w], 128)
-            sx = sigmoid(px)
-            col = base + (XF, XB)[w]
-            r.dpre[u.rows, col : col + 128] = (dx * (sx * (1.0 + px * (1.0 - sx)))).astype(BF16)
+            col = (XF, XB)[w]
+            grad = dx * u.slope(col, 128)
+            r.dpre[u.rows, base + col : base + col + 128] = grad.astype(BF16)
             col = (BCF, BCB)[w]
             for i, grad in enumerate((d_b, d_c)):
-                pb = u.pre(col + 128 * i, 128)
-                sb = sigmoid(pb)
                 at = base + col + 128 * i
-                r.dpre[u.rows, at : at + 128] = (
-                    grad * (sb * (1.0 + pb * (1.0 - sb)))
-                ).astype(BF16)
+                r.dpre[u.rows, at : at + 128] = (grad * u.slope(col + 128 * i, 128)).astype(BF16)
         yield
-        d_z = dgv * y * (sz * (1.0 + pz * (1.0 - sz)))
+        d_z = dgv * y * u.slope(ZZ, 128)
         r.dpre[u.rows, base + ZZ : base + ZZ + 128] = d_z.astype(BF16)
         inc = r.inc[:, u.rows]
         exc = r.exc[:, u.rows]
@@ -509,7 +519,8 @@
 
     for b0 in range(0, ns, GROUP_BACK):
         last = min(b0 + GROUP_BACK, ns)
-        together(body(st, b) for b in range(b0, last) for st in range(2))
+        bodies = [body(st, b) for b in range(b0, last) for st in range(2)]
+        together([spread(0), spread(1)] * (b0 == 0) + bodies)
         span = slice(b0 * BLOCK, last * BLOCK)
         d_tab = d_tab + mm(r.sym[:, span], r.dpre[span, :], NN)
     mid = SYM * (conv - 1)
@@ -595,8 +606,9 @@
             pltpu.VMEM((256, length), F32),
             pltpu.VMEM((64, length), F32),
             pltpu.VMEM((length, 64), BF16),
+            pltpu.VMEM((length, 2 * WIDE), F32),
         ],
-        compiler_params=params(8),
+        compiler_params=params(12),
         cost_estimate=pl.CostEstimate(
             flops=5 * 10**9, transcendentals=0, bytes_accessed=8 * LANES * length
         ),

time: 49.6 us -> 49.6 us (level)
    pallas_call x1, Pallas kernels: 3.53 us -> 4.18 us  [call_forward(): pl.pallas_call(functools.partial(forward_kernel, ns=ns, conv=conv), out_s...]
    ppermute x11, waiting for transfers between devices: 3.64 us -> 2.99 us  [across(): return lax.ppermute(x, ('head', 'sub'), pairs)]
  transfers between devices with their start and end apart: 20 -> 20, of which waited for: 7 -> 8; matrix products, arithmetic and copies ran while one was open for 6% -> 6% of each run, Pallas kernels for 26% -> 27%
where the time goes in v6:
time: 49.6 us; the launch traced here: 49.3 us
  starting transfers between devices  21.4 us (43%)
  Pallas kernels  15.4 us (31%)
  waiting for transfers between devices  6.45 us (13%)
  other arithmetic  3.73 us (8%)
  local copies, waits for them, and re-layouts  1.51 us (3%)
  between operations  0.75 us (2%)
    ppermute x6, starting transfers between devices, around(): lax.ppermute(x, axis, [(i, i ^ k) for i in range(n)])  9.34 us
    ppermute x11, starting transfers between devices, across(): return lax.ppermute(x, ('head', 'sub'), pairs)  6.05 us
    ppermute x3, starting transfers between devices, by_channel(): hop = lambda x, k: lax.ppermute(x, 'seq', [(i, i ^ k) for i in range(ns)])  6.05 us
    pallas_call x1, Pallas kernels, call_backward(): pl.pallas_call(functools.partial(backward_kernel, ns=ns, nq=len(cots), co...  4.88 us
    pallas_call x1, Pallas kernels, call_forward(): pl.pallas_call(functools.partial(forward_kernel, ns=ns, conv=conv), out_s...  4.18 us
    pallas_call x1, Pallas kernels, call_weight(): pl.pallas_call(functools.partial(weight_kernel, ns=ns, nh=nh, nc=nc), out...  3.3 us
    ppermute x6, waiting for transfers between devices, around(): lax.ppermute(x, axis, [(i, i ^ k) for i in range(n)])  3.09 us
    ppermute x11, waiting for transfers between devices, across(): return lax.ppermute(x, ('head', 'sub'), pairs)  2.99 us
  transfers between devices with their start and end apart: 20, of which 8 were waited for; matrix products, arithmetic and copies ran while one was open for 6% of the time, Pallas kernels for 27%

profile of v6, /device:TPU:0, one launch (start us, length us, event | category | flops | bytes accessed | tf_op | source)
XLA Modules:
  0.0 49.3 jit_solution(7051937108498226950)
XLA Ops:
  0.6 0.7 %convert_bitcast_fusion = bf16[1,128]{1,0:T(2,128)(2,1)S(1)} fusion(s32[128]{0:T(128)} %param.11), kind=kLoop, calls=%fused_computation.42 | loop fusion | flops 128 | bytes 768 | tf_op jit(solution)/shard_map/reshape | solution.py:787
  1.3 0.8 %fusion.1.refs_0_ = bf16[144,256]{1,0:T(8,128)(2,1)S(1)} fusion(bf16[1,128]{1,0:T(2,128)(2,1)S(1)} %convert_bitcast_fusion, bf16[128,256]{1,0:T(8,128)(2,1)} %param.21), kind=kLoop, calls=%fused_computation.3 | loop fusion | flops 221184 | bytes 139520 | tf_op jit(solution)/shard_map/concatenate | solution.py:788
  2.1 3.0 %collective-permute-start = (bf16[144,256]{1,0:T(8,128)(2,1)S(1)}, bf16[144,256]{1,0:T(8,128)(2,1)S(1)}, u32[]{:S(2)}, u32[]{:S(2)}) collective-permute-start(bf16[144,256]{1,0:T(8,128)(2,1)S(1)} %fusion.1.refs_0_), channel_id=1, source_target_pairs={{0,4},{4,0},{8,12},{12,8},{1,5},{5,1},{9,13},{13,9},{2,6},{6,2},{1... | collective-permute-start | bytes 221192 | tf_op jit(solution)/shard_map/ppermute | solution.py:767
  5.2 2.6 %collective-permute-start.1 = (bf16[144,256]{1,0:T(8,128)(2,1)S(1)}, bf16[144,256]{1,0:T(8,128)(2,1)S(1)}, u32[]{:S(2)}, u32[]{:S(2)}) collective-permute-start(bf16[144,256]{1,0:T(8,128)(2,1)S(1)} %fusion.1.refs_0_), channel_id=1, source_target_pairs={{0,8},{4,12},{8,0},{12,4},{1,9},{5,13},{9,1},{13,5},{2,10},{6,14},... | collective-permute-start | bytes 221192 | tf_op jit(solution)/shard_map/ppermute | solution.py:767
  7.8 0.7 %reshape.16 = bf16[10,1024]{1,0:T(8,128)(2,1)S(1)} reshape(bf16[5,2,1024]{2,1,0:T(2,128)(2,1)} %param.13) | data formatting | bytes 40960 | tf_op jit(solution)/shard_map/reshape | solution.py:590
  8.5 0.7 %pad_maximum_fusion.1.refs_0_ = bf16[14,1024]{1,0:T(8,128)(2,1)S(1)} fusion(bf16[4,1024]{1,0:T(4,128)(2,1)} %param.16, bf16[10,1024]{1,0:T(8,128)(2,1)S(1)} %reshape.16), kind=kLoop, calls=%fused_computation.7 | loop fusion | flops 57344 | bytes 57344 | tf_op jit(solution)/shard_map/concatenate | solution.py:590
  9.2 0.7 %pad_maximum_fusion.3.refs_1_ = bf16[9,2,128]{2,1,0:T(2,128)(2,1)S(1)} fusion(bf16[4,2,128]{2,1,0:T(2,128)(2,1)} %param.17, bf16[5,2,128]{2,1,0:T(2,128)(2,1)} %param.14), kind=kLoop, calls=%fused_computation.10 | loop fusion | flops 2304 | bytes 9216 | tf_op jit(solution)/shard_map/concatenate | solution.py:591
  10.0 0.7 %pad_maximum_fusion.4.refs_2_ = f32[7,16]{1,0:T(8,128)S(1)} fusion(f32[1,16]{1,0:T(1,128)} %bitcast.15, f32[1,16]{1,0:T(1,128)} %bitcast.16, f32[5,16]{1,0:T(8,128)} %param.15), kind=kLoop, calls=%fused_computation.11 | loop fusion | flops 224 | bytes 896 | tf_op jit(solution)/shard_map/concatenate | solution.py:592
  10.8 0.7 %copy-done.1 = s32[5]{0:T(128)S(1)} copy-done((s32[5]{0:T(128)S(1)}, s32[5]{0:T(128)}, u32[]{:S(2)}) %copy-start.1) | copy-done | bytes 44
  11.4 0.8 %tables.1 = (f32[32,128]{1,0:T(8,128)S(1)}, f32[16,256]{1,0:T(8,128)S(1)}, f32[8,128]{1,0:T(8,128)S(1)}, f32[8,128]{1,0:T(8,128)S(1)}, bf16[128,1792]{1,0:T(8,12...) custom-call(s32[15]{0:T(128)S(1)} %concatenate.18.scalars, s32[5]{0:T(128)S(1)} %copy-done.1, ...), custom_call_target="tpu_custom_call" | custom-call | flops 2000000000 | bytes 1000000 | tf_op jit(solution)/shard_map/tables/pallas_call | solution.py:578
  12.2 1.8 %collective-permute-done.2.refs_3_ = bf16[144,256]{1,0:T(8,128)(2,1)S(1)} collective-permute-done((bf16[144,256]{1,0:T(8,128)(2,1)S(1)}, bf16[144,256]{1,0:T(8,128)(2,1)S(1)}, u32[]{:S(2)}, u32[]{:S(2)}) %collective-permute-start.2) | collective-permute-done | bytes 73760 | tf_op jit(solution)/shard_map/ppermute | solution.py:767
  14.1 1.6 %collective-permute-start.3 = (bf16[4,128,256]{2,1,0:T(8,128)(2,1)S(1)}, bf16[4,128,256]{2,1,0:T(8,128)(2,1)S(1)}, u32[]{:S(2)}, u32[]{:S(2)}) collective-permute-start(bf16[4,128,256]{2,1,0:T(8,128)(2,1)S(1)} %pad_maximum_fusion.refs_4_.refs_8_), channel_id=1, source_target_pairs={{0,2},{1,3},{2,0},{3,1},{4,6},{5,7},{6,4},{7,5},{8,10},{9,11},{10,... | collective-permute-start | bytes 786440 | tf_op jit(solution)/shard_map/ppermute | solution.py:776
  15.7 4.2 %mix_forward.1 = (bf16[128,512]{1,0:T(8,128)(2,1)S(1)}, f32[8,512]{1,0:T(8,128)S(1)}, f32[8,512]{1,0:T(8,128)S(1)}, f32[8,512]{1,0:T(8,128)S(1)}, bf16[64,512]{1...) custom-call(s32[15]{0:T(128)S(1)} %concatenate.18.scalars, ...), custom_call_target="tpu_custom_call" | custom-call | flops 5000000000 | bytes 524288 | tf_op jit(solution)/shard_map/mix_forward/pallas_call | solution.py:600
  19.9 0.7 %collective-permute-done.3.refs_6_.refs_10_ = bf16[4,128,256]{2,1,0:T(8,128)(2,1)S(1)} collective-permute-done((bf16[4,128,256]{2,1,0:T(8,128)(2,1)S(1)}, bf16[4,128,256]{2,1,0:T(8,128)(2,1)S(1)}, u32[]{:S(2)}, u32[]{:S(2)}) %collective-permute-start.3) | collective-permute-done | bytes 262176 | tf_op jit(solution)/shard_map/ppermute | solution.py:776
  20.6 1.1 %collective-permute-start.12 = (bf16[128,512]{1,0:T(8,128)(2,1)S(1)}, bf16[128,512]{1,0:T(8,128)(2,1)S(1)}, u32[]{:S(2)}, u32[]{:S(2)}) collective-permute-start(bf16[128,512]{1,0:T(8,128)(2,1)S(1)} %get-tuple-element.45.refs_0_), channel_id=1, source_target_pairs={{0,4},{4,0},{8,12},{12,8},{1,5},{5,1},{9,13},{13,9},{2,6},{6,2},{1... | collective-permute-start | bytes 393224 | tf_op jit(solution)/shard_map/ppermute | solution.py:804
  21.6 2.4 %collective-permute-start.13 = (bf16[128,512]{1,0:T(8,128)(2,1)S(1)}, bf16[128,512]{1,0:T(8,128)(2,1)S(1)}, u32[]{:S(2)}, u32[]{:S(2)}) collective-permute-start(bf16[128,512]{1,0:T(8,128)(2,1)S(1)} %get-tuple-element.45.refs_0_), channel_id=1, source_target_pairs={{0,8},{4,12},{8,0},{12,4},{1,9},{5,13},{9,1},{13,5},{2,10},{6,14},... | collective-permute-start | bytes 393224 | tf_op jit(solution)/shard_map/ppermute | solution.py:804
  24.0 4.9 %mix_backward.1 = f32[8,640]{1,0:T(8,128)S(1)} custom-call(s32[15]{0:T(128)S(1)} %concatenate.18.scalars, f32[32,128]{1,0:T(8,128)S(1)} %get-tuple-element.38.refs_7_.refs_0_, f32[16,256]{1,0:T(8,128)S(1)} %get-tuple-element.39.refs_1_, f32[8,128]{1,0:T(8,128)S(1)} %get-tuple-element.40.refs_2_, f32[8,128]{1,0:T(8,128)S(1)} %get-tuple-element.41.refs_3_, ...), custom_call_target="tpu_custom_call" | custom-call | flops 6000000000 | bytes 524288 | tf_op jit(solution)/shard_map/mix_backward/pallas_call | solution.py:622
  28.9 0.4 collective-permute-done.12.refs_1_
  29.3 2.6 %collective-permute-start.14 = (bf16[128,512]{1,0:T(8,128)(2,1)S(1)}, bf16[128,512]{1,0:T(8,128)(2,1)S(1)}, u32[]{:S(2)}, u32[]{:S(2)}) collective-permute-start(bf16[128,512]{1,0:T(8,128)(2,1)S(1)} %collective-permute-done.13.refs_2_), channel_id=1, source_target_pairs={{0,4},{4,0},{8,12},{12,8},{1,5},{5,1},{9,13},{13,9},{2,6},{6,2},{1... | collective-permute-start | bytes 393224 | tf_op jit(solution)/shard_map/ppermute | solution.py:804
  31.9 1.5 %collective-permute-start.7 = (f32[8,256]{1,0:T(8,128)S(1)}, f32[8,256]{1,0:T(8,128)S(1)}, u32[]{:S(2)}, u32[]{:S(2)}) collective-permute-start(f32[8,256]{1,0:T(8,128)S(1)} %slice.35), channel_id=1, source_target_pairs={{0,2},{1,3},{2,0},{3,1},{4,6},{5,7},{6,4},{7,5},{8,10},{9,11},{10,... | collective-permute-start | bytes 24584 | tf_op jit(solution)/shard_map/ppermute | solution.py:776
  33.4 0.4 collective-permute-start.8
  34.2 1.3 %collective-permute-done.7 = f32[8,256]{1,0:T(8,128)S(1)} collective-permute-done((f32[8,256]{1,0:T(8,128)S(1)}, f32[8,256]{1,0:T(8,128)S(1)}, u32[]{:S(2)}, u32[]{:S(2)}) %collective-permute-start.7) | collective-permute-done | bytes 8224 | tf_op jit(solution)/shard_map/ppermute | solution.py:776
  35.5 0.5 %collective-permute-start.18 = (bf16[128,512]{1,0:T(8,128)(2,1)S(1)}, bf16[128,512]{1,0:T(8,128)(2,1)S(1)}, u32[]{:S(2)}, u32[]{:S(2)}) collective-permute-start(bf16[128,512]{1,0:T(8,128)(2,1)S(1)} %collective-permute-done.14.refs_3_), channel_id=1, source_target_pairs={{0,1},{1,0},{2,3},{3,2},{4,5},{5,4},{6,7},{7,6},{8,9},{9,8},{10,11... | collective-permute-start | bytes 393224 | tf_op jit(solution)/shard_map/ppermute | solution.py:776
  36.0 0.4 collective-permute-done.8
  36.4 0.4 collective-permute-done.16.refs_5_
  37.1 0.9 %layer_out.1 = (f32[128,256]{1,0:T(8,128)S(1)}, f32[128,256]{1,0:T(8,128)S(1)}) custom-call(s32[15]{0:T(128)S(1)} %concatenate.18.scalars, bf16[128,512]{1,0:T(8,128)(2,1)S(1)} %get-tuple-element.45.refs_0_, bf16[128,512]{1,0:T(8,128)(2,1)S(1)} %collective-permute-done.12.refs_1_, bf16[128,512]{1,0:T(8,128)(2,1)S(1)} %collective-permute-done.13.refs_2_, ...), custom_call_target="tpu_custom_call" | custom-call | tf_op jit(solution)/shard_map/layer_out/pallas_call | solution.py:660
  38.0 1.6 %collective-permute-start.19 = (f32[128,256]{1,0:T(8,128)S(1)}, f32[128,256]{1,0:T(8,128)S(1)}, u32[]{:S(2)}, u32[]{:S(2)}) collective-permute-start(f32[128,256]{1,0:T(8,128)S(1)} %get-tuple-element.64), channel_id=1, source_target_pairs={{0,2},{1,3},{2,0},{3,1},{4,6},{5,7},{6,4},{7,5},{8,10},{9,11},{10,... | collective-permute-start | bytes 393224 | tf_op jit(solution)/shard_map/ppermute | solution.py:776
  39.6 2.6 %collective-permute-start.10 = (f32[8,1024]{1,0:T(8,128)S(1)}, f32[8,1024]{1,0:T(8,128)S(1)}, u32[]{:S(2)}, u32[]{:S(2)}) collective-permute-start(f32[8,1024]{1,0:T(8,128)S(1)} %pad_maximum_fusion.2.refs_0_), channel_id=1, source_target_pairs={{0,8},{4,12},{8,0},{12,4},{1,9},{5,13},{9,1},{13,5},{2,10},{6,14},... | collective-permute-start | bytes 98312 | tf_op jit(solution)/shard_map/ppermute | solution.py:767
  42.2 0.9 %collective-permute-start.11 = (f32[8,1024]{1,0:T(8,128)S(1)}, f32[8,1024]{1,0:T(8,128)S(1)}, u32[]{:S(2)}, u32[]{:S(2)}) collective-permute-start(f32[8,1024]{1,0:T(8,128)S(1)} %pad_maximum_fusion.2.refs_0_), channel_id=1, source_target_pairs={{0,12},{4,8},{8,4},{12,0},{1,13},{5,9},{9,5},{13,1},{2,14},{6,10},... | collective-permute-start | bytes 98312 | tf_op jit(solution)/shard_map/ppermute | solution.py:767
  43.3 3.3 %weight_grad.1 = (f32[1024,1024]{1,0:T(8,128)}, f32[8,128]{1,0:T(8,128)S(1)}) custom-call(s32[15]{0:T(128)S(1)} %concatenate.18.scalars, bf16[128,512]{1,0:T(8,128)(2,1)S(1)} %get-tuple-element.45.refs_0_, bf16[128,512]{1,0:T(8,128)(2,1)S(1)} %collective-permute-done.12.refs_1_, bf16[128,512]{1,0:T(8,128)(2,1)S(1)} %collective-permute-done.13.refs_2_, ...), custom_call_target="tpu_custom_call" | custom-call | flops 1073741824 | bytes 6291456 | tf_op jit(solution)/shard_map/weight_grad/pallas_call | solution.py:700
  46.6 1.3 %collective-permute-done.11.refs_3_ = f32[8,1024]{1,0:T(8,128)S(1)} collective-permute-done((f32[8,1024]{1,0:T(8,128)S(1)}, f32[8,1024]{1,0:T(8,128)S(1)}, u32[]{:S(2)}, u32[]{:S(2)}) %collective-permute-start.11) | collective-permute-done | bytes 32800 | tf_op jit(solution)/shard_map/ppermute | solution.py:767
  47.9 1.3 %place_grads.1 = (bf16[128,256]{1,0:T(8,128)(2,1)}, f32[5,2,1024]{2,1,0:T(2,128)}, f32[5,2,128]{2,1,0:T(2,128)}, f32[5,16]{1,0:T(8,128)}) custom-call(s32[15]{0:T(128)S(1)} %concatenate.18.scalars, f32[8,1024]{1,0:T(8,128)S(1)} %pad_maximum_fusion.2.refs_0_, f32[8,1024]{1,0:T(8,128)S(1)} %collective-permute-done.9.refs_1_, ...), custom_call_target="tpu_custom_call" | custom-call | tf_op jit(solution)/shard_map/place_grads/pallas_call | solution.py:752
  (38 shorter events, 1.0 us)
Async XLA Ops:
  2.1 11.9 %collective-permute-start = (bf16[144,256]{1,0:T(8,128)(2,1)S(1)}, bf16[144,256]{1,0:T(8,128)(2,1)S(1)}, u32[]{:S(2)}, u32[]{:S(2)}) collective-permute-start(bf16[144,256]{1,0:T(8,128)(2,1)S(1)} %fusion.1.refs_0_), channel_id=1, source_target_pairs={{0,4},{4,0},{8,12},{12,8},{1,5},{5,1},{9,13},{13,9},{2,6},{6,2},{1... | collective-permute-start | bytes 221192 | tf_op jit(solution)/shard_map/ppermute | solution.py:767
  5.2 8.9 %collective-permute-start.1 = (bf16[144,256]{1,0:T(8,128)(2,1)S(1)}, bf16[144,256]{1,0:T(8,128)(2,1)S(1)}, u32[]{:S(2)}, u32[]{:S(2)}) collective-permute-start(bf16[144,256]{1,0:T(8,128)(2,1)S(1)} %fusion.1.refs_0_), channel_id=1, source_target_pairs={{0,8},{4,12},{8,0},{12,4},{1,9},{5,13},{9,1},{13,5},{2,10},{6,14},... | collective-permute-start | bytes 221192 | tf_op jit(solution)/shard_map/ppermute | solution.py:767
  7.7 6.3 %collective-permute-start.2 = (bf16[144,256]{1,0:T(8,128)(2,1)S(1)}, bf16[144,256]{1,0:T(8,128)(2,1)S(1)}, u32[]{:S(2)}, u32[]{:S(2)}) collective-permute-start(bf16[144,256]{1,0:T(8,128)(2,1)S(1)} %fusion.1.refs_0_), channel_id=1, source_target_pairs={{0,12},{4,8},{8,4},{12,0},{1,13},{5,9},{9,5},{13,1},{2,14},{6,10},... | collective-permute-start | bytes 221192 | tf_op jit(solution)/shard_map/ppermute | solution.py:767
  10.8 0.7 %copy-start.1 = (s32[5]{0:T(128)S(1)}, s32[5]{0:T(128)}, u32[]{:S(2)}) copy-start(s32[5]{0:T(128)} %basemap.1) | copy-start | bytes 64
  11.4 2.6 %copy-start.2 = (bf16[128,256]{1,0:T(8,128)(2,1)S(1)}, bf16[128,256]{1,0:T(8,128)(2,1)}, u32[]{:S(2)}) copy-start(bf16[128,256]{1,0:T(8,128)(2,1)} %param.21) | copy-start | bytes 196612
  14.1 6.4 %collective-permute-start.3 = (bf16[4,128,256]{2,1,0:T(8,128)(2,1)S(1)}, bf16[4,128,256]{2,1,0:T(8,128)(2,1)S(1)}, u32[]{:S(2)}, u32[]{:S(2)}) collective-permute-start(bf16[4,128,256]{2,1,0:T(8,128)(2,1)S(1)} %pad_maximum_fusion.refs_4_.refs_8_), channel_id=1, source_target_pairs={{0,2},{1,3},{2,0},{3,1},{4,6},{5,7},{6,4},{7,5},{8,10},{9,11},{10,... | collective-permute-start | bytes 786440 | tf_op jit(solution)/shard_map/ppermute | solution.py:776
  15.7 8.3 %collective-permute-start.4 = (bf16[4,128,256]{2,1,0:T(8,128)(2,1)S(1)}, bf16[4,128,256]{2,1,0:T(8,128)(2,1)S(1)}, u32[]{:S(2)}, u32[]{:S(2)}) collective-permute-start(bf16[4,128,256]{2,1,0:T(8,128)(2,1)S(1)} %pad_maximum_fusion.refs_4_.refs_8_), channel_id=1, source_target_pairs={{0,1},{1,0},{2,3},{3,2},{4,5},{5,4},{6,7},{7,6},{8,9},{9,8},{10,11... | collective-permute-start | bytes 786440 | tf_op jit(solution)/shard_map/ppermute | solution.py:776
  15.7 8.4 %copy-start = (bf16[1024,1024]{1,0:T(8,128)(2,1)S(1)}, bf16[1024,1024]{1,0:T(8,128)(2,1)}, u32[]{:S(2)}) copy-start(bf16[1024,1024]{1,0:T(8,128)(2,1)} %refs_8_.3) | copy-start | bytes 6291460
  20.5 3.5 %collective-permute-start.5 = (bf16[4,128,256]{2,1,0:T(8,128)(2,1)S(1)}, bf16[4,128,256]{2,1,0:T(8,128)(2,1)S(1)}, u32[]{:S(2)}, u32[]{:S(2)}) collective-permute-start(bf16[4,128,256]{2,1,0:T(8,128)(2,1)S(1)} %collective-permute-done.3.refs_6_.refs_10_), channel_id=1, source_target_pairs={{0,1},{1,0},{2,3},{3,2},{4,5},{5,4},{6,7},{7,6},{8,9},{9,8},{10,11... | collective-permute-start | bytes 786440 | tf_op jit(solution)/shard_map/ppermute | solution.py:776
  20.6 8.7 %collective-permute-start.12 = (bf16[128,512]{1,0:T(8,128)(2,1)S(1)}, bf16[128,512]{1,0:T(8,128)(2,1)S(1)}, u32[]{:S(2)}, u32[]{:S(2)}) collective-permute-start(bf16[128,512]{1,0:T(8,128)(2,1)S(1)} %get-tuple-element.45.refs_0_), channel_id=1, source_target_pairs={{0,4},{4,0},{8,12},{12,8},{1,5},{5,1},{9,13},{13,9},{2,6},{6,2},{1... | collective-permute-start | bytes 393224 | tf_op jit(solution)/shard_map/ppermute | solution.py:804
  21.6 7.6 %collective-permute-start.13 = (bf16[128,512]{1,0:T(8,128)(2,1)S(1)}, bf16[128,512]{1,0:T(8,128)(2,1)S(1)}, u32[]{:S(2)}, u32[]{:S(2)}) collective-permute-start(bf16[128,512]{1,0:T(8,128)(2,1)S(1)} %get-tuple-element.45.refs_0_), channel_id=1, source_target_pairs={{0,8},{4,12},{8,0},{12,4},{1,9},{5,13},{9,1},{13,5},{2,10},{6,14},... | collective-permute-start | bytes 393224 | tf_op jit(solution)/shard_map/ppermute | solution.py:804
  29.3 6.2 %collective-permute-start.14 = (bf16[128,512]{1,0:T(8,128)(2,1)S(1)}, bf16[128,512]{1,0:T(8,128)(2,1)S(1)}, u32[]{:S(2)}, u32[]{:S(2)}) collective-permute-start(bf16[128,512]{1,0:T(8,128)(2,1)S(1)} %collective-permute-done.13.refs_2_), channel_id=1, source_target_pairs={{0,4},{4,0},{8,12},{12,8},{1,5},{5,1},{9,13},{13,9},{2,6},{6,2},{1... | collective-permute-start | bytes 393224 | tf_op jit(solution)/shard_map/ppermute | solution.py:804
  31.9 2.2 %collective-permute-start.6 = (f32[8,640]{1,0:T(8,128)S(1)}, f32[8,640]{1,0:T(8,128)S(1)}, u32[]{:S(2)}, u32[]{:S(2)}) collective-permute-start(f32[8,640]{1,0:T(8,128)S(1)} %mix_backward.1), channel_id=1, source_target_pairs={{0,1},{1,0},{2,3},{3,2},{4,5},{5,4},{6,7},{7,6},{8,9},{9,8},{10,11... | collective-permute-start | bytes 61448 | tf_op jit(solution)/shard_map/ppermute | solution.py:776
  31.9 3.7 %collective-permute-start.7 = (f32[8,256]{1,0:T(8,128)S(1)}, f32[8,256]{1,0:T(8,128)S(1)}, u32[]{:S(2)}, u32[]{:S(2)}) collective-permute-start(f32[8,256]{1,0:T(8,128)S(1)} %slice.35), channel_id=1, source_target_pairs={{0,2},{1,3},{2,0},{3,1},{4,6},{5,7},{6,4},{7,5},{8,10},{9,11},{10,... | collective-permute-start | bytes 24584 | tf_op jit(solution)/shard_map/ppermute | solution.py:776
  33.4 3.1 %collective-permute-start.8 = (f32[8,256]{1,0:T(8,128)S(1)}, f32[8,256]{1,0:T(8,128)S(1)}, u32[]{:S(2)}, u32[]{:S(2)}) collective-permute-start(f32[8,256]{1,0:T(8,128)S(1)} %slice.35), channel_id=1, source_target_pairs={{0,3},{1,2},{2,1},{3,0},{4,7},{5,6},{6,5},{7,4},{8,11},{9,10},{10,... | collective-permute-start | bytes 24584 | tf_op jit(solution)/shard_map/ppermute | solution.py:776
  33.7 2.7 %collective-permute-start.15 = (bf16[128,512]{1,0:T(8,128)(2,1)S(1)}, bf16[128,512]{1,0:T(8,128)(2,1)S(1)}, u32[]{:S(2)}, u32[]{:S(2)}) collective-permute-start(bf16[128,512]{1,0:T(8,128)(2,1)S(1)} %get-tuple-element.45.refs_0_), channel_id=1, source_target_pairs={{0,1},{1,0},{2,3},{3,2},{4,5},{5,4},{6,7},{7,6},{8,9},{9,8},{10,11... | collective-permute-start | bytes 393224 | tf_op jit(solution)/shard_map/ppermute | solution.py:776
  34.0 2.9 %collective-permute-start.17 = (bf16[128,512]{1,0:T(8,128)(2,1)S(1)}, bf16[128,512]{1,0:T(8,128)(2,1)S(1)}, u32[]{:S(2)}, u32[]{:S(2)}) collective-permute-start(bf16[128,512]{1,0:T(8,128)(2,1)S(1)} %collective-permute-done.13.refs_2_), channel_id=1, source_target_pairs={{0,1},{1,0},{2,3},{3,2},{4,5},{5,4},{6,7},{7,6},{8,9},{9,8},{10,11... | collective-permute-start | bytes 393224 | tf_op jit(solution)/shard_map/ppermute | solution.py:776
  35.5 1.3 %collective-permute-start.16 = (bf16[128,512]{1,0:T(8,128)(2,1)S(1)}, bf16[128,512]{1,0:T(8,128)(2,1)S(1)}, u32[]{:S(2)}, u32[]{:S(2)}) collective-permute-start(bf16[128,512]{1,0:T(8,128)(2,1)S(1)} %collective-permute-done.12.refs_1_), channel_id=1, source_target_pairs={{0,1},{1,0},{2,3},{3,2},{4,5},{5,4},{6,7},{7,6},{8,9},{9,8},{10,11... | collective-permute-start | bytes 393224 | tf_op jit(solution)/shard_map/ppermute | solution.py:776
  35.5 1.5 %collective-permute-start.18 = (bf16[128,512]{1,0:T(8,128)(2,1)S(1)}, bf16[128,512]{1,0:T(8,128)(2,1)S(1)}, u32[]{:S(2)}, u32[]{:S(2)}) collective-permute-start(bf16[128,512]{1,0:T(8,128)(2,1)S(1)} %collective-permute-done.14.refs_3_), channel_id=1, source_target_pairs={{0,1},{1,0},{2,3},{3,2},{4,5},{5,4},{6,7},{7,6},{8,9},{9,8},{10,11... | collective-permute-start | bytes 393224 | tf_op jit(solution)/shard_map/ppermute | solution.py:776
  38.0 10.0 %collective-permute-start.19 = (f32[128,256]{1,0:T(8,128)S(1)}, f32[128,256]{1,0:T(8,128)S(1)}, u32[]{:S(2)}, u32[]{:S(2)}) collective-permute-start(f32[128,256]{1,0:T(8,128)S(1)} %get-tuple-element.64), channel_id=1, source_target_pairs={{0,2},{1,3},{2,0},{3,1},{4,6},{5,7},{6,4},{7,5},{8,10},{9,11},{10,... | collective-permute-start | bytes 393224 | tf_op jit(solution)/shard_map/ppermute | solution.py:776
  39.6 7.0 %collective-permute-start.10 = (f32[8,1024]{1,0:T(8,128)S(1)}, f32[8,1024]{1,0:T(8,128)S(1)}, u32[]{:S(2)}, u32[]{:S(2)}) collective-permute-start(f32[8,1024]{1,0:T(8,128)S(1)} %pad_maximum_fusion.2.refs_0_), channel_id=1, source_target_pairs={{0,8},{4,12},{8,0},{12,4},{1,9},{5,13},{9,1},{13,5},{2,10},{6,14},... | collective-permute-start | bytes 98312 | tf_op jit(solution)/shard_map/ppermute | solution.py:767
  42.2 5.7 %collective-permute-start.11 = (f32[8,1024]{1,0:T(8,128)S(1)}, f32[8,1024]{1,0:T(8,128)S(1)}, u32[]{:S(2)}, u32[]{:S(2)}) collective-permute-start(f32[8,1024]{1,0:T(8,128)S(1)} %pad_maximum_fusion.2.refs_0_), channel_id=1, source_target_pairs={{0,12},{4,8},{8,4},{12,0},{1,13},{5,9},{9,5},{13,1},{2,14},{6,10},... | collective-permute-start | bytes 98312 | tf_op jit(solution)/shard_map/ppermute | solution.py:767
  43.2 4.8 %collective-permute-start.9 = (f32[8,1024]{1,0:T(8,128)S(1)}, f32[8,1024]{1,0:T(8,128)S(1)}, u32[]{:S(2)}, u32[]{:S(2)}) collective-permute-start(f32[8,1024]{1,0:T(8,128)S(1)} %pad_maximum_fusion.2.refs_0_), channel_id=1, source_target_pairs={{0,4},{4,0},{8,12},{12,8},{1,5},{5,1},{9,13},{13,9},{2,6},{6,2},{1... | collective-permute-start | bytes 98312 | tf_op jit(solution)/shard_map/ppermute | solution.py:767

commit v7 on v5

--- a/solution.py
+++ b/solution.py
@@ -12,7 +12,7 @@
 SYM = 8
 F32 = jnp.float32
 BF16 = jnp.bfloat16
-GROUP = 2
+GROUP = 1
 GROUP_BACK = 4
 NN = (((1,), (0,)), ((), ()))
 NT = (((1,), (1,)), ((), ()))
@@ -371,20 +371,28 @@
             k * BLOCK : (k + 1) * BLOCK
         ]
     units = [[Unit(r, tabs_ref, st, b, ns) for b in range(ns)] for st in range(2)]
-    for st in range(2):
+
+    def spread(st):
+        backs, aheads = {}, {}
         for b in range(ns):
             u = units[st][b]
             dy = r.dg[u.rows, :] * u.act(ZZ, 128)
             cf = r.bc[u.rows, st * 512 + 128 : st * 512 + 256]
             cb = r.bc[u.rows, st * 512 + 384 : st * 512 + 512]
             if b > 0:
-                r.ds[st * 2, b - 1] = mm_fine(cf, jnp.exp(u.p) * dy, TN, 2)
+                backs[b - 1] = mm_fine(cf, jnp.exp(u.p) * dy, TN, 2)
             if b < ns - 1:
-                r.ds[st * 2 + 1, b + 1] = mm_fine(cb, jnp.exp(u.total - u.q) * dy, TN, 2)
-        for b in range(ns - 3, -1, -1):
-            r.ds[st * 2, b] += jnp.exp(units[st][b + 1].total) * r.ds[st * 2, b + 1]
-        for b in range(2, ns):
-            r.ds[st * 2 + 1, b] += jnp.exp(units[st][b - 1].total) * r.ds[st * 2 + 1, b - 1]
+                aheads[b + 1] = mm_fine(cb, jnp.exp(u.total - u.q) * dy, TN, 2)
+        yield
+        for b in range(ns - 2, -1, -1):
+            if b < ns - 2:
+                backs[b] = backs[b] + jnp.exp(units[st][b + 1].total) * backs[b + 1]
+            r.ds[st * 2, b] = backs[b]
+        for b in range(1, ns):
+            if b > 1:
+                aheads[b] = aheads[b] + jnp.exp(units[st][b - 1].total) * aheads[b - 1]
+            r.ds[st * 2 + 1, b] = aheads[b]
+
     d_steps = [jnp.zeros((SYM, LANES), F32)] * 2
     d_decays = [jnp.zeros((SYM, LANES), F32)] * 2
     d_tab = 0.0
@@ -509,7 +517,8 @@
 
     for b0 in range(0, ns, GROUP_BACK):
         last = min(b0 + GROUP_BACK, ns)
-        together(body(st, b) for b in range(b0, last) for st in range(2))
+        bodies = [body(st, b) for b in range(b0, last) for st in range(2)]
+        together([spread(0), spread(1)] * (b0 == 0) + bodies)
         span = slice(b0 * BLOCK, last * BLOCK)
         d_tab = d_tab + mm(r.sym[:, span], r.dpre[span, :], NN)
     mid = SYM * (conv - 1)
@@ -662,20 +671,20 @@
     places = QUARTERS + nh * nc
     cols = cots[0].shape[2]
     mark_ref[...] = jnp.zeros_like(mark_ref)
+    copies = []
     for n in range(ns * nc):
+        span = slice(n * LANES, (n + 1) * LANES)
         for k in range(ns):
-            at = jnp.bitwise_xor(mine, k)
-            left[n * LANES : (n + 1) * LANES, k * BLOCK : (k + 1) * BLOCK] = slices[n][
-                :, pl.ds(pl.multiple_of(at * BLOCK, BLOCK), BLOCK)
-            ]
-    copies = []
-    for q in range(nh * nc):
-        total = mm(left[...], cots[q][...].reshape(ns * BLOCK, cols), NN)
-        for n in range(ns * nc):
-            at = pl.multiple_of(scalars[places + n] * LANES, LANES)
-            buf[q, pl.ds(at, LANES), :] = total[n * LANES : (n + 1) * LANES]
-        at = pl.multiple_of(scalars[QUARTERS + q] * cols, LANES)
-        copy = pltpu.make_async_copy(buf.at[q], out_ref.at[:, pl.ds(at, cols)], sems.at[q])
+            at = pl.multiple_of(jnp.bitwise_xor(mine, k) * BLOCK, BLOCK)
+            left[span, k * BLOCK : (k + 1) * BLOCK] = slices[n][:, pl.ds(at, BLOCK)]
+        for q in range(nh * nc):
+            at = pl.multiple_of(scalars[QUARTERS + q] * cols, LANES)
+            right = cots[q][...].reshape(ns * BLOCK, cols)
+            buf[span, pl.ds(at, cols)] = mm(left[span, :], right, NN)
+        to = pl.multiple_of(scalars[places + n] * LANES, LANES)
+        copy = pltpu.make_async_copy(
+            buf.at[pl.ds(n * LANES, LANES), :], out_ref.at[pl.ds(to, LANES), :], sems.at[n]
+        )
         copy.start()
         copies.append(copy)
     for copy in copies:
@@ -695,8 +704,8 @@
         out_specs=[HBM, VMEM],
         scratch_shapes=[
             pltpu.VMEM((rows, length), BF16),
-            pltpu.VMEM((nh * nc, rows, width // (nh * nc)), F32),
-            pltpu.SemaphoreType.DMA((nh * nc,)),
+            pltpu.VMEM((rows, width), F32),
+            pltpu.SemaphoreType.DMA((ns * nc,)),
         ],
         compiler_params=params(12),
         cost_estimate=pl.CostEstimate(
@@ -790,7 +799,7 @@
     for a in heads[1:]:
         cots += [a, across(a, (0, 1), nh, nc)]
     hop = lambda x, k: lax.ppermute(x, "seq", [(i, i ^ k) for i in range(ns)])
-    direct = {k: hop(gated, k) for k in (1 << n for n in range(ns.bit_length() - 1))}
+    direct = {k: hop(gated, k) for k in (ns >> n for n in range(1, ns.bit_length()))}
     grads = call_backward(scalars, tables, cots, out_weight, kept, conv, vocab)
     direct, _ = lax.optimization_barrier((direct, grads))
     held = {0: gated, **direct}

time: 49.6 us -> 49.6 us (level)
  Pallas kernels: 15.2 us -> 14.7 us
  transfers between devices with their start and end apart: 20 -> 20, of which waited for: 7 -> 7; matrix products, arithmetic and copies ran while one was open for 6% -> 6% of each run, Pallas kernels for 26% -> 25%
where the time goes in v7:
time: 49.6 us; the launch traced here: 49.3 us
  starting transfers between devices  21.4 us (43%)
  Pallas kernels  14.7 us (30%)
  waiting for transfers between devices  7.12 us (14%)
  other arithmetic  3.73 us (8%)
  local copies, waits for them, and re-layouts  1.51 us (3%)
  between operations  0.77 us (2%)
    ppermute x6, starting transfers between devices, around(): lax.ppermute(x, axis, [(i, i ^ k) for i in range(n)])  9.34 us
    ppermute x11, starting transfers between devices, across(): return lax.ppermute(x, ('head', 'sub'), pairs)  6.05 us
    ppermute x3, starting transfers between devices, by_channel(): hop = lambda x, k: lax.ppermute(x, 'seq', [(i, i ^ k) for i in range(ns)])  6.03 us
    pallas_call x1, Pallas kernels, call_backward(): pl.pallas_call(functools.partial(backward_kernel, ns=ns, nq=len(cots), co...  5.23 us
    ppermute x11, waiting for transfers between devices, across(): return lax.ppermute(x, ('head', 'sub'), pairs)  3.67 us
    pallas_call x1, Pallas kernels, call_forward(): pl.pallas_call(functools.partial(forward_kernel, ns=ns, conv=conv), out_s...  3.49 us
    ppermute x6, waiting for transfers between devices, around(): lax.ppermute(x, axis, [(i, i ^ k) for i in range(n)])  3.44 us
    pallas_call x1, Pallas kernels, call_weight(): pl.pallas_call(functools.partial(weight_kernel, ns=ns, nh=nh, nc=nc), out...  2.96 us
  transfers between devices with their start and end apart: 20, of which 7 were waited for; matrix products, arithmetic and copies ran while one was open for 6% of the time, Pallas kernels for 25%

profile of v7, /device:TPU:0, one launch (start us, length us, event | category | flops | bytes accessed | tf_op | source)
XLA Modules:
  0.0 49.3 jit_solution(9384089777460283161)
XLA Ops:
  0.6 0.7 %convert_bitcast_fusion = bf16[1,128]{1,0:T(2,128)(2,1)S(1)} fusion(s32[128]{0:T(128)} %param.11), kind=kLoop, calls=%fused_computation.42 | loop fusion | flops 128 | bytes 768 | tf_op jit(solution)/shard_map/reshape | solution.py:784
  1.3 0.8 %fusion.1.refs_0_ = bf16[144,256]{1,0:T(8,128)(2,1)S(1)} fusion(bf16[1,128]{1,0:T(2,128)(2,1)S(1)} %convert_bitcast_fusion, bf16[128,256]{1,0:T(8,128)(2,1)} %param.21), kind=kLoop, calls=%fused_computation.3 | loop fusion | flops 221184 | bytes 139520 | tf_op jit(solution)/shard_map/concatenate | solution.py:785
  2.1 3.0 %collective-permute-start = (bf16[144,256]{1,0:T(8,128)(2,1)S(1)}, bf16[144,256]{1,0:T(8,128)(2,1)S(1)}, u32[]{:S(2)}, u32[]{:S(2)}) collective-permute-start(bf16[144,256]{1,0:T(8,128)(2,1)S(1)} %fusion.1.refs_0_), channel_id=1, source_target_pairs={{0,4},{4,0},{8,12},{12,8},{1,5},{5,1},{9,13},{13,9},{2,6},{6,2},{1... | collective-permute-start | bytes 221192 | tf_op jit(solution)/shard_map/ppermute | solution.py:764
  5.2 2.6 %collective-permute-start.1 = (bf16[144,256]{1,0:T(8,128)(2,1)S(1)}, bf16[144,256]{1,0:T(8,128)(2,1)S(1)}, u32[]{:S(2)}, u32[]{:S(2)}) collective-permute-start(bf16[144,256]{1,0:T(8,128)(2,1)S(1)} %fusion.1.refs_0_), channel_id=1, source_target_pairs={{0,8},{4,12},{8,0},{12,4},{1,9},{5,13},{9,1},{13,5},{2,10},{6,14},... | collective-permute-start | bytes 221192 | tf_op jit(solution)/shard_map/ppermute | solution.py:764
  7.8 0.7 %reshape.16 = bf16[10,1024]{1,0:T(8,128)(2,1)S(1)} reshape(bf16[5,2,1024]{2,1,0:T(2,128)(2,1)} %param.13) | data formatting | bytes 40960 | tf_op jit(solution)/shard_map/reshape | solution.py:588
  8.5 0.7 %pad_maximum_fusion.1.refs_0_ = bf16[14,1024]{1,0:T(8,128)(2,1)S(1)} fusion(bf16[4,1024]{1,0:T(4,128)(2,1)} %param.16, bf16[10,1024]{1,0:T(8,128)(2,1)S(1)} %reshape.16), kind=kLoop, calls=%fused_computation.7 | loop fusion | flops 57344 | bytes 57344 | tf_op jit(solution)/shard_map/concatenate | solution.py:588
  9.2 0.7 %pad_maximum_fusion.3.refs_1_ = bf16[9,2,128]{2,1,0:T(2,128)(2,1)S(1)} fusion(bf16[4,2,128]{2,1,0:T(2,128)(2,1)} %param.17, bf16[5,2,128]{2,1,0:T(2,128)(2,1)} %param.14), kind=kLoop, calls=%fused_computation.10 | loop fusion | flops 2304 | bytes 9216 | tf_op jit(solution)/shard_map/concatenate | solution.py:589
  10.0 0.7 %pad_maximum_fusion.4.refs_2_ = f32[7,16]{1,0:T(8,128)S(1)} fusion(f32[1,16]{1,0:T(1,128)} %bitcast.15, f32[1,16]{1,0:T(1,128)} %bitcast.16, f32[5,16]{1,0:T(8,128)} %param.15), kind=kLoop, calls=%fused_computation.11 | loop fusion | flops 224 | bytes 896 | tf_op jit(solution)/shard_map/concatenate | solution.py:590
  10.8 0.7 %copy-done.1 = s32[5]{0:T(128)S(1)} copy-done((s32[5]{0:T(128)S(1)}, s32[5]{0:T(128)}, u32[]{:S(2)}) %copy-start.1) | copy-done | bytes 44
  11.4 0.8 %tables.1 = (f32[32,128]{1,0:T(8,128)S(1)}, f32[16,256]{1,0:T(8,128)S(1)}, f32[8,128]{1,0:T(8,128)S(1)}, f32[8,128]{1,0:T(8,128)S(1)}, bf16[128,1792]{1,0:T(8,12...) custom-call(s32[15]{0:T(128)S(1)} %concatenate.18.scalars, s32[5]{0:T(128)S(1)} %copy-done.1, ...), custom_call_target="tpu_custom_call" | custom-call | flops 2000000000 | bytes 1000000 | tf_op jit(solution)/shard_map/tables/pallas_call | solution.py:576
  12.2 1.8 %collective-permute-done.2.refs_3_ = bf16[144,256]{1,0:T(8,128)(2,1)S(1)} collective-permute-done((bf16[144,256]{1,0:T(8,128)(2,1)S(1)}, bf16[144,256]{1,0:T(8,128)(2,1)S(1)}, u32[]{:S(2)}, u32[]{:S(2)}) %collective-permute-start.2) | collective-permute-done | bytes 73760 | tf_op jit(solution)/shard_map/ppermute | solution.py:764
  14.1 1.6 %collective-permute-start.3 = (bf16[4,128,256]{2,1,0:T(8,128)(2,1)S(1)}, bf16[4,128,256]{2,1,0:T(8,128)(2,1)S(1)}, u32[]{:S(2)}, u32[]{:S(2)}) collective-permute-start(bf16[4,128,256]{2,1,0:T(8,128)(2,1)S(1)} %pad_maximum_fusion.refs_4_.refs_8_), channel_id=1, source_target_pairs={{0,2},{1,3},{2,0},{3,1},{4,6},{5,7},{6,4},{7,5},{8,10},{9,11},{10,... | collective-permute-start | bytes 786440 | tf_op jit(solution)/shard_map/ppermute | solution.py:773
  15.7 3.5 %mix_forward.1 = (bf16[128,512]{1,0:T(8,128)(2,1)S(1)}, f32[8,512]{1,0:T(8,128)S(1)}, f32[8,512]{1,0:T(8,128)S(1)}, f32[8,512]{1,0:T(8,128)S(1)}, bf16[64,512]{1...) custom-call(s32[15]{0:T(128)S(1)} %concatenate.18.scalars, ...), custom_call_target="tpu_custom_call" | custom-call | flops 5000000000 | bytes 524288 | tf_op jit(solution)/shard_map/mix_forward/pallas_call | solution.py:598
  19.2 1.4 %collective-permute-done.3.refs_6_.refs_10_ = bf16[4,128,256]{2,1,0:T(8,128)(2,1)S(1)} collective-permute-done((bf16[4,128,256]{2,1,0:T(8,128)(2,1)S(1)}, bf16[4,128,256]{2,1,0:T(8,128)(2,1)S(1)}, u32[]{:S(2)}, u32[]{:S(2)}) %collective-permute-start.3) | collective-permute-done | bytes 262176 | tf_op jit(solution)/shard_map/ppermute | solution.py:773
  20.6 1.1 %collective-permute-start.12 = (bf16[128,512]{1,0:T(8,128)(2,1)S(1)}, bf16[128,512]{1,0:T(8,128)(2,1)S(1)}, u32[]{:S(2)}, u32[]{:S(2)}) collective-permute-start(bf16[128,512]{1,0:T(8,128)(2,1)S(1)} %get-tuple-element.44.refs_0_), channel_id=1, source_target_pairs={{0,4},{4,0},{8,12},{12,8},{1,5},{5,1},{9,13},{13,9},{2,6},{6,2},{1... | collective-permute-start | bytes 393224 | tf_op jit(solution)/shard_map/ppermute | solution.py:801
  21.6 2.4 %collective-permute-start.13 = (bf16[128,512]{1,0:T(8,128)(2,1)S(1)}, bf16[128,512]{1,0:T(8,128)(2,1)S(1)}, u32[]{:S(2)}, u32[]{:S(2)}) collective-permute-start(bf16[128,512]{1,0:T(8,128)(2,1)S(1)} %get-tuple-element.44.refs_0_), channel_id=1, source_target_pairs={{0,8},{4,12},{8,0},{12,4},{1,9},{5,13},{9,1},{13,5},{2,10},{6,14},... | collective-permute-start | bytes 393224 | tf_op jit(solution)/shard_map/ppermute | solution.py:801
  24.0 5.2 %mix_backward.1 = f32[8,640]{1,0:T(8,128)S(1)} custom-call(s32[15]{0:T(128)S(1)} %concatenate.18.scalars, f32[32,128]{1,0:T(8,128)S(1)} %get-tuple-element.37.refs_7_.refs_0_, f32[16,256]{1,0:T(8,128)S(1)} %get-tuple-element.38.refs_1_, f32[8,128]{1,0:T(8,128)S(1)} %get-tuple-element.39.refs_2_, f32[8,128]{1,0:T(8,128)S(1)} %get-tuple-element.40.refs_3_, ...), custom_call_target="tpu_custom_call" | custom-call | flops 6000000000 | bytes 524288 | tf_op jit(solution)/shard_map/mix_backward/pallas_call | solution.py:619
  29.3 2.6 %collective-permute-start.14 = (bf16[128,512]{1,0:T(8,128)(2,1)S(1)}, bf16[128,512]{1,0:T(8,128)(2,1)S(1)}, u32[]{:S(2)}, u32[]{:S(2)}) collective-permute-start(bf16[128,512]{1,0:T(8,128)(2,1)S(1)} %collective-permute-done.13.refs_2_), channel_id=1, source_target_pairs={{0,4},{4,0},{8,12},{12,8},{1,5},{5,1},{9,13},{13,9},{2,6},{6,2},{1... | collective-permute-start | bytes 393224 | tf_op jit(solution)/shard_map/ppermute | solution.py:801
  31.9 1.5 %collective-permute-start.7 = (f32[8,256]{1,0:T(8,128)S(1)}, f32[8,256]{1,0:T(8,128)S(1)}, u32[]{:S(2)}, u32[]{:S(2)}) collective-permute-start(f32[8,256]{1,0:T(8,128)S(1)} %slice.35), channel_id=1, source_target_pairs={{0,2},{1,3},{2,0},{3,1},{4,6},{5,7},{6,4},{7,5},{8,10},{9,11},{10,... | collective-permute-start | bytes 24584 | tf_op jit(solution)/shard_map/ppermute | solution.py:773
  33.4 0.4 collective-permute-start.8
  33.7 0.3 collective-permute-start.15
  34.2 1.3 %collective-permute-done.7 = f32[8,256]{1,0:T(8,128)S(1)} collective-permute-done((f32[8,256]{1,0:T(8,128)S(1)}, f32[8,256]{1,0:T(8,128)S(1)}, u32[]{:S(2)}, u32[]{:S(2)}) %collective-permute-start.7) | collective-permute-done | bytes 8224 | tf_op jit(solution)/shard_map/ppermute | solution.py:773
  35.5 0.5 %collective-permute-start.18 = (bf16[128,512]{1,0:T(8,128)(2,1)S(1)}, bf16[128,512]{1,0:T(8,128)(2,1)S(1)}, u32[]{:S(2)}, u32[]{:S(2)}) collective-permute-start(bf16[128,512]{1,0:T(8,128)(2,1)S(1)} %collective-permute-done.14.refs_3_), channel_id=1, source_target_pairs={{0,1},{1,0},{2,3},{3,2},{4,5},{5,4},{6,7},{7,6},{8,9},{9,8},{10,11... | collective-permute-start | bytes 393224 | tf_op jit(solution)/shard_map/ppermute | solution.py:773
  36.0 0.4 collective-permute-done.8
  36.4 0.4 collective-permute-done.16.refs_5_
  37.1 0.9 %layer_out.1 = (f32[128,256]{1,0:T(8,128)S(1)}, f32[128,256]{1,0:T(8,128)S(1)}) custom-call(s32[15]{0:T(128)S(1)} %concatenate.18.scalars, bf16[128,512]{1,0:T(8,128)(2,1)S(1)} %get-tuple-element.44.refs_0_, bf16[128,512]{1,0:T(8,128)(2,1)S(1)} %collective-permute-done.12.refs_1_, bf16[128,512]{1,0:T(8,128)(2,1)S(1)} %collective-permute-done.13.refs_2_, ...), custom_call_target="tpu_custom_call" | custom-call | tf_op jit(solution)/shard_map/layer_out/pallas_call | solution.py:657
  38.0 1.6 %collective-permute-start.19 = (f32[128,256]{1,0:T(8,128)S(1)}, f32[128,256]{1,0:T(8,128)S(1)}, u32[]{:S(2)}, u32[]{:S(2)}) collective-permute-start(f32[128,256]{1,0:T(8,128)S(1)} %get-tuple-element.62), channel_id=1, source_target_pairs={{0,2},{1,3},{2,0},{3,1},{4,6},{5,7},{6,4},{7,5},{8,10},{9,11},{10,... | collective-permute-start | bytes 393224 | tf_op jit(solution)/shard_map/ppermute | solution.py:773
  39.6 2.6 %collective-permute-start.10 = (f32[8,1024]{1,0:T(8,128)S(1)}, f32[8,1024]{1,0:T(8,128)S(1)}, u32[]{:S(2)}, u32[]{:S(2)}) collective-permute-start(f32[8,1024]{1,0:T(8,128)S(1)} %pad_maximum_fusion.2.refs_0_), channel_id=1, source_target_pairs={{0,8},{4,12},{8,0},{12,4},{1,9},{5,13},{9,1},{13,5},{2,10},{6,14},... | collective-permute-start | bytes 98312 | tf_op jit(solution)/shard_map/ppermute | solution.py:764
  42.2 0.9 %collective-permute-start.11 = (f32[8,1024]{1,0:T(8,128)S(1)}, f32[8,1024]{1,0:T(8,128)S(1)}, u32[]{:S(2)}, u32[]{:S(2)}) collective-permute-start(f32[8,1024]{1,0:T(8,128)S(1)} %pad_maximum_fusion.2.refs_0_), channel_id=1, source_target_pairs={{0,12},{4,8},{8,4},{12,0},{1,13},{5,9},{9,5},{13,1},{2,14},{6,10},... | collective-permute-start | bytes 98312 | tf_op jit(solution)/shard_map/ppermute | solution.py:764
  43.3 3.0 %weight_grad.1 = (f32[1024,1024]{1,0:T(8,128)}, f32[8,128]{1,0:T(8,128)S(1)}) custom-call(s32[15]{0:T(128)S(1)} %concatenate.18.scalars, bf16[128,512]{1,0:T(8,128)(2,1)S(1)} %get-tuple-element.44.refs_0_, bf16[128,512]{1,0:T(8,128)(2,1)S(1)} %collective-permute-done.12.refs_1_, bf16[128,512]{1,0:T(8,128)(2,1)S(1)} %collective-permute-done.13.refs_2_, ...), custom_call_target="tpu_custom_call" | custom-call | flops 1073741824 | bytes 6291456 | tf_op jit(solution)/shard_map/weight_grad/pallas_call | solution.py:697
  46.3 1.7 %collective-permute-done.11.refs_3_ = f32[8,1024]{1,0:T(8,128)S(1)} collective-permute-done((f32[8,1024]{1,0:T(8,128)S(1)}, f32[8,1024]{1,0:T(8,128)S(1)}, u32[]{:S(2)}, u32[]{:S(2)}) %collective-permute-start.11) | collective-permute-done | bytes 32800 | tf_op jit(solution)/shard_map/ppermute | solution.py:764
  47.9 1.3 %place_grads.1 = (bf16[128,256]{1,0:T(8,128)(2,1)}, f32[5,2,1024]{2,1,0:T(2,128)}, f32[5,2,128]{2,1,0:T(2,128)}, f32[5,16]{1,0:T(8,128)}) custom-call(s32[15]{0:T(128)S(1)} %concatenate.18.scalars, f32[8,1024]{1,0:T(8,128)S(1)} %pad_maximum_fusion.2.refs_0_, f32[8,1024]{1,0:T(8,128)S(1)} %collective-permute-done.9.refs_1_, ...), custom_call_target="tpu_custom_call" | custom-call | tf_op jit(solution)/shard_map/place_grads/pallas_call | solution.py:749
  (38 shorter events, 0.8 us)
Async XLA Ops:
  2.1 11.9 %collective-permute-start = (bf16[144,256]{1,0:T(8,128)(2,1)S(1)}, bf16[144,256]{1,0:T(8,128)(2,1)S(1)}, u32[]{:S(2)}, u32[]{:S(2)}) collective-permute-start(bf16[144,256]{1,0:T(8,128)(2,1)S(1)} %fusion.1.refs_0_), channel_id=1, source_target_pairs={{0,4},{4,0},{8,12},{12,8},{1,5},{5,1},{9,13},{13,9},{2,6},{6,2},{1... | collective-permute-start | bytes 221192 | tf_op jit(solution)/shard_map/ppermute | solution.py:764
  5.2 8.9 %collective-permute-start.1 = (bf16[144,256]{1,0:T(8,128)(2,1)S(1)}, bf16[144,256]{1,0:T(8,128)(2,1)S(1)}, u32[]{:S(2)}, u32[]{:S(2)}) collective-permute-start(bf16[144,256]{1,0:T(8,128)(2,1)S(1)} %fusion.1.refs_0_), channel_id=1, source_target_pairs={{0,8},{4,12},{8,0},{12,4},{1,9},{5,13},{9,1},{13,5},{2,10},{6,14},... | collective-permute-start | bytes 221192 | tf_op jit(solution)/shard_map/ppermute | solution.py:764
  7.7 6.3 %collective-permute-start.2 = (bf16[144,256]{1,0:T(8,128)(2,1)S(1)}, bf16[144,256]{1,0:T(8,128)(2,1)S(1)}, u32[]{:S(2)}, u32[]{:S(2)}) collective-permute-start(bf16[144,256]{1,0:T(8,128)(2,1)S(1)} %fusion.1.refs_0_), channel_id=1, source_target_pairs={{0,12},{4,8},{8,4},{12,0},{1,13},{5,9},{9,5},{13,1},{2,14},{6,10},... | collective-permute-start | bytes 221192 | tf_op jit(solution)/shard_map/ppermute | solution.py:764
  10.8 0.7 %copy-start.1 = (s32[5]{0:T(128)S(1)}, s32[5]{0:T(128)}, u32[]{:S(2)}) copy-start(s32[5]{0:T(128)} %basemap.1) | copy-start | bytes 64
  11.4 2.6 %copy-start.2 = (bf16[128,256]{1,0:T(8,128)(2,1)S(1)}, bf16[128,256]{1,0:T(8,128)(2,1)}, u32[]{:S(2)}) copy-start(bf16[128,256]{1,0:T(8,128)(2,1)} %param.21) | copy-start | bytes 196612
  14.1 6.4 %collective-permute-start.3 = (bf16[4,128,256]{2,1,0:T(8,128)(2,1)S(1)}, bf16[4,128,256]{2,1,0:T(8,128)(2,1)S(1)}, u32[]{:S(2)}, u32[]{:S(2)}) collective-permute-start(bf16[4,128,256]{2,1,0:T(8,128)(2,1)S(1)} %pad_maximum_fusion.refs_4_.refs_8_), channel_id=1, source_target_pairs={{0,2},{1,3},{2,0},{3,1},{4,6},{5,7},{6,4},{7,5},{8,10},{9,11},{10,... | collective-permute-start | bytes 786440 | tf_op jit(solution)/shard_map/ppermute | solution.py:773
  15.7 8.4 %collective-permute-start.4 = (bf16[4,128,256]{2,1,0:T(8,128)(2,1)S(1)}, bf16[4,128,256]{2,1,0:T(8,128)(2,1)S(1)}, u32[]{:S(2)}, u32[]{:S(2)}) collective-permute-start(bf16[4,128,256]{2,1,0:T(8,128)(2,1)S(1)} %pad_maximum_fusion.refs_4_.refs_8_), channel_id=1, source_target_pairs={{0,1},{1,0},{2,3},{3,2},{4,5},{5,4},{6,7},{7,6},{8,9},{9,8},{10,11... | collective-permute-start | bytes 786440 | tf_op jit(solution)/shard_map/ppermute | solution.py:773
  15.7 8.4 %copy-start = (bf16[1024,1024]{1,0:T(8,128)(2,1)S(1)}, bf16[1024,1024]{1,0:T(8,128)(2,1)}, u32[]{:S(2)}) copy-start(bf16[1024,1024]{1,0:T(8,128)(2,1)} %refs_8_.3) | copy-start | bytes 6291460
  20.5 3.5 %collective-permute-start.5 = (bf16[4,128,256]{2,1,0:T(8,128)(2,1)S(1)}, bf16[4,128,256]{2,1,0:T(8,128)(2,1)S(1)}, u32[]{:S(2)}, u32[]{:S(2)}) collective-permute-start(bf16[4,128,256]{2,1,0:T(8,128)(2,1)S(1)} %collective-permute-done.3.refs_6_.refs_10_), channel_id=1, source_target_pairs={{0,1},{1,0},{2,3},{3,2},{4,5},{5,4},{6,7},{7,6},{8,9},{9,8},{10,11... | collective-permute-start | bytes 786440 | tf_op jit(solution)/shard_map/ppermute | solution.py:773
  20.6 8.7 %collective-permute-start.12 = (bf16[128,512]{1,0:T(8,128)(2,1)S(1)}, bf16[128,512]{1,0:T(8,128)(2,1)S(1)}, u32[]{:S(2)}, u32[]{:S(2)}) collective-permute-start(bf16[128,512]{1,0:T(8,128)(2,1)S(1)} %get-tuple-element.44.refs_0_), channel_id=1, source_target_pairs={{0,4},{4,0},{8,12},{12,8},{1,5},{5,1},{9,13},{13,9},{2,6},{6,2},{1... | collective-permute-start | bytes 393224 | tf_op jit(solution)/shard_map/ppermute | solution.py:801
  21.6 7.6 %collective-permute-start.13 = (bf16[128,512]{1,0:T(8,128)(2,1)S(1)}, bf16[128,512]{1,0:T(8,128)(2,1)S(1)}, u32[]{:S(2)}, u32[]{:S(2)}) collective-permute-start(bf16[128,512]{1,0:T(8,128)(2,1)S(1)} %get-tuple-element.44.refs_0_), channel_id=1, source_target_pairs={{0,8},{4,12},{8,0},{12,4},{1,9},{5,13},{9,1},{13,5},{2,10},{6,14},... | collective-permute-start | bytes 393224 | tf_op jit(solution)/shard_map/ppermute | solution.py:801
  29.3 6.2 %collective-permute-start.14 = (bf16[128,512]{1,0:T(8,128)(2,1)S(1)}, bf16[128,512]{1,0:T(8,128)(2,1)S(1)}, u32[]{:S(2)}, u32[]{:S(2)}) collective-permute-start(bf16[128,512]{1,0:T(8,128)(2,1)S(1)} %collective-permute-done.13.refs_2_), channel_id=1, source_target_pairs={{0,4},{4,0},{8,12},{12,8},{1,5},{5,1},{9,13},{13,9},{2,6},{6,2},{1... | collective-permute-start | bytes 393224 | tf_op jit(solution)/shard_map/ppermute | solution.py:801
  31.9 2.2 %collective-permute-start.6 = (f32[8,640]{1,0:T(8,128)S(1)}, f32[8,640]{1,0:T(8,128)S(1)}, u32[]{:S(2)}, u32[]{:S(2)}) collective-permute-start(f32[8,640]{1,0:T(8,128)S(1)} %mix_backward.1), channel_id=1, source_target_pairs={{0,1},{1,0},{2,3},{3,2},{4,5},{5,4},{6,7},{7,6},{8,9},{9,8},{10,11... | collective-permute-start | bytes 61448 | tf_op jit(solution)/shard_map/ppermute | solution.py:773
  31.9 3.7 %collective-permute-start.7 = (f32[8,256]{1,0:T(8,128)S(1)}, f32[8,256]{1,0:T(8,128)S(1)}, u32[]{:S(2)}, u32[]{:S(2)}) collective-permute-start(f32[8,256]{1,0:T(8,128)S(1)} %slice.35), channel_id=1, source_target_pairs={{0,2},{1,3},{2,0},{3,1},{4,6},{5,7},{6,4},{7,5},{8,10},{9,11},{10,... | collective-permute-start | bytes 24584 | tf_op jit(solution)/shard_map/ppermute | solution.py:773
  33.4 3.1 %collective-permute-start.8 = (f32[8,256]{1,0:T(8,128)S(1)}, f32[8,256]{1,0:T(8,128)S(1)}, u32[]{:S(2)}, u32[]{:S(2)}) collective-permute-start(f32[8,256]{1,0:T(8,128)S(1)} %slice.35), channel_id=1, source_target_pairs={{0,3},{1,2},{2,1},{3,0},{4,7},{5,6},{6,5},{7,4},{8,11},{9,10},{10,... | collective-permute-start | bytes 24584 | tf_op jit(solution)/shard_map/ppermute | solution.py:773
  33.7 2.7 %collective-permute-start.15 = (bf16[128,512]{1,0:T(8,128)(2,1)S(1)}, bf16[128,512]{1,0:T(8,128)(2,1)S(1)}, u32[]{:S(2)}, u32[]{:S(2)}) collective-permute-start(bf16[128,512]{1,0:T(8,128)(2,1)S(1)} %get-tuple-element.44.refs_0_), channel_id=1, source_target_pairs={{0,1},{1,0},{2,3},{3,2},{4,5},{5,4},{6,7},{7,6},{8,9},{9,8},{10,11... | collective-permute-start | bytes 393224 | tf_op jit(solution)/shard_map/ppermute | solution.py:773
  34.0 2.9 %collective-permute-start.17 = (bf16[128,512]{1,0:T(8,128)(2,1)S(1)}, bf16[128,512]{1,0:T(8,128)(2,1)S(1)}, u32[]{:S(2)}, u32[]{:S(2)}) collective-permute-start(bf16[128,512]{1,0:T(8,128)(2,1)S(1)} %collective-permute-done.13.refs_2_), channel_id=1, source_target_pairs={{0,1},{1,0},{2,3},{3,2},{4,5},{5,4},{6,7},{7,6},{8,9},{9,8},{10,11... | collective-permute-start | bytes 393224 | tf_op jit(solution)/shard_map/ppermute | solution.py:773
  35.5 1.3 %collective-permute-start.16 = (bf16[128,512]{1,0:T(8,128)(2,1)S(1)}, bf16[128,512]{1,0:T(8,128)(2,1)S(1)}, u32[]{:S(2)}, u32[]{:S(2)}) collective-permute-start(bf16[128,512]{1,0:T(8,128)(2,1)S(1)} %collective-permute-done.12.refs_1_), channel_id=1, source_target_pairs={{0,1},{1,0},{2,3},{3,2},{4,5},{5,4},{6,7},{7,6},{8,9},{9,8},{10,11... | collective-permute-start | bytes 393224 | tf_op jit(solution)/shard_map/ppermute | solution.py:773
  35.5 1.5 %collective-permute-start.18 = (bf16[128,512]{1,0:T(8,128)(2,1)S(1)}, bf16[128,512]{1,0:T(8,128)(2,1)S(1)}, u32[]{:S(2)}, u32[]{:S(2)}) collective-permute-start(bf16[128,512]{1,0:T(8,128)(2,1)S(1)} %collective-permute-done.14.refs_3_), channel_id=1, source_target_pairs={{0,1},{1,0},{2,3},{3,2},{4,5},{5,4},{6,7},{7,6},{8,9},{9,8},{10,11... | collective-permute-start | bytes 393224 | tf_op jit(solution)/shard_map/ppermute | solution.py:773
  38.0 10.0 %collective-permute-start.19 = (f32[128,256]{1,0:T(8,128)S(1)}, f32[128,256]{1,0:T(8,128)S(1)}, u32[]{:S(2)}, u32[]{:S(2)}) collective-permute-start(f32[128,256]{1,0:T(8,128)S(1)} %get-tuple-element.62), channel_id=1, source_target_pairs={{0,2},{1,3},{2,0},{3,1},{4,6},{5,7},{6,4},{7,5},{8,10},{9,11},{10,... | collective-permute-start | bytes 393224 | tf_op jit(solution)/shard_map/ppermute | solution.py:773
  39.6 6.7 %collective-permute-start.10 = (f32[8,1024]{1,0:T(8,128)S(1)}, f32[8,1024]{1,0:T(8,128)S(1)}, u32[]{:S(2)}, u32[]{:S(2)}) collective-permute-start(f32[8,1024]{1,0:T(8,128)S(1)} %pad_maximum_fusion.2.refs_0_), channel_id=1, source_target_pairs={{0,8},{4,12},{8,0},{12,4},{1,9},{5,13},{9,1},{13,5},{2,10},{6,14},... | collective-permute-start | bytes 98312 | tf_op jit(solution)/shard_map/ppermute | solution.py:764
  42.2 5.7 %collective-permute-start.11 = (f32[8,1024]{1,0:T(8,128)S(1)}, f32[8,1024]{1,0:T(8,128)S(1)}, u32[]{:S(2)}, u32[]{:S(2)}) collective-permute-start(f32[8,1024]{1,0:T(8,128)S(1)} %pad_maximum_fusion.2.refs_0_), channel_id=1, source_target_pairs={{0,12},{4,8},{8,4},{12,0},{1,13},{5,9},{9,5},{13,1},{2,14},{6,10},... | collective-permute-start | bytes 98312 | tf_op jit(solution)/shard_map/ppermute | solution.py:764
  43.2 4.8 %collective-permute-start.9 = (f32[8,1024]{1,0:T(8,128)S(1)}, f32[8,1024]{1,0:T(8,128)S(1)}, u32[]{:S(2)}, u32[]{:S(2)}) collective-permute-start(f32[8,1024]{1,0:T(8,128)S(1)} %pad_maximum_fusion.2.refs_0_), channel_id=1, source_target_pairs={{0,4},{4,0},{8,12},{12,8},{1,5},{5,1},{9,13},{13,9},{2,6},{6,2},{1... | collective-permute-start | bytes 98312 | tf_op jit(solution)/shard_map/ppermute | solution.py:764

commit v8 on v7

--- a/solution.py
+++ b/solution.py
@@ -12,7 +12,7 @@
 SYM = 8
 F32 = jnp.float32
 BF16 = jnp.bfloat16
-GROUP = 1
+GROUP = 2
 GROUP_BACK = 4
 NN = (((1,), (0,)), ((), ()))
 NT = (((1,), (1,)), ((), ()))
@@ -371,28 +371,20 @@
             k * BLOCK : (k + 1) * BLOCK
         ]
     units = [[Unit(r, tabs_ref, st, b, ns) for b in range(ns)] for st in range(2)]
-
-    def spread(st):
-        backs, aheads = {}, {}
+    for st in range(2):
         for b in range(ns):
             u = units[st][b]
             dy = r.dg[u.rows, :] * u.act(ZZ, 128)
             cf = r.bc[u.rows, st * 512 + 128 : st * 512 + 256]
             cb = r.bc[u.rows, st * 512 + 384 : st * 512 + 512]
             if b > 0:
-                backs[b - 1] = mm_fine(cf, jnp.exp(u.p) * dy, TN, 2)
+                r.ds[st * 2, b - 1] = mm_fine(cf, jnp.exp(u.p) * dy, TN, 2)
             if b < ns - 1:
-                aheads[b + 1] = mm_fine(cb, jnp.exp(u.total - u.q) * dy, TN, 2)
-        yield
-        for b in range(ns - 2, -1, -1):
-            if b < ns - 2:
-                backs[b] = backs[b] + jnp.exp(units[st][b + 1].total) * backs[b + 1]
-            r.ds[st * 2, b] = backs[b]
-        for b in range(1, ns):
-            if b > 1:
-                aheads[b] = aheads[b] + jnp.exp(units[st][b - 1].total) * aheads[b - 1]
-            r.ds[st * 2 + 1, b] = aheads[b]
-
+                r.ds[st * 2 + 1, b + 1] = mm_fine(cb, jnp.exp(u.total - u.q) * dy, TN, 2)
+        for b in range(ns - 3, -1, -1):
+            r.ds[st * 2, b] += jnp.exp(units[st][b + 1].total) * r.ds[st * 2, b + 1]
+        for b in range(2, ns):
+            r.ds[st * 2 + 1, b] += jnp.exp(units[st][b - 1].total) * r.ds[st * 2 + 1, b - 1]
     d_steps = [jnp.zeros((SYM, LANES), F32)] * 2
     d_decays = [jnp.zeros((SYM, LANES), F32)] * 2
     d_tab = 0.0
@@ -517,8 +509,7 @@
 
     for b0 in range(0, ns, GROUP_BACK):
         last = min(b0 + GROUP_BACK, ns)
-        bodies = [body(st, b) for b in range(b0, last) for st in range(2)]
-        together([spread(0), spread(1)] * (b0 == 0) + bodies)
+        together(body(st, b) for b in range(b0, last) for st in range(2))
         span = slice(b0 * BLOCK, last * BLOCK)
         d_tab = d_tab + mm(r.sym[:, span], r.dpre[span, :], NN)
     mid = SYM * (conv - 1)
@@ -799,7 +790,7 @@
     for a in heads[1:]:
         cots += [a, across(a, (0, 1), nh, nc)]
     hop = lambda x, k: lax.ppermute(x, "seq", [(i, i ^ k) for i in range(ns)])
-    direct = {k: hop(gated, k) for k in (ns >> n for n in range(1, ns.bit_length()))}
+    direct = {k: hop(gated, k) for k in (1 << n for n in range(ns.bit_length() - 1))}
     grads = call_backward(scalars, tables, cots, out_weight, kept, conv, vocab)
     direct, _ = lax.optimization_barrier((direct, grads))
     held = {0: gated, **direct}

time: 49.6 us -> 49.6 us (level)
  transfers between devices with their start and end apart: 20 -> 20, of which waited for: 7 -> 7; matrix products, arithmetic and copies ran while one was open for 6% -> 6% of each run, Pallas kernels for 25% -> 26%
where the time goes in v8:
time: 49.6 us; the launch traced here: 49.3 us
  starting transfers between devices  21.4 us (43%)
  Pallas kernels  14.8 us (30%)
  waiting for transfers between devices  7.08 us (14%)
  other arithmetic  3.73 us (8%)
  local copies, waits for them, and re-layouts  1.51 us (3%)
  between operations  0.77 us (2%)
    ppermute x6, starting transfers between devices, around(): lax.ppermute(x, axis, [(i, i ^ k) for i in range(n)])  9.34 us
    ppermute x11, starting transfers between devices, across(): return lax.ppermute(x, ('head', 'sub'), pairs)  6.05 us
    ppermute x3, starting transfers between devices, by_channel(): hop = lambda x, k: lax.ppermute(x, 'seq', [(i, i ^ k) for i in range(ns)])  5.98 us
    pallas_call x1, Pallas kernels, call_backward(): pl.pallas_call(functools.partial(backward_kernel, ns=ns, nq=len(cots), co...  5.29 us
    ppermute x11, waiting for transfers between devices, across(): return lax.ppermute(x, ('head', 'sub'), pairs)  3.64 us
    pallas_call x1, Pallas kernels, call_forward(): pl.pallas_call(functools.partial(forward_kernel, ns=ns, conv=conv), out_s...  3.53 us
    ppermute x6, waiting for transfers between devices, around(): lax.ppermute(x, axis, [(i, i ^ k) for i in range(n)])  3.44 us
    pallas_call x1, Pallas kernels, call_weight(): pl.pallas_call(functools.partial(weight_kernel, ns=ns, nh=nh, nc=nc), out...  2.96 us
  transfers between devices with their start and end apart: 20, of which 7 were waited for; matrix products, arithmetic and copies ran while one was open for 6% of the time, Pallas kernels for 26%

profile of v8, /device:TPU:0, one launch (start us, length us, event | category | flops | bytes accessed | tf_op | source)
XLA Modules:
  0.0 49.3 jit_solution(9561472675126146033)
XLA Ops:
  0.6 0.7 %convert_bitcast_fusion = bf16[1,128]{1,0:T(2,128)(2,1)S(1)} fusion(s32[128]{0:T(128)} %param.11), kind=kLoop, calls=%fused_computation.42 | loop fusion | flops 128 | bytes 768 | tf_op jit(solution)/shard_map/reshape | solution.py:775
  1.3 0.8 %fusion.1.refs_0_ = bf16[144,256]{1,0:T(8,128)(2,1)S(1)} fusion(bf16[1,128]{1,0:T(2,128)(2,1)S(1)} %convert_bitcast_fusion, bf16[128,256]{1,0:T(8,128)(2,1)} %param.21), kind=kLoop, calls=%fused_computation.3 | loop fusion | flops 221184 | bytes 139520 | tf_op jit(solution)/shard_map/concatenate | solution.py:776
  2.1 3.0 %collective-permute-start = (bf16[144,256]{1,0:T(8,128)(2,1)S(1)}, bf16[144,256]{1,0:T(8,128)(2,1)S(1)}, u32[]{:S(2)}, u32[]{:S(2)}) collective-permute-start(bf16[144,256]{1,0:T(8,128)(2,1)S(1)} %fusion.1.refs_0_), channel_id=1, source_target_pairs={{0,4},{4,0},{8,12},{12,8},{1,5},{5,1},{9,13},{13,9},{2,6},{6,2},{1... | collective-permute-start | bytes 221192 | tf_op jit(solution)/shard_map/ppermute | solution.py:755
  5.2 2.6 %collective-permute-start.1 = (bf16[144,256]{1,0:T(8,128)(2,1)S(1)}, bf16[144,256]{1,0:T(8,128)(2,1)S(1)}, u32[]{:S(2)}, u32[]{:S(2)}) collective-permute-start(bf16[144,256]{1,0:T(8,128)(2,1)S(1)} %fusion.1.refs_0_), channel_id=1, source_target_pairs={{0,8},{4,12},{8,0},{12,4},{1,9},{5,13},{9,1},{13,5},{2,10},{6,14},... | collective-permute-start | bytes 221192 | tf_op jit(solution)/shard_map/ppermute | solution.py:755
  7.8 0.7 %reshape.16 = bf16[10,1024]{1,0:T(8,128)(2,1)S(1)} reshape(bf16[5,2,1024]{2,1,0:T(2,128)(2,1)} %param.13) | data formatting | bytes 40960 | tf_op jit(solution)/shard_map/reshape | solution.py:579
  8.5 0.7 %pad_maximum_fusion.1.refs_0_ = bf16[14,1024]{1,0:T(8,128)(2,1)S(1)} fusion(bf16[4,1024]{1,0:T(4,128)(2,1)} %param.16, bf16[10,1024]{1,0:T(8,128)(2,1)S(1)} %reshape.16), kind=kLoop, calls=%fused_computation.7 | loop fusion | flops 57344 | bytes 57344 | tf_op jit(solution)/shard_map/concatenate | solution.py:579
  9.2 0.7 %pad_maximum_fusion.3.refs_1_ = bf16[9,2,128]{2,1,0:T(2,128)(2,1)S(1)} fusion(bf16[4,2,128]{2,1,0:T(2,128)(2,1)} %param.17, bf16[5,2,128]{2,1,0:T(2,128)(2,1)} %param.14), kind=kLoop, calls=%fused_computation.10 | loop fusion | flops 2304 | bytes 9216 | tf_op jit(solution)/shard_map/concatenate | solution.py:580
  10.0 0.7 %pad_maximum_fusion.4.refs_2_ = f32[7,16]{1,0:T(8,128)S(1)} fusion(f32[1,16]{1,0:T(1,128)} %bitcast.15, f32[1,16]{1,0:T(1,128)} %bitcast.16, f32[5,16]{1,0:T(8,128)} %param.15), kind=kLoop, calls=%fused_computation.11 | loop fusion | flops 224 | bytes 896 | tf_op jit(solution)/shard_map/concatenate | solution.py:581
  10.8 0.7 %copy-done.1 = s32[5]{0:T(128)S(1)} copy-done((s32[5]{0:T(128)S(1)}, s32[5]{0:T(128)}, u32[]{:S(2)}) %copy-start.1) | copy-done | bytes 44
  11.4 0.8 %tables.1 = (f32[32,128]{1,0:T(8,128)S(1)}, f32[16,256]{1,0:T(8,128)S(1)}, f32[8,128]{1,0:T(8,128)S(1)}, f32[8,128]{1,0:T(8,128)S(1)}, bf16[128,1792]{1,0:T(8,12...) custom-call(s32[15]{0:T(128)S(1)} %concatenate.18.scalars, s32[5]{0:T(128)S(1)} %copy-done.1, ...), custom_call_target="tpu_custom_call" | custom-call | flops 2000000000 | bytes 1000000 | tf_op jit(solution)/shard_map/tables/pallas_call | solution.py:567
  12.2 1.8 %collective-permute-done.2.refs_3_ = bf16[144,256]{1,0:T(8,128)(2,1)S(1)} collective-permute-done((bf16[144,256]{1,0:T(8,128)(2,1)S(1)}, bf16[144,256]{1,0:T(8,128)(2,1)S(1)}, u32[]{:S(2)}, u32[]{:S(2)}) %collective-permute-start.2) | collective-permute-done | bytes 73760 | tf_op jit(solution)/shard_map/ppermute | solution.py:755
  14.1 1.6 %collective-permute-start.3 = (bf16[4,128,256]{2,1,0:T(8,128)(2,1)S(1)}, bf16[4,128,256]{2,1,0:T(8,128)(2,1)S(1)}, u32[]{:S(2)}, u32[]{:S(2)}) collective-permute-start(bf16[4,128,256]{2,1,0:T(8,128)(2,1)S(1)} %pad_maximum_fusion.refs_4_.refs_8_), channel_id=1, source_target_pairs={{0,2},{1,3},{2,0},{3,1},{4,6},{5,7},{6,4},{7,5},{8,10},{9,11},{10,... | collective-permute-start | bytes 786440 | tf_op jit(solution)/shard_map/ppermute | solution.py:764
  15.7 3.5 %mix_forward.1 = (bf16[128,512]{1,0:T(8,128)(2,1)S(1)}, f32[8,512]{1,0:T(8,128)S(1)}, f32[8,512]{1,0:T(8,128)S(1)}, f32[8,512]{1,0:T(8,128)S(1)}, bf16[64,512]{1...) custom-call(s32[15]{0:T(128)S(1)} %concatenate.18.scalars, ...), custom_call_target="tpu_custom_call" | custom-call | flops 5000000000 | bytes 524288 | tf_op jit(solution)/shard_map/mix_forward/pallas_call | solution.py:589
  19.2 1.3 %collective-permute-done.3.refs_6_.refs_10_ = bf16[4,128,256]{2,1,0:T(8,128)(2,1)S(1)} collective-permute-done((bf16[4,128,256]{2,1,0:T(8,128)(2,1)S(1)}, bf16[4,128,256]{2,1,0:T(8,128)(2,1)S(1)}, u32[]{:S(2)}, u32[]{:S(2)}) %collective-permute-start.3) | collective-permute-done | bytes 262176 | tf_op jit(solution)/shard_map/ppermute | solution.py:764
  20.6 1.1 %collective-permute-start.12 = (bf16[128,512]{1,0:T(8,128)(2,1)S(1)}, bf16[128,512]{1,0:T(8,128)(2,1)S(1)}, u32[]{:S(2)}, u32[]{:S(2)}) collective-permute-start(bf16[128,512]{1,0:T(8,128)(2,1)S(1)} %get-tuple-element.44.refs_0_), channel_id=1, source_target_pairs={{0,4},{4,0},{8,12},{12,8},{1,5},{5,1},{9,13},{13,9},{2,6},{6,2},{1... | collective-permute-start | bytes 393224 | tf_op jit(solution)/shard_map/ppermute | solution.py:792
  21.6 2.4 %collective-permute-start.13 = (bf16[128,512]{1,0:T(8,128)(2,1)S(1)}, bf16[128,512]{1,0:T(8,128)(2,1)S(1)}, u32[]{:S(2)}, u32[]{:S(2)}) collective-permute-start(bf16[128,512]{1,0:T(8,128)(2,1)S(1)} %get-tuple-element.44.refs_0_), channel_id=1, source_target_pairs={{0,8},{4,12},{8,0},{12,4},{1,9},{5,13},{9,1},{13,5},{2,10},{6,14},... | collective-permute-start | bytes 393224 | tf_op jit(solution)/shard_map/ppermute | solution.py:792
  24.0 5.3 %mix_backward.1 = f32[8,640]{1,0:T(8,128)S(1)} custom-call(s32[15]{0:T(128)S(1)} %concatenate.18.scalars, f32[32,128]{1,0:T(8,128)S(1)} %get-tuple-element.37.refs_7_.refs_0_, f32[16,256]{1,0:T(8,128)S(1)} %get-tuple-element.38.refs_1_, f32[8,128]{1,0:T(8,128)S(1)} %get-tuple-element.39.refs_2_, f32[8,128]{1,0:T(8,128)S(1)} %get-tuple-element.40.refs_3_, ...), custom_call_target="tpu_custom_call" | custom-call | flops 6000000000 | bytes 524288 | tf_op jit(solution)/shard_map/mix_backward/pallas_call | solution.py:610
  29.3 2.5 %collective-permute-start.14 = (bf16[128,512]{1,0:T(8,128)(2,1)S(1)}, bf16[128,512]{1,0:T(8,128)(2,1)S(1)}, u32[]{:S(2)}, u32[]{:S(2)}) collective-permute-start(bf16[128,512]{1,0:T(8,128)(2,1)S(1)} %collective-permute-done.13.refs_2_), channel_id=1, source_target_pairs={{0,4},{4,0},{8,12},{12,8},{1,5},{5,1},{9,13},{13,9},{2,6},{6,2},{1... | collective-permute-start | bytes 393224 | tf_op jit(solution)/shard_map/ppermute | solution.py:792
  31.9 1.5 %collective-permute-start.7 = (f32[8,256]{1,0:T(8,128)S(1)}, f32[8,256]{1,0:T(8,128)S(1)}, u32[]{:S(2)}, u32[]{:S(2)}) collective-permute-start(f32[8,256]{1,0:T(8,128)S(1)} %slice.35), channel_id=1, source_target_pairs={{0,2},{1,3},{2,0},{3,1},{4,6},{5,7},{6,4},{7,5},{8,10},{9,11},{10,... | collective-permute-start | bytes 24584 | tf_op jit(solution)/shard_map/ppermute | solution.py:764
  33.4 0.4 collective-permute-start.8
  33.7 0.3 collective-permute-start.15
  34.2 1.3 %collective-permute-done.7 = f32[8,256]{1,0:T(8,128)S(1)} collective-permute-done((f32[8,256]{1,0:T(8,128)S(1)}, f32[8,256]{1,0:T(8,128)S(1)}, u32[]{:S(2)}, u32[]{:S(2)}) %collective-permute-start.7) | collective-permute-done | bytes 8224 | tf_op jit(solution)/shard_map/ppermute | solution.py:764
  35.5 0.5 %collective-permute-start.18 = (bf16[128,512]{1,0:T(8,128)(2,1)S(1)}, bf16[128,512]{1,0:T(8,128)(2,1)S(1)}, u32[]{:S(2)}, u32[]{:S(2)}) collective-permute-start(bf16[128,512]{1,0:T(8,128)(2,1)S(1)} %collective-permute-done.14.refs_3_), channel_id=1, source_target_pairs={{0,1},{1,0},{2,3},{3,2},{4,5},{5,4},{6,7},{7,6},{8,9},{9,8},{10,11... | collective-permute-start | bytes 393224 | tf_op jit(solution)/shard_map/ppermute | solution.py:764
  36.0 0.4 collective-permute-done.8
  36.4 0.4 collective-permute-done.16.refs_5_
  37.1 0.9 %layer_out.1 = (f32[128,256]{1,0:T(8,128)S(1)}, f32[128,256]{1,0:T(8,128)S(1)}) custom-call(s32[15]{0:T(128)S(1)} %concatenate.18.scalars, bf16[128,512]{1,0:T(8,128)(2,1)S(1)} %get-tuple-element.44.refs_0_, bf16[128,512]{1,0:T(8,128)(2,1)S(1)} %collective-permute-done.12.refs_1_, bf16[128,512]{1,0:T(8,128)(2,1)S(1)} %collective-permute-done.13.refs_2_, ...), custom_call_target="tpu_custom_call" | custom-call | tf_op jit(solution)/shard_map/layer_out/pallas_call | solution.py:648
  38.0 1.6 %collective-permute-start.19 = (f32[128,256]{1,0:T(8,128)S(1)}, f32[128,256]{1,0:T(8,128)S(1)}, u32[]{:S(2)}, u32[]{:S(2)}) collective-permute-start(f32[128,256]{1,0:T(8,128)S(1)} %get-tuple-element.62), channel_id=1, source_target_pairs={{0,2},{1,3},{2,0},{3,1},{4,6},{5,7},{6,4},{7,5},{8,10},{9,11},{10,... | collective-permute-start | bytes 393224 | tf_op jit(solution)/shard_map/ppermute | solution.py:764
  39.6 2.6 %collective-permute-start.10 = (f32[8,1024]{1,0:T(8,128)S(1)}, f32[8,1024]{1,0:T(8,128)S(1)}, u32[]{:S(2)}, u32[]{:S(2)}) collective-permute-start(f32[8,1024]{1,0:T(8,128)S(1)} %pad_maximum_fusion.2.refs_0_), channel_id=1, source_target_pairs={{0,8},{4,12},{8,0},{12,4},{1,9},{5,13},{9,1},{13,5},{2,10},{6,14},... | collective-permute-start | bytes 98312 | tf_op jit(solution)/shard_map/ppermute | solution.py:755
  42.2 0.9 %collective-permute-start.11 = (f32[8,1024]{1,0:T(8,128)S(1)}, f32[8,1024]{1,0:T(8,128)S(1)}, u32[]{:S(2)}, u32[]{:S(2)}) collective-permute-start(f32[8,1024]{1,0:T(8,128)S(1)} %pad_maximum_fusion.2.refs_0_), channel_id=1, source_target_pairs={{0,12},{4,8},{8,4},{12,0},{1,13},{5,9},{9,5},{13,1},{2,14},{6,10},... | collective-permute-start | bytes 98312 | tf_op jit(solution)/shard_map/ppermute | solution.py:755
  43.3 3.0 %weight_grad.1 = (f32[1024,1024]{1,0:T(8,128)}, f32[8,128]{1,0:T(8,128)S(1)}) custom-call(s32[15]{0:T(128)S(1)} %concatenate.18.scalars, bf16[128,512]{1,0:T(8,128)(2,1)S(1)} %get-tuple-element.44.refs_0_, bf16[128,512]{1,0:T(8,128)(2,1)S(1)} %collective-permute-done.12.refs_1_, bf16[128,512]{1,0:T(8,128)(2,1)S(1)} %collective-permute-done.13.refs_2_, ...), custom_call_target="tpu_custom_call" | custom-call | flops 1073741824 | bytes 6291456 | tf_op jit(solution)/shard_map/weight_grad/pallas_call | solution.py:688
  46.3 1.7 %collective-permute-done.11.refs_3_ = f32[8,1024]{1,0:T(8,128)S(1)} collective-permute-done((f32[8,1024]{1,0:T(8,128)S(1)}, f32[8,1024]{1,0:T(8,128)S(1)}, u32[]{:S(2)}, u32[]{:S(2)}) %collective-permute-start.11) | collective-permute-done | bytes 32800 | tf_op jit(solution)/shard_map/ppermute | solution.py:755
  47.9 1.3 %place_grads.1 = (bf16[128,256]{1,0:T(8,128)(2,1)}, f32[5,2,1024]{2,1,0:T(2,128)}, f32[5,2,128]{2,1,0:T(2,128)}, f32[5,16]{1,0:T(8,128)}) custom-call(s32[15]{0:T(128)S(1)} %concatenate.18.scalars, f32[8,1024]{1,0:T(8,128)S(1)} %pad_maximum_fusion.2.refs_0_, f32[8,1024]{1,0:T(8,128)S(1)} %collective-permute-done.9.refs_1_, ...), custom_call_target="tpu_custom_call" | custom-call | tf_op jit(solution)/shard_map/place_grads/pallas_call | solution.py:740
  (38 shorter events, 0.8 us)
Async XLA Ops:
  2.1 11.9 %collective-permute-start = (bf16[144,256]{1,0:T(8,128)(2,1)S(1)}, bf16[144,256]{1,0:T(8,128)(2,1)S(1)}, u32[]{:S(2)}, u32[]{:S(2)}) collective-permute-start(bf16[144,256]{1,0:T(8,128)(2,1)S(1)} %fusion.1.refs_0_), channel_id=1, source_target_pairs={{0,4},{4,0},{8,12},{12,8},{1,5},{5,1},{9,13},{13,9},{2,6},{6,2},{1... | collective-permute-start | bytes 221192 | tf_op jit(solution)/shard_map/ppermute | solution.py:755
  5.2 8.9 %collective-permute-start.1 = (bf16[144,256]{1,0:T(8,128)(2,1)S(1)}, bf16[144,256]{1,0:T(8,128)(2,1)S(1)}, u32[]{:S(2)}, u32[]{:S(2)}) collective-permute-start(bf16[144,256]{1,0:T(8,128)(2,1)S(1)} %fusion.1.refs_0_), channel_id=1, source_target_pairs={{0,8},{4,12},{8,0},{12,4},{1,9},{5,13},{9,1},{13,5},{2,10},{6,14},... | collective-permute-start | bytes 221192 | tf_op jit(solution)/shard_map/ppermute | solution.py:755
  7.7 6.3 %collective-permute-start.2 = (bf16[144,256]{1,0:T(8,128)(2,1)S(1)}, bf16[144,256]{1,0:T(8,128)(2,1)S(1)}, u32[]{:S(2)}, u32[]{:S(2)}) collective-permute-start(bf16[144,256]{1,0:T(8,128)(2,1)S(1)} %fusion.1.refs_0_), channel_id=1, source_target_pairs={{0,12},{4,8},{8,4},{12,0},{1,13},{5,9},{9,5},{13,1},{2,14},{6,10},... | collective-permute-start | bytes 221192 | tf_op jit(solution)/shard_map/ppermute | solution.py:755
  10.8 0.7 %copy-start.1 = (s32[5]{0:T(128)S(1)}, s32[5]{0:T(128)}, u32[]{:S(2)}) copy-start(s32[5]{0:T(128)} %basemap.1) | copy-start | bytes 64
  11.4 2.6 %copy-start.2 = (bf16[128,256]{1,0:T(8,128)(2,1)S(1)}, bf16[128,256]{1,0:T(8,128)(2,1)}, u32[]{:S(2)}) copy-start(bf16[128,256]{1,0:T(8,128)(2,1)} %param.21) | copy-start | bytes 196612
  14.1 6.4 %collective-permute-start.3 = (bf16[4,128,256]{2,1,0:T(8,128)(2,1)S(1)}, bf16[4,128,256]{2,1,0:T(8,128)(2,1)S(1)}, u32[]{:S(2)}, u32[]{:S(2)}) collective-permute-start(bf16[4,128,256]{2,1,0:T(8,128)(2,1)S(1)} %pad_maximum_fusion.refs_4_.refs_8_), channel_id=1, source_target_pairs={{0,2},{1,3},{2,0},{3,1},{4,6},{5,7},{6,4},{7,5},{8,10},{9,11},{10,... | collective-permute-start | bytes 786440 | tf_op jit(solution)/shard_map/ppermute | solution.py:764
  15.7 8.4 %collective-permute-start.4 = (bf16[4,128,256]{2,1,0:T(8,128)(2,1)S(1)}, bf16[4,128,256]{2,1,0:T(8,128)(2,1)S(1)}, u32[]{:S(2)}, u32[]{:S(2)}) collective-permute-start(bf16[4,128,256]{2,1,0:T(8,128)(2,1)S(1)} %pad_maximum_fusion.refs_4_.refs_8_), channel_id=1, source_target_pairs={{0,1},{1,0},{2,3},{3,2},{4,5},{5,4},{6,7},{7,6},{8,9},{9,8},{10,11... | collective-permute-start | bytes 786440 | tf_op jit(solution)/shard_map/ppermute | solution.py:764
  15.7 8.4 %copy-start = (bf16[1024,1024]{1,0:T(8,128)(2,1)S(1)}, bf16[1024,1024]{1,0:T(8,128)(2,1)}, u32[]{:S(2)}) copy-start(bf16[1024,1024]{1,0:T(8,128)(2,1)} %refs_8_.3) | copy-start | bytes 6291460
  20.5 3.5 %collective-permute-start.5 = (bf16[4,128,256]{2,1,0:T(8,128)(2,1)S(1)}, bf16[4,128,256]{2,1,0:T(8,128)(2,1)S(1)}, u32[]{:S(2)}, u32[]{:S(2)}) collective-permute-start(bf16[4,128,256]{2,1,0:T(8,128)(2,1)S(1)} %collective-permute-done.3.refs_6_.refs_10_), channel_id=1, source_target_pairs={{0,1},{1,0},{2,3},{3,2},{4,5},{5,4},{6,7},{7,6},{8,9},{9,8},{10,11... | collective-permute-start | bytes 786440 | tf_op jit(solution)/shard_map/ppermute | solution.py:764
  20.6 8.8 %collective-permute-start.12 = (bf16[128,512]{1,0:T(8,128)(2,1)S(1)}, bf16[128,512]{1,0:T(8,128)(2,1)S(1)}, u32[]{:S(2)}, u32[]{:S(2)}) collective-permute-start(bf16[128,512]{1,0:T(8,128)(2,1)S(1)} %get-tuple-element.44.refs_0_), channel_id=1, source_target_pairs={{0,4},{4,0},{8,12},{12,8},{1,5},{5,1},{9,13},{13,9},{2,6},{6,2},{1... | collective-permute-start | bytes 393224 | tf_op jit(solution)/shard_map/ppermute | solution.py:792
  21.6 7.7 %collective-permute-start.13 = (bf16[128,512]{1,0:T(8,128)(2,1)S(1)}, bf16[128,512]{1,0:T(8,128)(2,1)S(1)}, u32[]{:S(2)}, u32[]{:S(2)}) collective-permute-start(bf16[128,512]{1,0:T(8,128)(2,1)S(1)} %get-tuple-element.44.refs_0_), channel_id=1, source_target_pairs={{0,8},{4,12},{8,0},{12,4},{1,9},{5,13},{9,1},{13,5},{2,10},{6,14},... | collective-permute-start | bytes 393224 | tf_op jit(solution)/shard_map/ppermute | solution.py:792
  29.3 6.2 %collective-permute-start.14 = (bf16[128,512]{1,0:T(8,128)(2,1)S(1)}, bf16[128,512]{1,0:T(8,128)(2,1)S(1)}, u32[]{:S(2)}, u32[]{:S(2)}) collective-permute-start(bf16[128,512]{1,0:T(8,128)(2,1)S(1)} %collective-permute-done.13.refs_2_), channel_id=1, source_target_pairs={{0,4},{4,0},{8,12},{12,8},{1,5},{5,1},{9,13},{13,9},{2,6},{6,2},{1... | collective-permute-start | bytes 393224 | tf_op jit(solution)/shard_map/ppermute | solution.py:792
  31.9 2.2 %collective-permute-start.6 = (f32[8,640]{1,0:T(8,128)S(1)}, f32[8,640]{1,0:T(8,128)S(1)}, u32[]{:S(2)}, u32[]{:S(2)}) collective-permute-start(f32[8,640]{1,0:T(8,128)S(1)} %mix_backward.1), channel_id=1, source_target_pairs={{0,1},{1,0},{2,3},{3,2},{4,5},{5,4},{6,7},{7,6},{8,9},{9,8},{10,11... | collective-permute-start | bytes 61448 | tf_op jit(solution)/shard_map/ppermute | solution.py:764
  31.9 3.7 %collective-permute-start.7 = (f32[8,256]{1,0:T(8,128)S(1)}, f32[8,256]{1,0:T(8,128)S(1)}, u32[]{:S(2)}, u32[]{:S(2)}) collective-permute-start(f32[8,256]{1,0:T(8,128)S(1)} %slice.35), channel_id=1, source_target_pairs={{0,2},{1,3},{2,0},{3,1},{4,6},{5,7},{6,4},{7,5},{8,10},{9,11},{10,... | collective-permute-start | bytes 24584 | tf_op jit(solution)/shard_map/ppermute | solution.py:764
  33.4 3.1 %collective-permute-start.8 = (f32[8,256]{1,0:T(8,128)S(1)}, f32[8,256]{1,0:T(8,128)S(1)}, u32[]{:S(2)}, u32[]{:S(2)}) collective-permute-start(f32[8,256]{1,0:T(8,128)S(1)} %slice.35), channel_id=1, source_target_pairs={{0,3},{1,2},{2,1},{3,0},{4,7},{5,6},{6,5},{7,4},{8,11},{9,10},{10,... | collective-permute-start | bytes 24584 | tf_op jit(solution)/shard_map/ppermute | solution.py:764
  33.7 2.7 %collective-permute-start.15 = (bf16[128,512]{1,0:T(8,128)(2,1)S(1)}, bf16[128,512]{1,0:T(8,128)(2,1)S(1)}, u32[]{:S(2)}, u32[]{:S(2)}) collective-permute-start(bf16[128,512]{1,0:T(8,128)(2,1)S(1)} %get-tuple-element.44.refs_0_), channel_id=1, source_target_pairs={{0,1},{1,0},{2,3},{3,2},{4,5},{5,4},{6,7},{7,6},{8,9},{9,8},{10,11... | collective-permute-start | bytes 393224 | tf_op jit(solution)/shard_map/ppermute | solution.py:764
  34.0 2.9 %collective-permute-start.17 = (bf16[128,512]{1,0:T(8,128)(2,1)S(1)}, bf16[128,512]{1,0:T(8,128)(2,1)S(1)}, u32[]{:S(2)}, u32[]{:S(2)}) collective-permute-start(bf16[128,512]{1,0:T(8,128)(2,1)S(1)} %collective-permute-done.13.refs_2_), channel_id=1, source_target_pairs={{0,1},{1,0},{2,3},{3,2},{4,5},{5,4},{6,7},{7,6},{8,9},{9,8},{10,11... | collective-permute-start | bytes 393224 | tf_op jit(solution)/shard_map/ppermute | solution.py:764
  35.5 1.3 %collective-permute-start.16 = (bf16[128,512]{1,0:T(8,128)(2,1)S(1)}, bf16[128,512]{1,0:T(8,128)(2,1)S(1)}, u32[]{:S(2)}, u32[]{:S(2)}) collective-permute-start(bf16[128,512]{1,0:T(8,128)(2,1)S(1)} %collective-permute-done.12.refs_1_), channel_id=1, source_target_pairs={{0,1},{1,0},{2,3},{3,2},{4,5},{5,4},{6,7},{7,6},{8,9},{9,8},{10,11... | collective-permute-start | bytes 393224 | tf_op jit(solution)/shard_map/ppermute | solution.py:764
  35.5 1.5 %collective-permute-start.18 = (bf16[128,512]{1,0:T(8,128)(2,1)S(1)}, bf16[128,512]{1,0:T(8,128)(2,1)S(1)}, u32[]{:S(2)}, u32[]{:S(2)}) collective-permute-start(bf16[128,512]{1,0:T(8,128)(2,1)S(1)} %collective-permute-done.14.refs_3_), channel_id=1, source_target_pairs={{0,1},{1,0},{2,3},{3,2},{4,5},{5,4},{6,7},{7,6},{8,9},{9,8},{10,11... | collective-permute-start | bytes 393224 | tf_op jit(solution)/shard_map/ppermute | solution.py:764
  38.0 10.0 %collective-permute-start.19 = (f32[128,256]{1,0:T(8,128)S(1)}, f32[128,256]{1,0:T(8,128)S(1)}, u32[]{:S(2)}, u32[]{:S(2)}) collective-permute-start(f32[128,256]{1,0:T(8,128)S(1)} %get-tuple-element.62), channel_id=1, source_target_pairs={{0,2},{1,3},{2,0},{3,1},{4,6},{5,7},{6,4},{7,5},{8,10},{9,11},{10,... | collective-permute-start | bytes 393224 | tf_op jit(solution)/shard_map/ppermute | solution.py:764
  39.6 6.7 %collective-permute-start.10 = (f32[8,1024]{1,0:T(8,128)S(1)}, f32[8,1024]{1,0:T(8,128)S(1)}, u32[]{:S(2)}, u32[]{:S(2)}) collective-permute-start(f32[8,1024]{1,0:T(8,128)S(1)} %pad_maximum_fusion.2.refs_0_), channel_id=1, source_target_pairs={{0,8},{4,12},{8,0},{12,4},{1,9},{5,13},{9,1},{13,5},{2,10},{6,14},... | collective-permute-start | bytes 98312 | tf_op jit(solution)/shard_map/ppermute | solution.py:755
  42.2 5.7 %collective-permute-start.11 = (f32[8,1024]{1,0:T(8,128)S(1)}, f32[8,1024]{1,0:T(8,128)S(1)}, u32[]{:S(2)}, u32[]{:S(2)}) collective-permute-start(f32[8,1024]{1,0:T(8,128)S(1)} %pad_maximum_fusion.2.refs_0_), channel_id=1, source_target_pairs={{0,12},{4,8},{8,4},{12,0},{1,13},{5,9},{9,5},{13,1},{2,14},{6,10},... | collective-permute-start | bytes 98312 | tf_op jit(solution)/shard_map/ppermute | solution.py:755
  43.2 4.8 %collective-permute-start.9 = (f32[8,1024]{1,0:T(8,128)S(1)}, f32[8,1024]{1,0:T(8,128)S(1)}, u32[]{:S(2)}, u32[]{:S(2)}) collective-permute-start(f32[8,1024]{1,0:T(8,128)S(1)} %pad_maximum_fusion.2.refs_0_), channel_id=1, source_target_pairs={{0,4},{4,0},{8,12},{12,8},{1,5},{5,1},{9,13},{13,9},{2,6},{6,2},{1... | collective-permute-start | bytes 98312 | tf_op jit(solution)/shard_map/ppermute | solution.py:755

commit v9 on v8

--- a/solution.py
+++ b/solution.py
@@ -781,12 +781,11 @@
     scalars = jnp.concatenate([jnp.stack([c * ns + s, s, c]), quarters, places]).astype(jnp.int32)
     stacked = jnp.stack([a[:BLOCK] for a in pays], 0)
     heads = [stacked] + [across(stacked, (k, 0), nh, nc) for k in range(1, nh)]
-    side = across(stacked, (0, 1), nh, nc)
     conv, vocab = conv_x.shape[0], xz_table.shape[0]
     *tables, w, w2, rate = call_tables(scalars, raw)
     gated, *kept = call_forward(scalars, pays, w, w2, rate, tables[0], conv)
     heads, _ = lax.optimization_barrier((heads, gated))
-    cots = [heads[0], side]
+    cots = [heads[0], across(heads[0], (0, 1), nh, nc)]
     for a in heads[1:]:
         cots += [a, across(a, (0, 1), nh, nc)]
     hop = lambda x, k: lax.ppermute(x, "seq", [(i, i ^ k) for i in range(ns)])

time: 49.6 us -> 49.6 us (level)
    ppermute x11, starting transfers between devices: 6.05 us -> 6.55 us  [across(): return lax.ppermute(x, ('head', 'sub'), pairs)]
    ppermute x3, starting transfers between devices: 5.98 us -> 5.48 us  [by_channel(): hop = lambda x, k: lax.ppermute(x, 'seq', [(i, i ^ k) for i in range(ns)])]
where the time goes in v9:
time: 49.6 us; the launch traced here: 49.3 us
  starting transfers between devices  21.4 us (43%)
  Pallas kernels  14.8 us (30%)
  waiting for transfers between devices  7.08 us (14%)
  other arithmetic  3.73 us (8%)
  local copies, waits for them, and re-layouts  1.51 us (3%)
  between operations  0.77 us (2%)
    ppermute x6, starting transfers between devices, around(): lax.ppermute(x, axis, [(i, i ^ k) for i in range(n)])  9.34 us
    ppermute x11, starting transfers between devices, across(): return lax.ppermute(x, ('head', 'sub'), pairs)  6.55 us
    ppermute x3, starting transfers between devices, by_channel(): hop = lambda x, k: lax.ppermute(x, 'seq', [(i, i ^ k) for i in range(ns)])  5.48 us
    pallas_call x1, Pallas kernels, call_backward(): pl.pallas_call(functools.partial(backward_kernel, ns=ns, nq=len(cots), co...  5.28 us
    ppermute x11, waiting for transfers between devices, across(): return lax.ppermute(x, ('head', 'sub'), pairs)  3.63 us
    pallas_call x1, Pallas kernels, call_forward(): pl.pallas_call(functools.partial(forward_kernel, ns=ns, conv=conv), out_s...  3.53 us
    ppermute x6, waiting for transfers between devices, around(): lax.ppermute(x, axis, [(i, i ^ k) for i in range(n)])  3.44 us
    pallas_call x1, Pallas kernels, call_weight(): pl.pallas_call(functools.partial(weight_kernel, ns=ns, nh=nh, nc=nc), out...  2.95 us
  transfers between devices with their start and end apart: 20, of which 7 were waited for; matrix products, arithmetic and copies ran while one was open for 6% of the time, Pallas kernels for 26%

profile of v9, /device:TPU:0, one launch (start us, length us, event | category | flops | bytes accessed | tf_op | source)
XLA Modules:
  0.0 49.3 jit_solution(18440058977604030099)
XLA Ops:
  0.6 0.7 %convert_bitcast_fusion = bf16[1,128]{1,0:T(2,128)(2,1)S(1)} fusion(s32[128]{0:T(128)} %param.11), kind=kLoop, calls=%fused_computation.42 | loop fusion | flops 128 | bytes 768 | tf_op jit(solution)/shard_map/reshape | solution.py:775
  1.3 0.8 %fusion.1.refs_0_ = bf16[144,256]{1,0:T(8,128)(2,1)S(1)} fusion(bf16[1,128]{1,0:T(2,128)(2,1)S(1)} %convert_bitcast_fusion, bf16[128,256]{1,0:T(8,128)(2,1)} %param.21), kind=kLoop, calls=%fused_computation.3 | loop fusion | flops 221184 | bytes 139520 | tf_op jit(solution)/shard_map/concatenate | solution.py:776
  2.1 3.0 %collective-permute-start = (bf16[144,256]{1,0:T(8,128)(2,1)S(1)}, bf16[144,256]{1,0:T(8,128)(2,1)S(1)}, u32[]{:S(2)}, u32[]{:S(2)}) collective-permute-start(bf16[144,256]{1,0:T(8,128)(2,1)S(1)} %fusion.1.refs_0_), channel_id=1, source_target_pairs={{0,4},{4,0},{8,12},{12,8},{1,5},{5,1},{9,13},{13,9},{2,6},{6,2},{1... | collective-permute-start | bytes 221192 | tf_op jit(solution)/shard_map/ppermute | solution.py:755
  5.2 2.6 %collective-permute-start.1 = (bf16[144,256]{1,0:T(8,128)(2,1)S(1)}, bf16[144,256]{1,0:T(8,128)(2,1)S(1)}, u32[]{:S(2)}, u32[]{:S(2)}) collective-permute-start(bf16[144,256]{1,0:T(8,128)(2,1)S(1)} %fusion.1.refs_0_), channel_id=1, source_target_pairs={{0,8},{4,12},{8,0},{12,4},{1,9},{5,13},{9,1},{13,5},{2,10},{6,14},... | collective-permute-start | bytes 221192 | tf_op jit(solution)/shard_map/ppermute | solution.py:755
  7.8 0.7 %reshape.16 = bf16[10,1024]{1,0:T(8,128)(2,1)S(1)} reshape(bf16[5,2,1024]{2,1,0:T(2,128)(2,1)} %param.13) | data formatting | bytes 40960 | tf_op jit(solution)/shard_map/reshape | solution.py:579
  8.5 0.7 %pad_maximum_fusion.1.refs_0_ = bf16[14,1024]{1,0:T(8,128)(2,1)S(1)} fusion(bf16[4,1024]{1,0:T(4,128)(2,1)} %param.16, bf16[10,1024]{1,0:T(8,128)(2,1)S(1)} %reshape.16), kind=kLoop, calls=%fused_computation.7 | loop fusion | flops 57344 | bytes 57344 | tf_op jit(solution)/shard_map/concatenate | solution.py:579
  9.2 0.7 %pad_maximum_fusion.3.refs_1_ = bf16[9,2,128]{2,1,0:T(2,128)(2,1)S(1)} fusion(bf16[4,2,128]{2,1,0:T(2,128)(2,1)} %param.17, bf16[5,2,128]{2,1,0:T(2,128)(2,1)} %param.14), kind=kLoop, calls=%fused_computation.10 | loop fusion | flops 2304 | bytes 9216 | tf_op jit(solution)/shard_map/concatenate | solution.py:580
  10.0 0.7 %pad_maximum_fusion.4.refs_2_ = f32[7,16]{1,0:T(8,128)S(1)} fusion(f32[1,16]{1,0:T(1,128)} %bitcast.15, f32[1,16]{1,0:T(1,128)} %bitcast.16, f32[5,16]{1,0:T(8,128)} %param.15), kind=kLoop, calls=%fused_computation.11 | loop fusion | flops 224 | bytes 896 | tf_op jit(solution)/shard_map/concatenate | solution.py:581
  10.8 0.7 %copy-done.1 = s32[5]{0:T(128)S(1)} copy-done((s32[5]{0:T(128)S(1)}, s32[5]{0:T(128)}, u32[]{:S(2)}) %copy-start.1) | copy-done | bytes 44
  11.4 0.8 %tables.1 = (f32[32,128]{1,0:T(8,128)S(1)}, f32[16,256]{1,0:T(8,128)S(1)}, f32[8,128]{1,0:T(8,128)S(1)}, f32[8,128]{1,0:T(8,128)S(1)}, bf16[128,1792]{1,0:T(8,12...) custom-call(s32[15]{0:T(128)S(1)} %concatenate.18.scalars, s32[5]{0:T(128)S(1)} %copy-done.1, ...), custom_call_target="tpu_custom_call" | custom-call | flops 2000000000 | bytes 1000000 | tf_op jit(solution)/shard_map/tables/pallas_call | solution.py:567
  12.2 1.8 %collective-permute-done.2.refs_3_ = bf16[144,256]{1,0:T(8,128)(2,1)S(1)} collective-permute-done((bf16[144,256]{1,0:T(8,128)(2,1)S(1)}, bf16[144,256]{1,0:T(8,128)(2,1)S(1)}, u32[]{:S(2)}, u32[]{:S(2)}) %collective-permute-start.2) | collective-permute-done | bytes 73760 | tf_op jit(solution)/shard_map/ppermute | solution.py:755
  14.1 1.6 %collective-permute-start.3 = (bf16[4,128,256]{2,1,0:T(8,128)(2,1)S(1)}, bf16[4,128,256]{2,1,0:T(8,128)(2,1)S(1)}, u32[]{:S(2)}, u32[]{:S(2)}) collective-permute-start(bf16[4,128,256]{2,1,0:T(8,128)(2,1)S(1)} %pad_maximum_fusion.refs_4_.refs_8_), channel_id=1, source_target_pairs={{0,2},{1,3},{2,0},{3,1},{4,6},{5,7},{6,4},{7,5},{8,10},{9,11},{10,... | collective-permute-start | bytes 786440 | tf_op jit(solution)/shard_map/ppermute | solution.py:764
  15.7 3.5 %mix_forward.1 = (bf16[128,512]{1,0:T(8,128)(2,1)S(1)}, f32[8,512]{1,0:T(8,128)S(1)}, f32[8,512]{1,0:T(8,128)S(1)}, f32[8,512]{1,0:T(8,128)S(1)}, bf16[64,512]{1...) custom-call(s32[15]{0:T(128)S(1)} %concatenate.18.scalars, ...), custom_call_target="tpu_custom_call" | custom-call | flops 5000000000 | bytes 524288 | tf_op jit(solution)/shard_map/mix_forward/pallas_call | solution.py:589
  19.2 1.3 %collective-permute-done.3.refs_6_.refs_10_ = bf16[4,128,256]{2,1,0:T(8,128)(2,1)S(1)} collective-permute-done((bf16[4,128,256]{2,1,0:T(8,128)(2,1)S(1)}, bf16[4,128,256]{2,1,0:T(8,128)(2,1)S(1)}, u32[]{:S(2)}, u32[]{:S(2)}) %collective-permute-start.3) | collective-permute-done | bytes 262176 | tf_op jit(solution)/shard_map/ppermute | solution.py:764
  20.6 0.5 %collective-permute-start.5 = (bf16[4,128,256]{2,1,0:T(8,128)(2,1)S(1)}, bf16[4,128,256]{2,1,0:T(8,128)(2,1)S(1)}, u32[]{:S(2)}, u32[]{:S(2)}) collective-permute-start(bf16[4,128,256]{2,1,0:T(8,128)(2,1)S(1)} %collective-permute-done.3.refs_6_.refs_10_), channel_id=1, source_target_pairs={{0,1},{1,0},{2,3},{3,2},{4,5},{5,4},{6,7},{7,6},{8,9},{9,8},{10,11... | collective-permute-start | bytes 786440 | tf_op jit(solution)/shard_map/ppermute | solution.py:764
  21.1 1.1 %collective-permute-start.12 = (bf16[128,512]{1,0:T(8,128)(2,1)S(1)}, bf16[128,512]{1,0:T(8,128)(2,1)S(1)}, u32[]{:S(2)}, u32[]{:S(2)}) collective-permute-start(bf16[128,512]{1,0:T(8,128)(2,1)S(1)} %get-tuple-element.44.refs_0_), channel_id=1, source_target_pairs={{0,4},{4,0},{8,12},{12,8},{1,5},{5,1},{9,13},{13,9},{2,6},{6,2},{1... | collective-permute-start | bytes 393224 | tf_op jit(solution)/shard_map/ppermute | solution.py:791
  22.1 2.4 %collective-permute-start.13 = (bf16[128,512]{1,0:T(8,128)(2,1)S(1)}, bf16[128,512]{1,0:T(8,128)(2,1)S(1)}, u32[]{:S(2)}, u32[]{:S(2)}) collective-permute-start(bf16[128,512]{1,0:T(8,128)(2,1)S(1)} %get-tuple-element.44.refs_0_), channel_id=1, source_target_pairs={{0,8},{4,12},{8,0},{12,4},{1,9},{5,13},{9,1},{13,5},{2,10},{6,14},... | collective-permute-start | bytes 393224 | tf_op jit(solution)/shard_map/ppermute | solution.py:791
  24.5 5.3 %mix_backward.1 = f32[8,640]{1,0:T(8,128)S(1)} custom-call(s32[15]{0:T(128)S(1)} %concatenate.18.scalars, f32[32,128]{1,0:T(8,128)S(1)} %get-tuple-element.37.refs_7_.refs_0_, f32[16,256]{1,0:T(8,128)S(1)} %get-tuple-element.38.refs_1_, f32[8,128]{1,0:T(8,128)S(1)} %get-tuple-element.39.refs_2_, f32[8,128]{1,0:T(8,128)S(1)} %get-tuple-element.40.refs_3_, ...), custom_call_target="tpu_custom_call" | custom-call | flops 6000000000 | bytes 524288 | tf_op jit(solution)/shard_map/mix_backward/pallas_call | solution.py:610
  29.8 2.0 %collective-permute-start.14 = (bf16[128,512]{1,0:T(8,128)(2,1)S(1)}, bf16[128,512]{1,0:T(8,128)(2,1)S(1)}, u32[]{:S(2)}, u32[]{:S(2)}) collective-permute-start(bf16[128,512]{1,0:T(8,128)(2,1)S(1)} %collective-permute-done.13.refs_2_), channel_id=1, source_target_pairs={{0,4},{4,0},{8,12},{12,8},{1,5},{5,1},{9,13},{13,9},{2,6},{6,2},{1... | collective-permute-start | bytes 393224 | tf_op jit(solution)/shard_map/ppermute | solution.py:791
  31.9 1.5 %collective-permute-start.7 = (f32[8,256]{1,0:T(8,128)S(1)}, f32[8,256]{1,0:T(8,128)S(1)}, u32[]{:S(2)}, u32[]{:S(2)}) collective-permute-start(f32[8,256]{1,0:T(8,128)S(1)} %slice.35), channel_id=1, source_target_pairs={{0,2},{1,3},{2,0},{3,1},{4,6},{5,7},{6,4},{7,5},{8,10},{9,11},{10,... | collective-permute-start | bytes 24584 | tf_op jit(solution)/shard_map/ppermute | solution.py:764
  33.4 0.4 collective-permute-start.8
  34.2 1.3 %collective-permute-done.7 = f32[8,256]{1,0:T(8,128)S(1)} collective-permute-done((f32[8,256]{1,0:T(8,128)S(1)}, f32[8,256]{1,0:T(8,128)S(1)}, u32[]{:S(2)}, u32[]{:S(2)}) %collective-permute-start.7) | collective-permute-done | bytes 8224 | tf_op jit(solution)/shard_map/ppermute | solution.py:764
  35.5 0.5 %collective-permute-start.18 = (bf16[128,512]{1,0:T(8,128)(2,1)S(1)}, bf16[128,512]{1,0:T(8,128)(2,1)S(1)}, u32[]{:S(2)}, u32[]{:S(2)}) collective-permute-start(bf16[128,512]{1,0:T(8,128)(2,1)S(1)} %collective-permute-done.14.refs_3_), channel_id=1, source_target_pairs={{0,1},{1,0},{2,3},{3,2},{4,5},{5,4},{6,7},{7,6},{8,9},{9,8},{10,11... | collective-permute-start | bytes 393224 | tf_op jit(solution)/shard_map/ppermute | solution.py:764
  36.0 0.4 collective-permute-done.8
  36.4 0.4 collective-permute-done.16.refs_5_
  37.1 0.9 %layer_out.1 = (f32[128,256]{1,0:T(8,128)S(1)}, f32[128,256]{1,0:T(8,128)S(1)}) custom-call(s32[15]{0:T(128)S(1)} %concatenate.18.scalars, bf16[128,512]{1,0:T(8,128)(2,1)S(1)} %get-tuple-element.44.refs_0_, bf16[128,512]{1,0:T(8,128)(2,1)S(1)} %collective-permute-done.12.refs_1_, bf16[128,512]{1,0:T(8,128)(2,1)S(1)} %collective-permute-done.13.refs_2_, ...), custom_call_target="tpu_custom_call" | custom-call | tf_op jit(solution)/shard_map/layer_out/pallas_call | solution.py:648
  38.0 1.6 %collective-permute-start.19 = (f32[128,256]{1,0:T(8,128)S(1)}, f32[128,256]{1,0:T(8,128)S(1)}, u32[]{:S(2)}, u32[]{:S(2)}) collective-permute-start(f32[128,256]{1,0:T(8,128)S(1)} %get-tuple-element.62), channel_id=1, source_target_pairs={{0,2},{1,3},{2,0},{3,1},{4,6},{5,7},{6,4},{7,5},{8,10},{9,11},{10,... | collective-permute-start | bytes 393224 | tf_op jit(solution)/shard_map/ppermute | solution.py:764
  39.6 2.6 %collective-permute-start.10 = (f32[8,1024]{1,0:T(8,128)S(1)}, f32[8,1024]{1,0:T(8,128)S(1)}, u32[]{:S(2)}, u32[]{:S(2)}) collective-permute-start(f32[8,1024]{1,0:T(8,128)S(1)} %pad_maximum_fusion.2.refs_0_), channel_id=1, source_target_pairs={{0,8},{4,12},{8,0},{12,4},{1,9},{5,13},{9,1},{13,5},{2,10},{6,14},... | collective-permute-start | bytes 98312 | tf_op jit(solution)/shard_map/ppermute | solution.py:755
  42.2 0.8 %collective-permute-start.11 = (f32[8,1024]{1,0:T(8,128)S(1)}, f32[8,1024]{1,0:T(8,128)S(1)}, u32[]{:S(2)}, u32[]{:S(2)}) collective-permute-start(f32[8,1024]{1,0:T(8,128)S(1)} %pad_maximum_fusion.2.refs_0_), channel_id=1, source_target_pairs={{0,12},{4,8},{8,4},{12,0},{1,13},{5,9},{9,5},{13,1},{2,14},{6,10},... | collective-permute-start | bytes 98312 | tf_op jit(solution)/shard_map/ppermute | solution.py:755
  43.3 3.0 %weight_grad.1 = (f32[1024,1024]{1,0:T(8,128)}, f32[8,128]{1,0:T(8,128)S(1)}) custom-call(s32[15]{0:T(128)S(1)} %concatenate.18.scalars, bf16[128,512]{1,0:T(8,128)(2,1)S(1)} %get-tuple-element.44.refs_0_, bf16[128,512]{1,0:T(8,128)(2,1)S(1)} %collective-permute-done.12.refs_1_, bf16[128,512]{1,0:T(8,128)(2,1)S(1)} %collective-permute-done.13.refs_2_, ...), custom_call_target="tpu_custom_call" | custom-call | flops 1073741824 | bytes 6291456 | tf_op jit(solution)/shard_map/weight_grad/pallas_call | solution.py:688
  46.3 1.7 %collective-permute-done.11.refs_3_ = f32[8,1024]{1,0:T(8,128)S(1)} collective-permute-done((f32[8,1024]{1,0:T(8,128)S(1)}, f32[8,1024]{1,0:T(8,128)S(1)}, u32[]{:S(2)}, u32[]{:S(2)}) %collective-permute-start.11) | collective-permute-done | bytes 32800 | tf_op jit(solution)/shard_map/ppermute | solution.py:755
  47.9 1.3 %place_grads.1 = (bf16[128,256]{1,0:T(8,128)(2,1)}, f32[5,2,1024]{2,1,0:T(2,128)}, f32[5,2,128]{2,1,0:T(2,128)}, f32[5,16]{1,0:T(8,128)}) custom-call(s32[15]{0:T(128)S(1)} %concatenate.18.scalars, f32[8,1024]{1,0:T(8,128)S(1)} %pad_maximum_fusion.2.refs_0_, f32[8,1024]{1,0:T(8,128)S(1)} %collective-permute-done.9.refs_1_, ...), custom_call_target="tpu_custom_call" | custom-call | tf_op jit(solution)/shard_map/place_grads/pallas_call | solution.py:740
  (38 shorter events, 1.2 us)
Async XLA Ops:
  2.1 11.9 %collective-permute-start = (bf16[144,256]{1,0:T(8,128)(2,1)S(1)}, bf16[144,256]{1,0:T(8,128)(2,1)S(1)}, u32[]{:S(2)}, u32[]{:S(2)}) collective-permute-start(bf16[144,256]{1,0:T(8,128)(2,1)S(1)} %fusion.1.refs_0_), channel_id=1, source_target_pairs={{0,4},{4,0},{8,12},{12,8},{1,5},{5,1},{9,13},{13,9},{2,6},{6,2},{1... | collective-permute-start | bytes 221192 | tf_op jit(solution)/shard_map/ppermute | solution.py:755
  5.2 8.9 %collective-permute-start.1 = (bf16[144,256]{1,0:T(8,128)(2,1)S(1)}, bf16[144,256]{1,0:T(8,128)(2,1)S(1)}, u32[]{:S(2)}, u32[]{:S(2)}) collective-permute-start(bf16[144,256]{1,0:T(8,128)(2,1)S(1)} %fusion.1.refs_0_), channel_id=1, source_target_pairs={{0,8},{4,12},{8,0},{12,4},{1,9},{5,13},{9,1},{13,5},{2,10},{6,14},... | collective-permute-start | bytes 221192 | tf_op jit(solution)/shard_map/ppermute | solution.py:755
  7.7 6.3 %collective-permute-start.2 = (bf16[144,256]{1,0:T(8,128)(2,1)S(1)}, bf16[144,256]{1,0:T(8,128)(2,1)S(1)}, u32[]{:S(2)}, u32[]{:S(2)}) collective-permute-start(bf16[144,256]{1,0:T(8,128)(2,1)S(1)} %fusion.1.refs_0_), channel_id=1, source_target_pairs={{0,12},{4,8},{8,4},{12,0},{1,13},{5,9},{9,5},{13,1},{2,14},{6,10},... | collective-permute-start | bytes 221192 | tf_op jit(solution)/shard_map/ppermute | solution.py:755
  10.8 0.7 %copy-start.1 = (s32[5]{0:T(128)S(1)}, s32[5]{0:T(128)}, u32[]{:S(2)}) copy-start(s32[5]{0:T(128)} %basemap.1) | copy-start | bytes 64
  11.4 2.6 %copy-start.2 = (bf16[128,256]{1,0:T(8,128)(2,1)S(1)}, bf16[128,256]{1,0:T(8,128)(2,1)}, u32[]{:S(2)}) copy-start(bf16[128,256]{1,0:T(8,128)(2,1)} %param.21) | copy-start | bytes 196612
  14.1 6.4 %collective-permute-start.3 = (bf16[4,128,256]{2,1,0:T(8,128)(2,1)S(1)}, bf16[4,128,256]{2,1,0:T(8,128)(2,1)S(1)}, u32[]{:S(2)}, u32[]{:S(2)}) collective-permute-start(bf16[4,128,256]{2,1,0:T(8,128)(2,1)S(1)} %pad_maximum_fusion.refs_4_.refs_8_), channel_id=1, source_target_pairs={{0,2},{1,3},{2,0},{3,1},{4,6},{5,7},{6,4},{7,5},{8,10},{9,11},{10,... | collective-permute-start | bytes 786440 | tf_op jit(solution)/shard_map/ppermute | solution.py:764
  15.7 8.9 %copy-start = (bf16[1024,1024]{1,0:T(8,128)(2,1)S(1)}, bf16[1024,1024]{1,0:T(8,128)(2,1)}, u32[]{:S(2)}) copy-start(bf16[1024,1024]{1,0:T(8,128)(2,1)} %refs_8_.3) | copy-start | bytes 6291460
  20.5 4.0 %collective-permute-start.4 = (bf16[4,128,256]{2,1,0:T(8,128)(2,1)S(1)}, bf16[4,128,256]{2,1,0:T(8,128)(2,1)S(1)}, u32[]{:S(2)}, u32[]{:S(2)}) collective-permute-start(bf16[4,128,256]{2,1,0:T(8,128)(2,1)S(1)} %pad_maximum_fusion.refs_4_.refs_8_), channel_id=1, source_target_pairs={{0,1},{1,0},{2,3},{3,2},{4,5},{5,4},{6,7},{7,6},{8,9},{9,8},{10,11... | collective-permute-start | bytes 786440 | tf_op jit(solution)/shard_map/ppermute | solution.py:764
  20.6 4.0 %collective-permute-start.5 = (bf16[4,128,256]{2,1,0:T(8,128)(2,1)S(1)}, bf16[4,128,256]{2,1,0:T(8,128)(2,1)S(1)}, u32[]{:S(2)}, u32[]{:S(2)}) collective-permute-start(bf16[4,128,256]{2,1,0:T(8,128)(2,1)S(1)} %collective-permute-done.3.refs_6_.refs_10_), channel_id=1, source_target_pairs={{0,1},{1,0},{2,3},{3,2},{4,5},{5,4},{6,7},{7,6},{8,9},{9,8},{10,11... | collective-permute-start | bytes 786440 | tf_op jit(solution)/shard_map/ppermute | solution.py:764
  21.1 8.8 %collective-permute-start.12 = (bf16[128,512]{1,0:T(8,128)(2,1)S(1)}, bf16[128,512]{1,0:T(8,128)(2,1)S(1)}, u32[]{:S(2)}, u32[]{:S(2)}) collective-permute-start(bf16[128,512]{1,0:T(8,128)(2,1)S(1)} %get-tuple-element.44.refs_0_), channel_id=1, source_target_pairs={{0,4},{4,0},{8,12},{12,8},{1,5},{5,1},{9,13},{13,9},{2,6},{6,2},{1... | collective-permute-start | bytes 393224 | tf_op jit(solution)/shard_map/ppermute | solution.py:791
  22.1 7.7 %collective-permute-start.13 = (bf16[128,512]{1,0:T(8,128)(2,1)S(1)}, bf16[128,512]{1,0:T(8,128)(2,1)S(1)}, u32[]{:S(2)}, u32[]{:S(2)}) collective-permute-start(bf16[128,512]{1,0:T(8,128)(2,1)S(1)} %get-tuple-element.44.refs_0_), channel_id=1, source_target_pairs={{0,8},{4,12},{8,0},{12,4},{1,9},{5,13},{9,1},{13,5},{2,10},{6,14},... | collective-permute-start | bytes 393224 | tf_op jit(solution)/shard_map/ppermute | solution.py:791
  29.8 5.7 %collective-permute-start.14 = (bf16[128,512]{1,0:T(8,128)(2,1)S(1)}, bf16[128,512]{1,0:T(8,128)(2,1)S(1)}, u32[]{:S(2)}, u32[]{:S(2)}) collective-permute-start(bf16[128,512]{1,0:T(8,128)(2,1)S(1)} %collective-permute-done.13.refs_2_), channel_id=1, source_target_pairs={{0,4},{4,0},{8,12},{12,8},{1,5},{5,1},{9,13},{13,9},{2,6},{6,2},{1... | collective-permute-start | bytes 393224 | tf_op jit(solution)/shard_map/ppermute | solution.py:791
  31.9 2.2 %collective-permute-start.6 = (f32[8,640]{1,0:T(8,128)S(1)}, f32[8,640]{1,0:T(8,128)S(1)}, u32[]{:S(2)}, u32[]{:S(2)}) collective-permute-start(f32[8,640]{1,0:T(8,128)S(1)} %mix_backward.1), channel_id=1, source_target_pairs={{0,1},{1,0},{2,3},{3,2},{4,5},{5,4},{6,7},{7,6},{8,9},{9,8},{10,11... | collective-permute-start | bytes 61448 | tf_op jit(solution)/shard_map/ppermute | solution.py:764
  31.9 3.7 %collective-permute-start.7 = (f32[8,256]{1,0:T(8,128)S(1)}, f32[8,256]{1,0:T(8,128)S(1)}, u32[]{:S(2)}, u32[]{:S(2)}) collective-permute-start(f32[8,256]{1,0:T(8,128)S(1)} %slice.35), channel_id=1, source_target_pairs={{0,2},{1,3},{2,0},{3,1},{4,6},{5,7},{6,4},{7,5},{8,10},{9,11},{10,... | collective-permute-start | bytes 24584 | tf_op jit(solution)/shard_map/ppermute | solution.py:764
  33.4 3.1 %collective-permute-start.8 = (f32[8,256]{1,0:T(8,128)S(1)}, f32[8,256]{1,0:T(8,128)S(1)}, u32[]{:S(2)}, u32[]{:S(2)}) collective-permute-start(f32[8,256]{1,0:T(8,128)S(1)} %slice.35), channel_id=1, source_target_pairs={{0,3},{1,2},{2,1},{3,0},{4,7},{5,6},{6,5},{7,4},{8,11},{9,10},{10,... | collective-permute-start | bytes 24584 | tf_op jit(solution)/shard_map/ppermute | solution.py:764
  33.7 2.7 %collective-permute-start.15 = (bf16[128,512]{1,0:T(8,128)(2,1)S(1)}, bf16[128,512]{1,0:T(8,128)(2,1)S(1)}, u32[]{:S(2)}, u32[]{:S(2)}) collective-permute-start(bf16[128,512]{1,0:T(8,128)(2,1)S(1)} %get-tuple-element.44.refs_0_), channel_id=1, source_target_pairs={{0,1},{1,0},{2,3},{3,2},{4,5},{5,4},{6,7},{7,6},{8,9},{9,8},{10,11... | collective-permute-start | bytes 393224 | tf_op jit(solution)/shard_map/ppermute | solution.py:764
  34.0 2.9 %collective-permute-start.17 = (bf16[128,512]{1,0:T(8,128)(2,1)S(1)}, bf16[128,512]{1,0:T(8,128)(2,1)S(1)}, u32[]{:S(2)}, u32[]{:S(2)}) collective-permute-start(bf16[128,512]{1,0:T(8,128)(2,1)S(1)} %collective-permute-done.13.refs_2_), channel_id=1, source_target_pairs={{0,1},{1,0},{2,3},{3,2},{4,5},{5,4},{6,7},{7,6},{8,9},{9,8},{10,11... | collective-permute-start | bytes 393224 | tf_op jit(solution)/shard_map/ppermute | solution.py:764
  35.5 1.3 %collective-permute-start.16 = (bf16[128,512]{1,0:T(8,128)(2,1)S(1)}, bf16[128,512]{1,0:T(8,128)(2,1)S(1)}, u32[]{:S(2)}, u32[]{:S(2)}) collective-permute-start(bf16[128,512]{1,0:T(8,128)(2,1)S(1)} %collective-permute-done.12.refs_1_), channel_id=1, source_target_pairs={{0,1},{1,0},{2,3},{3,2},{4,5},{5,4},{6,7},{7,6},{8,9},{9,8},{10,11... | collective-permute-start | bytes 393224 | tf_op jit(solution)/shard_map/ppermute | solution.py:764
  35.5 1.5 %collective-permute-start.18 = (bf16[128,512]{1,0:T(8,128)(2,1)S(1)}, bf16[128,512]{1,0:T(8,128)(2,1)S(1)}, u32[]{:S(2)}, u32[]{:S(2)}) collective-permute-start(bf16[128,512]{1,0:T(8,128)(2,1)S(1)} %collective-permute-done.14.refs_3_), channel_id=1, source_target_pairs={{0,1},{1,0},{2,3},{3,2},{4,5},{5,4},{6,7},{7,6},{8,9},{9,8},{10,11... | collective-permute-start | bytes 393224 | tf_op jit(solution)/shard_map/ppermute | solution.py:764
  38.0 10.0 %collective-permute-start.19 = (f32[128,256]{1,0:T(8,128)S(1)}, f32[128,256]{1,0:T(8,128)S(1)}, u32[]{:S(2)}, u32[]{:S(2)}) collective-permute-start(f32[128,256]{1,0:T(8,128)S(1)} %get-tuple-element.62), channel_id=1, source_target_pairs={{0,2},{1,3},{2,0},{3,1},{4,6},{5,7},{6,4},{7,5},{8,10},{9,11},{10,... | collective-permute-start | bytes 393224 | tf_op jit(solution)/shard_map/ppermute | solution.py:764
  39.6 6.7 %collective-permute-start.10 = (f32[8,1024]{1,0:T(8,128)S(1)}, f32[8,1024]{1,0:T(8,128)S(1)}, u32[]{:S(2)}, u32[]{:S(2)}) collective-permute-start(f32[8,1024]{1,0:T(8,128)S(1)} %pad_maximum_fusion.2.refs_0_), channel_id=1, source_target_pairs={{0,8},{4,12},{8,0},{12,4},{1,9},{5,13},{9,1},{13,5},{2,10},{6,14},... | collective-permute-start | bytes 98312 | tf_op jit(solution)/shard_map/ppermute | solution.py:755
  42.2 5.7 %collective-permute-start.11 = (f32[8,1024]{1,0:T(8,128)S(1)}, f32[8,1024]{1,0:T(8,128)S(1)}, u32[]{:S(2)}, u32[]{:S(2)}) collective-permute-start(f32[8,1024]{1,0:T(8,128)S(1)} %pad_maximum_fusion.2.refs_0_), channel_id=1, source_target_pairs={{0,12},{4,8},{8,4},{12,0},{1,13},{5,9},{9,5},{13,1},{2,14},{6,10},... | collective-permute-start | bytes 98312 | tf_op jit(solution)/shard_map/ppermute | solution.py:755
  43.0 4.9 %collective-permute-start.9 = (f32[8,1024]{1,0:T(8,128)S(1)}, f32[8,1024]{1,0:T(8,128)S(1)}, u32[]{:S(2)}, u32[]{:S(2)}) collective-permute-start(f32[8,1024]{1,0:T(8,128)S(1)} %pad_maximum_fusion.2.refs_0_), channel_id=1, source_target_pairs={{0,4},{4,0},{8,12},{12,8},{1,5},{5,1},{9,13},{13,9},{2,6},{6,2},{1... | collective-permute-start | bytes 98312 | tf_op jit(solution)/shard_map/ppermute | solution.py:755
